TPU v7x, 256 devices: a whole 4x4x8 slice. The times are simulated.
256 devices in a mesh: group: 32 (over z, x_lo, core), rep: 8 (over x_hi, y).
Axes of the slice: x: 4 (x_hi: 2, x_lo: 2; x = x_hi * 2 + x_lo), y: 4, z: 8, core: 2. Of those that a mesh axis runs over, the one named last changes fastest.
Arguments:
- queries: bfloat16 [256, 256, 3072], P(('group', 'rep')), may hold values from -46 to 46
- keys: bfloat16 [256, 256, 3072], P(('group', 'rep')), may hold values from -46 to 46
- values: bfloat16 [256, 256, 3072], P(('group', 'rep')), may hold values from -24 to 24
- grad_output: bfloat16 [256, 256, 3072], P(('group', 'rep')), may hold values from -6 to 6
- weight_codes: bfloat16 [3072, 3072], P('group'), may hold values from -4 to 4
- weight_scales: float32 [3072, 12], P('group'), may hold values from 0.006 to 0.06
Outputs:
- grad_queries: bfloat16 [256, 256, 3072], P(('group', 'rep'))
- grad_keys: bfloat16 [256, 256, 3072], P(('group', 'rep'))
- grad_values: bfloat16 [256, 256, 3072], P(('group', 'rep'))
- grad_weight: float32 [3072, 3072], P(('group', 'rep'))
All inputs are finite; a program needn't handle non-finite values.
Results may differ from a plain program's by a relative error of at most 0.029.
Values may be sent and summed in bfloat16 or wider, within the bound.
No kernel may reach another device: no remote copies, remote signals or barrier semaphores. Data moves between devices by JAX's collectives and lax.ppermute only.
A program may use at most 128 MiB of HBM per device.

v0:
```python
import jax
import jax.numpy as jnp
from jax import lax
from jax.sharding import Mesh
from jax.sharding import PartitionSpec as P

HD = 128
GROUP = ("group_0", "group_1", "group_2")
GROUP_REP = ("group_0", "group_1", "group_2", "rep")


def from_everyone(value, axis):
    count = lax.axis_size(axis)
    return lax.all_to_all(
        jnp.broadcast_to(value[None], (count, *value.shape)), axis, 0, 0, tiled=True
    )


def in_order(pieces, dim):
    shape = list(pieces.shape[1:])
    shape[dim] *= pieces.shape[0]
    return jnp.moveaxis(pieces, 0, dim).reshape(shape)


def gather_axes(value, axes, dim):
    far, near = axes
    pieces = from_everyone(from_everyone(value, far), near)
    return in_order(pieces.swapaxes(0, 1).reshape(-1, *value.shape), dim)


def cut_along(value, dim, count):
    before, after = (value.shape[:dim], value.shape[dim + 1 :])
    return jnp.moveaxis(value.reshape(*before, count, -1, *after), dim, 0)


def sent_and_summed(value, axis, dim):
    count = lax.axis_size(axis)
    pieces = lax.all_to_all(cut_along(value, dim, count), axis, 0, 0, tiled=True)
    return jnp.sum(pieces, axis=0)


def sum_in_two_steps(value, axes, dim):
    far, near = axes
    pieces = cut_along(value, dim, lax.axis_size(far))
    nearer = sent_and_summed(pieces, near, dim + 1)
    arrived = lax.all_to_all(nearer, far, split_axis=0, concat_axis=0, tiled=True)
    return arrived.sum(axis=0)


def restore(code_rows, scale_rows):
    row_count = code_rows.shape[0]
    block_count = scale_rows.shape[1]
    spread = (
        code_rows.astype(jnp.float32).reshape(row_count, block_count, -1) * scale_rows[:, :, None]
    )
    return spread.reshape(row_count, -1).astype(jnp.bfloat16)


def forward_image(arrays_in):
    query, keyset, valueset = arrays_in
    seq_len = query.shape[0]
    head_count = query.shape[1] // HD
    query_heads = query.reshape(seq_len, head_count, HD)
    key_heads = keyset.reshape(seq_len, head_count, HD)
    value_heads = valueset.reshape(seq_len, head_count, HD)
    scores = jnp.einsum(
        "qhd,khd->hqk", query_heads, key_heads, preferred_element_type=jnp.float32
    ) * HD ** (-0.5)
    highest = jnp.max(scores, axis=2, keepdims=True)
    exponent = jnp.exp(scores - highest)
    probability = exponent / jnp.sum(exponent, axis=2, keepdims=True)
    weight_half = probability.astype(jnp.bfloat16)
    context = jnp.einsum(
        "hqk,khd->qhd", weight_half, value_heads, preferred_element_type=jnp.float32
    )
    return (probability, context.astype(jnp.bfloat16).reshape(seq_len, -1))


def backward_image(arrays_in):
    query, keyset, valueset, probability, grad_context = arrays_in
    seq_len = query.shape[0]
    head_count = query.shape[1] // HD
    query_heads = query.reshape(seq_len, head_count, HD)
    key_heads = keyset.reshape(seq_len, head_count, HD)
    value_heads = valueset.reshape(seq_len, head_count, HD)
    grad_heads = grad_context.reshape(seq_len, head_count, HD)
    weight_half = probability.astype(jnp.bfloat16)
    grad_value = jnp.einsum(
        "hqk,qhd->khd", weight_half, grad_heads, preferred_element_type=jnp.float32
    )
    dprobs = jnp.einsum("qhd,khd->hqk", grad_heads, value_heads, preferred_element_type=jnp.float32)
    row_delta = jnp.sum(probability * dprobs, axis=2, keepdims=True)
    dscores = (probability * (dprobs - row_delta) * HD ** (-0.5)).astype(jnp.bfloat16)
    grad_query = jnp.einsum("hqk,khd->qhd", dscores, key_heads, preferred_element_type=jnp.float32)
    grad_key = jnp.einsum("hqk,qhd->khd", dscores, query_heads, preferred_element_type=jnp.float32)
    return (
        grad_query.astype(jnp.bfloat16).reshape(seq_len, -1),
        grad_key.astype(jnp.bfloat16).reshape(seq_len, -1),
        grad_value.astype(jnp.bfloat16).reshape(seq_len, -1),
    )


def per_device(queries, keys, values, grad_output, weight_codes, weight_scales):
    image_count, seq_len, row_total = queries.shape
    feature_count = grad_output.shape[2]
    local_rows = image_count * seq_len
    probability, contexts = lax.map(forward_image, (queries, keys, values))
    context_flat = contexts.reshape(local_rows, row_total)
    output_flat = grad_output.reshape(local_rows, feature_count)
    group_count = lax.axis_size(GROUP)
    replica_count = lax.axis_size("rep")
    slab_rows = row_total // (group_count * replica_count)
    first_row = lax.axis_index("rep") * slab_rows
    codes_part = lax.dynamic_slice_in_dim(weight_codes, first_row, slab_rows, 0)
    scales_part = lax.dynamic_slice_in_dim(weight_scales, first_row, slab_rows, 0)
    all_output = lax.all_gather(output_flat, "rep", axis=0, tiled=True)
    split_context = jnp.moveaxis(
        context_flat.reshape(local_rows, group_count, replica_count, slab_rows), 2, 0
    )
    split_context = split_context.reshape(replica_count, local_rows, group_count * slab_rows)
    gathered_ctx = lax.all_to_all(split_context, "rep", split_axis=0, concat_axis=1, tiled=True)
    gathered_ctx = gathered_ctx.reshape(replica_count, local_rows, group_count * slab_rows)
    grad_columns = jnp.dot(
        all_output,
        restore(
            gather_axes(codes_part, (("group_0", "group_1"), "group_2"), 0),
            gather_axes(
                scales_part.astype(jnp.bfloat16), (("group_0", "group_1"), "group_2"), 0
            ).astype(scales_part.dtype),
        ).T,
        preferred_element_type=jnp.float32,
    ).astype(jnp.bfloat16)
    output_blocks = all_output.reshape(replica_count, local_rows, feature_count)
    device_terms = jnp.einsum(
        "rlp,rle->rpe", gathered_ctx, output_blocks, preferred_element_type=jnp.float32
    ).astype(jnp.bfloat16)
    grad_weight = sum_in_two_steps(
        jnp.sum(lax.optimization_barrier(device_terms).astype(jnp.float32), axis=0),
        (("group_0", "group_1"), "group_2"),
        0,
    )
    returned = lax.all_to_all(
        grad_columns.reshape(1, replica_count * local_rows, group_count * slab_rows),
        "rep",
        split_axis=1,
        concat_axis=0,
        tiled=True,
    )
    returned = jnp.moveaxis(
        returned.reshape(replica_count, local_rows, group_count, slab_rows), 0, 2
    )
    grad_context = returned.reshape(image_count, seq_len, row_total)
    grad_queries, grad_keys, grad_values = lax.map(
        backward_image, (queries, keys, values, probability, grad_context)
    )
    return (grad_queries, grad_keys, grad_values, grad_weight)


def solution(mesh):
    split = Mesh(
        mesh.devices.reshape(8, 2, 2, mesh.shape["rep"]), ("group_0", "group_1", "group_2", "rep")
    )
    return jax.shard_map(
        per_device,
        mesh=split,
        in_specs=(
            P(GROUP_REP, None, None),
            P(GROUP_REP, None, None),
            P(GROUP_REP, None, None),
            P(GROUP_REP, None, None),
            P(GROUP, None),
            P(GROUP, None),
        ),
        out_specs=(
            P(GROUP_REP, None, None),
            P(GROUP_REP, None, None),
            P(GROUP_REP, None, None),
            P(GROUP_REP, None),
        ),
        check_vma=False,
    )
```

profile of v0, /device:TPU:4, one launch (start us, length us, event | category | flops | bytes accessed | tf_op | source)
XLA Modules:
  0.0 398.7 jit_solution(12941961424991909647)
XLA Ops:
  7.9 0.9 dynamic-slice_convert_fusion
  9.5 9.2 %all-to-all-start.2 = ((bf16[16,12,12]{1,2,0:T(8,128)(2,1)}), bf16[16,12,12]{1,2,0:T(8,128)(2,1)S(1)}, u32[]{:S(2)}, u32[]{:S(2)}) async-start(bf16[16,12,12]{1,2,0:T(8,128)(2,1)} %broadcast_in_dim.52), calls=%async_computation.2 | async-start | bytes 131072 | tf_op jit(solution)/shard_map/all_to_all | solution.py:14
  18.7 9.0 %all-to-all-done.2 = bf16[16,12,12]{1,2,0:T(8,128)(2,1)S(1)} async-done(((bf16[16,12,12]{1,2,0:T(8,128)(2,1)}), bf16[16,12,12]{1,2,0:T(8,128)(2,1)S(1)}, u32[]{:S(2)}, u32[]{:S(2)}) %all-to-all-start.2) | async-done | bytes 4640 | tf_op jit(solution)/shard_map/all_to_all | solution.py:14
  27.9 3.7 all_to_all.48
  31.6 1.3 broadcast_in_dim.50
  33.0 4.4 %all-to-all-start = ((bf16[16,12,3072]{2,1,0:T(8,128)(2,1)}), bf16[16,12,3072]{2,1,0:T(8,128)(2,1)}, u32[]{:S(2)}, u32[]{:S(2)}) async-start(bf16[16,12,3072]{2,1,0:T(8,128)(2,1)} %broadcast_in_dim.50), calls=%async_computation | async-start | bytes 3145728 | tf_op jit(solution)/shard_map/all_to_all | solution.py:14
  37.4 1.6 copy.148
  39.0 2.6 copy.147
  41.6 1.7 copy.149
  43.3 7.4 %fusion.43 = (f32[24,256]{1,0:T(8,128)S(1)}, f32[24,256,256]{1,2,0:T(8,128)}) fusion(bf16[256,24,128]{0,2,1:T(8,128)(2,1)} %bitcast.77, bf16[256,24,128]{0,2,1:T(8,128)(2,1)} %bitcast.79), kind=kOutput, calls=%fused_computation.38 | convolution fusion | flops 407372032 | bytes 9461760 | tf_op jit(solution)/shard_map/while/body/eval_jaxpr/sub | solution.py:70
  50.7 4.6 %fusion.33 = bf16[256,24,128]{0,2,1:T(8,128)(2,1)} fusion(bf16[256,24,128]{0,2,1:T(8,128)(2,1)S(1)} %bitcast.72, f32[24,256,256]{1,2,0:T(8,128)} %get-tuple-element.74, f32[24,256]{1,0:T(8,128)S(1)} %get-tuple-element.73), kind=kOutput, calls=%fused_computation.28 | convolution fusion | flops 406585344 | bytes 9461760 | tf_op jit(solution)/shard_map/while/body/eval_jaxpr/hqk,khd->qhd/dot_general | solution.py:73
  55.3 2.4 reshape_reshape.8
  58.4 1.5 copy.136
  60.5 2.4 mul.32
  63.0 6.1 %copy.122 = f32[384,3072]{1,0:T(8,128)} copy(f32[384,3072]{0,1:T(8,128)} %bitcast.67) | data formatting | bytes 9437184 | tf_op jit(solution)/shard_map/mul | solution.py:54
  69.0 8.3 %all-to-all-done = bf16[16,12,3072]{2,1,0:T(8,128)(2,1)} async-done(((bf16[16,12,3072]{2,1,0:T(8,128)(2,1)}), bf16[16,12,3072]{2,1,0:T(8,128)(2,1)}, u32[]{:S(2)}, u32[]{:S(2)}) %all-to-all-start) | async-done | bytes 1179680 | tf_op jit(solution)/shard_map/all_to_all | solution.py:14
  77.3 2.1 copy.118
  79.7 5.6 %all_to_all.49 = bf16[2,16,12,3072]{3,1,2,0:T(8,128)(2,1)S(1)} all-to-all(bf16[2,16,12,3072]{3,1,2,0:T(8,128)(2,1)S(1)} %broadcast_in_dim.51), channel_id=1, replica_groups=mesh['group_0'=8,'group_1'=2,'group_2'=2,'rep'=8] {'group_2'}, dimensions={0} | all-to-all | bytes 4718592 | tf_op jit(solution)/shard_map/all_to_all | solution.py:14
  85.3 8.0 %all-to-all-start.5 = ((bf16[8,256,384]{1,2,0:T(8,128)(2,1)}), bf16[8,256,384]{1,2,0:T(8,128)(2,1)}, u32[]{:S(2)}, u32[]{:S(2)}) async-start(bf16[8,256,384]{1,2,0:T(8,128)(2,1)} %copy.136), calls=%async_computation.5 | async-start | bytes 3145728 | tf_op jit(solution)/shard_map/all_to_all | solution.py:121
  93.8 5.5 %copy.119 = f32[16,2,12,3072]{3,2,1,0:T(8,128)} copy(f32[16,2,12,3072]{3,0,2,1:T(8,128)S(1)} %convert_bitcast_fusion) | data formatting | bytes 9437184 | tf_op jit(solution)/shard_map/convert_element_type | solution.py:54
  99.3 5.4 %reshape.105 = f32[384,3072]{1,0:T(8,128)} reshape(f32[16,2,12,3072]{3,2,1,0:T(8,128)} %copy.119) | data formatting | bytes 9437184 | tf_op jit(solution)/shard_map/convert_element_type | solution.py:54
  104.8 77.1 %all-gather.3.cloned.1.call-done = bf16[1,2048,3072]{2,1,0:T(8,128)(2,1)} async-done(((bf16[1,256,3072]{2,1,0:T(8,128)(2,1)}), bf16[1,2048,3072]{2,1,0:T(8,128)(2,1)}) %all-gather.3.cloned.1.call-update) | async-done | bytes 12582928 | tf_op jit(solution)/shard_map/all_gather | solution.py:116
  181.9 10.8 %fusion.22 = bf16[1,2048,384]{1,2,0:T(8,128)(2,1)S(1)} fusion(bf16[1,2048,3072]{2,1,0:T(8,128)(2,1)} %all-gather.3.cloned.1.call-done, f32[384,3072]{1,0:T(8,128)} %reshape.105, f32[384,3072]{1,0:T(8,128)} %copy.122), kind=kOutput, calls=%fused_computation.21 | convolution fusion | flops 4834983936 | bytes 23592960 | tf_op jit(solution)/shard_map/dot_general | solution.py:123
  192.7 5.6 %copy.123 = bf16[1,2048,384]{2,0,1:T(2,128)(2,1)} copy(bf16[1,2048,384]{1,2,0:T(8,128)(2,1)S(1)} %fusion.22) | data formatting | bytes 3145728 | tf_op jit(solution)/shard_map/reshape | solution.py:143
  198.9 34.3 %reduce = bf16[2048,384]{1,0:T(8,128)(2,1)S(1)} reduce(bf16[2048,1,384]{2,1,0:T(2,128)(2,1)} %bitcast.68, bf16[]{:T(256)} %broadcast.35), dimensions={1}, to_apply=%bitcast.50.reduce_sub_computation | reduce | bytes 3145730
  233.2 1.9 reshape.111
  235.0 14.1 %convolution_convert_fusion = bf16[8,384,3072]{2,1,0:T(8,128)(2,1)} fusion(bf16[8,256,384]{1,2,0:T(8,128)(2,1)} %all-to-all-done.5, bf16[8,256,3072]{2,1,0:T(8,128)(2,1)} %bitcast.70), kind=kOutput, calls=%fused_computation.5 | convolution fusion | flops 4841275392 | bytes 33030144 | tf_op jit(solution)/shard_map/rlp,rle->rpe/dot_general | solution.py:134
  249.1 12.8 %convert_reduce_fusion = f32[384,3072]{1,0:T(8,128)} fusion(bf16[8,384,3072]{2,1,0:T(8,128)(2,1)} %convolution_convert_fusion), kind=kLoop, calls=%fused_computation.2 | loop fusion | flops 17694720 | bytes 23592960 | tf_op jit(solution)/shard_map/reduce_sum | solution.py:138
  261.9 5.5 %reshape_reshape.9 = f32[16,2,12,3072]{3,2,1,0:T(8,128)} reshape(f32[384,3072]{1,0:T(8,128)} %convert_reduce_fusion) | data formatting | bytes 9437184 | tf_op jit(solution)/shard_map/reshape;reshape | solution.py:33
  267.4 5.5 %copy.137 = f32[2,16,12,3072]{3,1,2,0:T(8,128)S(1)} copy(f32[2,16,12,3072]{3,2,0,1:T(8,128)} %bitcast.66) | data formatting | bytes 9437184 | tf_op jit(solution)/shard_map/transpose | solution.py:33
  272.9 8.6 %all_to_all.50 = f32[2,16,12,3072]{3,1,2,0:T(8,128)} all-to-all(f32[2,16,12,3072]{3,1,2,0:T(8,128)S(1)} %copy.137), channel_id=1, replica_groups=mesh['group_0'=8,'group_1'=2,'group_2'=2,'rep'=8] {'group_2'}, dimensions={0} | all-to-all | bytes 9437184 | tf_op jit(solution)/shard_map/all_to_all | solution.py:38
  281.6 6.9 %all-to-all-start.4 = ((bf16[8,2,49152]{2,1,0:T(2,128)(2,1)}), bf16[8,2,49152]{2,1,0:T(2,128)(2,1)}, u32[]{:S(2)}, u32[]{:S(2)}) async-start(bf16[8,2,49152]{2,1,0:T(2,128)(2,1)} %reshape.111), calls=%async_computation.4 | async-start | bytes 3145728 | tf_op jit(solution)/shard_map/all_to_all | solution.py:142
  288.5 2.9 reduce_sum.50
  291.4 3.0 copy.138
  294.4 14.6 %all-to-all-done.4 = bf16[8,2,49152]{2,1,0:T(2,128)(2,1)} async-done(((bf16[8,2,49152]{2,1,0:T(2,128)(2,1)}), bf16[8,2,49152]{2,1,0:T(2,128)(2,1)}, u32[]{:S(2)}, u32[]{:S(2)}) %all-to-all-start.4) | async-done | bytes 1572896 | tf_op jit(solution)/shard_map/all_to_all | solution.py:142
  309.0 6.4 %all-to-all-start.7 = ((f32[16,12,3072]{2,1,0:T(8,128)}), f32[16,12,3072]{2,1,0:T(8,128)}, u32[]{:S(2)}, u32[]{:S(2)}) async-start(f32[16,12,3072]{2,1,0:T(8,128)} %copy.138), calls=%async_computation.7 | async-start | bytes 6291456 | tf_op jit(solution)/shard_map/all_to_all | solution.py:46
  315.5 6.3 %reshape.112 = bf16[2048,1,384]{2,1,0:T(2,128)(2,1)} reshape(bf16[8,2,49152]{2,1,0:T(2,128)(2,1)} %all-to-all-done.4) | data formatting | bytes 3145728
  321.8 6.8 %copy.124 = bf16[1,2048,384]{1,2,0:T(8,128)(2,1)S(1)} copy(bf16[1,2048,384]{2,0,1:T(2,128)(2,1)} %bitcast.69) | data formatting | bytes 3145728 | tf_op jit(solution)/shard_map/all_to_all | solution.py:142
  329.6 1.3 reshape.101
  331.0 5.6 %convolution_convert_fusion.2 = bf16[24,128,256]{2,1,0:T(8,128)(2,1)} fusion(bf16[256,24,128]{0,2,1:T(8,128)(2,1)} %reshape.101, f32[24,256,256]{1,2,0:T(8,128)} %get-tuple-element.74, f32[24,256]{1,0:T(8,128)S(1)} %get-tuple-element.73), kind=kOutput, calls=%fused_computation.25 | convolution fusion | flops 406585344 | bytes 9461760 | tf_op jit(solution)/shard_map/while/body/eval_jaxpr/hqk,qhd->khd/dot_general | solution.py:88
  336.6 2.7 copy.141
  339.3 5.1 %fusion.44 = f32[24,256,256]{1,2,0:T(8,128)} fusion(bf16[256,24,128]{0,2,1:T(8,128)(2,1)} %bitcast.73, bf16[256,24,128]{0,2,1:T(8,128)(2,1)S(1)} %copy-done.2), kind=kOutput, calls=%fused_computation.40 | convolution fusion | flops 402653184 | bytes 9437184 | tf_op jit(solution)/shard_map/while/body/eval_jaxpr/qhd,khd->hqk/dot_general | solution.py:91
  344.3 12.2 %fusion.25 = bf16[24,256,128]{1,2,0:T(8,128)(2,1)} fusion(bf16[256,24,128]{0,2,1:T(8,128)(2,1)} %bitcast.80, f32[24,256,256]{1,2,0:T(8,128)} %fusion.44, f32[24,256,256]{1,2,0:T(8,128)} %get-tuple-element.74, f32[24,256]{1,0:T(8,128)S(1)} %get-tuple-element.73), kind=kOutput, calls=%fused_computation.22 | convolution fusion | flops 414456064 | bytes 15753216 | tf_op jit(solution)/shard_map/while/body/eval_jaxpr/hqk,khd->qhd/dot_general | solution.py:94
  356.5 2.7 copy.139
  359.2 11.9 %fusion.28 = bf16[24,256,128]{1,2,0:T(8,128)(2,1)} fusion(bf16[256,24,128]{0,2,1:T(8,128)(2,1)S(1)} %bitcast.78, f32[24,256,256]{1,2,0:T(8,128)} %fusion.44, f32[24,256,256]{1,2,0:T(8,128)} %get-tuple-element.74, f32[24,256]{1,0:T(8,128)S(1)} %get-tuple-element.73), kind=kOutput, calls=%fused_computation.23 | convolution fusion | flops 414456064 | bytes 15753216 | tf_op jit(solution)/shard_map/while/body/eval_jaxpr/hqk,qhd->khd/dot_general | solution.py:95
  371.1 2.6 copy.140
  373.8 15.1 %all-to-all-done.7 = f32[16,12,3072]{2,1,0:T(8,128)} async-done(((f32[16,12,3072]{2,1,0:T(8,128)}), f32[16,12,3072]{2,1,0:T(8,128)}, u32[]{:S(2)}, u32[]{:S(2)}) %all-to-all-start.7) | async-done | bytes 2359328 | tf_op jit(solution)/shard_map/all_to_all | solution.py:46
  388.8 2.8 reduce_sum.51
  (30 shorter events, 5.4 us)
Async XLA Ops:
  7.2 11.5 %copy-start = (bf16[96,3072]{1,0:T(8,128)(2,1)S(1)}, bf16[96,3072]{1,0:T(8,128)(2,1)}, u32[]{:S(2)}) copy-start(bf16[96,3072]{1,0:T(8,128)(2,1)} %param.10) | copy-start | bytes 1769476
  7.2 174.7 %all-gather.3.cloned.1.call-start = ((), (), s32[]{:S(2)}) async-start(), calls=%async_computation.8 | async-start | bytes 14155776 | tf_op jit(solution)/shard_map/all_gather | solution.py:116
  7.9 29.5 %copy-start.4 = (bf16[1,256,3072]{2,1,0:T(8,128)(2,1)S(1)}, bf16[1,256,3072]{2,1,0:T(8,128)(2,1)}, u32[]{:S(2)}) copy-start(bf16[1,256,3072]{2,1,0:T(8,128)(2,1)} %param.6) | copy-start | bytes 4718596
  9.5 18.3 %all-to-all-start.2 = ((bf16[16,12,12]{1,2,0:T(8,128)(2,1)}), bf16[16,12,12]{1,2,0:T(8,128)(2,1)S(1)}, u32[]{:S(2)}, u32[]{:S(2)}) async-start(bf16[16,12,12]{1,2,0:T(8,128)(2,1)} %broadcast_in_dim.52), calls=%async_computation.2 | async-start | bytes 131072 | tf_op jit(solution)/shard_map/all_to_all | solution.py:14
  33.0 44.4 %all-to-all-start = ((bf16[16,12,3072]{2,1,0:T(8,128)(2,1)}), bf16[16,12,3072]{2,1,0:T(8,128)(2,1)}, u32[]{:S(2)}, u32[]{:S(2)}) async-start(bf16[16,12,3072]{2,1,0:T(8,128)(2,1)} %broadcast_in_dim.50), calls=%async_computation | async-start | bytes 3145728 | tf_op jit(solution)/shard_map/all_to_all | solution.py:14
  43.3 7.4 %copy-start.3 = (bf16[1,256,3072]{1,2,0:T(8,128)(2,1)}, bf16[1,256,3072]{1,2,0:T(8,128)(2,1)S(1)}, u32[]{:S(2)}) copy-start(bf16[1,256,3072]{1,2,0:T(8,128)(2,1)S(1)} %copy.149) | copy-start | bytes 4718596
  85.3 149.7 %all-to-all-start.5 = ((bf16[8,256,384]{1,2,0:T(8,128)(2,1)}), bf16[8,256,384]{1,2,0:T(8,128)(2,1)}, u32[]{:S(2)}, u32[]{:S(2)}) async-start(bf16[8,256,384]{1,2,0:T(8,128)(2,1)} %copy.136), calls=%async_computation.5 | async-start | bytes 3145728 | tf_op jit(solution)/shard_map/all_to_all | solution.py:121
  281.6 27.5 %all-to-all-start.4 = ((bf16[8,2,49152]{2,1,0:T(2,128)(2,1)}), bf16[8,2,49152]{2,1,0:T(2,128)(2,1)}, u32[]{:S(2)}, u32[]{:S(2)}) async-start(bf16[8,2,49152]{2,1,0:T(2,128)(2,1)} %reshape.111), calls=%async_computation.4 | async-start | bytes 3145728 | tf_op jit(solution)/shard_map/all_to_all | solution.py:142
  309.0 79.8 %all-to-all-start.7 = ((f32[16,12,3072]{2,1,0:T(8,128)}), f32[16,12,3072]{2,1,0:T(8,128)}, u32[]{:S(2)}, u32[]{:S(2)}) async-start(f32[16,12,3072]{2,1,0:T(8,128)} %copy.138), calls=%async_computation.7 | async-start | bytes 6291456 | tf_op jit(solution)/shard_map/all_to_all | solution.py:46
  336.6 2.7 copy-start.2
  356.5 2.7 copy-start.5
  371.1 20.5 %copy-start.1 = (bf16[96,3072]{1,0:T(8,128)(2,1)S(1)}, bf16[96,3072]{1,0:T(8,128)(2,1)}, u32[]{:S(2)}) copy-start(bf16[96,3072]{1,0:T(8,128)(2,1)} %param.10) | copy-start | bytes 1769476
Sparse Core Ops, SparseCore 0:
  10.6 171.2 all-gather.2
where the time goes:
time: 406 us; the launch traced here: 399 us
  waiting for transfers between devices  125 us (31%)
  local copies, waits for them, and re-layouts  81.5 us (20%)
  matrix products  71.7 us (18%)
  other arithmetic  53.3 us (13%)
  starting transfers between devices  35 us (9%)
  blocking collectives  18 us (4%)
  between operations  14.5 us (4%)
    all_gather x1, waiting for transfers between devices, per_device(): all_output = lax.all_gather(output_flat, 'rep', axis=0, tiled=True)  77.1 us
    unnamed x1, other arithmetic  34.3 us
    unnamed x22, local copies, waits for them, and re-layouts  17.7 us
    all_to_all x2, waiting for transfers between devices, from_everyone(): lax.all_to_all(jnp.broadcast_to(value[None], (count, *value.shape)), axis...  17.3 us
    all_to_all x1, waiting for transfers between devices, sum_in_two_steps(): lax.all_to_all(nearer, far, split_axis=0, concat_axis=0, tiled=True)  15.1 us
    all_to_all x1, waiting for transfers between devices, per_device(): lax.all_to_all(grad_columns.reshape(1, replica_count * local_rows, group_...  14.6 us
    dot_general x1, matrix products, per_device(): jnp.einsum('rlp,rle->rpe', gathered_ctx, output_blocks, preferred_element...  14.1 us
    all_to_all x2, starting transfers between devices, from_everyone(): lax.all_to_all(jnp.broadcast_to(value[None], (count, *value.shape)), axis...  13.6 us
  transfers between devices with their start and end apart: 6, of which 5 were waited for; matrix products, arithmetic and copies ran while one was open for 42% of the time, Pallas kernels for 0%

commit v1 on v0

v1 whole, which is shorter than its diff:
```python
import functools

import jax
import jax.numpy as jnp
from jax import lax
from jax.experimental import pallas as pl
from jax.experimental.pallas import tpu as pltpu
from jax.sharding import Mesh
from jax.sharding import PartitionSpec as P

AXES = ("zh", "zl", "xl", "c", "xh", "y")
SHARD = ("zh", "zl", "xl", "c")
HD = 128
SCALE = HD**-0.5
F32 = jnp.float32
BF16 = jnp.bfloat16
SWAP = [(0, 1), (1, 0)]
NT = (((1,), (1,)), ((), ()))
TN = (((0,), (0,)), ((), ()))
VMEM_LIMIT = 50 * 2**20


def ring(count, step):
    return [(i, (i + step) % count) for i in range(count)]


def x_ring(step):
    def place(x):
        return (x % 2) * 2 + x // 2

    return [(place(x), place((x + step) % 4)) for x in range(4)]


def dot(a, b, dims):
    return lax.dot_general(a, b, dims, preferred_element_type=F32)


def params():
    return pltpu.CompilerParams(
        dimension_semantics=("arbitrary",), vmem_limit_bytes=VMEM_LIMIT
    )


def cost(flops, moved, exps=0):
    return pl.CostEstimate(flops=flops, bytes_accessed=moved, transcendentals=exps)


def softmax(q, k):
    scores = dot(q, k, NT) * SCALE
    exponent = jnp.exp(scores - jnp.max(scores, axis=1, keepdims=True))
    return exponent * (1.0 / jnp.sum(exponent, axis=1, keepdims=True))


def forward_body(pick, q_ref, k_ref, v_ref, out_ref):
    for head in range(q_ref.shape[1] // HD):
        cols = slice(head * HD, (head + 1) * HD)
        probs = softmax(q_ref[:, cols], k_ref[:, cols]).astype(BF16)
        context_t = dot(v_ref[:, cols], probs, (((0,), (1,)), ((), ())))
        out_ref[cols, :] = context_t.astype(BF16)


def forward(parity, q, k, v, width):
    seq, total = q.shape
    blocks = total // width // 2
    spec = pl.BlockSpec((seq, width), lambda i, pick: (0, 2 * i + pick[0]))
    return pl.pallas_call(
        forward_body,
        grid_spec=pltpu.PrefetchScalarGridSpec(
            num_scalar_prefetch=1,
            grid=(blocks,),
            in_specs=[spec] * 3,
            out_specs=pl.BlockSpec((width, seq), lambda i, pick: (i, 0)),
        ),
        out_shape=jax.ShapeDtypeStruct((total // 2, seq), BF16),
        compiler_params=params(),
        cost_estimate=cost(2 * seq * seq * total, 2 * seq * total * 2, seq * seq * total // HD // 2),
        name="context_half",
    )(parity, q, k, v)


def backward_body(own, pick, q_ref, k_ref, v_ref, *refs):
    if own:
        g_ref, r_ref, gq_ref, gk_ref, gv_ref = refs
    else:
        g_ref, _, _, _, gq_ref, gk_ref, gv_ref = refs
    for head in range(q_ref.shape[1] // HD):
        cols = slice(head * HD, (head + 1) * HD)
        q, k, v = q_ref[:, cols], k_ref[:, cols], v_ref[:, cols]
        if own:
            g = (g_ref[:, cols] + r_ref[:, cols].astype(F32)).astype(BF16)
        else:
            g = g_ref[:, cols]
        probs = softmax(q, k)
        gv_ref[:, cols] = dot(probs.astype(BF16), g, TN).astype(BF16)
        dprobs = dot(g, v, NT)
        delta = jnp.sum(probs * dprobs, axis=1, keepdims=True)
        dscores = (probs * (dprobs - delta) * SCALE).astype(BF16)
        gq_ref[:, cols] = dot(dscores, k, (((1,), (0,)), ((), ()))).astype(BF16)
        gk_ref[:, cols] = dot(dscores, q, TN).astype(BF16)


def backward(parity, q, k, v, grads, width, before=None):
    seq, total = q.shape
    blocks = total // width // 2
    spec = pl.BlockSpec((seq, width), lambda i, pick: (0, 2 * i + pick[0]))
    half = pl.BlockSpec((seq, width), lambda i, pick: (0, i))
    whole = jax.ShapeDtypeStruct((seq, total), BF16)
    extra = [] if before is None else list(before)
    return pl.pallas_call(
        functools.partial(backward_body, before is None),
        grid_spec=pltpu.PrefetchScalarGridSpec(
            num_scalar_prefetch=1,
            grid=(blocks,),
            in_specs=[spec] * 3
            + [half] * len(grads)
            + [pl.BlockSpec(memory_space=pl.ANY)] * len(extra),
            out_specs=[spec] * 3,
        ),
        out_shape=[whole] * 3,
        input_output_aliases={} if before is None else {5: 0, 6: 1, 7: 2},
        compiler_params=params(),
        cost_estimate=cost(5 * seq * seq * total, 7 * seq * total, seq * seq * total // HD // 2),
        name="attention_gradients",
    )(parity, q, k, v, *grads, *extra)


def restore_body(place, codes_ref, scales_ref, out_ref):
    index = (place[pl.program_id(0)] * 3 + pl.program_id(1)) // 2
    scales = scales_ref[...]
    lanes = lax.broadcasted_iota(jnp.int32, scales.shape, 1)
    scale = jnp.sum(jnp.where(lanes == index, scales, 0.0), axis=1, keepdims=True)
    out_ref[0] = (codes_ref[...].astype(F32) * scale).astype(BF16)


def restore(places, codes, scales):
    rows = codes.shape[0]
    return pl.pallas_call(
        restore_body,
        grid_spec=pltpu.PrefetchScalarGridSpec(
            num_scalar_prefetch=1,
            grid=(2, 3),
            in_specs=[
                pl.BlockSpec((rows, 128), lambda h, j, place: (0, place[h] * 3 + j)),
                pl.BlockSpec(scales.shape, lambda h, j, place: (0, 0)),
            ],
            out_specs=pl.BlockSpec((1, rows, 128), lambda h, j, place: (h, 0, j)),
        ),
        out_shape=jax.ShapeDtypeStruct((2, rows, 384), BF16),
        cost_estimate=cost(rows * 768, rows * 3072),
        name="weight_pieces",
    )(places, codes, scales)


def context_gradient_body(place, d0, d1, d2, d3, w0, w1, w2, wa, wb, g0, g1, g2, g3):
    far = jnp.where(pl.program_id(0) < 2, wa[...], wb[...])
    width = w0.shape[1]
    total = None
    for part, weight in enumerate((w0[...], w1[...], w2[...], far)):
        cols = pl.ds(pl.multiple_of(place[part] * width, 128), width)
        rows = jnp.concatenate([d[:, cols] for d in (d0, d1, d2, d3)], axis=0)
        term = dot(rows, weight, NT)
        total = term if total is None else total + term
    seq = d0.shape[0]
    for image, out in enumerate((g0, g1, g2, g3)):
        out[...] = total[image * seq : (image + 1) * seq].astype(out.dtype)


def context_gradient(places, grads, weights):
    seq, features = grads[0].shape
    rows = weights[0].shape[0]
    width = weights[0].shape[1]
    block = rows // 4
    full = pl.BlockSpec((seq, features), lambda i, place: (0, 0))
    by_row = pl.BlockSpec((block, width), lambda i, place: (i, 0))
    out = pl.BlockSpec((seq, block), lambda i, place: (0, i))
    return pl.pallas_call(
        context_gradient_body,
        grid_spec=pltpu.PrefetchScalarGridSpec(
            num_scalar_prefetch=1,
            grid=(4,),
            in_specs=[full] * 4
            + [by_row] * 3
            + [
                pl.BlockSpec((block, width), lambda i, place: (jnp.minimum(i, 1), 0)),
                pl.BlockSpec((block, width), lambda i, place: (jnp.maximum(i - 2, 0), 0)),
            ],
            out_specs=[out] * 4,
        ),
        out_shape=[
            jax.ShapeDtypeStruct((seq, rows), kind) for kind in (F32, BF16, F32, BF16)
        ],
        compiler_params=params(),
        cost_estimate=cost(8 * seq * features * rows, 20 * 2**20),
        name="context_gradient",
    )(places, *grads, *weights)


def weight_gradient_body(c0, c1, c2, c3, d0, d1, d2, d3, out_ref):
    total = None
    for context_t, grad in ((c0, d0), (c1, d1), (c2, d2), (c3, d3)):
        term = dot(context_t[...], grad[...], (((1,), (0,)), ((), ())))
        total = term if total is None else total + term
    for xl in range(2):
        for core in range(2):
            for xh in range(2):
                first = (xl * 2 + core) * 96 + xh * 48
                for y in range(4):
                    piece = total[first : first + 48, y * 384 : (y + 1) * 384]
                    out_ref[xl, xh, y, 0, core] = piece.astype(BF16)


def weight_gradient(contexts, grads):
    rows, seq = contexts[0].shape
    features = grads[0].shape[1]
    return pl.pallas_call(
        weight_gradient_body,
        grid=(4,),
        in_specs=[pl.BlockSpec((rows // 4, seq), lambda i: (i, 0))] * 4
        + [pl.BlockSpec((seq, features), lambda i: (0, 0))] * 4,
        out_specs=pl.BlockSpec((2, 2, 4, 1, 2, 48, 384), lambda i: (0, 0, 0, i, 0, 0, 0)),
        out_shape=jax.ShapeDtypeStruct((2, 2, 4, 4, 2, 48, 384), BF16),
        compiler_params=params(),
        cost_estimate=cost(8 * seq * features * rows, 16 * 2**20),
        name="weight_gradient",
    )(*contexts, *grads)


def per_device(queries, keys, values, grad_output, weight_codes, weight_scales):
    _, seq, total = queries.shape
    features = grad_output.shape[2]
    q, k, v = (a.reshape(seq, total) for a in (queries, keys, values))
    grad = grad_output.reshape(seq, features)
    zh, zl, xl, c, y = (lax.axis_index(name) for name in ("zh", "zl", "xl", "c", "y"))
    half = features // 2
    width = 384
    own_parity = zl.astype(jnp.int32).reshape(1)
    other_parity = 1 - own_parity

    d0 = lax.dynamic_slice_in_dim(grad, c * half, half, 1)
    d1 = lax.ppermute(lax.dynamic_slice_in_dim(grad, (1 - c) * half, half, 1), "c", SWAP)
    d2 = lax.ppermute(d0, "zl", SWAP)
    d3 = lax.ppermute(d1, "zl", SWAP)
    grads = (d0, d1, d2, d3)

    places = jnp.stack([c * 4 + y, (1 - c) * 4 + y]).astype(jnp.int32)
    pieces = restore(places, weight_codes, weight_scales)
    arrived = lax.ppermute(pieces[1], "c", SWAP)
    pair = jnp.where(
        c == 0,
        jnp.concatenate([pieces[0], arrived], 0),
        jnp.concatenate([arrived, pieces[0]], 0),
    )
    from_behind = [lax.ppermute(pair, "zh", ring(4, step)) for step in (1, 2, 3)]
    turned = [pair, from_behind[2], from_behind[1], from_behind[0]]
    column = lax.dynamic_slice_in_dim(jnp.stack(turned + turned), (4 - zh) % 4, 4, 0)
    beside = jnp.concatenate(
        [
            lax.ppermute(column[:2], ("xl", "xh"), x_ring(1)),
            lax.ppermute(column[2:], ("xl", "xh"), x_ring(-1)),
        ],
        0,
    )
    here = jnp.where(xl == 0, jnp.stack([column, beside], 1), jnp.stack([beside, column], 1))
    here = here.reshape(-1, width)
    rows = here.shape[0]
    below = lax.ppermute(here, "y", ring(4, 1))
    above = lax.ppermute(here, "y", ring(4, -1))
    far_a = lax.ppermute(below[: rows // 2], "y", ring(4, 1))
    far_b = lax.ppermute(above[rows // 2 :], "y", ring(4, -1))

    context_other = forward(other_parity, q, k, v, width)
    c2 = lax.ppermute(context_other, "zl", SWAP)
    context_own = forward(own_parity, q, k, v, width)
    c1 = lax.ppermute(context_own, "c", SWAP)
    c3 = lax.ppermute(c2, "c", SWAP)
    terms = weight_gradient((context_own, c1, c2, c3), grads)
    terms = lax.all_to_all(
        terms.reshape(16, 8, 48, width), ("xl", "xh", "y"), 0, 0, tiled=True
    )
    sums = jnp.sum(terms.astype(F32), axis=0).astype(BF16)
    sums = lax.all_to_all(sums.reshape(32, 12, width), ("zh", "c", "y"), 0, 0, tiled=True)
    grad_weight = jnp.sum(sums.astype(F32).reshape(4, 8, 12, width), axis=0)
    grad_weight = jnp.moveaxis(grad_weight, 0, 1).reshape(12, features)

    places = jnp.stack([y, (y + 3) % 4, (y + 1) % 4, (y + 2) % 4]).astype(jnp.int32)
    g0, g1, g2, g3 = context_gradient(places, grads, (here, below, above, far_a, far_b))
    r3 = lax.ppermute(g3, "c", SWAP)
    r1 = lax.ppermute(g1, "c", SWAP)
    g_other = lax.ppermute((g2 + r3.astype(F32)).astype(BF16), "zl", SWAP)
    first = backward(own_parity, q, k, v, (g0, r1), width)
    outs = backward(other_parity, q, k, v, (g_other,), width, first)
    return tuple(out.reshape(1, seq, total) for out in outs) + (grad_weight,)


def solution(mesh):
    split = Mesh(mesh.devices.reshape(4, 2, 2, 2, 2, 4), AXES)
    image = P(AXES, None, None)
    return jax.shard_map(
        per_device,
        mesh=split,
        in_specs=(image, image, image, image, P(SHARD, None), P(SHARD, None)),
        out_specs=(image, image, image, P(AXES, None)),
        check_vma=False,
    )
```

time: 406 us -> 260 us (0.64)
  the two profiles are of different devices: /device:TPU:4 before, /device:TPU:19 now
where the time goes in v1:
time: 260 us; the launch traced here: 259 us
  waiting for transfers between devices  124 us (48%)
  Pallas kernels  56.6 us (22%)
  starting transfers between devices  55.7 us (21%)
  local copies, waits for them, and re-layouts  12.8 us (5%)
  other arithmetic  8.34 us (3%)
    ppermute x1, waiting for transfers between devices, per_device(): below = lax.ppermute(here, 'y', ring(4, 1))  70.7 us
    ppermute x3, waiting for transfers between devices, per_device(): lax.ppermute(pair, 'zh', ring(4, step))  27.4 us
    pallas_call x2, Pallas kernels, backward(): pl.pallas_call(functools.partial(backward_body, before is None), grid_spe...  20.5 us
    pallas_call x1, Pallas kernels, context_gradient(): pl.pallas_call(context_gradient_body, grid_spec=pltpu.PrefetchScalarGridS...  12.6 us
    ppermute x1, starting transfers between devices, per_device(): d3 = lax.ppermute(d1, 'zl', SWAP)  11.5 us
    ppermute x3, starting transfers between devices, per_device(): lax.ppermute(pair, 'zh', ring(4, step))  10.8 us
    all_to_all x1, starting transfers between devices, per_device(): lax.all_to_all(sums.reshape(32, 12, width), ('zh', 'c', 'y'), 0, 0, tiled...  10.1 us
    pallas_call x2, Pallas kernels, forward(): pl.pallas_call(forward_body, grid_spec=pltpu.PrefetchScalarGridSpec(num_s...  9.86 us
  transfers between devices with their start and end apart: 21, of which 7 were waited for; matrix products, arithmetic and copies ran while one was open for 6% of the time, Pallas kernels for 20%

profile of v1, /device:TPU:19, one launch (start us, length us, event | category | flops | bytes accessed | tf_op | source)
XLA Modules:
  0.0 258.7 jit_solution(15323016412190893873)
XLA Ops:
  0.6 1.4 copy.19.scales_ref
  2.1 0.6 pad_add_fusion.1.place
  2.6 4.5 %weight_pieces.1 = bf16[2,96,384]{2,1,0:T(8,128)(2,1)} custom-call(s32[2]{0:T(128)} %pad_add_fusion.1.place, bf16[96,3072]{1,0:T(8,128)(2,1)} %codes_ref.1, f32[96,12]{1,0:T(8,128)} %copy.19.scales_ref), custom_call_target="tpu_custom_call" | custom-call | flops 73728 | bytes 294912 | tf_op jit(solution)/shard_map/weight_pieces/pallas_call | solution.py:137
  7.1 0.9 slice_bitcast_fusion.1
  8.1 0.8 collective-permute-start.3
  8.8 2.8 %dynamic-slice_bitcast_fusion = (bf16[256,1536]{1,0:T(8,128)(2,1)}, bf16[256,1536]{1,0:T(8,128)(2,1)}) fusion(bf16[1,256,3072]{2,1,0:T(8,128)(2,1)} %param.9, s32[]{:T(128)S(6)} %select_n.63, s32[]{:T(128)S(6)} %select_n.62), kind=kLoop, calls=%fused_computation.3 | loop fusion | bytes 3145736 | tf_op jit(solution)/shard_map/dynamic_slice | solution.py:240
  11.7 1.6 collective-permute-start.1
  13.4 4.9 %context_half.3 = bf16[1536,256]{1,0:T(8,128)(2,1)} custom-call(s32[1]{0:T(128)S(6)} %sub.10.pick, bf16[256,3072]{1,0:T(8,128)(2,1)S(1)} %bitcast.43, bf16[256,3072]{1,0:T(8,128)(2,1)S(1)} %bitcast.47, bf16[256,3072]{1,0:T(8,128)(2,1)} %bitcast.51), custom_call_target="tpu_custom_call" | custom-call | flops 402653184 | bytes 3145728 | tf_op jit(solution)/shard_map/context_half/pallas_call | solution.py:66
  18.3 0.7 maximum_select_fusion.2
  19.0 5.8 %collective-permute-start.4 = (bf16[192,384]{1,0:T(8,128)(2,1)}, bf16[192,384]{1,0:T(8,128)(2,1)S(1)}, u32[]{:S(2)}, u32[]{:S(2)}) collective-permute-start(bf16[192,384]{1,0:T(8,128)(2,1)} %maximum_select_fusion.2), channel_id=1, source_target_pairs={{0,192},{64,0},{128,64},{192,128},{1,193},{65,1},{129,65},{193,129... | collective-permute-start | bytes 442376 | tf_op jit(solution)/shard_map/ppermute | solution.py:253
  24.8 4.9 %context_half.2.c0 = bf16[1536,256]{1,0:T(8,128)(2,1)} custom-call(s32[1]{0:T(128)} %bitcast.pick, bf16[256,3072]{1,0:T(8,128)(2,1)S(1)} %bitcast.44, bf16[256,3072]{1,0:T(8,128)(2,1)S(1)} %bitcast.48, bf16[256,3072]{1,0:T(8,128)(2,1)} %bitcast.52), custom_call_target="tpu_custom_call" | custom-call | flops 402653184 | bytes 3145728 | tf_op jit(solution)/shard_map/context_half/pallas_call | solution.py:66
  29.8 1.3 collective-permute-start.16
  31.1 0.7 collective-permute-start.5
  31.9 25.0 %collective-permute-done.5 = bf16[192,384]{1,0:T(8,128)(2,1)S(1)} collective-permute-done((bf16[192,384]{1,0:T(8,128)(2,1)}, bf16[192,384]{1,0:T(8,128)(2,1)S(1)}, u32[]{:S(2)}, u32[]{:S(2)}) %collective-permute-start.5) | collective-permute-done | bytes 147488 | tf_op jit(solution)/shard_map/ppermute | solution.py:253
  56.8 4.3 %collective-permute-start.6 = (bf16[192,384]{1,0:T(8,128)(2,1)}, bf16[192,384]{1,0:T(8,128)(2,1)S(1)}, u32[]{:S(2)}, u32[]{:S(2)}) collective-permute-start(bf16[192,384]{1,0:T(8,128)(2,1)} %maximum_select_fusion.2), channel_id=1, source_target_pairs={{0,64},{64,128},{128,192},{192,0},{1,65},{65,129},{129,193},{193,1... | collective-permute-start | bytes 442376 | tf_op jit(solution)/shard_map/ppermute | solution.py:253
  61.2 2.4 collective-permute-done.6
  63.6 11.5 %collective-permute-start.2 = (bf16[256,1536]{1,0:T(8,128)(2,1)}, bf16[256,1536]{1,0:T(8,128)(2,1)S(1)}, u32[]{:S(2)}, u32[]{:S(2)}) collective-permute-start(bf16[256,1536]{1,0:T(8,128)(2,1)} %collective-permute-done.d1), channel_id=1, source_target_pairs={{0,32},{32,0},{1,33},{33,1},{2,34},{34,2},{3,35},{35,3},{4,36},{36... | collective-permute-start | bytes 2359304 | tf_op jit(solution)/shard_map/ppermute | solution.py:242
  75.2 3.1 %collective-permute-start.18 = (bf16[1536,256]{1,0:T(8,128)(2,1)}, bf16[1536,256]{1,0:T(8,128)(2,1)S(1)}, u32[]{:S(2)}, u32[]{:S(2)}) collective-permute-start(bf16[1536,256]{1,0:T(8,128)(2,1)} %collective-permute-done.17.c2), channel_id=1, source_target_pairs={{0,8},{8,0},{1,9},{9,1},{2,10},{10,2},{3,11},{11,3},{4,12},{12,4},... | collective-permute-start | bytes 2359304 | tf_op jit(solution)/shard_map/ppermute | solution.py:275
  78.3 0.9 constant_dynamic-slice_fusion.1
  79.2 1.2 collective-permute-start.7
  80.4 0.3 collective-permute-start.8
  80.7 9.8 %collective-permute-done.2.d3 = bf16[256,1536]{1,0:T(8,128)(2,1)S(1)} collective-permute-done((bf16[256,1536]{1,0:T(8,128)(2,1)}, bf16[256,1536]{1,0:T(8,128)(2,1)S(1)}, u32[]{:S(2)}, u32[]{:S(2)}) %collective-permute-start.2) | collective-permute-done | bytes 786464 | tf_op jit(solution)/shard_map/ppermute | solution.py:242
  90.4 0.9 copy-done.6
  91.3 9.1 %weight_gradient.1 = bf16[2,2,4,4,2,48,384]{6,5,4,3,2,1,0:T(8,128)(2,1)} custom-call(bf16[1536,256]{1,0:T(8,128)(2,1)} %context_half.2.c0, bf16[1536,256]{1,0:T(8,128)(2,1)} %collective-permute-done.16.c1, bf16[1536,256]{1,0:T(8,128)(2,1)} %collective-permute-done.17.c2, bf16[1536,256]{1,0:T(8,128)(2,1)S(1)} %collective-permute-done.18.c3, ...), custom_call_target="tpu_custom_call" | custom-call | flops 4831838208 | bytes 16777216 | tf_op jit(solution)/shard_map/weight_gradient/pallas_call | solution.py:215
  100.4 6.7 %all-to-all-start = ((bf16[16,8,48,384]{3,2,1,0:T(8,128)(2,1)}), bf16[16,8,48,384]{3,2,1,0:T(8,128)(2,1)}, u32[]{:S(2)}, u32[]{:S(2)}) async-start(bf16[16,8,48,384]{3,2,1,0:T(8,128)(2,1)} %bitcast.55), calls=%async_computation | async-start | bytes 9437184 | tf_op jit(solution)/shard_map/all_to_all | solution.py:277
  107.1 1.1 dynamic-slice_bitcast_fusion.2
  108.2 1.1 maximum_bitcast_fusion
  109.4 0.2 maximum_select_fusion
  109.7 1.0 collective-permute-start.9
  110.7 0.6 collective-permute-start.10
  111.3 70.7 %collective-permute-done.9.w1 = bf16[1536,384]{1,0:T(8,128)(2,1)S(1)} collective-permute-done((bf16[1536,384]{1,0:T(8,128)(2,1)S(1)}, bf16[1536,384]{1,0:T(8,128)(2,1)S(1)}, u32[]{:S(2)}, u32[]{:S(2)}) %collective-permute-start.9) | collective-permute-done | bytes 1179680 | tf_op jit(solution)/shard_map/ppermute | solution.py:266
  182.0 0.9 slice.27
  183.0 2.2 collective-permute-start.11
  185.2 1.0 copy-done.5
  186.2 0.9 slice.28
  187.2 7.2 %collective-permute-done.11.wa = bf16[768,384]{1,0:T(8,128)(2,1)} collective-permute-done((bf16[768,384]{1,0:T(8,128)(2,1)}, bf16[768,384]{1,0:T(8,128)(2,1)}, u32[]{:S(2)}, u32[]{:S(2)}) %collective-permute-start.11) | collective-permute-done | bytes 589856 | tf_op jit(solution)/shard_map/ppermute | solution.py:268
  194.4 7.3 %collective-permute-done.12.wb = bf16[768,384]{1,0:T(8,128)(2,1)} collective-permute-done((bf16[768,384]{1,0:T(8,128)(2,1)}, bf16[768,384]{1,0:T(8,128)(2,1)}, u32[]{:S(2)}, u32[]{:S(2)}) %collective-permute-start.12) | collective-permute-done | bytes 589856 | tf_op jit(solution)/shard_map/ppermute | solution.py:269
  201.7 12.6 %context_gradient.1 = (f32[256,1536]{1,0:T(8,128)}, bf16[256,1536]{1,0:T(8,128)(2,1)}, f32[256,1536]{1,0:T(8,128)}, bf16[256,1536]{1,0:T(8,128)(2,1)S(1)}) custom-call(s32[4]{0:T(128)S(1)} %pad_add_fusion.place, bf16[256,1536]{1,0:T(8,128)(2,1)} %get-tuple-element.25.d0, bf16[256,1536]{1,0:T(8,128)(2,1)} %collective-permute-done.d1, ...), custom_call_target="tpu_custom_call" | custom-call | flops 4831838208 | bytes 20971520 | tf_op jit(solution)/shard_map/context_gradient/pallas_call | solution.py:176
  214.4 3.3 %collective-permute-start.13 = (bf16[256,1536]{1,0:T(8,128)(2,1)S(1)}, bf16[256,1536]{1,0:T(8,128)(2,1)S(1)}, u32[]{:S(2)}, u32[]{:S(2)}) collective-permute-start(bf16[256,1536]{1,0:T(8,128)(2,1)S(1)} %get-tuple-element.15), channel_id=1, source_target_pairs={{0,8},{8,0},{1,9},{9,1},{2,10},{10,2},{3,11},{11,3},{4,12},{12,4},... | collective-permute-start | bytes 2359304 | tf_op jit(solution)/shard_map/ppermute | solution.py:287
  217.7 1.9 collective-permute-done.13
  219.7 2.5 add_convert_fusion
  222.2 1.2 collective-permute-start.14
  223.4 3.0 %reduce_sum.21 = bf16[8,48,384]{2,1,0:T(8,128)(2,1)S(1)} reduce(bf16[16,8,48,384]{3,2,1,0:T(8,128)(2,1)} %all-to-all-done, bf16[]{:T(256)} %constant.64.clone.1), dimensions={0}, to_apply=%region_0.1 | reduce | flops 2211840 | bytes 5013506 | tf_op jit(solution)/shard_map/reduce_sum | solution.py:280
  226.4 0.8 reshape.111
  227.2 10.1 %all-to-all-start.1 = ((bf16[32,12,384]{2,1,0:T(8,128)(2,1)}), bf16[32,12,384]{2,1,0:T(8,128)(2,1)S(1)}, u32[]{:S(2)}, u32[]{:S(2)}) async-start(bf16[32,12,384]{2,1,0:T(8,128)(2,1)} %reshape.111), calls=%async_computation.1 | async-start | bytes 786432 | tf_op jit(solution)/shard_map/all_to_all | solution.py:281
  237.3 10.3 %attention_gradients.2 = (bf16[256,3072]{1,0:T(8,128)(2,1)}, bf16[256,3072]{1,0:T(8,128)(2,1)}, bf16[256,3072]{1,0:T(8,128)(2,1)}) custom-call(s32[1]{0:T(128)} %bitcast.pick, bf16[256,3072]{1,0:T(8,128)(2,1)S(1)} %bitcast.45, bf16[256,3072]{1,0:T(8,128)(2,1)S(1)} %bitcast.49, bf16[256,3072]{1,0:T(8,128)(2,1)} %bitcast.53, ...), custom_call_target="tpu_custom_call" | custom-call | flops 1006632960 | bytes 5505024 | tf_op jit(solution)/shard_map/attention_gradients/pallas_call | solution.py:109
  247.6 10.2 %attention_gradients.3 = (bf16[256,3072]{1,0:T(8,128)(2,1)}, bf16[256,3072]{1,0:T(8,128)(2,1)}, bf16[256,3072]{1,0:T(8,128)(2,1)}) custom-call(s32[1]{0:T(128)S(6)} %sub.10.pick, bf16[256,3072]{1,0:T(8,128)(2,1)S(1)} %bitcast.46, bf16[256,3072]{1,0:T(8,128)(2,1)S(1)} %bitcast.50, ...), custom_call_target="tpu_custom_call", output_to_operand_aliasing={{0}: (5, {}), {1}: (6, {}), {2}: (7, {})} | custom-call | flops 1006632960 | bytes 5505024 | tf_op jit(solution)/shard_map/attention_gradients/pallas_call | solution.py:109
  258.0 0.7 copy.22
  (43 shorter events, 0.8 us)
Async XLA Ops:
  8.1 10.3 %collective-permute-start.3 = (bf16[96,384]{1,0:T(8,128)(2,1)S(1)}, bf16[96,384]{1,0:T(8,128)(2,1)S(1)}, u32[]{:S(2)}, u32[]{:S(2)}) collective-permute-start(bf16[96,384]{1,0:T(8,128)(2,1)S(1)} %get-tuple-element.29), channel_id=1, source_target_pairs={{0,8},{8,0},{1,9},{9,1},{2,10},{10,2},{3,11},{11,3},{4,12},{12,4},... | collective-permute-start | bytes 221192 | tf_op jit(solution)/shard_map/ppermute | solution.py:247
  8.8 4.5 %copy-start = (bf16[1,256,3072]{2,1,0:T(8,128)(2,1)S(1)}, bf16[1,256,3072]{2,1,0:T(8,128)(2,1)}, u32[]{:S(2)}) copy-start(bf16[1,256,3072]{2,1,0:T(8,128)(2,1)} %param.6) | copy-start | bytes 4718596
  8.8 4.5 %copy-start.1 = (bf16[1,256,3072]{2,1,0:T(8,128)(2,1)S(1)}, bf16[1,256,3072]{2,1,0:T(8,128)(2,1)}, u32[]{:S(2)}) copy-start(bf16[1,256,3072]{2,1,0:T(8,128)(2,1)} %param.7) | copy-start | bytes 4718596
  11.7 51.9 %collective-permute-start = (bf16[256,1536]{1,0:T(8,128)(2,1)}, bf16[256,1536]{1,0:T(8,128)(2,1)}, u32[]{:S(2)}, u32[]{:S(2)}) collective-permute-start(bf16[256,1536]{1,0:T(8,128)(2,1)} %get-tuple-element.24), channel_id=1, source_target_pairs={{0,8},{8,0},{1,9},{9,1},{2,10},{10,2},{3,11},{11,3},{4,12},{12,4},... | collective-permute-start | bytes 2359304 | tf_op jit(solution)/shard_map/ppermute | solution.py:240
  11.7 68.7 %collective-permute-start.1 = (bf16[256,1536]{1,0:T(8,128)(2,1)}, bf16[256,1536]{1,0:T(8,128)(2,1)}, u32[]{:S(2)}, u32[]{:S(2)}) collective-permute-start(bf16[256,1536]{1,0:T(8,128)(2,1)} %get-tuple-element.25.d0), channel_id=1, source_target_pairs={{0,32},{32,0},{1,33},{33,1},{2,34},{34,2},{3,35},{35,3},{4,36},{36... | collective-permute-start | bytes 2359304 | tf_op jit(solution)/shard_map/ppermute | solution.py:241
  18.3 56.9 %collective-permute-start.17 = (bf16[1536,256]{1,0:T(8,128)(2,1)}, bf16[1536,256]{1,0:T(8,128)(2,1)}, u32[]{:S(2)}, u32[]{:S(2)}) collective-permute-start(bf16[1536,256]{1,0:T(8,128)(2,1)} %context_half.3), channel_id=1, source_target_pairs={{0,32},{32,0},{1,33},{33,1},{2,34},{34,2},{3,35},{35,3},{4,36},{36... | collective-permute-start | bytes 2359304 | tf_op jit(solution)/shard_map/ppermute | solution.py:272
  19.0 12.1 %collective-permute-start.4 = (bf16[192,384]{1,0:T(8,128)(2,1)}, bf16[192,384]{1,0:T(8,128)(2,1)S(1)}, u32[]{:S(2)}, u32[]{:S(2)}) collective-permute-start(bf16[192,384]{1,0:T(8,128)(2,1)} %maximum_select_fusion.2), channel_id=1, source_target_pairs={{0,192},{64,0},{128,64},{192,128},{1,193},{65,1},{129,65},{193,129... | collective-permute-start | bytes 442376 | tf_op jit(solution)/shard_map/ppermute | solution.py:253
  29.8 50.9 %collective-permute-start.16 = (bf16[1536,256]{1,0:T(8,128)(2,1)}, bf16[1536,256]{1,0:T(8,128)(2,1)}, u32[]{:S(2)}, u32[]{:S(2)}) collective-permute-start(bf16[1536,256]{1,0:T(8,128)(2,1)} %context_half.2.c0), channel_id=1, source_target_pairs={{0,8},{8,0},{1,9},{9,1},{2,10},{10,2},{3,11},{11,3},{4,12},{12,4},... | collective-permute-start | bytes 2359304 | tf_op jit(solution)/shard_map/ppermute | solution.py:274
  31.1 25.7 %collective-permute-start.5 = (bf16[192,384]{1,0:T(8,128)(2,1)}, bf16[192,384]{1,0:T(8,128)(2,1)S(1)}, u32[]{:S(2)}, u32[]{:S(2)}) collective-permute-start(bf16[192,384]{1,0:T(8,128)(2,1)} %maximum_select_fusion.2), channel_id=1, source_target_pairs={{0,128},{64,192},{128,0},{192,64},{1,129},{65,193},{129,1},{193,65... | collective-permute-start | bytes 442376 | tf_op jit(solution)/shard_map/ppermute | solution.py:253
  56.8 6.7 %collective-permute-start.6 = (bf16[192,384]{1,0:T(8,128)(2,1)}, bf16[192,384]{1,0:T(8,128)(2,1)S(1)}, u32[]{:S(2)}, u32[]{:S(2)}) collective-permute-start(bf16[192,384]{1,0:T(8,128)(2,1)} %maximum_select_fusion.2), channel_id=1, source_target_pairs={{0,64},{64,128},{128,192},{192,0},{1,65},{65,129},{129,193},{193,1... | collective-permute-start | bytes 442376 | tf_op jit(solution)/shard_map/ppermute | solution.py:253
  63.6 26.8 %collective-permute-start.2 = (bf16[256,1536]{1,0:T(8,128)(2,1)}, bf16[256,1536]{1,0:T(8,128)(2,1)S(1)}, u32[]{:S(2)}, u32[]{:S(2)}) collective-permute-start(bf16[256,1536]{1,0:T(8,128)(2,1)} %collective-permute-done.d1), channel_id=1, source_target_pairs={{0,32},{32,0},{1,33},{33,1},{2,34},{34,2},{3,35},{35,3},{4,36},{36... | collective-permute-start | bytes 2359304 | tf_op jit(solution)/shard_map/ppermute | solution.py:242
  75.2 15.3 %collective-permute-start.18 = (bf16[1536,256]{1,0:T(8,128)(2,1)}, bf16[1536,256]{1,0:T(8,128)(2,1)S(1)}, u32[]{:S(2)}, u32[]{:S(2)}) collective-permute-start(bf16[1536,256]{1,0:T(8,128)(2,1)} %collective-permute-done.17.c2), channel_id=1, source_target_pairs={{0,8},{8,0},{1,9},{9,1},{2,10},{10,2},{3,11},{11,3},{4,12},{12,4},... | collective-permute-start | bytes 2359304 | tf_op jit(solution)/shard_map/ppermute | solution.py:275
  78.3 2.3 copy-start.2
  79.2 29.0 %collective-permute-start.7 = (bf16[2,192,384]{2,1,0:T(8,128)(2,1)}, bf16[2,192,384]{2,1,0:T(8,128)(2,1)}, u32[]{:S(2)}, u32[]{:S(2)}) collective-permute-start(bf16[2,192,384]{2,1,0:T(8,128)(2,1)} %get-tuple-element.26), channel_id=1, source_target_pairs={{0,16},{16,4},{4,20},{20,0},{1,17},{17,5},{5,21},{21,1},{2,18},{18... | collective-permute-start | bytes 884744 | tf_op jit(solution)/shard_map/ppermute | solution.py:258
  80.4 27.8 %collective-permute-start.8 = (bf16[2,192,384]{2,1,0:T(8,128)(2,1)S(1)}, bf16[2,192,384]{2,1,0:T(8,128)(2,1)}, u32[]{:S(2)}, u32[]{:S(2)}) collective-permute-start(bf16[2,192,384]{2,1,0:T(8,128)(2,1)S(1)} %get-tuple-element.27), channel_id=1, source_target_pairs={{0,20},{16,0},{4,16},{20,4},{1,21},{17,1},{5,17},{21,5},{2,22},{18... | collective-permute-start | bytes 884744 | tf_op jit(solution)/shard_map/ppermute | solution.py:259
  90.4 0.9 copy-start.6
  100.4 122.9 %all-to-all-start = ((bf16[16,8,48,384]{3,2,1,0:T(8,128)(2,1)}), bf16[16,8,48,384]{3,2,1,0:T(8,128)(2,1)}, u32[]{:S(2)}, u32[]{:S(2)}) async-start(bf16[16,8,48,384]{3,2,1,0:T(8,128)(2,1)} %bitcast.55), calls=%async_computation | async-start | bytes 9437184 | tf_op jit(solution)/shard_map/all_to_all | solution.py:277
  109.7 77.4 %copy-start.3 = (bf16[4,2,192,384]{3,2,1,0:T(8,128)(2,1)}, bf16[4,2,192,384]{3,2,1,0:T(8,128)(2,1)S(1)}, u32[]{:S(2)}) copy-start(bf16[4,2,192,384]{3,2,1,0:T(8,128)(2,1)S(1)} %copy.20) | copy-start | bytes 3538948
  109.7 72.3 %collective-permute-start.9 = (bf16[1536,384]{1,0:T(8,128)(2,1)S(1)}, bf16[1536,384]{1,0:T(8,128)(2,1)S(1)}, u32[]{:S(2)}, u32[]{:S(2)}) collective-permute-start(bf16[1536,384]{1,0:T(8,128)(2,1)S(1)} %bitcast.60), channel_id=1, source_target_pairs={{0,1},{1,2},{2,3},{3,0},{4,5},{5,6},{6,7},{7,4},{8,9},{9,10},{10,1... | collective-permute-start | bytes 3538952 | tf_op jit(solution)/shard_map/ppermute | solution.py:266
  110.7 74.5 %collective-permute-start.10 = (bf16[1536,384]{1,0:T(8,128)(2,1)S(1)}, bf16[1536,384]{1,0:T(8,128)(2,1)S(1)}, u32[]{:S(2)}, u32[]{:S(2)}) collective-permute-start(bf16[1536,384]{1,0:T(8,128)(2,1)S(1)} %bitcast.61), channel_id=1, source_target_pairs={{0,3},{1,0},{2,1},{3,2},{4,7},{5,4},{6,5},{7,6},{8,11},{9,8},{10,9... | collective-permute-start | bytes 3538952 | tf_op jit(solution)/shard_map/ppermute | solution.py:267
  182.0 5.1 %copy-start.4 = (bf16[1536,384]{1,0:T(8,128)(2,1)}, bf16[1536,384]{1,0:T(8,128)(2,1)S(1)}, u32[]{:S(2)}) copy-start(bf16[1536,384]{1,0:T(8,128)(2,1)S(1)} %collective-permute-done.9.w1) | copy-start | bytes 3538948
  183.0 11.4 %collective-permute-start.11 = (bf16[768,384]{1,0:T(8,128)(2,1)}, bf16[768,384]{1,0:T(8,128)(2,1)}, u32[]{:S(2)}, u32[]{:S(2)}) collective-permute-start(bf16[768,384]{1,0:T(8,128)(2,1)} %slice.27), channel_id=1, source_target_pairs={{0,1},{1,2},{2,3},{3,0},{4,5},{5,6},{6,7},{7,4},{8,9},{9,10},{10,1... | collective-permute-start | bytes 1769480 | tf_op jit(solution)/shard_map/ppermute | solution.py:268
  185.2 1.0 copy-start.5
  187.1 14.6 %collective-permute-start.12 = (bf16[768,384]{1,0:T(8,128)(2,1)}, bf16[768,384]{1,0:T(8,128)(2,1)}, u32[]{:S(2)}, u32[]{:S(2)}) collective-permute-start(bf16[768,384]{1,0:T(8,128)(2,1)} %slice.28), channel_id=1, source_target_pairs={{0,3},{1,0},{2,1},{3,2},{4,7},{5,4},{6,5},{7,6},{8,11},{9,8},{10,9... | collective-permute-start | bytes 1769480 | tf_op jit(solution)/shard_map/ppermute | solution.py:269
  214.4 5.3 %collective-permute-start.13 = (bf16[256,1536]{1,0:T(8,128)(2,1)S(1)}, bf16[256,1536]{1,0:T(8,128)(2,1)S(1)}, u32[]{:S(2)}, u32[]{:S(2)}) collective-permute-start(bf16[256,1536]{1,0:T(8,128)(2,1)S(1)} %get-tuple-element.15), channel_id=1, source_target_pairs={{0,8},{8,0},{1,9},{9,1},{2,10},{10,2},{3,11},{11,3},{4,12},{12,4},... | collective-permute-start | bytes 2359304 | tf_op jit(solution)/shard_map/ppermute | solution.py:287
  217.6 19.7 %collective-permute-start.15 = (bf16[256,1536]{1,0:T(8,128)(2,1)}, bf16[256,1536]{1,0:T(8,128)(2,1)}, u32[]{:S(2)}, u32[]{:S(2)}) collective-permute-start(bf16[256,1536]{1,0:T(8,128)(2,1)} %get-tuple-element.17), channel_id=1, source_target_pairs={{0,8},{8,0},{1,9},{9,1},{2,10},{10,2},{3,11},{11,3},{4,12},{12,4},... | collective-permute-start | bytes 2359304 | tf_op jit(solution)/shard_map/ppermute | solution.py:288
  222.2 25.5 %collective-permute-start.14 = (bf16[256,1536]{1,0:T(8,128)(2,1)}, bf16[256,1536]{1,0:T(8,128)(2,1)}, u32[]{:S(2)}, u32[]{:S(2)}) collective-permute-start(bf16[256,1536]{1,0:T(8,128)(2,1)} %add_convert_fusion), channel_id=1, source_target_pairs={{0,32},{32,0},{1,33},{33,1},{2,34},{34,2},{3,35},{35,3},{4,36},{36... | collective-permute-start | bytes 2359304 | tf_op jit(solution)/shard_map/ppermute | solution.py:289
  227.2 30.6 %all-to-all-start.1 = ((bf16[32,12,384]{2,1,0:T(8,128)(2,1)}), bf16[32,12,384]{2,1,0:T(8,128)(2,1)S(1)}, u32[]{:S(2)}, u32[]{:S(2)}) async-start(bf16[32,12,384]{2,1,0:T(8,128)(2,1)} %reshape.111), calls=%async_computation.1 | async-start | bytes 786432 | tf_op jit(solution)/shard_map/all_to_all | solution.py:281

commit v2 on v1

--- a/solution.py
+++ b/solution.py
@@ -124,28 +124,32 @@
     )(parity, q, k, v, *grads, *extra)
 
 
-def restore_body(place, codes_ref, scales_ref, out_ref):
-    index = (place[pl.program_id(0)] * 3 + pl.program_id(1)) // 2
+def after(values, events):
+    return lax.optimization_barrier((values, events))[0]
+
+
+def restore_body(place, codes_ref, scales_ref, near_ref, away_ref):
     scales = scales_ref[...]
     lanes = lax.broadcasted_iota(jnp.int32, scales.shape, 1)
-    scale = jnp.sum(jnp.where(lanes == index, scales, 0.0), axis=1, keepdims=True)
-    out_ref[0] = (codes_ref[...].astype(F32) * scale).astype(BF16)
+    for part, out in enumerate((near_ref, away_ref)):
+        for tile in range(out.shape[1] // 128):
+            column = place[part] * (out.shape[1] // 128) + tile
+            codes = codes_ref[:, pl.ds(pl.multiple_of(column * 128, 128), 128)].astype(F32)
+            chosen = jnp.where(lanes == column // 2, scales, 0.0)
+            scale = jnp.sum(chosen, axis=1, keepdims=True)
+            out[:, tile * 128 : (tile + 1) * 128] = (codes * scale).astype(BF16)
 
 
 def restore(places, codes, scales):
     rows = codes.shape[0]
     return pl.pallas_call(
         restore_body,
-        grid_spec=pltpu.PrefetchScalarGridSpec(
-            num_scalar_prefetch=1,
-            grid=(2, 3),
-            in_specs=[
-                pl.BlockSpec((rows, 128), lambda h, j, place: (0, place[h] * 3 + j)),
-                pl.BlockSpec(scales.shape, lambda h, j, place: (0, 0)),
-            ],
-            out_specs=pl.BlockSpec((1, rows, 128), lambda h, j, place: (h, 0, j)),
-        ),
-        out_shape=jax.ShapeDtypeStruct((2, rows, 384), BF16),
+        in_specs=[
+            pl.BlockSpec(memory_space=pltpu.SMEM),
+            pl.BlockSpec(memory_space=pltpu.VMEM),
+            pl.BlockSpec(memory_space=pltpu.VMEM),
+        ],
+        out_shape=[jax.ShapeDtypeStruct((rows, 384), BF16)] * 2,
         cost_estimate=cost(rows * 768, rows * 3072),
         name="weight_pieces",
     )(places, codes, scales)
@@ -154,13 +158,13 @@
 def context_gradient_body(place, d0, d1, d2, d3, w0, w1, w2, wa, wb, g0, g1, g2, g3):
     far = jnp.where(pl.program_id(0) < 2, wa[...], wb[...])
     width = w0.shape[1]
-    total = None
-    for part, weight in enumerate((w0[...], w1[...], w2[...], far)):
+    seq = d0.shape[0]
+    weight = jnp.concatenate([w0[...], w1[...], w2[...], far], axis=1)
+    columns = []
+    for part in range(4):
         cols = pl.ds(pl.multiple_of(place[part] * width, 128), width)
-        rows = jnp.concatenate([d[:, cols] for d in (d0, d1, d2, d3)], axis=0)
-        term = dot(rows, weight, NT)
-        total = term if total is None else total + term
-    seq = d0.shape[0]
+        columns.append(jnp.concatenate([d[:, cols] for d in (d0, d1, d2, d3)], axis=0))
+    total = dot(jnp.concatenate(columns, axis=1), weight, NT)
     for image, out in enumerate((g0, g1, g2, g3)):
         out[...] = total[image * seq : (image + 1) * seq].astype(out.dtype)
 
@@ -196,17 +200,15 @@
 
 
 def weight_gradient_body(c0, c1, c2, c3, d0, d1, d2, d3, out_ref):
-    total = None
-    for context_t, grad in ((c0, d0), (c1, d1), (c2, d2), (c3, d3)):
-        term = dot(context_t[...], grad[...], (((1,), (0,)), ((), ())))
-        total = term if total is None else total + term
-    for xl in range(2):
-        for core in range(2):
-            for xh in range(2):
-                first = (xl * 2 + core) * 96 + xh * 48
-                for y in range(4):
-                    piece = total[first : first + 48, y * 384 : (y + 1) * 384]
-                    out_ref[xl, xh, y, 0, core] = piece.astype(BF16)
+    context_t = jnp.concatenate([c[...] for c in (c0, c1, c2, c3)], axis=1)
+    for y in range(4):
+        grad = jnp.concatenate([d[:, y * 384 : (y + 1) * 384] for d in (d0, d1, d2, d3)], axis=0)
+        total = dot(context_t, grad, (((1,), (0,)), ((), ())))
+        for xl in range(2):
+            for core in range(2):
+                for xh in range(2):
+                    first = (xl * 2 + core) * 96 + xh * 48
+                    out_ref[xl, xh, y, 0, core] = total[first : first + 48].astype(BF16)
 
 
 def weight_gradient(contexts, grads):
@@ -239,8 +241,6 @@
     d0 = lax.dynamic_slice_in_dim(grad, c * half, half, 1)
     d1 = lax.ppermute(lax.dynamic_slice_in_dim(grad, (1 - c) * half, half, 1), "c", SWAP)
     d2 = lax.ppermute(d0, "zl", SWAP)
-    d3 = lax.ppermute(d1, "zl", SWAP)
-    grads = (d0, d1, d2, d3)
 
     places = jnp.stack([c * 4 + y, (1 - c) * 4 + y]).astype(jnp.int32)
     pieces = restore(places, weight_codes, weight_scales)
@@ -253,6 +253,12 @@
     from_behind = [lax.ppermute(pair, "zh", ring(4, step)) for step in (1, 2, 3)]
     turned = [pair, from_behind[2], from_behind[1], from_behind[0]]
     column = lax.dynamic_slice_in_dim(jnp.stack(turned + turned), (4 - zh) % 4, 4, 0)
+    context_other = forward(other_parity, q, k, v, width)
+    (context_other,) = after((context_other,), (column, d2))
+    c2 = lax.ppermute(context_other, "zl", SWAP)
+    (d1,) = after((d1,), (c2,))
+    d3 = lax.ppermute(d1, "zl", SWAP)
+    grads = (d0, d1, d2, d3)
     beside = jnp.concatenate(
         [
             lax.ppermute(column[:2], ("xl", "xh"), x_ring(1)),
@@ -268,19 +274,16 @@
     far_a = lax.ppermute(below[: rows // 2], "y", ring(4, 1))
     far_b = lax.ppermute(above[rows // 2 :], "y", ring(4, -1))
 
-    context_other = forward(other_parity, q, k, v, width)
-    c2 = lax.ppermute(context_other, "zl", SWAP)
     context_own = forward(own_parity, q, k, v, width)
     c1 = lax.ppermute(context_own, "c", SWAP)
+    (c2,) = after((c2,), (here,))
     c3 = lax.ppermute(c2, "c", SWAP)
+    (c3,) = after((c3,), (below, above))
     terms = weight_gradient((context_own, c1, c2, c3), grads)
+    (terms,) = after((terms,), (far_a, far_b))
     terms = lax.all_to_all(
         terms.reshape(16, 8, 48, width), ("xl", "xh", "y"), 0, 0, tiled=True
     )
-    sums = jnp.sum(terms.astype(F32), axis=0).astype(BF16)
-    sums = lax.all_to_all(sums.reshape(32, 12, width), ("zh", "c", "y"), 0, 0, tiled=True)
-    grad_weight = jnp.sum(sums.astype(F32).reshape(4, 8, 12, width), axis=0)
-    grad_weight = jnp.moveaxis(grad_weight, 0, 1).reshape(12, features)
 
     places = jnp.stack([y, (y + 3) % 4, (y + 1) % 4, (y + 2) % 4]).astype(jnp.int32)
     g0, g1, g2, g3 = context_gradient(places, grads, (here, below, above, far_a, far_b))
@@ -289,6 +292,12 @@
     g_other = lax.ppermute((g2 + r3.astype(F32)).astype(BF16), "zl", SWAP)
     first = backward(own_parity, q, k, v, (g0, r1), width)
     outs = backward(other_parity, q, k, v, (g_other,), width, first)
+
+    (terms,) = after((terms,), tuple(outs))
+    sums = jnp.sum(terms.astype(F32), axis=0).astype(BF16)
+    sums = lax.all_to_all(sums.reshape(32, 12, width), ("zh", "c", "y"), 0, 0, tiled=True)
+    grad_weight = jnp.sum(sums.astype(F32).reshape(4, 8, 12, width), axis=0)
+    grad_weight = jnp.moveaxis(grad_weight, 0, 1).reshape(12, features)
     return tuple(out.reshape(1, seq, total) for out in outs) + (grad_weight,)
 
 

time: 260 us -> 220 us (0.85)
  waiting for transfers between devices: 124 us -> 88.9 us
  starting transfers between devices: 55.7 us -> 30.8 us
  blocking collectives: 0 us -> 23.6 us
  Pallas kernels: 56.6 us -> 51.9 us
    ppermute x1, waiting for transfers between devices: 70.7 us -> 0.01 us  [per_device(): below = lax.ppermute(here, 'y', ring(4, 1))]
    all_to_all x1, waiting for transfers between devices: 0.01 us -> 25.6 us  [per_device(): lax.all_to_all(terms.reshape(16, 8, 48, width), ('xl', 'xh', 'y'), 0, 0,...]
    all_to_all x0 -> x1, blocking collectives: none -> 23.6 us  [per_device(): lax.all_to_all(sums.reshape(32, 12, width), ('zh', 'c', 'y'), 0, 0, tiled...]
    ppermute x1, starting transfers between devices: 11.5 us -> 0.01 us  [per_device(): d3 = lax.ppermute(d1, 'zl', SWAP)]
    all_to_all x1 -> x0, starting transfers between devices: 10.1 us -> none  [per_device(): lax.all_to_all(sums.reshape(32, 12, width), ('zh', 'c', 'y'), 0, 0, tiled...]
    ppermute x1, waiting for transfers between devices: 0.01 us -> 8.56 us  [per_device(): c2 = lax.ppermute(context_other, 'zl', SWAP)]
    ppermute x1, waiting for transfers between devices: 0.01 us -> 8.5 us  [per_device(): g_other = lax.ppermute((g2 + r3.astype(F32)).astype(BF16), 'zl', SWAP)]
    ppermute x1, waiting for transfers between devices: 7.34 us -> 0.01 us  [per_device(): far_b = lax.ppermute(above[rows // 2:], 'y', ring(4, -1))]
  transfers between devices with their start and end apart: 21 -> 20, of which waited for: 7 -> 8; matrix products, arithmetic and copies ran while one was open for 6% -> 3% of each run, Pallas kernels for 20% -> 23%
where the time goes in v2:
time: 220 us; the launch traced here: 217 us
  waiting for transfers between devices  88.9 us (40%)
  Pallas kernels  51.9 us (24%)
  starting transfers between devices  30.8 us (14%)
  blocking collectives  23.6 us (11%)
  local copies, waits for them, and re-layouts  12.9 us (6%)
  other arithmetic  7.78 us (4%)
    ppermute x3, waiting for transfers between devices, per_device(): lax.ppermute(pair, 'zh', ring(4, step))  27.7 us
    all_to_all x1, waiting for transfers between devices, per_device(): lax.all_to_all(terms.reshape(16, 8, 48, width), ('xl', 'xh', 'y'), 0, 0,...  25.6 us
    all_to_all x1, blocking collectives, per_device(): lax.all_to_all(sums.reshape(32, 12, width), ('zh', 'c', 'y'), 0, 0, tiled...  23.6 us
    pallas_call x2, Pallas kernels, backward(): pl.pallas_call(functools.partial(backward_body, before is None), grid_spe...  20.4 us
    pallas_call x1, Pallas kernels, context_gradient(): pl.pallas_call(context_gradient_body, grid_spec=pltpu.PrefetchScalarGridS...  11 us
    pallas_call x1, Pallas kernels, weight_gradient(): pl.pallas_call(weight_gradient_body, grid=(4,), in_specs=[pl.BlockSpec((r...  10.1 us
    ppermute x3, starting transfers between devices, per_device(): lax.ppermute(pair, 'zh', ring(4, step))  9.35 us
    ppermute x1, waiting for transfers between devices, per_device(): d3 = lax.ppermute(d1, 'zl', SWAP)  9.13 us
  transfers between devices with their start and end apart: 20, of which 8 were waited for; matrix products, arithmetic and copies ran while one was open for 3% of the time, Pallas kernels for 23%

profile of v2, /device:TPU:19, one launch (start us, length us, event | category | flops | bytes accessed | tf_op | source)
XLA Modules:
  0.0 216.8 jit_solution(2312482194316666224)
XLA Ops:
  0.6 1.4 copy.19.scales_ref
  2.1 0.6 pad_add_fusion.1.place
  2.6 1.9 weight_pieces.1
  4.5 0.7 collective-permute-start.1
  5.2 1.1 collective-permute-done.1
  6.3 1.0 maximum_select_fusion.2
  7.3 6.1 %collective-permute-start.2 = (bf16[192,384]{1,0:T(8,128)(2,1)S(1)}, bf16[192,384]{1,0:T(8,128)(2,1)S(1)}, u32[]{:S(2)}, u32[]{:S(2)}) collective-permute-start(bf16[192,384]{1,0:T(8,128)(2,1)S(1)} %maximum_select_fusion.2), channel_id=1, source_target_pairs={{0,192},{64,0},{128,64},{192,128},{1,193},{65,1},{129,65},{193,129... | collective-permute-start | bytes 442376 | tf_op jit(solution)/shard_map/ppermute | solution.py:253
  13.4 2.7 %dynamic-slice_bitcast_fusion = (bf16[256,1536]{1,0:T(8,128)(2,1)}, bf16[256,1536]{1,0:T(8,128)(2,1)}) fusion(bf16[1,256,3072]{2,1,0:T(8,128)(2,1)} %param.9, s32[]{:T(128)S(6)} %select_n.63, s32[]{:T(128)S(6)} %select_n.62), kind=kLoop, calls=%fused_computation.3 | loop fusion | bytes 3145736 | tf_op jit(solution)/shard_map/dynamic_slice | solution.py:242
  16.1 0.7 collective-permute-start.5
  16.8 3.3 %collective-permute-start.3 = (bf16[192,384]{1,0:T(8,128)(2,1)S(1)}, bf16[192,384]{1,0:T(8,128)(2,1)S(1)}, u32[]{:S(2)}, u32[]{:S(2)}) collective-permute-start(bf16[192,384]{1,0:T(8,128)(2,1)S(1)} %maximum_select_fusion.2), channel_id=1, source_target_pairs={{0,128},{64,192},{128,0},{192,64},{1,129},{65,193},{129,1},{193,65... | collective-permute-start | bytes 442376 | tf_op jit(solution)/shard_map/ppermute | solution.py:253
  20.2 27.7 %collective-permute-done.3 = bf16[192,384]{1,0:T(8,128)(2,1)S(1)} collective-permute-done((bf16[192,384]{1,0:T(8,128)(2,1)S(1)}, bf16[192,384]{1,0:T(8,128)(2,1)S(1)}, u32[]{:S(2)}, u32[]{:S(2)}) %collective-permute-start.3) | collective-permute-done | bytes 147488 | tf_op jit(solution)/shard_map/ppermute | solution.py:253
  48.1 1.0 copy-done.6
  49.1 0.8 constant_dynamic-slice_fusion.1
  49.9 1.2 collective-permute-start.8
  51.1 0.3 collective-permute-start.9
  51.3 2.1 collective-permute-start
  53.4 4.3 %context_half.2 = bf16[1536,256]{1,0:T(8,128)(2,1)S(1)} custom-call(s32[1]{0:T(128)S(6)} %sub.10.pick, bf16[256,3072]{1,0:T(8,128)(2,1)S(1)} %bitcast.40, bf16[256,3072]{1,0:T(8,128)(2,1)S(1)} %bitcast.44, bf16[256,3072]{1,0:T(8,128)(2,1)} %bitcast.48), custom_call_target="tpu_custom_call" | custom-call | flops 402653184 | bytes 3145728 | tf_op jit(solution)/shard_map/context_half/pallas_call | solution.py:66
  58.0 1.1 maximum_bitcast_fusion
  59.1 0.2 maximum_select_fusion
  59.5 0.2 collective-permute-start.11
  59.7 1.3 collective-permute-start.10
  61.0 4.2 %context_half.3.c0 = bf16[1536,256]{1,0:T(8,128)(2,1)S(1)} custom-call(s32[1]{0:T(128)} %bitcast.pick, bf16[256,3072]{1,0:T(8,128)(2,1)S(1)} %bitcast.41, bf16[256,3072]{1,0:T(8,128)(2,1)S(1)} %bitcast.45, bf16[256,3072]{1,0:T(8,128)(2,1)} %bitcast.49), custom_call_target="tpu_custom_call" | custom-call | flops 402653184 | bytes 3145728 | tf_op jit(solution)/shard_map/context_half/pallas_call | solution.py:66
  65.2 3.3 %collective-permute-start.17 = (bf16[1536,256]{1,0:T(8,128)(2,1)S(1)}, bf16[1536,256]{1,0:T(8,128)(2,1)S(1)}, u32[]{:S(2)}, u32[]{:S(2)}) collective-permute-start(bf16[1536,256]{1,0:T(8,128)(2,1)S(1)} %context_half.3.c0), channel_id=1, source_target_pairs={{0,8},{8,0},{1,9},{9,1},{2,10},{10,2},{3,11},{11,3},{4,12},{12,4},... | collective-permute-start | bytes 2359304 | tf_op jit(solution)/shard_map/ppermute | solution.py:278
  68.5 8.6 %collective-permute-done.6.c2 = bf16[1536,256]{1,0:T(8,128)(2,1)S(1)} collective-permute-done((bf16[1536,256]{1,0:T(8,128)(2,1)S(1)}, bf16[1536,256]{1,0:T(8,128)(2,1)S(1)}, u32[]{:S(2)}, u32[]{:S(2)}) %collective-permute-start.6) | collective-permute-done | bytes 786464 | tf_op jit(solution)/shard_map/ppermute | solution.py:258
  77.1 0.8 collective-permute-start.18
  77.9 6.5 %collective-permute-done.11.w2 = bf16[1536,384]{1,0:T(8,128)(2,1)S(1)} collective-permute-done((bf16[1536,384]{1,0:T(8,128)(2,1)S(1)}, bf16[1536,384]{1,0:T(8,128)(2,1)S(1)}, u32[]{:S(2)}, u32[]{:S(2)}) %collective-permute-start.11) | collective-permute-done | bytes 1179680 | tf_op jit(solution)/shard_map/ppermute | solution.py:273
  84.4 1.0 copy-done.10
  85.5 0.4 collective-permute-start.13
  86.0 2.2 collective-permute-start.12
  88.1 9.1 %collective-permute-done.7.d3 = bf16[256,1536]{1,0:T(8,128)(2,1)S(1)} collective-permute-done((bf16[256,1536]{1,0:T(8,128)(2,1)}, bf16[256,1536]{1,0:T(8,128)(2,1)S(1)}, u32[]{:S(2)}, u32[]{:S(2)}) %collective-permute-start.7) | collective-permute-done | bytes 786464 | tf_op jit(solution)/shard_map/ppermute | solution.py:260
  97.3 0.9 copy-done.12
  98.2 10.1 %weight_gradient.1 = bf16[2,2,4,4,2,48,384]{6,5,4,3,2,1,0:T(8,128)(2,1)} custom-call(bf16[1536,256]{1,0:T(8,128)(2,1)S(1)} %context_half.3.c0, bf16[1536,256]{1,0:T(8,128)(2,1)S(1)} %collective-permute-done.17.c1, bf16[1536,256]{1,0:T(8,128)(2,1)S(1)} %collective-permute-done.6.c2, bf16[1536,256]{1,0:T(8,128)(2,1)S(1)} %collective-permute-done.18.c3, ...), custom_call_target="tpu_custom_call" | custom-call | flops 4831838208 | bytes 16777216 | tf_op jit(solution)/shard_map/weight_gradient/pallas_call | solution.py:217
  108.3 0.8 copy-done.2
  109.1 0.8 copy-done.4
  109.9 6.7 %all-to-all-start = ((bf16[16,8,48,384]{3,2,1,0:T(8,128)(2,1)}), bf16[16,8,48,384]{3,2,1,0:T(8,128)(2,1)}, u32[]{:S(2)}, u32[]{:S(2)}) async-start(bf16[16,8,48,384]{3,2,1,0:T(8,128)(2,1)} %bitcast.52), calls=%async_computation | async-start | bytes 9437184 | tf_op jit(solution)/shard_map/all_to_all | solution.py:284
  116.7 1.1 copy-done.3
  117.8 1.1 copy-done.5
  118.8 11.0 %context_gradient.1 = (f32[256,1536]{1,0:T(8,128)}, bf16[256,1536]{1,0:T(8,128)(2,1)S(1)}, f32[256,1536]{1,0:T(8,128)}, bf16[256,1536]{1,0:T(8,128)(2,1)S(1)}) custom-call(s32[4]{0:T(128)S(1)} %pad_add_fusion.place, bf16[256,1536]{1,0:T(8,128)(2,1)} %get-tuple-element.41.d0, bf16[256,1536]{1,0:T(8,128)(2,1)} %collective-permute-done.d1, ...), custom_call_target="tpu_custom_call" | custom-call | flops 4831838208 | bytes 20971520 | tf_op jit(solution)/shard_map/context_gradient/pallas_call | solution.py:180
  129.8 1.3 collective-permute-start.14
  131.2 1.8 collective-permute-done.14
  133.0 1.6 add_convert_fusion
  134.8 10.3 %attention_gradients.2 = (bf16[256,3072]{1,0:T(8,128)(2,1)}, bf16[256,3072]{1,0:T(8,128)(2,1)}, bf16[256,3072]{1,0:T(8,128)(2,1)}) custom-call(s32[1]{0:T(128)} %bitcast.pick, bf16[256,3072]{1,0:T(8,128)(2,1)S(1)} %bitcast.42, bf16[256,3072]{1,0:T(8,128)(2,1)S(1)} %bitcast.46, bf16[256,3072]{1,0:T(8,128)(2,1)} %bitcast.50, ...), custom_call_target="tpu_custom_call" | custom-call | flops 1006632960 | bytes 5505024 | tf_op jit(solution)/shard_map/attention_gradients/pallas_call | solution.py:109
  145.1 8.5 %collective-permute-done.15.refs_0_ = bf16[256,1536]{1,0:T(8,128)(2,1)S(1)} collective-permute-done((bf16[256,1536]{1,0:T(8,128)(2,1)S(1)}, bf16[256,1536]{1,0:T(8,128)(2,1)S(1)}, u32[]{:S(2)}, u32[]{:S(2)}) %collective-permute-start.15) | collective-permute-done | bytes 786464 | tf_op jit(solution)/shard_map/ppermute | solution.py:292
  153.6 10.1 %attention_gradients.3 = (bf16[256,3072]{1,0:T(8,128)(2,1)}, bf16[256,3072]{1,0:T(8,128)(2,1)}, bf16[256,3072]{1,0:T(8,128)(2,1)}) custom-call(s32[1]{0:T(128)S(6)} %sub.10.pick, bf16[256,3072]{1,0:T(8,128)(2,1)S(1)} %bitcast.43, bf16[256,3072]{1,0:T(8,128)(2,1)S(1)} %bitcast.47, ...), custom_call_target="tpu_custom_call", output_to_operand_aliasing={{0}: (5, {}), {1}: (6, {}), {2}: (7, {})} | custom-call | flops 1006632960 | bytes 5505024 | tf_op jit(solution)/shard_map/attention_gradients/pallas_call | solution.py:109
  163.7 25.6 %all-to-all-done = bf16[16,8,48,384]{3,2,1,0:T(8,128)(2,1)} async-done(((bf16[16,8,48,384]{3,2,1,0:T(8,128)(2,1)}), bf16[16,8,48,384]{3,2,1,0:T(8,128)(2,1)}, u32[]{:S(2)}, u32[]{:S(2)}) %all-to-all-start) | async-done | bytes 4718624 | tf_op jit(solution)/shard_map/all_to_all | solution.py:284
  189.3 3.0 %reduce_sum.21 = bf16[8,48,384]{2,1,0:T(8,128)(2,1)S(1)} reduce(bf16[16,8,48,384]{3,2,1,0:T(8,128)(2,1)} %all-to-all-done, bf16[]{:T(256)} %constant.64.clone.1), dimensions={0}, to_apply=%region_0.1 | reduce | flops 2211840 | bytes 5013506 | tf_op jit(solution)/shard_map/reduce_sum | solution.py:297
  192.3 23.6 %all_to_all.10 = bf16[32,12,384]{2,1,0:T(8,128)(2,1)S(1)} all-to-all(bf16[32,12,384]{2,1,0:T(8,128)(2,1)S(1)} %reshape.115), channel_id=1, replica_groups=mesh['zh'=4,'zl'=2,'xl'=2,'c'=2,'xh'=2,'y'=4] {'zh','c','y'}, dimensions={0} | all-to-all | bytes 589824 | tf_op jit(solution)/shard_map/all_to_all | solution.py:298
  216.1 0.7 copy.22
  (53 shorter events, 1.2 us)
Async XLA Ops:
  4.5 1.8 collective-permute-start.1
  7.3 12.8 %copy-start.9 = (bf16[96,384]{1,0:T(8,128)(2,1)S(1)}, bf16[96,384]{1,0:T(8,128)(2,1)}, u32[]{:S(2)}) copy-start(bf16[96,384]{1,0:T(8,128)(2,1)} %get-tuple-element.22) | copy-start | bytes 221188
  7.3 12.8 %collective-permute-start.2 = (bf16[192,384]{1,0:T(8,128)(2,1)S(1)}, bf16[192,384]{1,0:T(8,128)(2,1)S(1)}, u32[]{:S(2)}, u32[]{:S(2)}) collective-permute-start(bf16[192,384]{1,0:T(8,128)(2,1)S(1)} %maximum_select_fusion.2), channel_id=1, source_target_pairs={{0,192},{64,0},{128,64},{192,128},{1,193},{65,1},{129,65},{193,129... | collective-permute-start | bytes 442376 | tf_op jit(solution)/shard_map/ppermute | solution.py:253
  16.1 41.7 %collective-permute-start.5 = (bf16[256,1536]{1,0:T(8,128)(2,1)}, bf16[256,1536]{1,0:T(8,128)(2,1)}, u32[]{:S(2)}, u32[]{:S(2)}) collective-permute-start(bf16[256,1536]{1,0:T(8,128)(2,1)} %get-tuple-element.41.d0), channel_id=1, source_target_pairs={{0,32},{32,0},{1,33},{33,1},{2,34},{34,2},{3,35},{35,3},{4,36},{36... | collective-permute-start | bytes 2359304 | tf_op jit(solution)/shard_map/ppermute | solution.py:243
  16.8 31.0 %collective-permute-start.4 = (bf16[192,384]{1,0:T(8,128)(2,1)S(1)}, bf16[192,384]{1,0:T(8,128)(2,1)S(1)}, u32[]{:S(2)}, u32[]{:S(2)}) collective-permute-start(bf16[192,384]{1,0:T(8,128)(2,1)S(1)} %maximum_select_fusion.2), channel_id=1, source_target_pairs={{0,64},{64,128},{128,192},{192,0},{1,65},{65,129},{129,193},{193,1... | collective-permute-start | bytes 442376 | tf_op jit(solution)/shard_map/ppermute | solution.py:253
  16.8 31.0 %collective-permute-start.3 = (bf16[192,384]{1,0:T(8,128)(2,1)S(1)}, bf16[192,384]{1,0:T(8,128)(2,1)S(1)}, u32[]{:S(2)}, u32[]{:S(2)}) collective-permute-start(bf16[192,384]{1,0:T(8,128)(2,1)S(1)} %maximum_select_fusion.2), channel_id=1, source_target_pairs={{0,128},{64,192},{128,0},{192,64},{1,129},{65,193},{129,1},{193,65... | collective-permute-start | bytes 442376 | tf_op jit(solution)/shard_map/ppermute | solution.py:253
  20.1 33.3 %copy-start.1 = (bf16[1,256,3072]{2,1,0:T(8,128)(2,1)S(1)}, bf16[1,256,3072]{2,1,0:T(8,128)(2,1)}, u32[]{:S(2)}) copy-start(bf16[1,256,3072]{2,1,0:T(8,128)(2,1)} %param.7) | copy-start | bytes 4718596
  47.9 5.5 %copy-start = (bf16[1,256,3072]{2,1,0:T(8,128)(2,1)S(1)}, bf16[1,256,3072]{2,1,0:T(8,128)(2,1)}, u32[]{:S(2)}) copy-start(bf16[1,256,3072]{2,1,0:T(8,128)(2,1)} %param.6) | copy-start | bytes 4718596
  48.1 1.0 copy-start.6
  49.9 8.1 %collective-permute-start.8 = (bf16[2,192,384]{2,1,0:T(8,128)(2,1)}, bf16[2,192,384]{2,1,0:T(8,128)(2,1)}, u32[]{:S(2)}, u32[]{:S(2)}) collective-permute-start(bf16[2,192,384]{2,1,0:T(8,128)(2,1)} %get-tuple-element.42), channel_id=1, source_target_pairs={{0,16},{16,4},{4,20},{20,0},{1,17},{17,5},{5,21},{21,1},{2,18},{18... | collective-permute-start | bytes 884744 | tf_op jit(solution)/shard_map/ppermute | solution.py:264
  51.1 6.9 %collective-permute-start.9 = (bf16[2,192,384]{2,1,0:T(8,128)(2,1)S(1)}, bf16[2,192,384]{2,1,0:T(8,128)(2,1)}, u32[]{:S(2)}, u32[]{:S(2)}) collective-permute-start(bf16[2,192,384]{2,1,0:T(8,128)(2,1)S(1)} %get-tuple-element.43), channel_id=1, source_target_pairs={{0,20},{16,0},{4,16},{20,4},{1,21},{17,1},{5,17},{21,5},{2,22},{18... | collective-permute-start | bytes 884744 | tf_op jit(solution)/shard_map/ppermute | solution.py:265
  51.3 26.6 %collective-permute-start = (bf16[256,1536]{1,0:T(8,128)(2,1)}, bf16[256,1536]{1,0:T(8,128)(2,1)}, u32[]{:S(2)}, u32[]{:S(2)}) collective-permute-start(bf16[256,1536]{1,0:T(8,128)(2,1)} %get-tuple-element.40), channel_id=1, source_target_pairs={{0,8},{8,0},{1,9},{9,1},{2,10},{10,2},{3,11},{11,3},{4,12},{12,4},... | collective-permute-start | bytes 2359304 | tf_op jit(solution)/shard_map/ppermute | solution.py:242
  53.4 4.3 %copy-start.7 = (bf16[8,192,384]{2,1,0:T(8,128)(2,1)S(1)}, bf16[8,192,384]{2,1,0:T(8,128)(2,1)}, u32[]{:S(2)}) copy-start(bf16[8,192,384]{2,1,0:T(8,128)(2,1)} %copy-done.6) | copy-start | bytes 3538948
  57.8 19.2 %collective-permute-start.6 = (bf16[1536,256]{1,0:T(8,128)(2,1)S(1)}, bf16[1536,256]{1,0:T(8,128)(2,1)S(1)}, u32[]{:S(2)}, u32[]{:S(2)}) collective-permute-start(bf16[1536,256]{1,0:T(8,128)(2,1)S(1)} %context_half.2), channel_id=1, source_target_pairs={{0,32},{32,0},{1,33},{33,1},{2,34},{34,2},{3,35},{35,3},{4,36},{36... | collective-permute-start | bytes 2359304 | tf_op jit(solution)/shard_map/ppermute | solution.py:258
  59.4 5.8 %copy-start.8 = (bf16[4,2,192,384]{3,2,1,0:T(8,128)(2,1)}, bf16[4,2,192,384]{3,2,1,0:T(8,128)(2,1)S(1)}, u32[]{:S(2)}) copy-start(bf16[4,2,192,384]{3,2,1,0:T(8,128)(2,1)S(1)} %copy.20) | copy-start | bytes 3538948
  59.5 24.9 %collective-permute-start.11 = (bf16[1536,384]{1,0:T(8,128)(2,1)S(1)}, bf16[1536,384]{1,0:T(8,128)(2,1)S(1)}, u32[]{:S(2)}, u32[]{:S(2)}) collective-permute-start(bf16[1536,384]{1,0:T(8,128)(2,1)S(1)} %bitcast.57), channel_id=1, source_target_pairs={{0,3},{1,0},{2,1},{3,2},{4,7},{5,4},{6,5},{7,6},{8,11},{9,8},{10,9... | collective-permute-start | bytes 3538952 | tf_op jit(solution)/shard_map/ppermute | solution.py:273
  59.7 26.2 %collective-permute-start.10 = (bf16[1536,384]{1,0:T(8,128)(2,1)S(1)}, bf16[1536,384]{1,0:T(8,128)(2,1)S(1)}, u32[]{:S(2)}, u32[]{:S(2)}) collective-permute-start(bf16[1536,384]{1,0:T(8,128)(2,1)S(1)} %bitcast.58), channel_id=1, source_target_pairs={{0,1},{1,2},{2,3},{3,0},{4,5},{5,6},{6,7},{7,4},{8,9},{9,10},{10,1... | collective-permute-start | bytes 3538952 | tf_op jit(solution)/shard_map/ppermute | solution.py:272
  65.2 22.9 %collective-permute-start.17 = (bf16[1536,256]{1,0:T(8,128)(2,1)S(1)}, bf16[1536,256]{1,0:T(8,128)(2,1)S(1)}, u32[]{:S(2)}, u32[]{:S(2)}) collective-permute-start(bf16[1536,256]{1,0:T(8,128)(2,1)S(1)} %context_half.3.c0), channel_id=1, source_target_pairs={{0,8},{8,0},{1,9},{9,1},{2,10},{10,2},{3,11},{11,3},{4,12},{12,4},... | collective-permute-start | bytes 2359304 | tf_op jit(solution)/shard_map/ppermute | solution.py:278
  77.1 11.0 %collective-permute-start.18 = (bf16[1536,256]{1,0:T(8,128)(2,1)S(1)}, bf16[1536,256]{1,0:T(8,128)(2,1)S(1)}, u32[]{:S(2)}, u32[]{:S(2)}) collective-permute-start(bf16[1536,256]{1,0:T(8,128)(2,1)S(1)} %collective-permute-done.6.c2), channel_id=1, source_target_pairs={{0,8},{8,0},{1,9},{9,1},{2,10},{10,2},{3,11},{11,3},{4,12},{12,4},... | collective-permute-start | bytes 2359304 | tf_op jit(solution)/shard_map/ppermute | solution.py:280
  77.9 19.4 %collective-permute-start.7 = (bf16[256,1536]{1,0:T(8,128)(2,1)}, bf16[256,1536]{1,0:T(8,128)(2,1)S(1)}, u32[]{:S(2)}, u32[]{:S(2)}) collective-permute-start(bf16[256,1536]{1,0:T(8,128)(2,1)} %collective-permute-done.d1), channel_id=1, source_target_pairs={{0,32},{32,0},{1,33},{33,1},{2,34},{34,2},{3,35},{35,3},{4,36},{36... | collective-permute-start | bytes 2359304 | tf_op jit(solution)/shard_map/ppermute | solution.py:260
  84.4 1.0 copy-start.10
  85.5 22.8 %collective-permute-start.13 = (bf16[768,384]{1,0:T(8,128)(2,1)S(1)}, bf16[768,384]{1,0:T(8,128)(2,1)S(1)}, u32[]{:S(2)}, u32[]{:S(2)}) collective-permute-start(bf16[768,384]{1,0:T(8,128)(2,1)S(1)} %slice.17), channel_id=1, source_target_pairs={{0,3},{1,0},{2,1},{3,2},{4,7},{5,4},{6,5},{7,6},{8,11},{9,8},{10,9... | collective-permute-start | bytes 1769480 | tf_op jit(solution)/shard_map/ppermute | solution.py:275
  85.9 22.4 %copy-start.11 = (bf16[1536,384]{1,0:T(8,128)(2,1)}, bf16[1536,384]{1,0:T(8,128)(2,1)S(1)}, u32[]{:S(2)}) copy-start(bf16[1536,384]{1,0:T(8,128)(2,1)S(1)} %collective-permute-done.10.w1) | copy-start | bytes 3538948
  86.0 23.1 %collective-permute-start.12 = (bf16[768,384]{1,0:T(8,128)(2,1)S(1)}, bf16[768,384]{1,0:T(8,128)(2,1)S(1)}, u32[]{:S(2)}, u32[]{:S(2)}) collective-permute-start(bf16[768,384]{1,0:T(8,128)(2,1)S(1)} %slice.16), channel_id=1, source_target_pairs={{0,1},{1,2},{2,3},{3,0},{4,5},{5,6},{6,7},{7,4},{8,9},{9,10},{10,1... | collective-permute-start | bytes 1769480 | tf_op jit(solution)/shard_map/ppermute | solution.py:274
  97.3 0.9 copy-start.12
  108.3 0.8 copy-start.2
  109.1 0.8 copy-start.4
  109.9 79.3 %all-to-all-start = ((bf16[16,8,48,384]{3,2,1,0:T(8,128)(2,1)}), bf16[16,8,48,384]{3,2,1,0:T(8,128)(2,1)}, u32[]{:S(2)}, u32[]{:S(2)}) async-start(bf16[16,8,48,384]{3,2,1,0:T(8,128)(2,1)} %bitcast.52), calls=%async_computation | async-start | bytes 9437184 | tf_op jit(solution)/shard_map/all_to_all | solution.py:284
  116.7 1.1 copy-start.3
  117.7 1.1 copy-start.5
  129.8 3.3 %collective-permute-start.14 = (bf16[256,1536]{1,0:T(8,128)(2,1)S(1)}, bf16[256,1536]{1,0:T(8,128)(2,1)S(1)}, u32[]{:S(2)}, u32[]{:S(2)}) collective-permute-start(bf16[256,1536]{1,0:T(8,128)(2,1)S(1)} %get-tuple-element.27), channel_id=1, source_target_pairs={{0,8},{8,0},{1,9},{9,1},{2,10},{10,2},{3,11},{11,3},{4,12},{12,4},... | collective-permute-start | bytes 2359304 | tf_op jit(solution)/shard_map/ppermute | solution.py:290
  131.1 3.6 %collective-permute-start.16 = (bf16[256,1536]{1,0:T(8,128)(2,1)S(1)}, bf16[256,1536]{1,0:T(8,128)(2,1)S(1)}, u32[]{:S(2)}, u32[]{:S(2)}) collective-permute-start(bf16[256,1536]{1,0:T(8,128)(2,1)S(1)} %get-tuple-element.29), channel_id=1, source_target_pairs={{0,8},{8,0},{1,9},{9,1},{2,10},{10,2},{3,11},{11,3},{4,12},{12,4},... | collective-permute-start | bytes 2359304 | tf_op jit(solution)/shard_map/ppermute | solution.py:291
  134.7 18.9 %collective-permute-start.15 = (bf16[256,1536]{1,0:T(8,128)(2,1)S(1)}, bf16[256,1536]{1,0:T(8,128)(2,1)S(1)}, u32[]{:S(2)}, u32[]{:S(2)}) collective-permute-start(bf16[256,1536]{1,0:T(8,128)(2,1)S(1)} %add_convert_fusion), channel_id=1, source_target_pairs={{0,32},{32,0},{1,33},{33,1},{2,34},{34,2},{3,35},{35,3},{4,36},{36... | collective-permute-start | bytes 2359304 | tf_op jit(solution)/shard_map/ppermute | solution.py:292

commit v3 on v2

--- a/solution.py
+++ b/solution.py
@@ -51,12 +51,19 @@
     return exponent * (1.0 / jnp.sum(exponent, axis=1, keepdims=True))
 
 
-def forward_body(pick, q_ref, k_ref, v_ref, out_ref):
+def forward_body(pick, q_ref, k_ref, v_ref, out_ref, plain, sorted_rows):
     for head in range(q_ref.shape[1] // HD):
         cols = slice(head * HD, (head + 1) * HD)
         probs = softmax(q_ref[:, cols], k_ref[:, cols]).astype(BF16)
-        context_t = dot(v_ref[:, cols], probs, (((0,), (1,)), ((), ())))
-        out_ref[cols, :] = context_t.astype(BF16)
+        plain[cols, :] = dot(v_ref[:, cols], probs, (((0,), (1,)), ((), ())))
+    for xl in range(2):
+        for xh in range(2):
+            for y in range(4):
+                for core in range(2):
+                    old = xl * 192 + core * 96 + xh * 48 + y * 12
+                    new = xl * 192 + xh * 96 + y * 24 + core * 12
+                    sorted_rows[new : new + 12, :] = plain[old : old + 12, :]
+    out_ref[...] = sorted_rows[...].astype(BF16)
 
 
 def forward(parity, q, k, v, width):
@@ -70,6 +77,7 @@
             grid=(blocks,),
             in_specs=[spec] * 3,
             out_specs=pl.BlockSpec((width, seq), lambda i, pick: (i, 0)),
+            scratch_shapes=[pltpu.VMEM((width, seq), F32)] * 2,
         ),
         out_shape=jax.ShapeDtypeStruct((total // 2, seq), BF16),
         compiler_params=params(),
@@ -155,26 +163,27 @@
     )(places, codes, scales)
 
 
-def context_gradient_body(place, d0, d1, d2, d3, w0, w1, w2, wa, wb, g0, g1, g2, g3):
+def four_images(near, away):
+    return jnp.concatenate([near[0], near[1], away[0], away[1]], axis=0)
+
+
+def context_gradient_body(place, a0, a1, b0, b1, w0, w1, w2, wa, wb, g0, g1, g2, g3, rows_ref):
     far = jnp.where(pl.program_id(0) < 2, wa[...], wb[...])
     width = w0.shape[1]
-    seq = d0.shape[0]
-    weight = jnp.concatenate([w0[...], w1[...], w2[...], far], axis=1)
-    columns = []
-    for part in range(4):
-        cols = pl.ds(pl.multiple_of(place[part] * width, 128), width)
-        columns.append(jnp.concatenate([d[:, cols] for d in (d0, d1, d2, d3)], axis=0))
-    total = dot(jnp.concatenate(columns, axis=1), weight, NT)
+    seq = a0.shape[1]
+    for part, weight in enumerate((w0[...], w1[...], w2[...], far)):
+        rows_ref[:, pl.ds(pl.multiple_of(place[part] * width, 128), width)] = weight
+    grads = jnp.concatenate([four_images(a0, a1), four_images(b0, b1)], axis=1)
+    total = dot(grads, rows_ref[...], NT)
     for image, out in enumerate((g0, g1, g2, g3)):
         out[...] = total[image * seq : (image + 1) * seq].astype(out.dtype)
 
 
 def context_gradient(places, grads, weights):
-    seq, features = grads[0].shape
-    rows = weights[0].shape[0]
-    width = weights[0].shape[1]
+    _, seq, part = grads[0].shape
+    rows, width = weights[0].shape
     block = rows // 4
-    full = pl.BlockSpec((seq, features), lambda i, place: (0, 0))
+    full = pl.BlockSpec((2, seq, part), lambda i, place: (0, 0, 0))
     by_row = pl.BlockSpec((block, width), lambda i, place: (i, 0))
     out = pl.BlockSpec((seq, block), lambda i, place: (0, i))
     return pl.pallas_call(
@@ -189,42 +198,50 @@
                 pl.BlockSpec((block, width), lambda i, place: (jnp.maximum(i - 2, 0), 0)),
             ],
             out_specs=[out] * 4,
+            scratch_shapes=[pltpu.VMEM((block, 2 * part), BF16)],
         ),
         out_shape=[
             jax.ShapeDtypeStruct((seq, rows), kind) for kind in (F32, BF16, F32, BF16)
         ],
         compiler_params=params(),
-        cost_estimate=cost(8 * seq * features * rows, 20 * 2**20),
+        cost_estimate=cost(16 * seq * part * rows, 20 * 2**20),
         name="context_gradient",
     )(places, *grads, *weights)
 
 
-def weight_gradient_body(c0, c1, c2, c3, d0, d1, d2, d3, out_ref):
+def weight_gradient_body(c0, c1, c2, c3, near, away, out_ref):
     context_t = jnp.concatenate([c[...] for c in (c0, c1, c2, c3)], axis=1)
-    for y in range(4):
-        grad = jnp.concatenate([d[:, y * 384 : (y + 1) * 384] for d in (d0, d1, d2, d3)], axis=0)
-        total = dot(context_t, grad, (((1,), (0,)), ((), ())))
-        for xl in range(2):
-            for core in range(2):
-                for xh in range(2):
-                    first = (xl * 2 + core) * 96 + xh * 48
-                    out_ref[xl, xh, y, 0, core] = total[first : first + 48].astype(BF16)
-
-
-def weight_gradient(contexts, grads):
+    total = dot(context_t, four_images(near, away), (((1,), (0,)), ((), ())))
+    for chip in range(16):
+        out_ref[chip, 0] = total[chip * 24 : (chip + 1) * 24].astype(BF16)
+
+
+def weight_gradient(contexts, near, away):
     rows, seq = contexts[0].shape
-    features = grads[0].shape[1]
+    features = near.shape[2]
+    whole = pl.BlockSpec(near.shape, lambda i: (0, 0, 0))
     return pl.pallas_call(
         weight_gradient_body,
         grid=(4,),
-        in_specs=[pl.BlockSpec((rows // 4, seq), lambda i: (i, 0))] * 4
-        + [pl.BlockSpec((seq, features), lambda i: (0, 0))] * 4,
-        out_specs=pl.BlockSpec((2, 2, 4, 1, 2, 48, 384), lambda i: (0, 0, 0, i, 0, 0, 0)),
-        out_shape=jax.ShapeDtypeStruct((2, 2, 4, 4, 2, 48, 384), BF16),
+        in_specs=[pl.BlockSpec((rows // 4, seq), lambda i: (i, 0))] * 4 + [whole] * 2,
+        out_specs=pl.BlockSpec((16, 1, 24, features), lambda i: (0, i, 0, 0)),
+        out_shape=jax.ShapeDtypeStruct((16, 4, 24, features), BF16),
         compiler_params=params(),
-        cost_estimate=cost(8 * seq * features * rows, 16 * 2**20),
+        cost_estimate=cost(8 * seq * features * rows, 8 * 2**20),
         name="weight_gradient",
-    )(*contexts, *grads)
+    )(*contexts, near, away)
+
+
+def sums_on_owners(terms, zh, c):
+    sums = jnp.sum(terms.astype(F32), axis=0).astype(BF16)
+    mine = lax.dynamic_index_in_dim(sums, zh, 0, False).astype(F32)
+    for step in (1, 2, 3):
+        away = lax.dynamic_index_in_dim(sums, (zh + step) % 4, 0, False)
+        mine = mine + lax.ppermute(away, "zh", ring(4, step)).astype(F32)
+    mine = mine.reshape(2, 12, -1)
+    kept = jnp.where(c == 0, mine[0], mine[1])
+    sent = jnp.where(c == 0, mine[1], mine[0])
+    return kept, lax.ppermute(sent, "c", SWAP)
 
 
 def per_device(queries, keys, values, grad_output, weight_codes, weight_scales):
@@ -238,10 +255,6 @@
     own_parity = zl.astype(jnp.int32).reshape(1)
     other_parity = 1 - own_parity
 
-    d0 = lax.dynamic_slice_in_dim(grad, c * half, half, 1)
-    d1 = lax.ppermute(lax.dynamic_slice_in_dim(grad, (1 - c) * half, half, 1), "c", SWAP)
-    d2 = lax.ppermute(d0, "zl", SWAP)
-
     places = jnp.stack([c * 4 + y, (1 - c) * 4 + y]).astype(jnp.int32)
     pieces = restore(places, weight_codes, weight_scales)
     arrived = lax.ppermute(pieces[1], "c", SWAP)
@@ -253,12 +266,13 @@
     from_behind = [lax.ppermute(pair, "zh", ring(4, step)) for step in (1, 2, 3)]
     turned = [pair, from_behind[2], from_behind[1], from_behind[0]]
     column = lax.dynamic_slice_in_dim(jnp.stack(turned + turned), (4 - zh) % 4, 4, 0)
+
     context_other = forward(other_parity, q, k, v, width)
-    (context_other,) = after((context_other,), (column, d2))
+    (context_other,) = after((context_other,), (column,))
     c2 = lax.ppermute(context_other, "zl", SWAP)
-    (d1,) = after((d1,), (c2,))
-    d3 = lax.ppermute(d1, "zl", SWAP)
-    grads = (d0, d1, d2, d3)
+    context_own = forward(own_parity, q, k, v, width)
+    c1 = lax.ppermute(context_own, "c", SWAP)
+
     beside = jnp.concatenate(
         [
             lax.ppermute(column[:2], ("xl", "xh"), x_ring(1)),
@@ -267,37 +281,46 @@
         0,
     )
     here = jnp.where(xl == 0, jnp.stack([column, beside], 1), jnp.stack([beside, column], 1))
-    here = here.reshape(-1, width)
+    (here,) = after((here.reshape(-1, width),), (c1,))
     rows = here.shape[0]
     below = lax.ppermute(here, "y", ring(4, 1))
     above = lax.ppermute(here, "y", ring(4, -1))
     far_a = lax.ppermute(below[: rows // 2], "y", ring(4, 1))
     far_b = lax.ppermute(above[rows // 2 :], "y", ring(4, -1))
-
-    context_own = forward(own_parity, q, k, v, width)
-    c1 = lax.ppermute(context_own, "c", SWAP)
-    (c2,) = after((c2,), (here,))
-    c3 = lax.ppermute(c2, "c", SWAP)
-    (c3,) = after((c3,), (below, above))
-    terms = weight_gradient((context_own, c1, c2, c3), grads)
-    (terms,) = after((terms,), (far_a, far_b))
-    terms = lax.all_to_all(
-        terms.reshape(16, 8, 48, width), ("xl", "xh", "y"), 0, 0, tiled=True
-    )
+    (event,) = after((c2,), (here,))
+    c3 = lax.ppermute(event, "c", SWAP)
+
+    part = half // 2
+    grads = []
+    for index in range(2):
+        own, partner = (
+            lax.dynamic_slice_in_dim(grad, side * half + index * part, part, 1)
+            for side in (c, 1 - c)
+        )
+        near = jnp.stack([own, lax.ppermute(partner, "c", SWAP)])
+        (sent,) = after((near,), (column,) if index == 0 else (c2,))
+        grads.append((near, lax.ppermute(sent, "zl", SWAP)))
+
+    terms = []
+    for near, away in grads:
+        term = weight_gradient((context_own, c1, c2, c3), near, away)
+        terms.append(lax.all_to_all(term, ("xl", "xh", "y"), 0, 0, tiled=True))
 
     places = jnp.stack([y, (y + 3) % 4, (y + 1) % 4, (y + 2) % 4]).astype(jnp.int32)
-    g0, g1, g2, g3 = context_gradient(places, grads, (here, below, above, far_a, far_b))
+    g0, g1, g2, g3 = context_gradient(
+        places, grads[0] + grads[1], (here, below, above, far_a, far_b)
+    )
     r3 = lax.ppermute(g3, "c", SWAP)
     r1 = lax.ppermute(g1, "c", SWAP)
     g_other = lax.ppermute((g2 + r3.astype(F32)).astype(BF16), "zl", SWAP)
     first = backward(own_parity, q, k, v, (g0, r1), width)
     outs = backward(other_parity, q, k, v, (g_other,), width, first)
 
-    (terms,) = after((terms,), tuple(outs))
-    sums = jnp.sum(terms.astype(F32), axis=0).astype(BF16)
-    sums = lax.all_to_all(sums.reshape(32, 12, width), ("zh", "c", "y"), 0, 0, tiled=True)
-    grad_weight = jnp.sum(sums.astype(F32).reshape(4, 8, 12, width), axis=0)
-    grad_weight = jnp.moveaxis(grad_weight, 0, 1).reshape(12, features)
+    (last,) = after((terms[1],), tuple(outs))
+    kept, got = zip(*(sums_on_owners(term, zh, c) for term in (terms[0], last)))
+    grad_weight = jnp.where(
+        c == 0, jnp.concatenate(kept + got, 1), jnp.concatenate(got + kept, 1)
+    )
     return tuple(out.reshape(1, seq, total) for out in outs) + (grad_weight,)
 
 

time: 220 us -> 222 us (level)
  starting transfers between devices: 30.8 us -> 58.1 us
  blocking collectives: 23.6 us -> 0 us
  waiting for transfers between devices: 88.9 us -> 66 us
  local copies, waits for them, and re-layouts: 12.9 us -> 22.8 us
  other arithmetic: 7.78 us -> 15.8 us
  Pallas kernels: 51.9 us -> 56.5 us
    all_to_all x1 -> x2, waiting for transfers between devices: 25.6 us -> 0.01 us  [per_device(): terms.append(lax.all_to_all(term, ('xl', 'xh', 'y'), 0, 0, tiled=True))]
    ppermute x4 -> x13, waiting for transfers between devices: 9.14 us -> 32.8 us  [the longest x2 25 us: per_device(): grads.append((near, lax.ppermute(sent, 'zl', SWAP)))]
    all_to_all x1 -> x0, blocking collectives: 23.6 us -> none  [per_device(): lax.all_to_all(sums.reshape(32, 12, width), ('zh', 'c', 'y'), 0, 0, tiled...]
    ppermute x4 -> x13, starting transfers between devices: 3.61 us -> 24.9 us  [the longest x6 13.1 us: sums_on_owners(): mine = mine + lax.ppermute(away, 'zh', ring(4, step)).astype(F32)]
    ppermute x3, waiting for transfers between devices: 27.7 us -> 6.85 us  [per_device(): lax.ppermute(pair, 'zh', ring(4, step))]
    ppermute x1, waiting for transfers between devices: 0.01 us -> 17.2 us  [per_device(): far_a = lax.ppermute(below[:rows // 2], 'y', ring(4, 1))]
    ppermute x1, waiting for transfers between devices: 8.5 us -> 0.01 us  [per_device(): g_other = lax.ppermute((g2 + r3.astype(F32)).astype(BF16), 'zl', SWAP)]
    all_to_all x1 -> x2, starting transfers between devices: 6.69 us -> 13.4 us  [per_device(): terms.append(lax.all_to_all(term, ('xl', 'xh', 'y'), 0, 0, tiled=True))]
  transfers between devices with their start and end apart: 20 -> 30, of which waited for: 8 -> 13; matrix products, arithmetic and copies ran while one was open for 3% -> 12% of each run, Pallas kernels for 23% -> 25%
where the time goes in v3:
time: 222 us; the launch traced here: 220 us
  waiting for transfers between devices  66 us (30%)
  starting transfers between devices  58.1 us (26%)
  Pallas kernels  56.5 us (25%)
  local copies, waits for them, and re-layouts  22.8 us (10%)
  other arithmetic  15.8 us (7%)
    ppermute x2, waiting for transfers between devices, per_device(): grads.append((near, lax.ppermute(sent, 'zl', SWAP)))  25 us
    pallas_call x2, Pallas kernels, backward(): pl.pallas_call(functools.partial(backward_body, before is None), grid_spe...  20.5 us
    ppermute x1, waiting for transfers between devices, per_device(): far_a = lax.ppermute(below[:rows // 2], 'y', ring(4, 1))  17.2 us
    all_to_all x2, starting transfers between devices, per_device(): terms.append(lax.all_to_all(term, ('xl', 'xh', 'y'), 0, 0, tiled=True))  13.4 us
    ppermute x6, starting transfers between devices, sums_on_owners(): mine = mine + lax.ppermute(away, 'zh', ring(4, step)).astype(F32)  13.1 us
    pallas_call x2, Pallas kernels, weight_gradient(): pl.pallas_call(weight_gradient_body, grid=(4,), in_specs=[pl.BlockSpec((r...  12.4 us
    pallas_call x1, Pallas kernels, context_gradient(): pl.pallas_call(context_gradient_body, grid_spec=pltpu.PrefetchScalarGridS...  11.7 us
    unnamed x30, local copies, waits for them, and re-layouts  11.4 us
  transfers between devices with their start and end apart: 30, of which 13 were waited for; matrix products, arithmetic and copies ran while one was open for 12% of the time, Pallas kernels for 25%

profile of v3, /device:TPU:19, one launch (start us, length us, event | category | flops | bytes accessed | tf_op | source)
XLA Modules:
  0.0 220.0 jit_solution(13175318663869455312)
XLA Ops:
  0.6 1.4 copy.13.scales_ref
  2.6 1.9 weight_pieces.1
  5.2 1.4 copy-done
  6.6 1.4 copy-done.2
  8.0 5.0 %context_half.3.c0 = bf16[1536,256]{1,0:T(8,128)(2,1)} custom-call(s32[1]{0:T(128)} %bitcast.pick, bf16[256,3072]{1,0:T(8,128)(2,1)S(1)} %bitcast.53, bf16[256,3072]{1,0:T(8,128)(2,1)S(1)} %bitcast.57, bf16[256,3072]{1,0:T(8,128)(2,1)} %bitcast.61), custom_call_target="tpu_custom_call" | custom-call | flops 402653184 | bytes 3145728 | tf_op jit(solution)/shard_map/context_half/pallas_call | solution.py:73
  13.0 2.6 %constant_dynamic-slice_fusion.2 = (bf16[1,256,768]{2,1,0:T(8,128)(2,1)S(1)}, bf16[256,768]{1,0:T(8,128)(2,1)}, bf16[1,256,768]{2,1,0:T(8,128)(2,1)}, bf16[256,768]{1,0:T(8,128)(2,1)}) fusion(bf16[1,256,3072]{2,1,0:T(8,128)(2,1)} %param.9, s32[]{:T(128)S(6)} %select_n.139, s32[]{:T(128)S(6)} %select_n.132, s32[]{:T(128)S(6)} %select_n.131, s32[]{:T(128)S(6)} %select_n.140), kind=kLoop, calls=%fused_computation.36 | loop fusion | bytes 3145744 | tf_op jit(solution)/shard_map/dynamic_slice | solution.py:297
  17.1 6.1 %collective-permute-start.2 = (bf16[192,384]{1,0:T(8,128)(2,1)S(1)}, bf16[192,384]{1,0:T(8,128)(2,1)S(1)}, u32[]{:S(2)}, u32[]{:S(2)}) collective-permute-start(bf16[192,384]{1,0:T(8,128)(2,1)S(1)} %maximum_select_fusion.3), channel_id=1, source_target_pairs={{0,192},{64,0},{128,64},{192,128},{1,193},{65,1},{129,65},{193,129... | collective-permute-start | bytes 442376 | tf_op jit(solution)/shard_map/ppermute | solution.py:266
  23.2 5.0 %context_half.2 = bf16[1536,256]{1,0:T(8,128)(2,1)} custom-call(s32[1]{0:T(128)S(6)} %sub.11.pick, bf16[256,3072]{1,0:T(8,128)(2,1)S(1)} %bitcast.54, bf16[256,3072]{1,0:T(8,128)(2,1)S(1)} %bitcast.58, bf16[256,3072]{1,0:T(8,128)(2,1)} %bitcast.62), custom_call_target="tpu_custom_call" | custom-call | flops 402653184 | bytes 3145728 | tf_op jit(solution)/shard_map/context_half/pallas_call | solution.py:73
  29.2 2.3 %collective-permute-start.4 = (bf16[192,384]{1,0:T(8,128)(2,1)S(1)}, bf16[192,384]{1,0:T(8,128)(2,1)S(1)}, u32[]{:S(2)}, u32[]{:S(2)}) collective-permute-start(bf16[192,384]{1,0:T(8,128)(2,1)S(1)} %maximum_select_fusion.3), channel_id=1, source_target_pairs={{0,64},{64,128},{128,192},{192,0},{1,65},{65,129},{129,193},{193,1... | collective-permute-start | bytes 442376 | tf_op jit(solution)/shard_map/ppermute | solution.py:266
  31.5 1.7 fusion.4
  33.8 6.8 %collective-permute-done.3 = bf16[192,384]{1,0:T(8,128)(2,1)S(1)} collective-permute-done((bf16[192,384]{1,0:T(8,128)(2,1)S(1)}, bf16[192,384]{1,0:T(8,128)(2,1)S(1)}, u32[]{:S(2)}, u32[]{:S(2)}) %collective-permute-start.3) | collective-permute-done | bytes 147488 | tf_op jit(solution)/shard_map/ppermute | solution.py:266
  42.0 1.7 fusion.5
  45.7 2.7 %collective-permute-start.7 = (bf16[1536,256]{1,0:T(8,128)(2,1)}, bf16[1536,256]{1,0:T(8,128)(2,1)}, u32[]{:S(2)}, u32[]{:S(2)}) collective-permute-start(bf16[1536,256]{1,0:T(8,128)(2,1)} %context_half.2), channel_id=1, source_target_pairs={{0,32},{32,0},{1,33},{33,1},{2,34},{34,2},{3,35},{35,3},{4,36},{36... | collective-permute-start | bytes 2359304 | tf_op jit(solution)/shard_map/ppermute | solution.py:272
  48.4 1.9 constant_dynamic-slice_fusion.1
  50.6 1.2 collective-permute-start.9
  51.8 1.2 fusion.6
  54.2 3.8 %collective-permute-done.10 = bf16[2,192,384]{2,1,0:T(8,128)(2,1)} collective-permute-done((bf16[2,192,384]{2,1,0:T(8,128)(2,1)}, bf16[2,192,384]{2,1,0:T(8,128)(2,1)}, u32[]{:S(2)}, u32[]{:S(2)}) %collective-permute-start.10) | collective-permute-done | bytes 294944 | tf_op jit(solution)/shard_map/ppermute | solution.py:279
  58.0 1.3 collective-permute-done.9
  60.7 1.1 copy.14
  61.8 4.0 %collective-permute-done.7.c2 = bf16[1536,256]{1,0:T(8,128)(2,1)} collective-permute-done((bf16[1536,256]{1,0:T(8,128)(2,1)}, bf16[1536,256]{1,0:T(8,128)(2,1)}, u32[]{:S(2)}, u32[]{:S(2)}) %collective-permute-start.7) | collective-permute-done | bytes 786464 | tf_op jit(solution)/shard_map/ppermute | solution.py:272
  65.8 2.5 %collective-permute-start.19 = (bf16[1536,256]{1,0:T(8,128)(2,1)}, bf16[1536,256]{1,0:T(8,128)(2,1)S(1)}, u32[]{:S(2)}, u32[]{:S(2)}) collective-permute-start(bf16[1536,256]{1,0:T(8,128)(2,1)} %collective-permute-done.7.c2), channel_id=1, source_target_pairs={{0,8},{8,0},{1,9},{9,1},{2,10},{10,2},{3,11},{11,3},{4,12},{12,4},... | collective-permute-start | bytes 2359304 | tf_op jit(solution)/shard_map/ppermute | solution.py:291
  69.8 12.9 %collective-permute-done.5.a1.away = bf16[2,256,768]{2,1,0:T(8,128)(2,1)S(1)} collective-permute-done((bf16[2,256,768]{2,1,0:T(8,128)(2,1)S(1)}, bf16[2,256,768]{2,1,0:T(8,128)(2,1)S(1)}, u32[]{:S(2)}, u32[]{:S(2)}) %collective-permute-start.5) | collective-permute-done | bytes 786464 | tf_op jit(solution)/shard_map/ppermute | solution.py:302
  83.5 6.1 %weight_gradient.2 = bf16[16,4,24,768]{3,2,1,0:T(8,128)(2,1)} custom-call(bf16[1536,256]{1,0:T(8,128)(2,1)} %context_half.3.c0, bf16[1536,256]{1,0:T(8,128)(2,1)} %collective-permute-done.11.c1, bf16[1536,256]{1,0:T(8,128)(2,1)} %collective-permute-done.7.c2, bf16[1536,256]{1,0:T(8,128)(2,1)S(1)} %collective-permute-done.19.c3, ...), custom_call_target="tpu_custom_call" | custom-call | flops 2415919104 | bytes 8388608 | tf_op jit(solution)/shard_map/weight_gradient/pallas_call | solution.py:223
  90.5 6.7 %all-to-all-start = ((bf16[16,4,24,768]{3,2,1,0:T(8,128)(2,1)}), bf16[16,4,24,768]{3,2,1,0:T(8,128)(2,1)}, u32[]{:S(2)}, u32[]{:S(2)}) async-start(bf16[16,4,24,768]{3,2,1,0:T(8,128)(2,1)} %weight_gradient.2), calls=%async_computation | async-start | bytes 4718592 | tf_op jit(solution)/shard_map/all_to_all | solution.py:307
  97.2 1.9 collective-permute-start.6
  99.1 1.6 collective-permute-done.6
  101.6 1.5 collective-permute-start.8
  103.1 1.9 slice.40
  105.9 2.0 slice.41
  108.5 12.1 %collective-permute-done.8.b1.away = bf16[2,256,768]{2,1,0:T(8,128)(2,1)} collective-permute-done((bf16[2,256,768]{2,1,0:T(8,128)(2,1)}, bf16[2,256,768]{2,1,0:T(8,128)(2,1)}, u32[]{:S(2)}, u32[]{:S(2)}) %collective-permute-start.8) | collective-permute-done | bytes 786464 | tf_op jit(solution)/shard_map/ppermute | solution.py:302
  120.7 17.2 %collective-permute-done.14.wa = bf16[768,384]{1,0:T(8,128)(2,1)} collective-permute-done((bf16[768,384]{1,0:T(8,128)(2,1)}, bf16[768,384]{1,0:T(8,128)(2,1)}, u32[]{:S(2)}, u32[]{:S(2)}) %collective-permute-start.14) | collective-permute-done | bytes 589856 | tf_op jit(solution)/shard_map/ppermute | solution.py:288
  139.0 11.7 %context_gradient.1 = (f32[256,1536]{1,0:T(8,128)}, bf16[256,1536]{1,0:T(8,128)(2,1)S(1)}, f32[256,1536]{1,0:T(8,128)}, bf16[256,1536]{1,0:T(8,128)(2,1)}) custom-call(s32[4]{0:T(128)S(1)} %pad_add_fusion.place, bf16[2,256,768]{2,1,0:T(8,128)(2,1)S(1)} %copy-done.5, bf16[2,256,768]{2,1,0:T(8,128)(2,1)} %copy-done.11, ...), custom_call_target="tpu_custom_call" | custom-call | flops 4831838208 | bytes 20971520 | tf_op jit(solution)/shard_map/context_gradient/pallas_call | solution.py:189
  152.2 6.3 %weight_gradient.3 = bf16[16,4,24,768]{3,2,1,0:T(8,128)(2,1)} custom-call(bf16[1536,256]{1,0:T(8,128)(2,1)} %context_half.3.c0, bf16[1536,256]{1,0:T(8,128)(2,1)} %collective-permute-done.11.c1, bf16[1536,256]{1,0:T(8,128)(2,1)} %collective-permute-done.7.c2, bf16[1536,256]{1,0:T(8,128)(2,1)S(1)} %copy-done.8, ...), custom_call_target="tpu_custom_call" | custom-call | flops 2415919104 | bytes 8388608 | tf_op jit(solution)/shard_map/weight_gradient/pallas_call | solution.py:223
  158.5 6.7 %all-to-all-start.1 = ((bf16[16,4,24,768]{3,2,1,0:T(8,128)(2,1)}), bf16[16,4,24,768]{3,2,1,0:T(8,128)(2,1)}, u32[]{:S(2)}, u32[]{:S(2)}) async-start(bf16[16,4,24,768]{3,2,1,0:T(8,128)(2,1)} %weight_gradient.3), calls=%async_computation.1 | async-start | bytes 4718592 | tf_op jit(solution)/shard_map/all_to_all | solution.py:307
  165.8 2.7 %add_convert_fusion = bf16[256,1536]{1,0:T(8,128)(2,1)} fusion(f32[256,1536]{1,0:T(8,128)} %get-tuple-element.28, bf16[256,1536]{1,0:T(8,128)(2,1)} %collective-permute-done.16), kind=kLoop, calls=%fused_computation | loop fusion | flops 1179648 | bytes 3145728 | tf_op jit(solution)/shard_map/convert_element_type | solution.py:315
  168.6 1.4 collective-permute-start.17
  170.0 2.0 reduce_sum.24
  172.0 2.6 %collective-permute-start.20 = (bf16[24,768]{1,0:T(8,128)(2,1)S(1)}, bf16[24,768]{1,0:T(8,128)(2,1)S(1)}, u32[]{:S(2)}, u32[]{:S(2)}) collective-permute-start(bf16[24,768]{1,0:T(8,128)(2,1)S(1)} %get-tuple-element.46), channel_id=1, source_target_pairs={{0,64},{64,128},{128,192},{192,0},{1,65},{65,129},{129,193},{193,1... | collective-permute-start | bytes 110600 | tf_op jit(solution)/shard_map/ppermute | solution.py:240
  174.6 3.5 %collective-permute-start.21 = (bf16[24,768]{1,0:T(8,128)(2,1)S(1)}, bf16[24,768]{1,0:T(8,128)(2,1)S(1)}, u32[]{:S(2)}, u32[]{:S(2)}) collective-permute-start(bf16[24,768]{1,0:T(8,128)(2,1)S(1)} %get-tuple-element.48), channel_id=1, source_target_pairs={{0,128},{64,192},{128,0},{192,64},{1,129},{65,193},{129,1},{193,65... | collective-permute-start | bytes 110600 | tf_op jit(solution)/shard_map/ppermute | solution.py:240
  178.1 3.2 %collective-permute-start.22 = (bf16[24,768]{1,0:T(8,128)(2,1)S(1)}, bf16[24,768]{1,0:T(8,128)(2,1)S(1)}, u32[]{:S(2)}, u32[]{:S(2)}) collective-permute-start(bf16[24,768]{1,0:T(8,128)(2,1)S(1)} %get-tuple-element.47), channel_id=1, source_target_pairs={{0,192},{64,0},{128,64},{192,128},{1,193},{65,1},{129,65},{193,129... | collective-permute-start | bytes 110600 | tf_op jit(solution)/shard_map/ppermute | solution.py:240
  181.3 10.3 %attention_gradients.2 = (bf16[256,3072]{1,0:T(8,128)(2,1)}, bf16[256,3072]{1,0:T(8,128)(2,1)}, bf16[256,3072]{1,0:T(8,128)(2,1)}) custom-call(s32[1]{0:T(128)} %bitcast.pick, bf16[256,3072]{1,0:T(8,128)(2,1)S(1)} %bitcast.55, bf16[256,3072]{1,0:T(8,128)(2,1)S(1)} %bitcast.59, bf16[256,3072]{1,0:T(8,128)(2,1)} %bitcast.63, ...), custom_call_target="tpu_custom_call" | custom-call | flops 1006632960 | bytes 5505024 | tf_op jit(solution)/shard_map/attention_gradients/pallas_call | solution.py:117
  191.6 1.5 collective-permute-done.20
  193.1 2.6 %collective-permute-done.21 = bf16[24,768]{1,0:T(8,128)(2,1)S(1)} collective-permute-done((bf16[24,768]{1,0:T(8,128)(2,1)S(1)}, bf16[24,768]{1,0:T(8,128)(2,1)S(1)}, u32[]{:S(2)}, u32[]{:S(2)}) %collective-permute-start.21) | collective-permute-done | bytes 36896 | tf_op jit(solution)/shard_map/ppermute | solution.py:240
  195.8 10.2 %attention_gradients.3 = (bf16[256,3072]{1,0:T(8,128)(2,1)}, bf16[256,3072]{1,0:T(8,128)(2,1)}, bf16[256,3072]{1,0:T(8,128)(2,1)}) custom-call(s32[1]{0:T(128)S(6)} %sub.11.pick, bf16[256,3072]{1,0:T(8,128)(2,1)S(1)} %bitcast.56, bf16[256,3072]{1,0:T(8,128)(2,1)S(1)} %bitcast.60, ...), custom_call_target="tpu_custom_call", output_to_operand_aliasing={{0}: (5, {}), {1}: (6, {}), {2}: (7, {})} | custom-call | flops 1006632960 | bytes 5505024 | tf_op jit(solution)/shard_map/attention_gradients/pallas_call | solution.py:117
  206.0 2.0 reduce_sum.25
  208.4 2.6 %collective-permute-start.24 = (bf16[24,768]{1,0:T(8,128)(2,1)S(1)}, bf16[24,768]{1,0:T(8,128)(2,1)S(1)}, u32[]{:S(2)}, u32[]{:S(2)}) collective-permute-start(bf16[24,768]{1,0:T(8,128)(2,1)S(1)} %get-tuple-element.51), channel_id=1, source_target_pairs={{0,128},{64,192},{128,0},{192,64},{1,129},{65,193},{129,1},{193,65... | collective-permute-start | bytes 110600 | tf_op jit(solution)/shard_map/ppermute | solution.py:240
  211.8 2.4 %collective-permute-start.26 = (f32[12,768]{1,0:T(8,128)S(1)}, f32[12,768]{1,0:T(8,128)S(1)}, u32[]{:S(2)}, u32[]{:S(2)}) collective-permute-start(f32[12,768]{1,0:T(8,128)S(1)} %get-tuple-element.53), channel_id=1, source_target_pairs={{0,8},{8,0},{1,9},{9,1},{2,10},{10,2},{3,11},{11,3},{4,12},{12,4},... | collective-permute-start | bytes 110600 | tf_op jit(solution)/shard_map/ppermute | solution.py:244
  215.4 3.0 %collective-permute-start.27 = (f32[12,768]{1,0:T(8,128)S(1)}, f32[12,768]{1,0:T(8,128)S(1)}, u32[]{:S(2)}, u32[]{:S(2)}) collective-permute-start(f32[12,768]{1,0:T(8,128)S(1)} %get-tuple-element.55), channel_id=1, source_target_pairs={{0,8},{8,0},{1,9},{9,1},{2,10},{10,2},{3,11},{11,3},{4,12},{12,4},... | collective-permute-start | bytes 110600 | tf_op jit(solution)/shard_map/ppermute | solution.py:244
  (76 shorter events, 23.5 us)
Async XLA Ops:
  4.5 11.6 %collective-permute-start.1 = (bf16[96,384]{1,0:T(8,128)(2,1)}, bf16[96,384]{1,0:T(8,128)(2,1)}, u32[]{:S(2)}, u32[]{:S(2)}) collective-permute-start(bf16[96,384]{1,0:T(8,128)(2,1)} %get-tuple-element.23), channel_id=1, source_target_pairs={{0,8},{8,0},{1,9},{9,1},{2,10},{10,2},{3,11},{11,3},{4,12},{12,4},... | collective-permute-start | bytes 221192 | tf_op jit(solution)/shard_map/ppermute | solution.py:260
  5.2 1.4 copy-start
  6.6 1.4 copy-start.2
  13.0 48.8 %collective-permute-start.11 = (bf16[1536,256]{1,0:T(8,128)(2,1)}, bf16[1536,256]{1,0:T(8,128)(2,1)}, u32[]{:S(2)}, u32[]{:S(2)}) collective-permute-start(bf16[1536,256]{1,0:T(8,128)(2,1)} %context_half.3.c0), channel_id=1, source_target_pairs={{0,8},{8,0},{1,9},{9,1},{2,10},{10,2},{3,11},{11,3},{4,12},{12,4},... | collective-permute-start | bytes 2359304 | tf_op jit(solution)/shard_map/ppermute | solution.py:274
  13.0 10.2 %copy-start.1 = (bf16[1,256,3072]{2,1,0:T(8,128)(2,1)S(1)}, bf16[1,256,3072]{2,1,0:T(8,128)(2,1)}, u32[]{:S(2)}) copy-start(bf16[1,256,3072]{2,1,0:T(8,128)(2,1)} %param.6) | copy-start | bytes 4718596
  13.0 10.2 %copy-start.3 = (bf16[1,256,3072]{2,1,0:T(8,128)(2,1)S(1)}, bf16[1,256,3072]{2,1,0:T(8,128)(2,1)}, u32[]{:S(2)}) copy-start(bf16[1,256,3072]{2,1,0:T(8,128)(2,1)} %param.7) | copy-start | bytes 4718596
  15.6 37.4 %collective-permute-start = (bf16[256,768]{1,0:T(8,128)(2,1)}, bf16[256,768]{1,0:T(8,128)(2,1)}, u32[]{:S(2)}, u32[]{:S(2)}) collective-permute-start(bf16[256,768]{1,0:T(8,128)(2,1)} %get-tuple-element.41), channel_id=1, source_target_pairs={{0,8},{8,0},{1,9},{9,1},{2,10},{10,2},{3,11},{11,3},{4,12},{12,4},... | collective-permute-start | bytes 1179656 | tf_op jit(solution)/shard_map/ppermute | solution.py:300
  17.1 14.4 %copy-start.10 = (bf16[96,384]{1,0:T(8,128)(2,1)S(1)}, bf16[96,384]{1,0:T(8,128)(2,1)}, u32[]{:S(2)}) copy-start(bf16[96,384]{1,0:T(8,128)(2,1)} %get-tuple-element.22) | copy-start | bytes 221188
  17.1 16.0 %collective-permute-start.2 = (bf16[192,384]{1,0:T(8,128)(2,1)S(1)}, bf16[192,384]{1,0:T(8,128)(2,1)S(1)}, u32[]{:S(2)}, u32[]{:S(2)}) collective-permute-start(bf16[192,384]{1,0:T(8,128)(2,1)S(1)} %maximum_select_fusion.3), channel_id=1, source_target_pairs={{0,192},{64,0},{128,64},{192,128},{1,193},{65,1},{129,65},{193,129... | collective-permute-start | bytes 442376 | tf_op jit(solution)/shard_map/ppermute | solution.py:266
  28.2 12.4 %collective-permute-start.3 = (bf16[192,384]{1,0:T(8,128)(2,1)S(1)}, bf16[192,384]{1,0:T(8,128)(2,1)S(1)}, u32[]{:S(2)}, u32[]{:S(2)}) collective-permute-start(bf16[192,384]{1,0:T(8,128)(2,1)S(1)} %maximum_select_fusion.3), channel_id=1, source_target_pairs={{0,128},{64,192},{128,0},{192,64},{1,129},{65,193},{129,1},{193,65... | collective-permute-start | bytes 442376 | tf_op jit(solution)/shard_map/ppermute | solution.py:266
  29.2 12.2 %collective-permute-start.4 = (bf16[192,384]{1,0:T(8,128)(2,1)S(1)}, bf16[192,384]{1,0:T(8,128)(2,1)S(1)}, u32[]{:S(2)}, u32[]{:S(2)}) collective-permute-start(bf16[192,384]{1,0:T(8,128)(2,1)S(1)} %maximum_select_fusion.3), channel_id=1, source_target_pairs={{0,64},{64,128},{128,192},{192,0},{1,65},{65,129},{129,193},{193,1... | collective-permute-start | bytes 442376 | tf_op jit(solution)/shard_map/ppermute | solution.py:266
  45.7 20.1 %collective-permute-start.7 = (bf16[1536,256]{1,0:T(8,128)(2,1)}, bf16[1536,256]{1,0:T(8,128)(2,1)}, u32[]{:S(2)}, u32[]{:S(2)}) collective-permute-start(bf16[1536,256]{1,0:T(8,128)(2,1)} %context_half.2), channel_id=1, source_target_pairs={{0,32},{32,0},{1,33},{33,1},{2,34},{34,2},{3,35},{35,3},{4,36},{36... | collective-permute-start | bytes 2359304 | tf_op jit(solution)/shard_map/ppermute | solution.py:272
  50.4 7.7 %collective-permute-start.10 = (bf16[2,192,384]{2,1,0:T(8,128)(2,1)}, bf16[2,192,384]{2,1,0:T(8,128)(2,1)}, u32[]{:S(2)}, u32[]{:S(2)}) collective-permute-start(bf16[2,192,384]{2,1,0:T(8,128)(2,1)} %get-tuple-element.45), channel_id=1, source_target_pairs={{0,20},{16,0},{4,16},{20,4},{1,21},{17,1},{5,17},{21,5},{2,22},{18... | collective-permute-start | bytes 884744 | tf_op jit(solution)/shard_map/ppermute | solution.py:279
  50.6 8.7 %collective-permute-start.9 = (bf16[2,192,384]{2,1,0:T(8,128)(2,1)}, bf16[2,192,384]{2,1,0:T(8,128)(2,1)}, u32[]{:S(2)}, u32[]{:S(2)}) collective-permute-start(bf16[2,192,384]{2,1,0:T(8,128)(2,1)} %get-tuple-element.44), channel_id=1, source_target_pairs={{0,16},{16,4},{4,20},{20,0},{1,17},{17,5},{5,21},{21,1},{2,18},{18... | collective-permute-start | bytes 884744 | tf_op jit(solution)/shard_map/ppermute | solution.py:278
  51.8 1.2 copy-start.9
  54.1 28.5 %copy-start.4 = (bf16[2,256,768]{2,1,0:T(8,128)(2,1)}, bf16[2,256,768]{2,1,0:T(8,128)(2,1)S(1)}, u32[]{:S(2)}) copy-start(bf16[2,256,768]{2,1,0:T(8,128)(2,1)S(1)} %pad_maximum_fusion.a0.near) | copy-start | bytes 2359300
  54.1 28.5 %collective-permute-start.5 = (bf16[2,256,768]{2,1,0:T(8,128)(2,1)S(1)}, bf16[2,256,768]{2,1,0:T(8,128)(2,1)S(1)}, u32[]{:S(2)}, u32[]{:S(2)}) collective-permute-start(bf16[2,256,768]{2,1,0:T(8,128)(2,1)S(1)} %pad_maximum_fusion.a0.near), channel_id=1, source_target_pairs={{0,32},{32,0},{1,33},{33,1},{2,34},{34,2},{3,35},{35,3},{4,36},{36... | collective-permute-start | bytes 2359304 | tf_op jit(solution)/shard_map/ppermute | solution.py:302
  65.8 16.9 %collective-permute-start.19 = (bf16[1536,256]{1,0:T(8,128)(2,1)}, bf16[1536,256]{1,0:T(8,128)(2,1)S(1)}, u32[]{:S(2)}, u32[]{:S(2)}) collective-permute-start(bf16[1536,256]{1,0:T(8,128)(2,1)} %collective-permute-done.7.c2), channel_id=1, source_target_pairs={{0,8},{8,0},{1,9},{9,1},{2,10},{10,2},{3,11},{11,3},{4,12},{12,4},... | collective-permute-start | bytes 2359304 | tf_op jit(solution)/shard_map/ppermute | solution.py:291
  68.3 34.8 %collective-permute-start.12 = (bf16[1536,384]{1,0:T(8,128)(2,1)}, bf16[1536,384]{1,0:T(8,128)(2,1)}, u32[]{:S(2)}, u32[]{:S(2)}) collective-permute-start(bf16[1536,384]{1,0:T(8,128)(2,1)} %bitcast.21.w0), channel_id=1, source_target_pairs={{0,1},{1,2},{2,3},{3,0},{4,5},{5,6},{6,7},{7,4},{8,9},{9,10},{10,1... | collective-permute-start | bytes 3538952 | tf_op jit(solution)/shard_map/ppermute | solution.py:286
  69.3 36.6 %collective-permute-start.13 = (bf16[1536,384]{1,0:T(8,128)(2,1)}, bf16[1536,384]{1,0:T(8,128)(2,1)}, u32[]{:S(2)}, u32[]{:S(2)}) collective-permute-start(bf16[1536,384]{1,0:T(8,128)(2,1)} %bitcast.21.w0), channel_id=1, source_target_pairs={{0,3},{1,0},{2,1},{3,2},{4,7},{5,4},{6,5},{7,6},{8,11},{9,8},{10,9... | collective-permute-start | bytes 3538952 | tf_op jit(solution)/shard_map/ppermute | solution.py:287
  82.6 0.9 copy-start.11
  89.6 0.9 copy-start.7
  90.5 68.1 %all-to-all-start = ((bf16[16,4,24,768]{3,2,1,0:T(8,128)(2,1)}), bf16[16,4,24,768]{3,2,1,0:T(8,128)(2,1)}, u32[]{:S(2)}, u32[]{:S(2)}) async-start(bf16[16,4,24,768]{3,2,1,0:T(8,128)(2,1)} %weight_gradient.2), calls=%async_computation | async-start | bytes 4718592 | tf_op jit(solution)/shard_map/all_to_all | solution.py:307
  97.2 3.5 %collective-permute-start.6 = (bf16[256,768]{1,0:T(8,128)(2,1)}, bf16[256,768]{1,0:T(8,128)(2,1)S(1)}, u32[]{:S(2)}, u32[]{:S(2)}) collective-permute-start(bf16[256,768]{1,0:T(8,128)(2,1)} %get-tuple-element.43), channel_id=1, source_target_pairs={{0,8},{8,0},{1,9},{9,1},{2,10},{10,2},{3,11},{11,3},{4,12},{12,4},... | collective-permute-start | bytes 1179656 | tf_op jit(solution)/shard_map/ppermute | solution.py:300
  101.6 19.1 %collective-permute-start.8 = (bf16[2,256,768]{2,1,0:T(8,128)(2,1)}, bf16[2,256,768]{2,1,0:T(8,128)(2,1)}, u32[]{:S(2)}, u32[]{:S(2)}) collective-permute-start(bf16[2,256,768]{2,1,0:T(8,128)(2,1)} %pad_maximum_fusion.1.b0.near), channel_id=1, source_target_pairs={{0,32},{32,0},{1,33},{33,1},{2,34},{34,2},{3,35},{35,3},{4,36},{36... | collective-permute-start | bytes 2359304 | tf_op jit(solution)/shard_map/ppermute | solution.py:302
  105.0 32.9 %collective-permute-start.14 = (bf16[768,384]{1,0:T(8,128)(2,1)}, bf16[768,384]{1,0:T(8,128)(2,1)}, u32[]{:S(2)}, u32[]{:S(2)}) collective-permute-start(bf16[768,384]{1,0:T(8,128)(2,1)} %slice.40), channel_id=1, source_target_pairs={{0,1},{1,2},{2,3},{3,0},{4,5},{5,6},{6,7},{7,4},{8,9},{9,10},{10,1... | collective-permute-start | bytes 1769480 | tf_op jit(solution)/shard_map/ppermute | solution.py:288
  107.9 30.0 %collective-permute-start.15 = (bf16[768,384]{1,0:T(8,128)(2,1)}, bf16[768,384]{1,0:T(8,128)(2,1)}, u32[]{:S(2)}, u32[]{:S(2)}) collective-permute-start(bf16[768,384]{1,0:T(8,128)(2,1)} %slice.41), channel_id=1, source_target_pairs={{0,3},{1,0},{2,1},{3,2},{4,7},{5,4},{6,5},{7,6},{8,11},{9,8},{10,9... | collective-permute-start | bytes 1769480 | tf_op jit(solution)/shard_map/ppermute | solution.py:289
  137.9 1.1 copy-start.5
  139.0 13.2 %copy-start.8 = (bf16[1536,256]{1,0:T(8,128)(2,1)S(1)}, bf16[1536,256]{1,0:T(8,128)(2,1)}, u32[]{:S(2)}) copy-start(bf16[1536,256]{1,0:T(8,128)(2,1)} %copy-done.7) | copy-start | bytes 2359300
  150.7 0.9 copy-start.6
  151.6 14.2 %collective-permute-start.16 = (bf16[256,1536]{1,0:T(8,128)(2,1)}, bf16[256,1536]{1,0:T(8,128)(2,1)}, u32[]{:S(2)}, u32[]{:S(2)}) collective-permute-start(bf16[256,1536]{1,0:T(8,128)(2,1)} %get-tuple-element.29), channel_id=1, source_target_pairs={{0,8},{8,0},{1,9},{9,1},{2,10},{10,2},{3,11},{11,3},{4,12},{12,4},... | collective-permute-start | bytes 2359304 | tf_op jit(solution)/shard_map/ppermute | solution.py:313
  158.5 47.4 %all-to-all-start.1 = ((bf16[16,4,24,768]{3,2,1,0:T(8,128)(2,1)}), bf16[16,4,24,768]{3,2,1,0:T(8,128)(2,1)}, u32[]{:S(2)}, u32[]{:S(2)}) async-start(bf16[16,4,24,768]{3,2,1,0:T(8,128)(2,1)} %weight_gradient.3), calls=%async_computation.1 | async-start | bytes 4718592 | tf_op jit(solution)/shard_map/all_to_all | solution.py:307
  165.3 16.1 %collective-permute-start.18 = (bf16[256,1536]{1,0:T(8,128)(2,1)}, bf16[256,1536]{1,0:T(8,128)(2,1)}, u32[]{:S(2)}, u32[]{:S(2)}) collective-permute-start(bf16[256,1536]{1,0:T(8,128)(2,1)} %copy-done.6), channel_id=1, source_target_pairs={{0,8},{8,0},{1,9},{9,1},{2,10},{10,2},{3,11},{11,3},{4,12},{12,4},... | collective-permute-start | bytes 2359304 | tf_op jit(solution)/shard_map/ppermute | solution.py:314
  168.6 27.2 %collective-permute-start.17 = (bf16[256,1536]{1,0:T(8,128)(2,1)}, bf16[256,1536]{1,0:T(8,128)(2,1)}, u32[]{:S(2)}, u32[]{:S(2)}) collective-permute-start(bf16[256,1536]{1,0:T(8,128)(2,1)} %add_convert_fusion), channel_id=1, source_target_pairs={{0,32},{32,0},{1,33},{33,1},{2,34},{34,2},{3,35},{35,3},{4,36},{36... | collective-permute-start | bytes 2359304 | tf_op jit(solution)/shard_map/ppermute | solution.py:315
  172.0 21.1 %collective-permute-start.20 = (bf16[24,768]{1,0:T(8,128)(2,1)S(1)}, bf16[24,768]{1,0:T(8,128)(2,1)S(1)}, u32[]{:S(2)}, u32[]{:S(2)}) collective-permute-start(bf16[24,768]{1,0:T(8,128)(2,1)S(1)} %get-tuple-element.46), channel_id=1, source_target_pairs={{0,64},{64,128},{128,192},{192,0},{1,65},{65,129},{129,193},{193,1... | collective-permute-start | bytes 110600 | tf_op jit(solution)/shard_map/ppermute | solution.py:240
  174.6 21.1 %collective-permute-start.21 = (bf16[24,768]{1,0:T(8,128)(2,1)S(1)}, bf16[24,768]{1,0:T(8,128)(2,1)S(1)}, u32[]{:S(2)}, u32[]{:S(2)}) collective-permute-start(bf16[24,768]{1,0:T(8,128)(2,1)S(1)} %get-tuple-element.48), channel_id=1, source_target_pairs={{0,128},{64,192},{128,0},{192,64},{1,129},{65,193},{129,1},{193,65... | collective-permute-start | bytes 110600 | tf_op jit(solution)/shard_map/ppermute | solution.py:240
  178.1 17.6 %collective-permute-start.22 = (bf16[24,768]{1,0:T(8,128)(2,1)S(1)}, bf16[24,768]{1,0:T(8,128)(2,1)S(1)}, u32[]{:S(2)}, u32[]{:S(2)}) collective-permute-start(bf16[24,768]{1,0:T(8,128)(2,1)S(1)} %get-tuple-element.47), channel_id=1, source_target_pairs={{0,192},{64,0},{128,64},{192,128},{1,193},{65,1},{129,65},{193,129... | collective-permute-start | bytes 110600 | tf_op jit(solution)/shard_map/ppermute | solution.py:240
  208.0 6.2 %collective-permute-start.23 = (bf16[24,768]{1,0:T(8,128)(2,1)S(1)}, bf16[24,768]{1,0:T(8,128)(2,1)S(1)}, u32[]{:S(2)}, u32[]{:S(2)}) collective-permute-start(bf16[24,768]{1,0:T(8,128)(2,1)S(1)} %get-tuple-element.49), channel_id=1, source_target_pairs={{0,64},{64,128},{128,192},{192,0},{1,65},{65,129},{129,193},{193,1... | collective-permute-start | bytes 110600 | tf_op jit(solution)/shard_map/ppermute | solution.py:240
  208.4 6.7 %collective-permute-start.24 = (bf16[24,768]{1,0:T(8,128)(2,1)S(1)}, bf16[24,768]{1,0:T(8,128)(2,1)S(1)}, u32[]{:S(2)}, u32[]{:S(2)}) collective-permute-start(bf16[24,768]{1,0:T(8,128)(2,1)S(1)} %get-tuple-element.51), channel_id=1, source_target_pairs={{0,128},{64,192},{128,0},{192,64},{1,129},{65,193},{129,1},{193,65... | collective-permute-start | bytes 110600 | tf_op jit(solution)/shard_map/ppermute | solution.py:240
  211.0 4.4 %collective-permute-start.25 = (bf16[24,768]{1,0:T(8,128)(2,1)S(1)}, bf16[24,768]{1,0:T(8,128)(2,1)S(1)}, u32[]{:S(2)}, u32[]{:S(2)}) collective-permute-start(bf16[24,768]{1,0:T(8,128)(2,1)S(1)} %get-tuple-element.50), channel_id=1, source_target_pairs={{0,192},{64,0},{128,64},{192,128},{1,193},{65,1},{129,65},{193,129... | collective-permute-start | bytes 110600 | tf_op jit(solution)/shard_map/ppermute | solution.py:240
  211.8 6.7 %collective-permute-start.26 = (f32[12,768]{1,0:T(8,128)S(1)}, f32[12,768]{1,0:T(8,128)S(1)}, u32[]{:S(2)}, u32[]{:S(2)}) collective-permute-start(f32[12,768]{1,0:T(8,128)S(1)} %get-tuple-element.53), channel_id=1, source_target_pairs={{0,8},{8,0},{1,9},{9,1},{2,10},{10,2},{3,11},{11,3},{4,12},{12,4},... | collective-permute-start | bytes 110600 | tf_op jit(solution)/shard_map/ppermute | solution.py:244
  215.4 3.9 %collective-permute-start.27 = (f32[12,768]{1,0:T(8,128)S(1)}, f32[12,768]{1,0:T(8,128)S(1)}, u32[]{:S(2)}, u32[]{:S(2)}) collective-permute-start(f32[12,768]{1,0:T(8,128)S(1)} %get-tuple-element.55), channel_id=1, source_target_pairs={{0,8},{8,0},{1,9},{9,1},{2,10},{10,2},{3,11},{11,3},{4,12},{12,4},... | collective-permute-start | bytes 110600 | tf_op jit(solution)/shard_map/ppermute | solution.py:244

commit v4 on v3

--- a/solution.py
+++ b/solution.py
@@ -136,67 +136,114 @@
     return lax.optimization_barrier((values, events))[0]
 
 
-def restore_body(place, codes_ref, scales_ref, near_ref, away_ref):
-    scales = scales_ref[...]
-    lanes = lax.broadcasted_iota(jnp.int32, scales.shape, 1)
-    for part, out in enumerate((near_ref, away_ref)):
-        for tile in range(out.shape[1] // 128):
-            column = place[part] * (out.shape[1] // 128) + tile
+def restore_body(codes_ref, scales_ref, near_ref, away_ref):
+    core, y = lax.axis_index("c"), lax.axis_index("y")
+    blocks = scales_ref.shape[0]
+    width = near_ref.shape[1]
+    for side, out in ((core, near_ref), (1 - core, away_ref)):
+        first = (side * 4 + y) * (width // 128)
+        for tile in range(width // 128):
+            column = first + tile
             codes = codes_ref[:, pl.ds(pl.multiple_of(column * 128, 128), 128)].astype(F32)
-            chosen = jnp.where(lanes == column // 2, scales, 0.0)
-            scale = jnp.sum(chosen, axis=1, keepdims=True)
+            lane = lax.broadcasted_iota(jnp.int32, (blocks, 128), 0)
+            chosen = jnp.where(lane == column // 2, 1.0, 0.0)
+            scale = lax.dot_general(
+                scales_ref[...],
+                chosen,
+                TN,
+                precision=lax.Precision.HIGHEST,
+                preferred_element_type=F32,
+            )
             out[:, tile * 128 : (tile + 1) * 128] = (codes * scale).astype(BF16)
 
 
-def restore(places, codes, scales):
+def restore(codes, scales):
     rows = codes.shape[0]
     return pl.pallas_call(
         restore_body,
-        in_specs=[
-            pl.BlockSpec(memory_space=pltpu.SMEM),
-            pl.BlockSpec(memory_space=pltpu.VMEM),
-            pl.BlockSpec(memory_space=pltpu.VMEM),
-        ],
         out_shape=[jax.ShapeDtypeStruct((rows, 384), BF16)] * 2,
         cost_estimate=cost(rows * 768, rows * 3072),
         name="weight_pieces",
-    )(places, codes, scales)
+    )(codes, scales)
+
+
+def by_zh_body(own_ref, b1, b2, b3, low_ref, high_ref):
+    zh = lax.axis_index("zh")
+    for step, piece in enumerate((own_ref, b1, b2, b3)):
+        place = lax.rem(zh - step + 4, 4)
+
+        @pl.when(place < 2)
+        def _():
+            low_ref[place] = piece[...]
+
+        @pl.when(place >= 2)
+        def _():
+            high_ref[place - 2] = piece[...]
+
+
+def by_zh(own, pieces):
+    return pl.pallas_call(
+        by_zh_body,
+        out_shape=[jax.ShapeDtypeStruct((2, *own.shape), BF16)] * 2,
+        cost_estimate=cost(own.size, own.size * 16),
+        name="weight_by_zh",
+    )(own, *pieces)
+
+
+def by_xl_body(low, high, beside_low, beside_high, low_ref, high_ref):
+    xl = lax.axis_index("xl")
+    for mine, beside, out in ((low, beside_low, low_ref), (high, beside_high, high_ref)):
+        for place in range(2):
+            out[place, xl] = mine[place]
+            out[place, 1 - xl] = beside[place]
+
+
+def by_xl(low, high, beside_low, beside_high):
+    shape = (2, 2, *low.shape[1:])
+    return pl.pallas_call(
+        by_xl_body,
+        out_shape=[jax.ShapeDtypeStruct(shape, BF16)] * 2,
+        cost_estimate=cost(low.size, low.size * 16),
+        name="weight_by_xl",
+    )(low, high, beside_low, beside_high)
 
 
 def four_images(near, away):
     return jnp.concatenate([near[0], near[1], away[0], away[1]], axis=0)
 
 
-def context_gradient_body(place, a0, a1, b0, b1, w0, w1, w2, wa, wb, g0, g1, g2, g3, rows_ref):
-    far = jnp.where(pl.program_id(0) < 2, wa[...], wb[...])
-    width = w0.shape[1]
+def context_gradient_body(place, a0, a1, b0, b1, *refs):
+    lows, highs, outs, rows_ref = refs[:4], refs[4:8], refs[8:12], refs[12]
     seq = a0.shape[1]
-    for part, weight in enumerate((w0[...], w1[...], w2[...], far)):
-        rows_ref[:, pl.ds(pl.multiple_of(place[part] * width, 128), width)] = weight
+
+    def gather(weights):
+        width = weights[0].shape[1]
+        for part, weight in enumerate(weights):
+            cols = pl.ds(pl.multiple_of(place[part] * width, 128), width)
+            rows_ref[:, cols] = weight[...]
+
+    pl.when(pl.program_id(0) < 2)(functools.partial(gather, lows))
+    pl.when(pl.program_id(0) >= 2)(functools.partial(gather, highs))
     grads = jnp.concatenate([four_images(a0, a1), four_images(b0, b1)], axis=1)
     total = dot(grads, rows_ref[...], NT)
-    for image, out in enumerate((g0, g1, g2, g3)):
+    for image, out in enumerate(outs):
         out[...] = total[image * seq : (image + 1) * seq].astype(out.dtype)
 
 
-def context_gradient(places, grads, weights):
+def context_gradient(places, grads, lows, highs):
     _, seq, part = grads[0].shape
-    rows, width = weights[0].shape
-    block = rows // 4
+    block, width = lows[0].shape[0] // 2, lows[0].shape[1]
+    rows = 4 * block
     full = pl.BlockSpec((2, seq, part), lambda i, place: (0, 0, 0))
-    by_row = pl.BlockSpec((block, width), lambda i, place: (i, 0))
+    low = pl.BlockSpec((block, width), lambda i, place: (jnp.minimum(i, 1), 0))
+    high = pl.BlockSpec((block, width), lambda i, place: (jnp.maximum(i - 2, 0), 0))
     out = pl.BlockSpec((seq, block), lambda i, place: (0, i))
     return pl.pallas_call(
         context_gradient_body,
         grid_spec=pltpu.PrefetchScalarGridSpec(
             num_scalar_prefetch=1,
             grid=(4,),
-            in_specs=[full] * 4
-            + [by_row] * 3
-            + [
-                pl.BlockSpec((block, width), lambda i, place: (jnp.minimum(i, 1), 0)),
-                pl.BlockSpec((block, width), lambda i, place: (jnp.maximum(i - 2, 0), 0)),
-            ],
+            in_specs=[full] * 4 + [low] * 4 + [high] * 4,
             out_specs=[out] * 4,
             scratch_shapes=[pltpu.VMEM((block, 2 * part), BF16)],
         ),
@@ -206,7 +253,7 @@
         compiler_params=params(),
         cost_estimate=cost(16 * seq * part * rows, 20 * 2**20),
         name="context_gradient",
-    )(places, *grads, *weights)
+    )(places, *grads, *lows, *highs)
 
 
 def weight_gradient_body(c0, c1, c2, c3, near, away, out_ref):
@@ -255,39 +302,32 @@
     own_parity = zl.astype(jnp.int32).reshape(1)
     other_parity = 1 - own_parity
 
-    places = jnp.stack([c * 4 + y, (1 - c) * 4 + y]).astype(jnp.int32)
-    pieces = restore(places, weight_codes, weight_scales)
-    arrived = lax.ppermute(pieces[1], "c", SWAP)
+    piece, sent = restore(weight_codes, weight_scales.T)
+    arrived = lax.ppermute(sent, "c", SWAP)
     pair = jnp.where(
-        c == 0,
-        jnp.concatenate([pieces[0], arrived], 0),
-        jnp.concatenate([arrived, pieces[0]], 0),
-    )
-    from_behind = [lax.ppermute(pair, "zh", ring(4, step)) for step in (1, 2, 3)]
-    turned = [pair, from_behind[2], from_behind[1], from_behind[0]]
-    column = lax.dynamic_slice_in_dim(jnp.stack(turned + turned), (4 - zh) % 4, 4, 0)
-
+        c == 0, jnp.concatenate([piece, arrived], 0), jnp.concatenate([arrived, piece], 0)
+    )
+    behind = [lax.ppermute(pair, "zh", ring(4, step)) for step in (1, 2, 3)]
+    low, high = by_zh(pair, behind)
+    start = low
+    beside_low = lax.ppermute(low, ("xl", "xh"), x_ring(1))
+    beside_high = lax.ppermute(high, ("xl", "xh"), x_ring(-1))
+
+    q, k = after((q, k), (behind[0],))
     context_other = forward(other_parity, q, k, v, width)
-    (context_other,) = after((context_other,), (column,))
+    (context_other,) = after((context_other,), (low,))
     c2 = lax.ppermute(context_other, "zl", SWAP)
     context_own = forward(own_parity, q, k, v, width)
     c1 = lax.ppermute(context_own, "c", SWAP)
 
-    beside = jnp.concatenate(
-        [
-            lax.ppermute(column[:2], ("xl", "xh"), x_ring(1)),
-            lax.ppermute(column[2:], ("xl", "xh"), x_ring(-1)),
-        ],
-        0,
-    )
-    here = jnp.where(xl == 0, jnp.stack([column, beside], 1), jnp.stack([beside, column], 1))
-    (here,) = after((here.reshape(-1, width),), (c1,))
-    rows = here.shape[0]
-    below = lax.ppermute(here, "y", ring(4, 1))
-    above = lax.ppermute(here, "y", ring(4, -1))
-    far_a = lax.ppermute(below[: rows // 2], "y", ring(4, 1))
-    far_b = lax.ppermute(above[rows // 2 :], "y", ring(4, -1))
-    (event,) = after((c2,), (here,))
+    low, high = by_xl(low, high, beside_low, beside_high)
+    lows, highs = ([piece.reshape(-1, width)] for piece in (low, high))
+    for step in (1, -1):
+        lows.append(lax.ppermute(lows[0], "y", ring(4, step)))
+        highs.append(lax.ppermute(highs[0], "y", ring(4, step)))
+    lows.append(lax.ppermute(lows[1], "y", ring(4, 1)))
+    highs.append(lax.ppermute(highs[2], "y", ring(4, -1)))
+    (event,) = after((c2,), (lows[1], highs[2]))
     c3 = lax.ppermute(event, "c", SWAP)
 
     part = half // 2
@@ -298,17 +338,20 @@
             for side in (c, 1 - c)
         )
         near = jnp.stack([own, lax.ppermute(partner, "c", SWAP)])
-        (sent,) = after((near,), (column,) if index == 0 else (c2,))
+        (sent,) = after((near,), (start,) if index == 0 else (c2,))
         grads.append((near, lax.ppermute(sent, "zl", SWAP)))
 
+    (c1,) = after((c1,), (lows[2], highs[1]))
     terms = []
     for near, away in grads:
         term = weight_gradient((context_own, c1, c2, c3), near, away)
+        (term,) = after((term,), (lows[3], highs[3]))
         terms.append(lax.all_to_all(term, ("xl", "xh", "y"), 0, 0, tiled=True))
 
     places = jnp.stack([y, (y + 3) % 4, (y + 1) % 4, (y + 2) % 4]).astype(jnp.int32)
+    (near,) = after(grads[0][:1], (term,))
     g0, g1, g2, g3 = context_gradient(
-        places, grads[0] + grads[1], (here, below, above, far_a, far_b)
+        places, (near, grads[0][1]) + grads[1], lows, highs
     )
     r3 = lax.ppermute(g3, "c", SWAP)
     r1 = lax.ppermute(g1, "c", SWAP)

time: 222 us -> 208 us (0.937)
  local copies, waits for them, and re-layouts: 22.8 us -> 13.5 us
  other arithmetic: 15.8 us -> 9.56 us
  Pallas kernels: 56.5 us -> 59.6 us
  waiting for transfers between devices: 66 us -> 63.1 us
    ppermute x1, waiting for transfers between devices: 0.01 us -> 7.73 us  [per_device(): g_other = lax.ppermute((g2 + r3.astype(F32)).astype(BF16), 'zl', SWAP)]
    ppermute x2, waiting for transfers between devices: 25 us -> 17.8 us  [per_device(): grads.append((near, lax.ppermute(sent, 'zl', SWAP)))]
    slice x3 -> x0, local copies, waits for them, and re-layouts: 5.85 us -> none  [the longest x1 1.98 us: per_device(): far_b = lax.ppermute(above[rows // 2:], 'y', ring(4, -1))]
    ppermute x6, waiting for transfers between devices: 5.36 us -> 0.02 us  [sums_on_owners(): mine = mine + lax.ppermute(away, 'zh', ring(4, step)).astype(F32)]
    pallas_call x1 -> x3, Pallas kernels: 1.87 us -> 6.61 us  [the longest x1 2.45 us: by_xl(): pl.pallas_call(by_xl_body, out_shape=[jax.ShapeDtypeStruct(shape, BF16)]...]
    unnamed x2 -> x0, other arithmetic: 3.32 us -> none
    ppermute x1, starting transfers between devices: 2.7 us -> 0.01 us  [per_device(): c2 = lax.ppermute(context_other, 'zl', SWAP)]
    ppermute x10 -> x12, starting transfers between devices: 14.4 us -> 16.1 us  [the longest x3 10.6 us: per_device(): behind = [lax.ppermute(pair, 'zh', ring(4, step)) for step in (1, 2, 3)]]
  transfers between devices with their start and end apart: 30 -> 32, of which waited for: 13 -> 12; matrix products, arithmetic and copies ran while one was open for 12% -> 5% of each run, Pallas kernels for 25% -> 27%
where the time goes in v4:
time: 208 us; the launch traced here: 206 us
  waiting for transfers between devices  63.1 us (30%)
  Pallas kernels  59.6 us (29%)
  starting transfers between devices  59.2 us (28%)
  local copies, waits for them, and re-layouts  13.5 us (6%)
  other arithmetic  9.56 us (5%)
    pallas_call x2, Pallas kernels, backward(): pl.pallas_call(functools.partial(backward_body, before is None), grid_spe...  20.4 us
    ppermute x2, waiting for transfers between devices, per_device(): grads.append((near, lax.ppermute(sent, 'zl', SWAP)))  17.8 us
    all_to_all x2, starting transfers between devices, per_device(): terms.append(lax.all_to_all(term, ('xl', 'xh', 'y'), 0, 0, tiled=True))  13.6 us
    ppermute x6, starting transfers between devices, sums_on_owners(): mine = mine + lax.ppermute(away, 'zh', ring(4, step)).astype(F32)  12.9 us
    ppermute x3, waiting for transfers between devices, per_device(): behind = [lax.ppermute(pair, 'zh', ring(4, step)) for step in (1, 2, 3)]  11.9 us
    pallas_call x2, Pallas kernels, weight_gradient(): pl.pallas_call(weight_gradient_body, grid=(4,), in_specs=[pl.BlockSpec((r...  11.9 us
    pallas_call x1, Pallas kernels, context_gradient(): pl.pallas_call(context_gradient_body, grid_spec=pltpu.PrefetchScalarGridS...  11.4 us
    unnamed x60, local copies, waits for them, and re-layouts  11 us
  transfers between devices with their start and end apart: 32, of which 12 were waited for; matrix products, arithmetic and copies ran while one was open for 5% of the time, Pallas kernels for 27%

profile of v4, /device:TPU:19, one launch (start us, length us, event | category | flops | bytes accessed | tf_op | source)
XLA Modules:
  0.0 205.8 jit_solution(10832802242147202922)
XLA Ops:
  0.6 2.1 %weight_pieces.1 = (bf16[96,384]{1,0:T(8,128)(2,1)}, bf16[96,384]{1,0:T(8,128)(2,1)}) custom-call(bf16[96,3072]{1,0:T(8,128)(2,1)} %codes_ref.1, f32[12,96]{1,0:T(8,128)} %bitcast.61), custom_call_target="tpu_custom_call" | custom-call | flops 73728 | bytes 294912 | tf_op jit(solution)/shard_map/weight_pieces/pallas_call | solution.py:162
  3.5 1.1 collective-permute-done
  5.6 3.1 %collective-permute-start.1 = (bf16[192,384]{1,0:T(8,128)(2,1)S(1)}, bf16[192,384]{1,0:T(8,128)(2,1)S(1)}, u32[]{:S(2)}, u32[]{:S(2)}) collective-permute-start(bf16[192,384]{1,0:T(8,128)(2,1)S(1)} %maximum_select_fusion.1.own_ref), channel_id=1, source_target_pairs={{0,64},{64,128},{128,192},{192,0},{1,65},{65,129},{129,193},{193,1... | collective-permute-start | bytes 442376 | tf_op jit(solution)/shard_map/ppermute | solution.py:310
  8.6 5.1 %collective-permute-start.4 = (bf16[192,384]{1,0:T(8,128)(2,1)S(1)}, bf16[192,384]{1,0:T(8,128)(2,1)S(1)}, u32[]{:S(2)}, u32[]{:S(2)}) collective-permute-start(bf16[192,384]{1,0:T(8,128)(2,1)S(1)} %maximum_select_fusion.1.own_ref), channel_id=1, source_target_pairs={{0,128},{64,192},{128,0},{192,64},{1,129},{65,193},{129,1},{193,65... | collective-permute-start | bytes 442376 | tf_op jit(solution)/shard_map/ppermute | solution.py:310
  13.8 2.4 %collective-permute-start.5 = (bf16[192,384]{1,0:T(8,128)(2,1)S(1)}, bf16[192,384]{1,0:T(8,128)(2,1)S(1)}, u32[]{:S(2)}, u32[]{:S(2)}) collective-permute-start(bf16[192,384]{1,0:T(8,128)(2,1)S(1)} %maximum_select_fusion.1.own_ref), channel_id=1, source_target_pairs={{0,192},{64,0},{128,64},{192,128},{1,193},{65,1},{129,65},{193,129... | collective-permute-start | bytes 442376 | tf_op jit(solution)/shard_map/ppermute | solution.py:310
  16.2 7.5 %collective-permute-done.4.b2 = bf16[192,384]{1,0:T(8,128)(2,1)S(1)} collective-permute-done((bf16[192,384]{1,0:T(8,128)(2,1)S(1)}, bf16[192,384]{1,0:T(8,128)(2,1)S(1)}, u32[]{:S(2)}, u32[]{:S(2)}) %collective-permute-start.4) | collective-permute-done | bytes 147488 | tf_op jit(solution)/shard_map/ppermute | solution.py:310
  23.7 4.4 %collective-permute-done.5.b3 = bf16[192,384]{1,0:T(8,128)(2,1)S(1)} collective-permute-done((bf16[192,384]{1,0:T(8,128)(2,1)S(1)}, bf16[192,384]{1,0:T(8,128)(2,1)S(1)}, u32[]{:S(2)}, u32[]{:S(2)}) %collective-permute-start.5) | collective-permute-done | bytes 147488 | tf_op jit(solution)/shard_map/ppermute | solution.py:310
  28.8 2.0 weight_by_zh.1
  30.8 1.2 collective-permute-start.6
  32.3 1.4 copy-done
  33.7 1.4 copy-done.2
  35.1 5.0 %context_half.3 = bf16[1536,256]{1,0:T(8,128)(2,1)} custom-call(s32[1]{0:T(128)S(6)} %sub.7.pick, bf16[256,3072]{1,0:T(8,128)(2,1)S(1)} %bitcast.38, bf16[256,3072]{1,0:T(8,128)(2,1)S(1)} %bitcast.42, bf16[256,3072]{1,0:T(8,128)(2,1)} %bitcast.52), custom_call_target="tpu_custom_call" | custom-call | flops 402653184 | bytes 3145728 | tf_op jit(solution)/shard_map/context_half/pallas_call | solution.py:73
  40.8 2.4 %weight_by_xl.1 = (bf16[2,2,192,384]{3,2,1,0:T(8,128)(2,1)}, bf16[2,2,192,384]{3,2,1,0:T(8,128)(2,1)}) custom-call(bf16[2,192,384]{2,1,0:T(8,128)(2,1)} %get-tuple-element.35.low, bf16[2,192,384]{2,1,0:T(8,128)(2,1)} %get-tuple-element.36.high, bf16[2,192,384]{2,1,0:T(8,128)(2,1)} %copy-done.24, bf16[2,192,384]{2,1,0:T(8,128)(2,1)} %collective-permute-done.7.beside_high), custom_call_target="tpu_custom_call" | custom-call | flops 147456 | bytes 2359296 | tf_op jit(solution)/shard_map/weight_by_xl/pallas_call | solution.py:203
  44.7 2.4 %constant_dynamic-slice_fusion = (bf16[1,256,768]{2,1,0:T(8,128)(2,1)S(1)}, bf16[256,768]{1,0:T(8,128)(2,1)S(1)}, bf16[1,256,768]{2,1,0:T(8,128)(2,1)S(1)}, bf16[256,768]{1,0:T(8,128)(2,1)}) fusion(bf16[1,256,3072]{2,1,0:T(8,128)(2,1)} %param.9, s32[]{:T(128)S(6)} %select_n.105, s32[]{:T(128)S(6)} %select_n.104, s32[]{:T(128)S(6)} %select_n.103, ...), kind=kLoop, calls=%fused_computation.23 | loop fusion | bytes 3145744 | tf_op jit(solution)/shard_map/dynamic_slice | solution.py:337
  47.1 1.6 collective-permute-start.2
  48.7 4.3 %context_half.2.c0 = bf16[1536,256]{1,0:T(8,128)(2,1)S(1)} custom-call(s32[1]{0:T(128)} %bitcast.pick, bf16[256,3072]{1,0:T(8,128)(2,1)S(1)} %bitcast.39, bf16[256,3072]{1,0:T(8,128)(2,1)S(1)} %bitcast.43, bf16[256,3072]{1,0:T(8,128)(2,1)} %bitcast.53), custom_call_target="tpu_custom_call" | custom-call | flops 402653184 | bytes 3145728 | tf_op jit(solution)/shard_map/context_half/pallas_call | solution.py:73
  53.6 4.8 %collective-permute-done.10.c2 = bf16[1536,256]{1,0:T(8,128)(2,1)} collective-permute-done((bf16[1536,256]{1,0:T(8,128)(2,1)}, bf16[1536,256]{1,0:T(8,128)(2,1)}, u32[]{:S(2)}, u32[]{:S(2)}) %collective-permute-start.10) | collective-permute-done | bytes 786464 | tf_op jit(solution)/shard_map/ppermute | solution.py:319
  58.7 3.3 %collective-permute-start.13 = (bf16[1536,256]{1,0:T(8,128)(2,1)}, bf16[1536,256]{1,0:T(8,128)(2,1)S(1)}, u32[]{:S(2)}, u32[]{:S(2)}) collective-permute-start(bf16[1536,256]{1,0:T(8,128)(2,1)} %collective-permute-done.10.c2), channel_id=1, source_target_pairs={{0,8},{8,0},{1,9},{9,1},{2,10},{10,2},{3,11},{11,3},{4,12},{12,4},... | collective-permute-start | bytes 2359304 | tf_op jit(solution)/shard_map/ppermute | solution.py:331
  62.0 1.2 collective-permute-start.9
  63.3 7.3 %collective-permute-done.8.refs_2_ = bf16[768,384]{1,0:T(8,128)(2,1)S(1)} collective-permute-done((bf16[768,384]{1,0:T(8,128)(2,1)S(1)}, bf16[768,384]{1,0:T(8,128)(2,1)S(1)}, u32[]{:S(2)}, u32[]{:S(2)}) %collective-permute-start.8) | collective-permute-done | bytes 589856 | tf_op jit(solution)/shard_map/ppermute | solution.py:326
  71.9 4.9 %collective-permute-done.9.refs_5_ = bf16[768,384]{1,0:T(8,128)(2,1)S(1)} collective-permute-done((bf16[768,384]{1,0:T(8,128)(2,1)S(1)}, bf16[768,384]{1,0:T(8,128)(2,1)S(1)}, u32[]{:S(2)}, u32[]{:S(2)}) %collective-permute-start.9) | collective-permute-done | bytes 589856 | tf_op jit(solution)/shard_map/ppermute | solution.py:327
  78.4 5.9 %weight_gradient.3 = bf16[16,4,24,768]{3,2,1,0:T(8,128)(2,1)} custom-call(bf16[1536,256]{1,0:T(8,128)(2,1)S(1)} %context_half.2.c0, bf16[1536,256]{1,0:T(8,128)(2,1)S(1)} %collective-permute-done.3.c1, bf16[1536,256]{1,0:T(8,128)(2,1)} %collective-permute-done.10.c2, bf16[1536,256]{1,0:T(8,128)(2,1)S(1)} %collective-permute-done.13.c3, ...), custom_call_target="tpu_custom_call" | custom-call | flops 2415919104 | bytes 8388608 | tf_op jit(solution)/shard_map/weight_gradient/pallas_call | solution.py:270
  84.4 5.0 %collective-permute-done.16.refs_3_ = bf16[768,384]{1,0:T(8,128)(2,1)S(1)} collective-permute-done((bf16[768,384]{1,0:T(8,128)(2,1)S(1)}, bf16[768,384]{1,0:T(8,128)(2,1)S(1)}, u32[]{:S(2)}, u32[]{:S(2)}) %collective-permute-start.16) | collective-permute-done | bytes 589856 | tf_op jit(solution)/shard_map/ppermute | solution.py:328
  90.2 7.0 %all-to-all-start = ((bf16[16,4,24,768]{3,2,1,0:T(8,128)(2,1)}), bf16[16,4,24,768]{3,2,1,0:T(8,128)(2,1)}, u32[]{:S(2)}, u32[]{:S(2)}) async-start(bf16[16,4,24,768]{3,2,1,0:T(8,128)(2,1)} %weight_gradient.3), calls=%async_computation | async-start | bytes 4718592 | tf_op jit(solution)/shard_map/all_to_all | solution.py:349
  97.2 1.4 collective-permute-start.14
  98.5 1.6 collective-permute-done.14
  101.1 1.7 collective-permute-start.15
  102.9 17.8 %collective-permute-done.15.away.b1 = bf16[2,256,768]{2,1,0:T(8,128)(2,1)} collective-permute-done((bf16[2,256,768]{2,1,0:T(8,128)(2,1)}, bf16[2,256,768]{2,1,0:T(8,128)(2,1)}, u32[]{:S(2)}, u32[]{:S(2)}) %collective-permute-start.15) | collective-permute-done | bytes 786464 | tf_op jit(solution)/shard_map/ppermute | solution.py:342
  120.8 1.1 copy-done.6
  121.9 1.1 copy-done.8
  123.0 1.1 copy-done.10
  124.2 6.0 %weight_gradient.2 = bf16[16,4,24,768]{3,2,1,0:T(8,128)(2,1)} custom-call(bf16[1536,256]{1,0:T(8,128)(2,1)S(1)} %copy-done.6, bf16[1536,256]{1,0:T(8,128)(2,1)S(1)} %copy-done.8, bf16[1536,256]{1,0:T(8,128)(2,1)} %collective-permute-done.10.c2, bf16[1536,256]{1,0:T(8,128)(2,1)S(1)} %copy-done.10, bf16[2,256,768]{2,1,0:T(8,128)(2,1)} %pad_maximum_fusion.1.near.b0, ...), custom_call_target="tpu_custom_call" | custom-call | flops 2415919104 | bytes 8388608 | tf_op jit(solution)/shard_map/weight_gradient/pallas_call | solution.py:270
  130.2 11.4 %context_gradient.1 = (f32[256,1536]{1,0:T(8,128)}, bf16[256,1536]{1,0:T(8,128)(2,1)}, f32[256,1536]{1,0:T(8,128)}, bf16[256,1536]{1,0:T(8,128)(2,1)}) custom-call(s32[4]{0:T(128)S(1)} %pad_add_fusion.place, bf16[2,256,768]{2,1,0:T(8,128)(2,1)} %copy-done.4, bf16[2,256,768]{2,1,0:T(8,128)(2,1)} %copy-done.28, ...), custom_call_target="tpu_custom_call" | custom-call | flops 4831838208 | bytes 20971520 | tf_op jit(solution)/shard_map/context_gradient/pallas_call | solution.py:241
  142.5 6.7 %all-to-all-start.1 = ((bf16[16,4,24,768]{3,2,1,0:T(8,128)(2,1)}), bf16[16,4,24,768]{3,2,1,0:T(8,128)(2,1)}, u32[]{:S(2)}, u32[]{:S(2)}) async-start(bf16[16,4,24,768]{3,2,1,0:T(8,128)(2,1)} %weight_gradient.2), calls=%async_computation.1 | async-start | bytes 4718592 | tf_op jit(solution)/shard_map/all_to_all | solution.py:349
  149.7 2.7 %add_convert_fusion = bf16[256,1536]{1,0:T(8,128)(2,1)} fusion(f32[256,1536]{1,0:T(8,128)} %get-tuple-element.46, bf16[256,1536]{1,0:T(8,128)(2,1)} %collective-permute-done.19), kind=kLoop, calls=%fused_computation | loop fusion | flops 1179648 | bytes 3145728 | tf_op jit(solution)/shard_map/convert_element_type | solution.py:358
  152.4 1.5 collective-permute-start.20
  153.9 10.3 %attention_gradients.2 = (bf16[256,3072]{1,0:T(8,128)(2,1)}, bf16[256,3072]{1,0:T(8,128)(2,1)}, bf16[256,3072]{1,0:T(8,128)(2,1)}) custom-call(s32[1]{0:T(128)} %bitcast.pick, bf16[256,3072]{1,0:T(8,128)(2,1)S(1)} %bitcast.40, bf16[256,3072]{1,0:T(8,128)(2,1)S(1)} %bitcast.44, bf16[256,3072]{1,0:T(8,128)(2,1)} %bitcast.54, ...), custom_call_target="tpu_custom_call" | custom-call | flops 1006632960 | bytes 5505024 | tf_op jit(solution)/shard_map/attention_gradients/pallas_call | solution.py:117
  164.2 7.7 %collective-permute-done.20.refs_0_ = bf16[256,1536]{1,0:T(8,128)(2,1)} collective-permute-done((bf16[256,1536]{1,0:T(8,128)(2,1)}, bf16[256,1536]{1,0:T(8,128)(2,1)}, u32[]{:S(2)}, u32[]{:S(2)}) %collective-permute-start.20) | collective-permute-done | bytes 786464 | tf_op jit(solution)/shard_map/ppermute | solution.py:358
  171.9 10.1 %attention_gradients.3 = (bf16[256,3072]{1,0:T(8,128)(2,1)}, bf16[256,3072]{1,0:T(8,128)(2,1)}, bf16[256,3072]{1,0:T(8,128)(2,1)}) custom-call(s32[1]{0:T(128)S(6)} %sub.7.pick, bf16[256,3072]{1,0:T(8,128)(2,1)S(1)} %bitcast.41, bf16[256,3072]{1,0:T(8,128)(2,1)S(1)} %bitcast.45, ...), custom_call_target="tpu_custom_call", output_to_operand_aliasing={{0}: (5, {}), {1}: (6, {}), {2}: (7, {})} | custom-call | flops 1006632960 | bytes 5505024 | tf_op jit(solution)/shard_map/attention_gradients/pallas_call | solution.py:117
  182.0 2.0 reduce_sum.24
  184.1 1.6 collective-permute-start.22
  185.7 4.0 %collective-permute-start.23 = (bf16[24,768]{1,0:T(8,128)(2,1)S(1)}, bf16[24,768]{1,0:T(8,128)(2,1)S(1)}, u32[]{:S(2)}, u32[]{:S(2)}) collective-permute-start(bf16[24,768]{1,0:T(8,128)(2,1)S(1)} %get-tuple-element.64), channel_id=1, source_target_pairs={{0,128},{64,192},{128,0},{192,64},{1,129},{65,193},{129,1},{193,65... | collective-permute-start | bytes 110600 | tf_op jit(solution)/shard_map/ppermute | solution.py:287
  189.8 2.1 %collective-permute-start.24 = (bf16[24,768]{1,0:T(8,128)(2,1)S(1)}, bf16[24,768]{1,0:T(8,128)(2,1)S(1)}, u32[]{:S(2)}, u32[]{:S(2)}) collective-permute-start(bf16[24,768]{1,0:T(8,128)(2,1)S(1)} %get-tuple-element.63), channel_id=1, source_target_pairs={{0,192},{64,0},{128,64},{192,128},{1,193},{65,1},{129,65},{193,129... | collective-permute-start | bytes 110600 | tf_op jit(solution)/shard_map/ppermute | solution.py:287
  191.9 2.0 reduce_sum.25
  194.2 1.9 collective-permute-start.26
  196.1 2.9 %collective-permute-start.27 = (bf16[24,768]{1,0:T(8,128)(2,1)S(1)}, bf16[24,768]{1,0:T(8,128)(2,1)S(1)}, u32[]{:S(2)}, u32[]{:S(2)}) collective-permute-start(bf16[24,768]{1,0:T(8,128)(2,1)S(1)} %get-tuple-element.66), channel_id=1, source_target_pairs={{0,192},{64,0},{128,64},{192,128},{1,193},{65,1},{129,65},{193,129... | collective-permute-start | bytes 110600 | tf_op jit(solution)/shard_map/ppermute | solution.py:287
  199.1 2.6 %collective-permute-start.28 = (f32[12,768]{1,0:T(8,128)S(1)}, f32[12,768]{1,0:T(8,128)S(1)}, u32[]{:S(2)}, u32[]{:S(2)}) collective-permute-start(f32[12,768]{1,0:T(8,128)S(1)} %get-tuple-element.69), channel_id=1, source_target_pairs={{0,8},{8,0},{1,9},{9,1},{2,10},{10,2},{3,11},{11,3},{4,12},{12,4},... | collective-permute-start | bytes 110600 | tf_op jit(solution)/shard_map/ppermute | solution.py:291
  201.7 2.5 %collective-permute-start.29 = (f32[12,768]{1,0:T(8,128)S(1)}, f32[12,768]{1,0:T(8,128)S(1)}, u32[]{:S(2)}, u32[]{:S(2)}) collective-permute-start(f32[12,768]{1,0:T(8,128)S(1)} %get-tuple-element.71), channel_id=1, source_target_pairs={{0,8},{8,0},{1,9},{9,1},{2,10},{10,2},{3,11},{11,3},{4,12},{12,4},... | collective-permute-start | bytes 110600 | tf_op jit(solution)/shard_map/ppermute | solution.py:291
  (101 shorter events, 14.1 us)
Async XLA Ops:
  2.8 1.8 collective-permute-start
  5.6 22.5 %copy-start.23 = (bf16[192,384]{1,0:T(8,128)(2,1)}, bf16[192,384]{1,0:T(8,128)(2,1)S(1)}, u32[]{:S(2)}) copy-start(bf16[192,384]{1,0:T(8,128)(2,1)S(1)} %maximum_select_fusion.1.own_ref) | copy-start | bytes 442372
  5.6 10.6 %collective-permute-start.1 = (bf16[192,384]{1,0:T(8,128)(2,1)S(1)}, bf16[192,384]{1,0:T(8,128)(2,1)S(1)}, u32[]{:S(2)}, u32[]{:S(2)}) collective-permute-start(bf16[192,384]{1,0:T(8,128)(2,1)S(1)} %maximum_select_fusion.1.own_ref), channel_id=1, source_target_pairs={{0,64},{64,128},{128,192},{192,0},{1,65},{65,129},{129,193},{193,1... | collective-permute-start | bytes 442376 | tf_op jit(solution)/shard_map/ppermute | solution.py:310
  8.6 15.1 %collective-permute-start.4 = (bf16[192,384]{1,0:T(8,128)(2,1)S(1)}, bf16[192,384]{1,0:T(8,128)(2,1)S(1)}, u32[]{:S(2)}, u32[]{:S(2)}) collective-permute-start(bf16[192,384]{1,0:T(8,128)(2,1)S(1)} %maximum_select_fusion.1.own_ref), channel_id=1, source_target_pairs={{0,128},{64,192},{128,0},{192,64},{1,129},{65,193},{129,1},{193,65... | collective-permute-start | bytes 442376 | tf_op jit(solution)/shard_map/ppermute | solution.py:310
  13.8 14.3 %collective-permute-start.5 = (bf16[192,384]{1,0:T(8,128)(2,1)S(1)}, bf16[192,384]{1,0:T(8,128)(2,1)S(1)}, u32[]{:S(2)}, u32[]{:S(2)}) collective-permute-start(bf16[192,384]{1,0:T(8,128)(2,1)S(1)} %maximum_select_fusion.1.own_ref), channel_id=1, source_target_pairs={{0,192},{64,0},{128,64},{192,128},{1,193},{65,1},{129,65},{193,129... | collective-permute-start | bytes 442376 | tf_op jit(solution)/shard_map/ppermute | solution.py:310
  16.2 11.9 %copy-start.25 = (bf16[192,384]{1,0:T(8,128)(2,1)}, bf16[192,384]{1,0:T(8,128)(2,1)S(1)}, u32[]{:S(2)}) copy-start(bf16[192,384]{1,0:T(8,128)(2,1)S(1)} %collective-permute-done.1.b1) | copy-start | bytes 442372
  30.8 9.3 %collective-permute-start.6 = (bf16[2,192,384]{2,1,0:T(8,128)(2,1)}, bf16[2,192,384]{2,1,0:T(8,128)(2,1)S(1)}, u32[]{:S(2)}, u32[]{:S(2)}) collective-permute-start(bf16[2,192,384]{2,1,0:T(8,128)(2,1)} %get-tuple-element.35.low), channel_id=1, source_target_pairs={{0,16},{16,4},{4,20},{20,0},{1,17},{17,5},{5,21},{21,1},{2,18},{18... | collective-permute-start | bytes 884744 | tf_op jit(solution)/shard_map/ppermute | solution.py:313
  32.0 8.1 %collective-permute-start.7 = (bf16[2,192,384]{2,1,0:T(8,128)(2,1)}, bf16[2,192,384]{2,1,0:T(8,128)(2,1)}, u32[]{:S(2)}, u32[]{:S(2)}) collective-permute-start(bf16[2,192,384]{2,1,0:T(8,128)(2,1)} %get-tuple-element.36.high), channel_id=1, source_target_pairs={{0,20},{16,0},{4,16},{20,4},{1,21},{17,1},{5,17},{21,5},{2,22},{18... | collective-permute-start | bytes 884744 | tf_op jit(solution)/shard_map/ppermute | solution.py:314
  40.1 18.3 %collective-permute-start.10 = (bf16[1536,256]{1,0:T(8,128)(2,1)}, bf16[1536,256]{1,0:T(8,128)(2,1)}, u32[]{:S(2)}, u32[]{:S(2)}) collective-permute-start(bf16[1536,256]{1,0:T(8,128)(2,1)} %context_half.3), channel_id=1, source_target_pairs={{0,32},{32,0},{1,33},{33,1},{2,34},{34,2},{3,35},{35,3},{4,36},{36... | collective-permute-start | bytes 2359304 | tf_op jit(solution)/shard_map/ppermute | solution.py:319
  43.2 15.5 %collective-permute-start.11 = (bf16[768,384]{1,0:T(8,128)(2,1)}, bf16[768,384]{1,0:T(8,128)(2,1)S(1)}, u32[]{:S(2)}, u32[]{:S(2)}) collective-permute-start(bf16[768,384]{1,0:T(8,128)(2,1)} %bitcast.46), channel_id=1, source_target_pairs={{0,1},{1,2},{2,3},{3,0},{4,5},{5,6},{6,7},{7,4},{8,9},{9,10},{10,1... | collective-permute-start | bytes 1769480 | tf_op jit(solution)/shard_map/ppermute | solution.py:326
  44.2 14.5 %collective-permute-start.12 = (bf16[768,384]{1,0:T(8,128)(2,1)}, bf16[768,384]{1,0:T(8,128)(2,1)S(1)}, u32[]{:S(2)}, u32[]{:S(2)}) collective-permute-start(bf16[768,384]{1,0:T(8,128)(2,1)} %bitcast.49), channel_id=1, source_target_pairs={{0,3},{1,0},{2,1},{3,2},{4,7},{5,4},{6,5},{7,6},{8,11},{9,8},{10,9... | collective-permute-start | bytes 1769480 | tf_op jit(solution)/shard_map/ppermute | solution.py:327
  47.1 6.1 %copy-start.11 = (bf16[2,2,192,384]{3,2,1,0:T(8,128)(2,1)S(1)}, bf16[2,2,192,384]{3,2,1,0:T(8,128)(2,1)}, u32[]{:S(2)}) copy-start(bf16[2,2,192,384]{3,2,1,0:T(8,128)(2,1)} %get-tuple-element.37) | copy-start | bytes 1769476
  47.1 6.1 %collective-permute-start.2 = (bf16[256,768]{1,0:T(8,128)(2,1)S(1)}, bf16[256,768]{1,0:T(8,128)(2,1)S(1)}, u32[]{:S(2)}, u32[]{:S(2)}) collective-permute-start(bf16[256,768]{1,0:T(8,128)(2,1)S(1)} %get-tuple-element.59), channel_id=1, source_target_pairs={{0,8},{8,0},{1,9},{9,1},{2,10},{10,2},{3,11},{11,3},{4,12},{12,4},... | collective-permute-start | bytes 1179656 | tf_op jit(solution)/shard_map/ppermute | solution.py:340
  53.0 31.3 %copy-start.5 = (bf16[1536,256]{1,0:T(8,128)(2,1)}, bf16[1536,256]{1,0:T(8,128)(2,1)S(1)}, u32[]{:S(2)}) copy-start(bf16[1536,256]{1,0:T(8,128)(2,1)S(1)} %context_half.2.c0) | copy-start | bytes 2359300
  53.1 9.0 %copy-start.13 = (bf16[2,2,192,384]{3,2,1,0:T(8,128)(2,1)S(1)}, bf16[2,2,192,384]{3,2,1,0:T(8,128)(2,1)}, u32[]{:S(2)}) copy-start(bf16[2,2,192,384]{3,2,1,0:T(8,128)(2,1)} %get-tuple-element.38) | copy-start | bytes 1769476
  53.1 10.1 %collective-permute-start.3 = (bf16[1536,256]{1,0:T(8,128)(2,1)S(1)}, bf16[1536,256]{1,0:T(8,128)(2,1)S(1)}, u32[]{:S(2)}, u32[]{:S(2)}) collective-permute-start(bf16[1536,256]{1,0:T(8,128)(2,1)S(1)} %context_half.2.c0), channel_id=1, source_target_pairs={{0,8},{8,0},{1,9},{9,1},{2,10},{10,2},{3,11},{11,3},{4,12},{12,4},... | collective-permute-start | bytes 2359304 | tf_op jit(solution)/shard_map/ppermute | solution.py:321
  53.2 17.3 %collective-permute-start.8 = (bf16[768,384]{1,0:T(8,128)(2,1)S(1)}, bf16[768,384]{1,0:T(8,128)(2,1)S(1)}, u32[]{:S(2)}, u32[]{:S(2)}) collective-permute-start(bf16[768,384]{1,0:T(8,128)(2,1)S(1)} %bitcast.47), channel_id=1, source_target_pairs={{0,3},{1,0},{2,1},{3,2},{4,7},{5,4},{6,5},{7,6},{8,11},{9,8},{10,9... | collective-permute-start | bytes 1769480 | tf_op jit(solution)/shard_map/ppermute | solution.py:326
  53.5 30.8 %copy-start.4 = (bf16[2,256,768]{2,1,0:T(8,128)(2,1)}, bf16[2,256,768]{2,1,0:T(8,128)(2,1)S(1)}, u32[]{:S(2)}) copy-start(bf16[2,256,768]{2,1,0:T(8,128)(2,1)S(1)} %pad_maximum_fusion.a0.near) | copy-start | bytes 2359300
  58.4 19.2 %collective-permute-start.18 = (bf16[2,256,768]{2,1,0:T(8,128)(2,1)S(1)}, bf16[2,256,768]{2,1,0:T(8,128)(2,1)S(1)}, u32[]{:S(2)}, u32[]{:S(2)}) collective-permute-start(bf16[2,256,768]{2,1,0:T(8,128)(2,1)S(1)} %pad_maximum_fusion.a0.near), channel_id=1, source_target_pairs={{0,32},{32,0},{1,33},{33,1},{2,34},{34,2},{3,35},{35,3},{4,36},{36... | collective-permute-start | bytes 2359304 | tf_op jit(solution)/shard_map/ppermute | solution.py:342
  58.7 25.7 %copy-start.15 = (bf16[768,384]{1,0:T(8,128)(2,1)}, bf16[768,384]{1,0:T(8,128)(2,1)S(1)}, u32[]{:S(2)}) copy-start(bf16[768,384]{1,0:T(8,128)(2,1)S(1)} %collective-permute-done.11.refs_1_) | copy-start | bytes 1769476
  58.7 30.7 %copy-start.29 = (bf16[768,384]{1,0:T(8,128)(2,1)}, bf16[768,384]{1,0:T(8,128)(2,1)S(1)}, u32[]{:S(2)}) copy-start(bf16[768,384]{1,0:T(8,128)(2,1)S(1)} %collective-permute-done.12.refs_6_) | copy-start | bytes 1769476
  58.7 18.8 %collective-permute-start.13 = (bf16[1536,256]{1,0:T(8,128)(2,1)}, bf16[1536,256]{1,0:T(8,128)(2,1)S(1)}, u32[]{:S(2)}, u32[]{:S(2)}) collective-permute-start(bf16[1536,256]{1,0:T(8,128)(2,1)} %collective-permute-done.10.c2), channel_id=1, source_target_pairs={{0,8},{8,0},{1,9},{9,1},{2,10},{10,2},{3,11},{11,3},{4,12},{12,4},... | collective-permute-start | bytes 2359304 | tf_op jit(solution)/shard_map/ppermute | solution.py:331
  62.0 14.7 %collective-permute-start.9 = (bf16[768,384]{1,0:T(8,128)(2,1)S(1)}, bf16[768,384]{1,0:T(8,128)(2,1)S(1)}, u32[]{:S(2)}, u32[]{:S(2)}) collective-permute-start(bf16[768,384]{1,0:T(8,128)(2,1)S(1)} %bitcast.50), channel_id=1, source_target_pairs={{0,1},{1,2},{2,3},{3,0},{4,5},{5,6},{6,7},{7,4},{8,9},{9,10},{10,1... | collective-permute-start | bytes 1769480 | tf_op jit(solution)/shard_map/ppermute | solution.py:327
  63.2 21.1 %copy-start.7 = (bf16[1536,256]{1,0:T(8,128)(2,1)}, bf16[1536,256]{1,0:T(8,128)(2,1)S(1)}, u32[]{:S(2)}) copy-start(bf16[1536,256]{1,0:T(8,128)(2,1)S(1)} %collective-permute-done.3.c1) | copy-start | bytes 2359300
  63.2 26.1 %collective-permute-start.16 = (bf16[768,384]{1,0:T(8,128)(2,1)S(1)}, bf16[768,384]{1,0:T(8,128)(2,1)S(1)}, u32[]{:S(2)}, u32[]{:S(2)}) collective-permute-start(bf16[768,384]{1,0:T(8,128)(2,1)S(1)} %collective-permute-done.11.refs_1_), channel_id=1, source_target_pairs={{0,1},{1,2},{2,3},{3,0},{4,5},{5,6},{6,7},{7,4},{8,9},{9,10},{10,1... | collective-permute-start | bytes 1769480 | tf_op jit(solution)/shard_map/ppermute | solution.py:328
  71.4 18.8 %collective-permute-start.17 = (bf16[768,384]{1,0:T(8,128)(2,1)S(1)}, bf16[768,384]{1,0:T(8,128)(2,1)}, u32[]{:S(2)}, u32[]{:S(2)}) collective-permute-start(bf16[768,384]{1,0:T(8,128)(2,1)S(1)} %collective-permute-done.12.refs_6_), channel_id=1, source_target_pairs={{0,3},{1,0},{2,1},{3,2},{4,7},{5,4},{6,5},{7,6},{8,11},{9,8},{10,9... | collective-permute-start | bytes 1769480 | tf_op jit(solution)/shard_map/ppermute | solution.py:329
  78.4 5.9 %copy-start.9 = (bf16[1536,256]{1,0:T(8,128)(2,1)}, bf16[1536,256]{1,0:T(8,128)(2,1)S(1)}, u32[]{:S(2)}) copy-start(bf16[1536,256]{1,0:T(8,128)(2,1)S(1)} %collective-permute-done.13.c3) | copy-start | bytes 2359300
  90.2 52.3 %all-to-all-start = ((bf16[16,4,24,768]{3,2,1,0:T(8,128)(2,1)}), bf16[16,4,24,768]{3,2,1,0:T(8,128)(2,1)}, u32[]{:S(2)}, u32[]{:S(2)}) async-start(bf16[16,4,24,768]{3,2,1,0:T(8,128)(2,1)} %weight_gradient.3), calls=%async_computation | async-start | bytes 4718592 | tf_op jit(solution)/shard_map/all_to_all | solution.py:349
  97.2 2.9 %collective-permute-start.14 = (bf16[256,768]{1,0:T(8,128)(2,1)}, bf16[256,768]{1,0:T(8,128)(2,1)S(1)}, u32[]{:S(2)}, u32[]{:S(2)}) collective-permute-start(bf16[256,768]{1,0:T(8,128)(2,1)} %get-tuple-element.61), channel_id=1, source_target_pairs={{0,8},{8,0},{1,9},{9,1},{2,10},{10,2},{3,11},{11,3},{4,12},{12,4},... | collective-permute-start | bytes 1179656 | tf_op jit(solution)/shard_map/ppermute | solution.py:340
  101.1 19.7 %collective-permute-start.15 = (bf16[2,256,768]{2,1,0:T(8,128)(2,1)}, bf16[2,256,768]{2,1,0:T(8,128)(2,1)}, u32[]{:S(2)}, u32[]{:S(2)}) collective-permute-start(bf16[2,256,768]{2,1,0:T(8,128)(2,1)} %pad_maximum_fusion.1.near.b0), channel_id=1, source_target_pairs={{0,32},{32,0},{1,33},{33,1},{2,34},{34,2},{3,35},{35,3},{4,36},{36... | collective-permute-start | bytes 2359304 | tf_op jit(solution)/shard_map/ppermute | solution.py:342
  124.1 6.1 %copy-start.12 = (bf16[2,2,192,384]{3,2,1,0:T(8,128)(2,1)S(1)}, bf16[2,2,192,384]{3,2,1,0:T(8,128)(2,1)}, u32[]{:S(2)}) copy-start(bf16[2,2,192,384]{3,2,1,0:T(8,128)(2,1)} %get-tuple-element.37) | copy-start | bytes 1769476
  124.2 6.1 %copy-start.14 = (bf16[2,2,192,384]{3,2,1,0:T(8,128)(2,1)S(1)}, bf16[2,2,192,384]{3,2,1,0:T(8,128)(2,1)}, u32[]{:S(2)}) copy-start(bf16[2,2,192,384]{3,2,1,0:T(8,128)(2,1)} %get-tuple-element.38) | copy-start | bytes 1769476
  124.2 6.1 %copy-start.16 = (bf16[768,384]{1,0:T(8,128)(2,1)S(1)}, bf16[768,384]{1,0:T(8,128)(2,1)}, u32[]{:S(2)}) copy-start(bf16[768,384]{1,0:T(8,128)(2,1)} %copy-done.15) | copy-start | bytes 1769476
  124.2 6.1 %copy-start.18 = (bf16[768,384]{1,0:T(8,128)(2,1)S(1)}, bf16[768,384]{1,0:T(8,128)(2,1)}, u32[]{:S(2)}) copy-start(bf16[768,384]{1,0:T(8,128)(2,1)} %copy-done.17) | copy-start | bytes 1769476
  124.2 6.1 %copy-start.20 = (bf16[768,384]{1,0:T(8,128)(2,1)S(1)}, bf16[768,384]{1,0:T(8,128)(2,1)}, u32[]{:S(2)}) copy-start(bf16[768,384]{1,0:T(8,128)(2,1)} %copy-done.19) | copy-start | bytes 1769476
  124.2 6.1 %copy-start.22 = (bf16[768,384]{1,0:T(8,128)(2,1)S(1)}, bf16[768,384]{1,0:T(8,128)(2,1)}, u32[]{:S(2)}) copy-start(bf16[768,384]{1,0:T(8,128)(2,1)} %copy-done.21) | copy-start | bytes 1769476
  141.6 8.1 %collective-permute-start.19 = (bf16[256,1536]{1,0:T(8,128)(2,1)}, bf16[256,1536]{1,0:T(8,128)(2,1)}, u32[]{:S(2)}, u32[]{:S(2)}) collective-permute-start(bf16[256,1536]{1,0:T(8,128)(2,1)} %get-tuple-element.47), channel_id=1, source_target_pairs={{0,8},{8,0},{1,9},{9,1},{2,10},{10,2},{3,11},{11,3},{4,12},{12,4},... | collective-permute-start | bytes 2359304 | tf_op jit(solution)/shard_map/ppermute | solution.py:356
  142.5 49.4 %all-to-all-start.1 = ((bf16[16,4,24,768]{3,2,1,0:T(8,128)(2,1)}), bf16[16,4,24,768]{3,2,1,0:T(8,128)(2,1)}, u32[]{:S(2)}, u32[]{:S(2)}) async-start(bf16[16,4,24,768]{3,2,1,0:T(8,128)(2,1)} %weight_gradient.2), calls=%async_computation.1 | async-start | bytes 4718592 | tf_op jit(solution)/shard_map/all_to_all | solution.py:349
  149.1 4.7 %collective-permute-start.21 = (bf16[256,1536]{1,0:T(8,128)(2,1)}, bf16[256,1536]{1,0:T(8,128)(2,1)}, u32[]{:S(2)}, u32[]{:S(2)}) collective-permute-start(bf16[256,1536]{1,0:T(8,128)(2,1)} %get-tuple-element.49), channel_id=1, source_target_pairs={{0,8},{8,0},{1,9},{9,1},{2,10},{10,2},{3,11},{11,3},{4,12},{12,4},... | collective-permute-start | bytes 2359304 | tf_op jit(solution)/shard_map/ppermute | solution.py:357
  152.4 19.5 %collective-permute-start.20 = (bf16[256,1536]{1,0:T(8,128)(2,1)}, bf16[256,1536]{1,0:T(8,128)(2,1)}, u32[]{:S(2)}, u32[]{:S(2)}) collective-permute-start(bf16[256,1536]{1,0:T(8,128)(2,1)} %add_convert_fusion), channel_id=1, source_target_pairs={{0,32},{32,0},{1,33},{33,1},{2,34},{34,2},{3,35},{35,3},{4,36},{36... | collective-permute-start | bytes 2359304 | tf_op jit(solution)/shard_map/ppermute | solution.py:358
  184.1 12.0 %collective-permute-start.22 = (bf16[24,768]{1,0:T(8,128)(2,1)S(1)}, bf16[24,768]{1,0:T(8,128)(2,1)S(1)}, u32[]{:S(2)}, u32[]{:S(2)}) collective-permute-start(bf16[24,768]{1,0:T(8,128)(2,1)S(1)} %get-tuple-element.62), channel_id=1, source_target_pairs={{0,64},{64,128},{128,192},{192,0},{1,65},{65,129},{129,193},{193,1... | collective-permute-start | bytes 110600 | tf_op jit(solution)/shard_map/ppermute | solution.py:287
  185.7 13.3 %collective-permute-start.23 = (bf16[24,768]{1,0:T(8,128)(2,1)S(1)}, bf16[24,768]{1,0:T(8,128)(2,1)S(1)}, u32[]{:S(2)}, u32[]{:S(2)}) collective-permute-start(bf16[24,768]{1,0:T(8,128)(2,1)S(1)} %get-tuple-element.64), channel_id=1, source_target_pairs={{0,128},{64,192},{128,0},{192,64},{1,129},{65,193},{129,1},{193,65... | collective-permute-start | bytes 110600 | tf_op jit(solution)/shard_map/ppermute | solution.py:287
  189.8 9.3 %collective-permute-start.24 = (bf16[24,768]{1,0:T(8,128)(2,1)S(1)}, bf16[24,768]{1,0:T(8,128)(2,1)S(1)}, u32[]{:S(2)}, u32[]{:S(2)}) collective-permute-start(bf16[24,768]{1,0:T(8,128)(2,1)S(1)} %get-tuple-element.63), channel_id=1, source_target_pairs={{0,192},{64,0},{128,64},{192,128},{1,193},{65,1},{129,65},{193,129... | collective-permute-start | bytes 110600 | tf_op jit(solution)/shard_map/ppermute | solution.py:287
  193.9 7.7 %collective-permute-start.25 = (bf16[24,768]{1,0:T(8,128)(2,1)S(1)}, bf16[24,768]{1,0:T(8,128)(2,1)S(1)}, u32[]{:S(2)}, u32[]{:S(2)}) collective-permute-start(bf16[24,768]{1,0:T(8,128)(2,1)S(1)} %get-tuple-element.65), channel_id=1, source_target_pairs={{0,64},{64,128},{128,192},{192,0},{1,65},{65,129},{129,193},{193,1... | collective-permute-start | bytes 110600 | tf_op jit(solution)/shard_map/ppermute | solution.py:287
  194.2 7.4 %collective-permute-start.26 = (bf16[24,768]{1,0:T(8,128)(2,1)S(1)}, bf16[24,768]{1,0:T(8,128)(2,1)S(1)}, u32[]{:S(2)}, u32[]{:S(2)}) collective-permute-start(bf16[24,768]{1,0:T(8,128)(2,1)S(1)} %get-tuple-element.67), channel_id=1, source_target_pairs={{0,128},{64,192},{128,0},{192,64},{1,129},{65,193},{129,1},{193,65... | collective-permute-start | bytes 110600 | tf_op jit(solution)/shard_map/ppermute | solution.py:287
  196.1 5.5 %collective-permute-start.27 = (bf16[24,768]{1,0:T(8,128)(2,1)S(1)}, bf16[24,768]{1,0:T(8,128)(2,1)S(1)}, u32[]{:S(2)}, u32[]{:S(2)}) collective-permute-start(bf16[24,768]{1,0:T(8,128)(2,1)S(1)} %get-tuple-element.66), channel_id=1, source_target_pairs={{0,192},{64,0},{128,64},{192,128},{1,193},{65,1},{129,65},{193,129... | collective-permute-start | bytes 110600 | tf_op jit(solution)/shard_map/ppermute | solution.py:287
  199.1 5.2 %collective-permute-start.28 = (f32[12,768]{1,0:T(8,128)S(1)}, f32[12,768]{1,0:T(8,128)S(1)}, u32[]{:S(2)}, u32[]{:S(2)}) collective-permute-start(f32[12,768]{1,0:T(8,128)S(1)} %get-tuple-element.69), channel_id=1, source_target_pairs={{0,8},{8,0},{1,9},{9,1},{2,10},{10,2},{3,11},{11,3},{4,12},{12,4},... | collective-permute-start | bytes 110600 | tf_op jit(solution)/shard_map/ppermute | solution.py:291
  201.7 3.4 %collective-permute-start.29 = (f32[12,768]{1,0:T(8,128)S(1)}, f32[12,768]{1,0:T(8,128)S(1)}, u32[]{:S(2)}, u32[]{:S(2)}) collective-permute-start(f32[12,768]{1,0:T(8,128)S(1)} %get-tuple-element.71), channel_id=1, source_target_pairs={{0,8},{8,0},{1,9},{9,1},{2,10},{10,2},{3,11},{11,3},{4,12},{12,4},... | collective-permute-start | bytes 110600 | tf_op jit(solution)/shard_map/ppermute | solution.py:291
  (14 other events, 24.3 us)

commit v5 on v4

--- a/solution.py
+++ b/solution.py
@@ -17,7 +17,7 @@
 SWAP = [(0, 1), (1, 0)]
 NT = (((1,), (1,)), ((), ()))
 TN = (((0,), (0,)), ((), ()))
-VMEM_LIMIT = 50 * 2**20
+VMEM_LIMIT = 60 * 2**20
 
 
 def ring(count, step):
@@ -162,6 +162,7 @@
     return pl.pallas_call(
         restore_body,
         out_shape=[jax.ShapeDtypeStruct((rows, 384), BF16)] * 2,
+        compiler_params=pltpu.CompilerParams(vmem_limit_bytes=VMEM_LIMIT),
         cost_estimate=cost(rows * 768, rows * 3072),
         name="weight_pieces",
     )(codes, scales)
@@ -185,6 +186,7 @@
     return pl.pallas_call(
         by_zh_body,
         out_shape=[jax.ShapeDtypeStruct((2, *own.shape), BF16)] * 2,
+        compiler_params=pltpu.CompilerParams(vmem_limit_bytes=VMEM_LIMIT),
         cost_estimate=cost(own.size, own.size * 16),
         name="weight_by_zh",
     )(own, *pieces)
@@ -203,6 +205,7 @@
     return pl.pallas_call(
         by_xl_body,
         out_shape=[jax.ShapeDtypeStruct(shape, BF16)] * 2,
+        compiler_params=pltpu.CompilerParams(vmem_limit_bytes=VMEM_LIMIT),
         cost_estimate=cost(low.size, low.size * 16),
         name="weight_by_xl",
     )(low, high, beside_low, beside_high)
@@ -308,17 +311,29 @@
         c == 0, jnp.concatenate([piece, arrived], 0), jnp.concatenate([arrived, piece], 0)
     )
     behind = [lax.ppermute(pair, "zh", ring(4, step)) for step in (1, 2, 3)]
+    (late_parity,) = after((other_parity,), (behind[0],))
+    context_other = forward(late_parity, q, k, v, width)
+    (pair,) = after((pair,), (context_other,))
     low, high = by_zh(pair, behind)
     start = low
     beside_low = lax.ppermute(low, ("xl", "xh"), x_ring(1))
     beside_high = lax.ppermute(high, ("xl", "xh"), x_ring(-1))
 
-    q, k = after((q, k), (behind[0],))
-    context_other = forward(other_parity, q, k, v, width)
-    (context_other,) = after((context_other,), (low,))
+    (context_other,) = after((context_other,), (behind[1], behind[2]))
     c2 = lax.ppermute(context_other, "zl", SWAP)
     context_own = forward(own_parity, q, k, v, width)
     c1 = lax.ppermute(context_own, "c", SWAP)
+
+    part = half // 2
+    nears, grads = [], []
+    for index in range(2):
+        own, partner = (
+            lax.dynamic_slice_in_dim(grad, side * half + index * part, part, 1)
+            for side in (c, 1 - c)
+        )
+        nears.append(jnp.stack([own, lax.ppermute(partner, "c", SWAP)]))
+        (sent,) = after(nears[-1:], (grads[0][1] if index else start,))
+        grads.append((nears[-1], lax.ppermute(sent, "zl", SWAP)))
 
     low, high = by_xl(low, high, beside_low, beside_high)
     lows, highs = ([piece.reshape(-1, width)] for piece in (low, high))
@@ -327,19 +342,8 @@
         highs.append(lax.ppermute(highs[0], "y", ring(4, step)))
     lows.append(lax.ppermute(lows[1], "y", ring(4, 1)))
     highs.append(lax.ppermute(highs[2], "y", ring(4, -1)))
-    (event,) = after((c2,), (lows[1], highs[2]))
+    (event,) = after((c2,), (lows[1], highs[2], nears[1]))
     c3 = lax.ppermute(event, "c", SWAP)
-
-    part = half // 2
-    grads = []
-    for index in range(2):
-        own, partner = (
-            lax.dynamic_slice_in_dim(grad, side * half + index * part, part, 1)
-            for side in (c, 1 - c)
-        )
-        near = jnp.stack([own, lax.ppermute(partner, "c", SWAP)])
-        (sent,) = after((near,), (start,) if index == 0 else (c2,))
-        grads.append((near, lax.ppermute(sent, "zl", SWAP)))
 
     (c1,) = after((c1,), (lows[2], highs[1]))
     terms = []
@@ -349,18 +353,18 @@
         terms.append(lax.all_to_all(term, ("xl", "xh", "y"), 0, 0, tiled=True))
 
     places = jnp.stack([y, (y + 3) % 4, (y + 1) % 4, (y + 2) % 4]).astype(jnp.int32)
-    (near,) = after(grads[0][:1], (term,))
-    g0, g1, g2, g3 = context_gradient(
-        places, (near, grads[0][1]) + grads[1], lows, highs
-    )
+    g0, g1, g2, g3 = context_gradient(places, grads[0] + grads[1], lows, highs)
     r3 = lax.ppermute(g3, "c", SWAP)
     r1 = lax.ppermute(g1, "c", SWAP)
     g_other = lax.ppermute((g2 + r3.astype(F32)).astype(BF16), "zl", SWAP)
     first = backward(own_parity, q, k, v, (g0, r1), width)
+
+    kept_a, got_a = sums_on_owners(terms[0], zh, c)
+    (g_other,) = after((g_other,), (kept_a, got_a))
     outs = backward(other_parity, q, k, v, (g_other,), width, first)
-
     (last,) = after((terms[1],), tuple(outs))
-    kept, got = zip(*(sums_on_owners(term, zh, c) for term in (terms[0], last)))
+    kept_b, got_b = sums_on_owners(last, zh, c)
+    kept, got = (kept_a, kept_b), (got_a, got_b)
     grad_weight = jnp.where(
         c == 0, jnp.concatenate(kept + got, 1), jnp.concatenate(got + kept, 1)
     )

time: 208 us -> 213 us (1.024)
  starting transfers between devices: 59.2 us -> 78.4 us
  local copies, waits for them, and re-layouts: 13.5 us -> 5.71 us
  waiting for transfers between devices: 63.1 us -> 56 us
  Pallas kernels: 59.6 us -> 63.2 us
  other arithmetic: 9.56 us -> 7.4 us
    ppermute x6, waiting for transfers between devices: 0.02 us -> 21.1 us  [sums_on_owners(): mine = mine + lax.ppermute(away, 'zh', ring(4, step)).astype(F32)]
    ppermute x3, waiting for transfers between devices: 11.9 us -> 3.43 us  [per_device(): behind = [lax.ppermute(pair, 'zh', ring(4, step)) for step in (1, 2, 3)]]
    ppermute x1, waiting for transfers between devices: 7.73 us -> 0.01 us  [per_device(): g_other = lax.ppermute((g2 + r3.astype(F32)).astype(BF16), 'zl', SWAP)]
    ppermute x4, starting transfers between devices: 5 us -> 11.7 us  [the longest x2 9.7 us: per_device(): grads.append((nears[-1], lax.ppermute(sent, 'zl', SWAP)))]
    unnamed x60 -> x32, local copies, waits for them, and re-layouts: 11 us -> 5.52 us
    ppermute x1, waiting for transfers between devices: 4.99 us -> 0.01 us  [per_device(): lows.append(lax.ppermute(lows[1], 'y', ring(4, 1)))]
    ppermute x1, waiting for transfers between devices: 4.82 us -> 0.01 us  [per_device(): c2 = lax.ppermute(context_other, 'zl', SWAP)]
    ppermute x1, starting transfers between devices: 0.01 us -> 4.63 us  [per_device(): c2 = lax.ppermute(context_other, 'zl', SWAP)]
  transfers between devices with their start and end apart: 32 -> 32, of which waited for: 12 -> 13; matrix products, arithmetic and copies ran while one was open for 5% -> 2% of each run, Pallas kernels for 27% -> 28%
where the time goes in v5:
time: 213 us; the launch traced here: 211 us
  starting transfers between devices  78.4 us (37%)
  Pallas kernels  63.2 us (30%)
  waiting for transfers between devices  56 us (26%)
  other arithmetic  7.4 us (3%)
  local copies, waits for them, and re-layouts  5.71 us (3%)
    ppermute x6, waiting for transfers between devices, sums_on_owners(): mine = mine + lax.ppermute(away, 'zh', ring(4, step)).astype(F32)  21.1 us
    pallas_call x2, Pallas kernels, backward(): pl.pallas_call(functools.partial(backward_body, before is None), grid_spe...  20.7 us
    ppermute x2, waiting for transfers between devices, per_device(): grads.append((nears[-1], lax.ppermute(sent, 'zl', SWAP)))  16.4 us
    all_to_all x2, starting transfers between devices, per_device(): terms.append(lax.all_to_all(term, ('xl', 'xh', 'y'), 0, 0, tiled=True))  16.2 us
    pallas_call x2, Pallas kernels, weight_gradient(): pl.pallas_call(weight_gradient_body, grid=(4,), in_specs=[pl.BlockSpec((r...  13 us
    ppermute x6, starting transfers between devices, sums_on_owners(): mine = mine + lax.ppermute(away, 'zh', ring(4, step)).astype(F32)  12.7 us
    pallas_call x1, Pallas kernels, context_gradient(): pl.pallas_call(context_gradient_body, grid_spec=pltpu.PrefetchScalarGridS...  12.3 us
    pallas_call x2, Pallas kernels, forward(): pl.pallas_call(forward_body, grid_spec=pltpu.PrefetchScalarGridSpec(num_s...  10.7 us
  transfers between devices with their start and end apart: 32, of which 13 were waited for; matrix products, arithmetic and copies ran while one was open for 2% of the time, Pallas kernels for 28%

profile of v5, /device:TPU:19, one launch (start us, length us, event | category | flops | bytes accessed | tf_op | source)
XLA Modules:
  0.0 211.4 jit_solution(8373797532385637971)
XLA Ops:
  0.6 2.1 %weight_pieces.1 = (bf16[96,384]{1,0:T(8,128)(2,1)}, bf16[96,384]{1,0:T(8,128)(2,1)}) custom-call(bf16[96,3072]{1,0:T(8,128)(2,1)} %codes_ref.1, f32[12,96]{1,0:T(8,128)} %bitcast.55), custom_call_target="tpu_custom_call" | custom-call | flops 73728 | bytes 294912 | tf_op jit(solution)/shard_map/weight_pieces/pallas_call | solution.py:162
  3.5 1.1 collective-permute-done.1
  4.6 1.0 maximum_select_fusion.1.own_ref
  5.6 3.1 %collective-permute-start.2 = (bf16[192,384]{1,0:T(8,128)(2,1)S(1)}, bf16[192,384]{1,0:T(8,128)(2,1)S(1)}, u32[]{:S(2)}, u32[]{:S(2)}) collective-permute-start(bf16[192,384]{1,0:T(8,128)(2,1)S(1)} %maximum_select_fusion.1.own_ref), channel_id=1, source_target_pairs={{0,64},{64,128},{128,192},{192,0},{1,65},{65,129},{129,193},{193,1... | collective-permute-start | bytes 442376 | tf_op jit(solution)/shard_map/ppermute | solution.py:313
  8.6 3.1 %collective-permute-start.4 = (bf16[192,384]{1,0:T(8,128)(2,1)S(1)}, bf16[192,384]{1,0:T(8,128)(2,1)S(1)}, u32[]{:S(2)}, u32[]{:S(2)}) collective-permute-start(bf16[192,384]{1,0:T(8,128)(2,1)S(1)} %maximum_select_fusion.1.own_ref), channel_id=1, source_target_pairs={{0,192},{64,0},{128,64},{192,128},{1,193},{65,1},{129,65},{193,129... | collective-permute-start | bytes 442376 | tf_op jit(solution)/shard_map/ppermute | solution.py:313
  11.8 4.4 %collective-permute-start.3 = (bf16[192,384]{1,0:T(8,128)(2,1)S(1)}, bf16[192,384]{1,0:T(8,128)(2,1)S(1)}, u32[]{:S(2)}, u32[]{:S(2)}) collective-permute-start(bf16[192,384]{1,0:T(8,128)(2,1)S(1)} %maximum_select_fusion.1.own_ref), channel_id=1, source_target_pairs={{0,128},{64,192},{128,0},{192,64},{1,129},{65,193},{129,1},{193,65... | collective-permute-start | bytes 442376 | tf_op jit(solution)/shard_map/ppermute | solution.py:313
  16.2 5.4 %context_half.2 = bf16[1536,256]{1,0:T(8,128)(2,1)} custom-call(s32[1]{0:T(128)S(6)} %sub.7.pick, bf16[256,3072]{1,0:T(8,128)(2,1)} %bitcast.38, bf16[256,3072]{1,0:T(8,128)(2,1)} %bitcast.42, bf16[256,3072]{1,0:T(8,128)(2,1)} %bitcast.46), custom_call_target="tpu_custom_call" | custom-call | flops 402653184 | bytes 3145728 | tf_op jit(solution)/shard_map/context_half/pallas_call | solution.py:73
  21.6 1.6 collective-permute-done.4.b3
  23.2 1.8 collective-permute-done.3.b2
  25.7 2.0 weight_by_zh.1
  28.0 1.2 collective-permute-start.8
  29.2 4.6 %collective-permute-start.19 = (bf16[1536,256]{1,0:T(8,128)(2,1)}, bf16[1536,256]{1,0:T(8,128)(2,1)}, u32[]{:S(2)}, u32[]{:S(2)}) collective-permute-start(bf16[1536,256]{1,0:T(8,128)(2,1)} %context_half.2), channel_id=1, source_target_pairs={{0,32},{32,0},{1,33},{33,1},{2,34},{34,2},{3,35},{35,3},{4,36},{36... | collective-permute-start | bytes 2359304 | tf_op jit(solution)/shard_map/ppermute | solution.py:323
  33.9 1.9 collective-permute-start
  37.4 2.4 %weight_by_xl.1 = (bf16[2,2,192,384]{3,2,1,0:T(8,128)(2,1)}, bf16[2,2,192,384]{3,2,1,0:T(8,128)(2,1)}) custom-call(bf16[2,192,384]{2,1,0:T(8,128)(2,1)} %get-tuple-element.35.low, bf16[2,192,384]{2,1,0:T(8,128)(2,1)} %get-tuple-element.38.high, bf16[2,192,384]{2,1,0:T(8,128)(2,1)} %copy-done.6, bf16[2,192,384]{2,1,0:T(8,128)(2,1)} %copy-done.5), custom_call_target="tpu_custom_call" | custom-call | flops 147456 | bytes 2359296 | tf_op jit(solution)/shard_map/weight_by_xl/pallas_call | solution.py:205
  39.9 1.3 collective-permute-start.10
  41.2 5.3 %context_half.3.c0 = bf16[1536,256]{1,0:T(8,128)(2,1)} custom-call(s32[1]{0:T(128)} %bitcast.pick, bf16[256,3072]{1,0:T(8,128)(2,1)} %bitcast.39, bf16[256,3072]{1,0:T(8,128)(2,1)} %bitcast.43, bf16[256,3072]{1,0:T(8,128)(2,1)} %bitcast.47), custom_call_target="tpu_custom_call" | custom-call | flops 402653184 | bytes 3145728 | tf_op jit(solution)/shard_map/context_half/pallas_call | solution.py:73
  46.5 2.5 %collective-permute-start.18 = (bf16[1536,256]{1,0:T(8,128)(2,1)}, bf16[1536,256]{1,0:T(8,128)(2,1)S(1)}, u32[]{:S(2)}, u32[]{:S(2)}) collective-permute-start(bf16[1536,256]{1,0:T(8,128)(2,1)} %context_half.3.c0), channel_id=1, source_target_pairs={{0,8},{8,0},{1,9},{9,1},{2,10},{10,2},{3,11},{11,3},{4,12},{12,4},... | collective-permute-start | bytes 2359304 | tf_op jit(solution)/shard_map/ppermute | solution.py:325
  49.0 2.2 %collective-permute-start.13 = (bf16[768,384]{1,0:T(8,128)(2,1)}, bf16[768,384]{1,0:T(8,128)(2,1)S(1)}, u32[]{:S(2)}, u32[]{:S(2)}) collective-permute-start(bf16[768,384]{1,0:T(8,128)(2,1)} %bitcast.14.refs_4_), channel_id=1, source_target_pairs={{0,1},{1,2},{2,3},{3,0},{4,5},{5,6},{6,7},{7,4},{8,9},{9,10},{10,1... | collective-permute-start | bytes 1769480 | tf_op jit(solution)/shard_map/ppermute | solution.py:342
  51.4 4.7 %collective-permute-start.5 = (bf16[2,256,768]{2,1,0:T(8,128)(2,1)S(1)}, bf16[2,256,768]{2,1,0:T(8,128)(2,1)S(1)}, u32[]{:S(2)}, u32[]{:S(2)}) collective-permute-start(bf16[2,256,768]{2,1,0:T(8,128)(2,1)S(1)} %pad_maximum_fusion.a0.near), channel_id=1, source_target_pairs={{0,32},{32,0},{1,33},{33,1},{2,34},{34,2},{3,35},{35,3},{4,36},{36... | collective-permute-start | bytes 2359304 | tf_op jit(solution)/shard_map/ppermute | solution.py:336
  56.1 2.6 %collective-permute-start.20 = (bf16[1536,256]{1,0:T(8,128)(2,1)}, bf16[1536,256]{1,0:T(8,128)(2,1)S(1)}, u32[]{:S(2)}, u32[]{:S(2)}) collective-permute-start(bf16[1536,256]{1,0:T(8,128)(2,1)} %collective-permute-done.19.c2), channel_id=1, source_target_pairs={{0,8},{8,0},{1,9},{9,1},{2,10},{10,2},{3,11},{11,3},{4,12},{12,4},... | collective-permute-start | bytes 2359304 | tf_op jit(solution)/shard_map/ppermute | solution.py:346
  58.7 1.2 collective-permute-start.11
  59.9 3.0 %collective-permute-start.15 = (bf16[768,384]{1,0:T(8,128)(2,1)}, bf16[768,384]{1,0:T(8,128)(2,1)}, u32[]{:S(2)}, u32[]{:S(2)}) collective-permute-start(bf16[768,384]{1,0:T(8,128)(2,1)} %collective-permute-done.14.refs_6_), channel_id=1, source_target_pairs={{0,3},{1,0},{2,1},{3,2},{4,7},{5,4},{6,5},{7,6},{8,11},{9,8},{10,9... | collective-permute-start | bytes 1769480 | tf_op jit(solution)/shard_map/ppermute | solution.py:344
  62.9 2.5 %collective-permute-done.13.refs_5_ = bf16[768,384]{1,0:T(8,128)(2,1)S(1)} collective-permute-done((bf16[768,384]{1,0:T(8,128)(2,1)}, bf16[768,384]{1,0:T(8,128)(2,1)S(1)}, u32[]{:S(2)}, u32[]{:S(2)}) %collective-permute-start.13) | collective-permute-done | bytes 589856 | tf_op jit(solution)/shard_map/ppermute | solution.py:342
  65.4 1.5 collective-permute-start.12
  66.9 6.9 %collective-permute-done.11.refs_2_ = bf16[768,384]{1,0:T(8,128)(2,1)S(1)} collective-permute-done((bf16[768,384]{1,0:T(8,128)(2,1)S(1)}, bf16[768,384]{1,0:T(8,128)(2,1)S(1)}, u32[]{:S(2)}, u32[]{:S(2)}) %collective-permute-start.11) | collective-permute-done | bytes 589856 | tf_op jit(solution)/shard_map/ppermute | solution.py:341
  75.5 0.9 copy-done.11
  76.4 6.5 %weight_gradient.2 = bf16[16,4,24,768]{3,2,1,0:T(8,128)(2,1)} custom-call(bf16[1536,256]{1,0:T(8,128)(2,1)} %context_half.3.c0, bf16[1536,256]{1,0:T(8,128)(2,1)} %copy-done.10, bf16[1536,256]{1,0:T(8,128)(2,1)} %collective-permute-done.19.c2, bf16[1536,256]{1,0:T(8,128)(2,1)} %copy-done.11, bf16[2,256,768]{2,1,0:T(8,128)(2,1)} %copy-done.3, ...), custom_call_target="tpu_custom_call" | custom-call | flops 2415919104 | bytes 8388608 | tf_op jit(solution)/shard_map/weight_gradient/pallas_call | solution.py:273
  82.9 3.6 %collective-permute-done.15.refs_7_ = bf16[768,384]{1,0:T(8,128)(2,1)} collective-permute-done((bf16[768,384]{1,0:T(8,128)(2,1)}, bf16[768,384]{1,0:T(8,128)(2,1)}, u32[]{:S(2)}, u32[]{:S(2)}) %collective-permute-start.15) | collective-permute-done | bytes 589856 | tf_op jit(solution)/shard_map/ppermute | solution.py:344
  86.4 9.6 %all-to-all-start = ((bf16[16,4,24,768]{3,2,1,0:T(8,128)(2,1)}), bf16[16,4,24,768]{3,2,1,0:T(8,128)(2,1)S(1)}, u32[]{:S(2)}, u32[]{:S(2)}) async-start(bf16[16,4,24,768]{3,2,1,0:T(8,128)(2,1)} %weight_gradient.2), calls=%async_computation | async-start | bytes 4718592 | tf_op jit(solution)/shard_map/all_to_all | solution.py:353
  96.0 5.0 %collective-permute-start.7 = (bf16[2,256,768]{2,1,0:T(8,128)(2,1)S(1)}, bf16[2,256,768]{2,1,0:T(8,128)(2,1)}, u32[]{:S(2)}, u32[]{:S(2)}) collective-permute-start(bf16[2,256,768]{2,1,0:T(8,128)(2,1)S(1)} %pad_maximum_fusion.1.b0.near), channel_id=1, source_target_pairs={{0,32},{32,0},{1,33},{33,1},{2,34},{34,2},{3,35},{35,3},{4,36},{36... | collective-permute-start | bytes 2359304 | tf_op jit(solution)/shard_map/ppermute | solution.py:336
  101.6 16.4 %collective-permute-done.7.b1.away = bf16[2,256,768]{2,1,0:T(8,128)(2,1)} collective-permute-done((bf16[2,256,768]{2,1,0:T(8,128)(2,1)S(1)}, bf16[2,256,768]{2,1,0:T(8,128)(2,1)}, u32[]{:S(2)}, u32[]{:S(2)}) %collective-permute-start.7) | collective-permute-done | bytes 786464 | tf_op jit(solution)/shard_map/ppermute | solution.py:336
  118.0 12.3 %context_gradient.1 = (f32[256,1536]{1,0:T(8,128)}, bf16[256,1536]{1,0:T(8,128)(2,1)}, f32[256,1536]{1,0:T(8,128)}, bf16[256,1536]{1,0:T(8,128)(2,1)}) custom-call(s32[4]{0:T(128)} %pad_add_fusion.place, bf16[2,256,768]{2,1,0:T(8,128)(2,1)} %copy-done.3, bf16[2,256,768]{2,1,0:T(8,128)(2,1)} %copy-done.12, bf16[2,256,768]{2,1,0:T(8,128)(2,1)} %copy-done.2, ...), custom_call_target="tpu_custom_call" | custom-call | flops 4831838208 | bytes 20971520 | tf_op jit(solution)/shard_map/context_gradient/pallas_call | solution.py:244
  130.3 1.7 collective-permute-start.16
  132.0 6.5 %weight_gradient.3 = bf16[16,4,24,768]{3,2,1,0:T(8,128)(2,1)} custom-call(bf16[1536,256]{1,0:T(8,128)(2,1)} %context_half.3.c0, bf16[1536,256]{1,0:T(8,128)(2,1)} %copy-done.10, bf16[1536,256]{1,0:T(8,128)(2,1)} %collective-permute-done.19.c2, bf16[1536,256]{1,0:T(8,128)(2,1)} %copy-done.11, bf16[2,256,768]{2,1,0:T(8,128)(2,1)} %copy-done.2, ...), custom_call_target="tpu_custom_call" | custom-call | flops 2415919104 | bytes 8388608 | tf_op jit(solution)/shard_map/weight_gradient/pallas_call | solution.py:273
  138.5 6.6 %all-to-all-start.1 = ((bf16[16,4,24,768]{3,2,1,0:T(8,128)(2,1)}), bf16[16,4,24,768]{3,2,1,0:T(8,128)(2,1)}, u32[]{:S(2)}, u32[]{:S(2)}) async-start(bf16[16,4,24,768]{3,2,1,0:T(8,128)(2,1)} %weight_gradient.3), calls=%async_computation.1 | async-start | bytes 4718592 | tf_op jit(solution)/shard_map/all_to_all | solution.py:353
  145.7 2.6 %add_convert_fusion = bf16[256,1536]{1,0:T(8,128)(2,1)} fusion(f32[256,1536]{1,0:T(8,128)} %get-tuple-element.41, bf16[256,1536]{1,0:T(8,128)(2,1)S(1)} %collective-permute-done.16), kind=kLoop, calls=%fused_computation | loop fusion | flops 1179648 | bytes 3145728 | tf_op jit(solution)/shard_map/convert_element_type | solution.py:359
  148.3 1.5 collective-permute-start.17
  150.2 3.6 %collective-permute-start.23 = (bf16[24,768]{1,0:T(8,128)(2,1)S(1)}, bf16[24,768]{1,0:T(8,128)(2,1)S(1)}, u32[]{:S(2)}, u32[]{:S(2)}) collective-permute-start(bf16[24,768]{1,0:T(8,128)(2,1)S(1)} %get-tuple-element.66), channel_id=1, source_target_pairs={{0,192},{64,0},{128,64},{192,128},{1,193},{65,1},{129,65},{193,129... | collective-permute-start | bytes 110600 | tf_op jit(solution)/shard_map/ppermute | solution.py:290
  153.7 2.0 collective-permute-start.22
  155.7 12.9 %collective-permute-done.21 = bf16[24,768]{1,0:T(8,128)(2,1)S(1)} collective-permute-done((bf16[24,768]{1,0:T(8,128)(2,1)S(1)}, bf16[24,768]{1,0:T(8,128)(2,1)S(1)}, u32[]{:S(2)}, u32[]{:S(2)}) %collective-permute-start.21) | collective-permute-done | bytes 36896 | tf_op jit(solution)/shard_map/ppermute | solution.py:290
  168.6 3.8 %collective-permute-done.22 = bf16[24,768]{1,0:T(8,128)(2,1)S(1)} collective-permute-done((bf16[24,768]{1,0:T(8,128)(2,1)S(1)}, bf16[24,768]{1,0:T(8,128)(2,1)S(1)}, u32[]{:S(2)}, u32[]{:S(2)}) %collective-permute-start.22) | collective-permute-done | bytes 36896 | tf_op jit(solution)/shard_map/ppermute | solution.py:290
  172.5 1.4 collective-permute-start.24
  173.9 10.4 %attention_gradients.2 = (bf16[256,3072]{1,0:T(8,128)(2,1)}, bf16[256,3072]{1,0:T(8,128)(2,1)}, bf16[256,3072]{1,0:T(8,128)(2,1)}) custom-call(s32[1]{0:T(128)} %bitcast.pick, bf16[256,3072]{1,0:T(8,128)(2,1)} %bitcast.40, bf16[256,3072]{1,0:T(8,128)(2,1)} %bitcast.44, bf16[256,3072]{1,0:T(8,128)(2,1)} %bitcast.48, f32[256,1536]{1,0:T(8,128)} %get-tuple-element.48.refs_0_, ...), custom_call_target="tpu_custom_call" | custom-call | flops 1006632960 | bytes 5505024 | tf_op jit(solution)/shard_map/attention_gradients/pallas_call | solution.py:117
  185.2 10.3 %attention_gradients.3 = (bf16[256,3072]{1,0:T(8,128)(2,1)}, bf16[256,3072]{1,0:T(8,128)(2,1)}, bf16[256,3072]{1,0:T(8,128)(2,1)}) custom-call(s32[1]{0:T(128)S(6)} %sub.7.pick, bf16[256,3072]{1,0:T(8,128)(2,1)} %bitcast.41, bf16[256,3072]{1,0:T(8,128)(2,1)} %bitcast.45, ...), custom_call_target="tpu_custom_call", output_to_operand_aliasing={{0}: (5, {}), {1}: (6, {}), {2}: (7, {})} | custom-call | flops 1006632960 | bytes 5505024 | tf_op jit(solution)/shard_map/attention_gradients/pallas_call | solution.py:117
  195.5 2.0 reduce_sum.25
  197.6 3.6 %collective-permute-start.28 = (bf16[24,768]{1,0:T(8,128)(2,1)S(1)}, bf16[24,768]{1,0:T(8,128)(2,1)S(1)}, u32[]{:S(2)}, u32[]{:S(2)}) collective-permute-start(bf16[24,768]{1,0:T(8,128)(2,1)S(1)} %get-tuple-element.63), channel_id=1, source_target_pairs={{0,192},{64,0},{128,64},{192,128},{1,193},{65,1},{129,65},{193,129... | collective-permute-start | bytes 110600 | tf_op jit(solution)/shard_map/ppermute | solution.py:290
  201.2 3.4 %collective-permute-start.27 = (bf16[24,768]{1,0:T(8,128)(2,1)S(1)}, bf16[24,768]{1,0:T(8,128)(2,1)S(1)}, u32[]{:S(2)}, u32[]{:S(2)}) collective-permute-start(bf16[24,768]{1,0:T(8,128)(2,1)S(1)} %get-tuple-element.64), channel_id=1, source_target_pairs={{0,128},{64,192},{128,0},{192,64},{1,129},{65,193},{129,1},{193,65... | collective-permute-start | bytes 110600 | tf_op jit(solution)/shard_map/ppermute | solution.py:290
  204.6 4.3 %collective-permute-done.27 = bf16[24,768]{1,0:T(8,128)(2,1)S(1)} collective-permute-done((bf16[24,768]{1,0:T(8,128)(2,1)S(1)}, bf16[24,768]{1,0:T(8,128)(2,1)S(1)}, u32[]{:S(2)}, u32[]{:S(2)}) %collective-permute-start.27) | collective-permute-done | bytes 36896 | tf_op jit(solution)/shard_map/ppermute | solution.py:290
  (73 shorter events, 10.6 us)
Async XLA Ops:
  2.8 1.8 collective-permute-start.1
  5.6 16.1 %copy-start.4 = (bf16[192,384]{1,0:T(8,128)(2,1)}, bf16[192,384]{1,0:T(8,128)(2,1)S(1)}, u32[]{:S(2)}) copy-start(bf16[192,384]{1,0:T(8,128)(2,1)S(1)} %maximum_select_fusion.1.own_ref) | copy-start | bytes 442372
  5.6 10.6 %collective-permute-start.2 = (bf16[192,384]{1,0:T(8,128)(2,1)S(1)}, bf16[192,384]{1,0:T(8,128)(2,1)S(1)}, u32[]{:S(2)}, u32[]{:S(2)}) collective-permute-start(bf16[192,384]{1,0:T(8,128)(2,1)S(1)} %maximum_select_fusion.1.own_ref), channel_id=1, source_target_pairs={{0,64},{64,128},{128,192},{192,0},{1,65},{65,129},{129,193},{193,1... | collective-permute-start | bytes 442376 | tf_op jit(solution)/shard_map/ppermute | solution.py:313
  8.6 14.6 %collective-permute-start.4 = (bf16[192,384]{1,0:T(8,128)(2,1)S(1)}, bf16[192,384]{1,0:T(8,128)(2,1)S(1)}, u32[]{:S(2)}, u32[]{:S(2)}) collective-permute-start(bf16[192,384]{1,0:T(8,128)(2,1)S(1)} %maximum_select_fusion.1.own_ref), channel_id=1, source_target_pairs={{0,192},{64,0},{128,64},{192,128},{1,193},{65,1},{129,65},{193,129... | collective-permute-start | bytes 442376 | tf_op jit(solution)/shard_map/ppermute | solution.py:313
  11.8 13.2 %collective-permute-start.3 = (bf16[192,384]{1,0:T(8,128)(2,1)S(1)}, bf16[192,384]{1,0:T(8,128)(2,1)S(1)}, u32[]{:S(2)}, u32[]{:S(2)}) collective-permute-start(bf16[192,384]{1,0:T(8,128)(2,1)S(1)} %maximum_select_fusion.1.own_ref), channel_id=1, source_target_pairs={{0,128},{64,192},{128,0},{192,64},{1,129},{65,193},{129,1},{193,65... | collective-permute-start | bytes 442376 | tf_op jit(solution)/shard_map/ppermute | solution.py:313
  16.2 5.4 %copy-start.7 = (bf16[192,384]{1,0:T(8,128)(2,1)}, bf16[192,384]{1,0:T(8,128)(2,1)S(1)}, u32[]{:S(2)}) copy-start(bf16[192,384]{1,0:T(8,128)(2,1)S(1)} %collective-permute-done.2.b1) | copy-start | bytes 442372
  16.2 17.6 %copy-start = (bf16[1,256,3072]{2,1,0:T(8,128)(2,1)S(1)}, bf16[1,256,3072]{2,1,0:T(8,128)(2,1)}, u32[]{:S(2)}) copy-start(bf16[1,256,3072]{2,1,0:T(8,128)(2,1)} %param.9) | copy-start | bytes 4718596
  23.2 1.8 copy-start.8
  25.0 0.7 copy-start.9
  27.7 8.2 %collective-permute-start.9 = (bf16[2,192,384]{2,1,0:T(8,128)(2,1)}, bf16[2,192,384]{2,1,0:T(8,128)(2,1)S(1)}, u32[]{:S(2)}, u32[]{:S(2)}) collective-permute-start(bf16[2,192,384]{2,1,0:T(8,128)(2,1)} %get-tuple-element.38.high), channel_id=1, source_target_pairs={{0,20},{16,0},{4,16},{20,4},{1,21},{17,1},{5,17},{21,5},{2,22},{18... | collective-permute-start | bytes 884744 | tf_op jit(solution)/shard_map/ppermute | solution.py:320
  28.0 8.0 %collective-permute-start.8 = (bf16[2,192,384]{2,1,0:T(8,128)(2,1)}, bf16[2,192,384]{2,1,0:T(8,128)(2,1)S(1)}, u32[]{:S(2)}, u32[]{:S(2)}) collective-permute-start(bf16[2,192,384]{2,1,0:T(8,128)(2,1)} %get-tuple-element.35.low), channel_id=1, source_target_pairs={{0,16},{16,4},{4,20},{20,0},{1,17},{17,5},{5,21},{21,1},{2,18},{18... | collective-permute-start | bytes 884744 | tf_op jit(solution)/shard_map/ppermute | solution.py:319
  29.2 22.3 %collective-permute-start.19 = (bf16[1536,256]{1,0:T(8,128)(2,1)}, bf16[1536,256]{1,0:T(8,128)(2,1)}, u32[]{:S(2)}, u32[]{:S(2)}) collective-permute-start(bf16[1536,256]{1,0:T(8,128)(2,1)} %context_half.2), channel_id=1, source_target_pairs={{0,32},{32,0},{1,33},{33,1},{2,34},{34,2},{3,35},{35,3},{4,36},{36... | collective-permute-start | bytes 2359304 | tf_op jit(solution)/shard_map/ppermute | solution.py:323
  33.9 12.6 %collective-permute-start = (bf16[256,768]{1,0:T(8,128)(2,1)S(1)}, bf16[256,768]{1,0:T(8,128)(2,1)S(1)}, u32[]{:S(2)}, u32[]{:S(2)}) collective-permute-start(bf16[256,768]{1,0:T(8,128)(2,1)S(1)} %get-tuple-element.59), channel_id=1, source_target_pairs={{0,8},{8,0},{1,9},{9,1},{2,10},{10,2},{3,11},{11,3},{4,12},{12,4},... | collective-permute-start | bytes 1179656 | tf_op jit(solution)/shard_map/ppermute | solution.py:334
  35.8 13.2 %collective-permute-start.6 = (bf16[256,768]{1,0:T(8,128)(2,1)S(1)}, bf16[256,768]{1,0:T(8,128)(2,1)S(1)}, u32[]{:S(2)}, u32[]{:S(2)}) collective-permute-start(bf16[256,768]{1,0:T(8,128)(2,1)S(1)} %get-tuple-element.61), channel_id=1, source_target_pairs={{0,8},{8,0},{1,9},{9,1},{2,10},{10,2},{3,11},{11,3},{4,12},{12,4},... | collective-permute-start | bytes 1179656 | tf_op jit(solution)/shard_map/ppermute | solution.py:334
  35.9 0.7 copy-start.5
  36.7 0.7 copy-start.6
  39.7 16.4 %collective-permute-start.14 = (bf16[768,384]{1,0:T(8,128)(2,1)}, bf16[768,384]{1,0:T(8,128)(2,1)}, u32[]{:S(2)}, u32[]{:S(2)}) collective-permute-start(bf16[768,384]{1,0:T(8,128)(2,1)} %bitcast.14.refs_4_), channel_id=1, source_target_pairs={{0,3},{1,0},{2,1},{3,2},{4,7},{5,4},{6,5},{7,6},{8,11},{9,8},{10,9... | collective-permute-start | bytes 1769480 | tf_op jit(solution)/shard_map/ppermute | solution.py:342
  39.9 16.2 %collective-permute-start.10 = (bf16[768,384]{1,0:T(8,128)(2,1)}, bf16[768,384]{1,0:T(8,128)(2,1)}, u32[]{:S(2)}, u32[]{:S(2)}) collective-permute-start(bf16[768,384]{1,0:T(8,128)(2,1)} %bitcast.56), channel_id=1, source_target_pairs={{0,1},{1,2},{2,3},{3,0},{4,5},{5,6},{6,7},{7,4},{8,9},{9,10},{10,1... | collective-permute-start | bytes 1769480 | tf_op jit(solution)/shard_map/ppermute | solution.py:341
  46.5 13.4 %collective-permute-start.18 = (bf16[1536,256]{1,0:T(8,128)(2,1)}, bf16[1536,256]{1,0:T(8,128)(2,1)S(1)}, u32[]{:S(2)}, u32[]{:S(2)}) collective-permute-start(bf16[1536,256]{1,0:T(8,128)(2,1)} %context_half.3.c0), channel_id=1, source_target_pairs={{0,8},{8,0},{1,9},{9,1},{2,10},{10,2},{3,11},{11,3},{4,12},{12,4},... | collective-permute-start | bytes 2359304 | tf_op jit(solution)/shard_map/ppermute | solution.py:325
  49.0 16.4 %collective-permute-start.13 = (bf16[768,384]{1,0:T(8,128)(2,1)}, bf16[768,384]{1,0:T(8,128)(2,1)S(1)}, u32[]{:S(2)}, u32[]{:S(2)}) collective-permute-start(bf16[768,384]{1,0:T(8,128)(2,1)} %bitcast.14.refs_4_), channel_id=1, source_target_pairs={{0,1},{1,2},{2,3},{3,0},{4,5},{5,6},{6,7},{7,4},{8,9},{9,10},{10,1... | collective-permute-start | bytes 1769480 | tf_op jit(solution)/shard_map/ppermute | solution.py:342
  51.2 7.5 %copy-start.13 = (bf16[2,2,192,384]{3,2,1,0:T(8,128)(2,1)S(1)}, bf16[2,2,192,384]{3,2,1,0:T(8,128)(2,1)}, u32[]{:S(2)}) copy-start(bf16[2,2,192,384]{3,2,1,0:T(8,128)(2,1)} %get-tuple-element.39) | copy-start | bytes 1769476
  51.3 23.3 %copy-start.3 = (bf16[2,256,768]{2,1,0:T(8,128)(2,1)}, bf16[2,256,768]{2,1,0:T(8,128)(2,1)S(1)}, u32[]{:S(2)}) copy-start(bf16[2,256,768]{2,1,0:T(8,128)(2,1)S(1)} %pad_maximum_fusion.a0.near) | copy-start | bytes 2359300
  51.4 44.6 %copy-start.2 = (bf16[2,256,768]{2,1,0:T(8,128)(2,1)}, bf16[2,256,768]{2,1,0:T(8,128)(2,1)S(1)}, u32[]{:S(2)}) copy-start(bf16[2,256,768]{2,1,0:T(8,128)(2,1)S(1)} %pad_maximum_fusion.1.b0.near) | copy-start | bytes 2359300
  51.4 22.4 %collective-permute-start.5 = (bf16[2,256,768]{2,1,0:T(8,128)(2,1)S(1)}, bf16[2,256,768]{2,1,0:T(8,128)(2,1)S(1)}, u32[]{:S(2)}, u32[]{:S(2)}) collective-permute-start(bf16[2,256,768]{2,1,0:T(8,128)(2,1)S(1)} %pad_maximum_fusion.a0.near), channel_id=1, source_target_pairs={{0,32},{32,0},{1,33},{33,1},{2,34},{34,2},{3,35},{35,3},{4,36},{36... | collective-permute-start | bytes 2359304 | tf_op jit(solution)/shard_map/ppermute | solution.py:336
  56.1 18.5 %collective-permute-start.20 = (bf16[1536,256]{1,0:T(8,128)(2,1)}, bf16[1536,256]{1,0:T(8,128)(2,1)S(1)}, u32[]{:S(2)}, u32[]{:S(2)}) collective-permute-start(bf16[1536,256]{1,0:T(8,128)(2,1)} %collective-permute-done.19.c2), channel_id=1, source_target_pairs={{0,8},{8,0},{1,9},{9,1},{2,10},{10,2},{3,11},{11,3},{4,12},{12,4},... | collective-permute-start | bytes 2359304 | tf_op jit(solution)/shard_map/ppermute | solution.py:346
  58.7 15.1 %collective-permute-start.11 = (bf16[768,384]{1,0:T(8,128)(2,1)S(1)}, bf16[768,384]{1,0:T(8,128)(2,1)S(1)}, u32[]{:S(2)}, u32[]{:S(2)}) collective-permute-start(bf16[768,384]{1,0:T(8,128)(2,1)S(1)} %bitcast.58), channel_id=1, source_target_pairs={{0,3},{1,0},{2,1},{3,2},{4,7},{5,4},{6,5},{7,6},{8,11},{9,8},{10,9... | collective-permute-start | bytes 1769480 | tf_op jit(solution)/shard_map/ppermute | solution.py:341
  59.9 14.0 %copy-start.10 = (bf16[1536,256]{1,0:T(8,128)(2,1)}, bf16[1536,256]{1,0:T(8,128)(2,1)S(1)}, u32[]{:S(2)}) copy-start(bf16[1536,256]{1,0:T(8,128)(2,1)S(1)} %collective-permute-done.18.c1) | copy-start | bytes 2359300
  59.9 26.5 %collective-permute-start.15 = (bf16[768,384]{1,0:T(8,128)(2,1)}, bf16[768,384]{1,0:T(8,128)(2,1)}, u32[]{:S(2)}, u32[]{:S(2)}) collective-permute-start(bf16[768,384]{1,0:T(8,128)(2,1)} %collective-permute-done.14.refs_6_), channel_id=1, source_target_pairs={{0,3},{1,0},{2,1},{3,2},{4,7},{5,4},{6,5},{7,6},{8,11},{9,8},{10,9... | collective-permute-start | bytes 1769480 | tf_op jit(solution)/shard_map/ppermute | solution.py:344
  65.4 8.5 %copy-start.14 = (bf16[768,384]{1,0:T(8,128)(2,1)}, bf16[768,384]{1,0:T(8,128)(2,1)S(1)}, u32[]{:S(2)}) copy-start(bf16[768,384]{1,0:T(8,128)(2,1)S(1)} %collective-permute-done.13.refs_5_) | copy-start | bytes 1769476
  65.4 21.0 %collective-permute-start.12 = (bf16[768,384]{1,0:T(8,128)(2,1)}, bf16[768,384]{1,0:T(8,128)(2,1)}, u32[]{:S(2)}, u32[]{:S(2)}) collective-permute-start(bf16[768,384]{1,0:T(8,128)(2,1)} %collective-permute-done.10.refs_1_), channel_id=1, source_target_pairs={{0,1},{1,2},{2,3},{3,0},{4,5},{5,6},{6,7},{7,4},{8,9},{9,10},{10,1... | collective-permute-start | bytes 1769480 | tf_op jit(solution)/shard_map/ppermute | solution.py:343
  73.8 0.8 copy-start.15
  74.6 0.9 copy-start.12
  75.5 0.9 copy-start.11
  86.4 52.0 %all-to-all-start = ((bf16[16,4,24,768]{3,2,1,0:T(8,128)(2,1)}), bf16[16,4,24,768]{3,2,1,0:T(8,128)(2,1)S(1)}, u32[]{:S(2)}, u32[]{:S(2)}) async-start(bf16[16,4,24,768]{3,2,1,0:T(8,128)(2,1)} %weight_gradient.2), calls=%async_computation | async-start | bytes 4718592 | tf_op jit(solution)/shard_map/all_to_all | solution.py:353
  96.0 22.0 %collective-permute-start.7 = (bf16[2,256,768]{2,1,0:T(8,128)(2,1)S(1)}, bf16[2,256,768]{2,1,0:T(8,128)(2,1)}, u32[]{:S(2)}, u32[]{:S(2)}) collective-permute-start(bf16[2,256,768]{2,1,0:T(8,128)(2,1)S(1)} %pad_maximum_fusion.1.b0.near), channel_id=1, source_target_pairs={{0,32},{32,0},{1,33},{33,1},{2,34},{34,2},{3,35},{35,3},{4,36},{36... | collective-permute-start | bytes 2359304 | tf_op jit(solution)/shard_map/ppermute | solution.py:336
  130.3 15.5 %collective-permute-start.16 = (bf16[256,1536]{1,0:T(8,128)(2,1)}, bf16[256,1536]{1,0:T(8,128)(2,1)S(1)}, u32[]{:S(2)}, u32[]{:S(2)}) collective-permute-start(bf16[256,1536]{1,0:T(8,128)(2,1)} %get-tuple-element.42), channel_id=1, source_target_pairs={{0,8},{8,0},{1,9},{9,1},{2,10},{10,2},{3,11},{11,3},{4,12},{12,4},... | collective-permute-start | bytes 2359304 | tf_op jit(solution)/shard_map/ppermute | solution.py:357
  138.5 57.0 %all-to-all-start.1 = ((bf16[16,4,24,768]{3,2,1,0:T(8,128)(2,1)}), bf16[16,4,24,768]{3,2,1,0:T(8,128)(2,1)}, u32[]{:S(2)}, u32[]{:S(2)}) async-start(bf16[16,4,24,768]{3,2,1,0:T(8,128)(2,1)} %weight_gradient.3), calls=%async_computation.1 | async-start | bytes 4718592 | tf_op jit(solution)/shard_map/all_to_all | solution.py:353
  145.1 28.8 %collective-permute-start.25 = (bf16[256,1536]{1,0:T(8,128)(2,1)}, bf16[256,1536]{1,0:T(8,128)(2,1)}, u32[]{:S(2)}, u32[]{:S(2)}) collective-permute-start(bf16[256,1536]{1,0:T(8,128)(2,1)} %get-tuple-element.49), channel_id=1, source_target_pairs={{0,8},{8,0},{1,9},{9,1},{2,10},{10,2},{3,11},{11,3},{4,12},{12,4},... | collective-permute-start | bytes 2359304 | tf_op jit(solution)/shard_map/ppermute | solution.py:358
  148.3 36.0 %collective-permute-start.17 = (bf16[256,1536]{1,0:T(8,128)(2,1)}, bf16[256,1536]{1,0:T(8,128)(2,1)S(1)}, u32[]{:S(2)}, u32[]{:S(2)}) collective-permute-start(bf16[256,1536]{1,0:T(8,128)(2,1)} %add_convert_fusion), channel_id=1, source_target_pairs={{0,32},{32,0},{1,33},{33,1},{2,34},{34,2},{3,35},{35,3},{4,36},{36... | collective-permute-start | bytes 2359304 | tf_op jit(solution)/shard_map/ppermute | solution.py:359
  150.1 18.5 %collective-permute-start.21 = (bf16[24,768]{1,0:T(8,128)(2,1)S(1)}, bf16[24,768]{1,0:T(8,128)(2,1)S(1)}, u32[]{:S(2)}, u32[]{:S(2)}) collective-permute-start(bf16[24,768]{1,0:T(8,128)(2,1)S(1)} %get-tuple-element.65), channel_id=1, source_target_pairs={{0,64},{64,128},{128,192},{192,0},{1,65},{65,129},{129,193},{193,1... | collective-permute-start | bytes 110600 | tf_op jit(solution)/shard_map/ppermute | solution.py:290
  150.2 18.4 %collective-permute-start.23 = (bf16[24,768]{1,0:T(8,128)(2,1)S(1)}, bf16[24,768]{1,0:T(8,128)(2,1)S(1)}, u32[]{:S(2)}, u32[]{:S(2)}) collective-permute-start(bf16[24,768]{1,0:T(8,128)(2,1)S(1)} %get-tuple-element.66), channel_id=1, source_target_pairs={{0,192},{64,0},{128,64},{192,128},{1,193},{65,1},{129,65},{193,129... | collective-permute-start | bytes 110600 | tf_op jit(solution)/shard_map/ppermute | solution.py:290
  153.7 18.7 %collective-permute-start.22 = (bf16[24,768]{1,0:T(8,128)(2,1)S(1)}, bf16[24,768]{1,0:T(8,128)(2,1)S(1)}, u32[]{:S(2)}, u32[]{:S(2)}) collective-permute-start(bf16[24,768]{1,0:T(8,128)(2,1)S(1)} %get-tuple-element.67), channel_id=1, source_target_pairs={{0,128},{64,192},{128,0},{192,64},{1,129},{65,193},{129,1},{193,65... | collective-permute-start | bytes 110600 | tf_op jit(solution)/shard_map/ppermute | solution.py:290
  172.5 11.8 %collective-permute-start.24 = (f32[12,768]{1,0:T(8,128)S(1)}, f32[12,768]{1,0:T(8,128)S(1)}, u32[]{:S(2)}, u32[]{:S(2)}) collective-permute-start(f32[12,768]{1,0:T(8,128)S(1)} %get-tuple-element.70), channel_id=1, source_target_pairs={{0,8},{8,0},{1,9},{9,1},{2,10},{10,2},{3,11},{11,3},{4,12},{12,4},... | collective-permute-start | bytes 110600 | tf_op jit(solution)/shard_map/ppermute | solution.py:294
  184.3 0.9 copy-start.1
  197.5 7.1 %collective-permute-start.26 = (bf16[24,768]{1,0:T(8,128)(2,1)S(1)}, bf16[24,768]{1,0:T(8,128)(2,1)S(1)}, u32[]{:S(2)}, u32[]{:S(2)}) collective-permute-start(bf16[24,768]{1,0:T(8,128)(2,1)S(1)} %get-tuple-element.62), channel_id=1, source_target_pairs={{0,64},{64,128},{128,192},{192,0},{1,65},{65,129},{129,193},{193,1... | collective-permute-start | bytes 110600 | tf_op jit(solution)/shard_map/ppermute | solution.py:290
  197.6 7.0 %collective-permute-start.28 = (bf16[24,768]{1,0:T(8,128)(2,1)S(1)}, bf16[24,768]{1,0:T(8,128)(2,1)S(1)}, u32[]{:S(2)}, u32[]{:S(2)}) collective-permute-start(bf16[24,768]{1,0:T(8,128)(2,1)S(1)} %get-tuple-element.63), channel_id=1, source_target_pairs={{0,192},{64,0},{128,64},{192,128},{1,193},{65,1},{129,65},{193,129... | collective-permute-start | bytes 110600 | tf_op jit(solution)/shard_map/ppermute | solution.py:290
  201.2 7.7 %collective-permute-start.27 = (bf16[24,768]{1,0:T(8,128)(2,1)S(1)}, bf16[24,768]{1,0:T(8,128)(2,1)S(1)}, u32[]{:S(2)}, u32[]{:S(2)}) collective-permute-start(bf16[24,768]{1,0:T(8,128)(2,1)S(1)} %get-tuple-element.64), channel_id=1, source_target_pairs={{0,128},{64,192},{128,0},{192,64},{1,129},{65,193},{129,1},{193,65... | collective-permute-start | bytes 110600 | tf_op jit(solution)/shard_map/ppermute | solution.py:290
  209.0 1.8 collective-permute-start.29

commit v6 on v5

--- a/solution.py
+++ b/solution.py
@@ -211,13 +211,13 @@
     )(low, high, beside_low, beside_high)
 
 
-def four_images(near, away):
-    return jnp.concatenate([near[0], near[1], away[0], away[1]], axis=0)
-
-
-def context_gradient_body(place, a0, a1, b0, b1, *refs):
-    lows, highs, outs, rows_ref = refs[:4], refs[4:8], refs[8:12], refs[12]
-    seq = a0.shape[1]
+def stacked(refs):
+    return jnp.concatenate([ref[...] for ref in refs], axis=0)
+
+
+def context_gradient_body(place, *refs):
+    images, lows, highs, outs, rows_ref = refs[:4], refs[4:8], refs[8:12], refs[12:16], refs[16]
+    seq = images[0].shape[0]
 
     def gather(weights):
         width = weights[0].shape[1]
@@ -227,17 +227,16 @@
 
     pl.when(pl.program_id(0) < 2)(functools.partial(gather, lows))
     pl.when(pl.program_id(0) >= 2)(functools.partial(gather, highs))
-    grads = jnp.concatenate([four_images(a0, a1), four_images(b0, b1)], axis=1)
-    total = dot(grads, rows_ref[...], NT)
+    total = dot(stacked(images), rows_ref[...], NT)
     for image, out in enumerate(outs):
         out[...] = total[image * seq : (image + 1) * seq].astype(out.dtype)
 
 
 def context_gradient(places, grads, lows, highs):
-    _, seq, part = grads[0].shape
+    seq, half = grads[0].shape[0], grads[0].shape[1] // 2
     block, width = lows[0].shape[0] // 2, lows[0].shape[1]
     rows = 4 * block
-    full = pl.BlockSpec((2, seq, part), lambda i, place: (0, 0, 0))
+    image = pl.BlockSpec((seq, half), lambda i, place: (0, place[4]))
     low = pl.BlockSpec((block, width), lambda i, place: (jnp.minimum(i, 1), 0))
     high = pl.BlockSpec((block, width), lambda i, place: (jnp.maximum(i - 2, 0), 0))
     out = pl.BlockSpec((seq, block), lambda i, place: (0, i))
@@ -246,40 +245,47 @@
         grid_spec=pltpu.PrefetchScalarGridSpec(
             num_scalar_prefetch=1,
             grid=(4,),
-            in_specs=[full] * 4 + [low] * 4 + [high] * 4,
+            in_specs=[image] * 4 + [low] * 4 + [high] * 4,
             out_specs=[out] * 4,
-            scratch_shapes=[pltpu.VMEM((block, 2 * part), BF16)],
+            scratch_shapes=[pltpu.VMEM((block, half), BF16)],
         ),
         out_shape=[
             jax.ShapeDtypeStruct((seq, rows), kind) for kind in (F32, BF16, F32, BF16)
         ],
         compiler_params=params(),
-        cost_estimate=cost(16 * seq * part * rows, 20 * 2**20),
+        cost_estimate=cost(8 * seq * half * rows, 20 * 2**20),
         name="context_gradient",
     )(places, *grads, *lows, *highs)
 
 
-def weight_gradient_body(c0, c1, c2, c3, near, away, out_ref):
+def weight_gradient_body(place, c0, c1, c2, c3, d0, d1, d2, d3, out_ref):
     context_t = jnp.concatenate([c[...] for c in (c0, c1, c2, c3)], axis=1)
-    total = dot(context_t, four_images(near, away), (((1,), (0,)), ((), ())))
-    for chip in range(16):
-        out_ref[chip, 0] = total[chip * 24 : (chip + 1) * 24].astype(BF16)
-
-
-def weight_gradient(contexts, near, away):
+    part = d0.shape[1] // 2
+    for half in range(2):
+        cols = slice(half * part, (half + 1) * part)
+        grads = jnp.concatenate([d[:, cols] for d in (d0, d1, d2, d3)], axis=0)
+        total = dot(context_t, grads, (((1,), (0,)), ((), ())))
+        for chip in range(16):
+            out_ref[chip, 0, :, cols] = total[chip * 24 : (chip + 1) * 24].astype(BF16)
+
+
+def weight_gradient(core, contexts, grads):
     rows, seq = contexts[0].shape
-    features = near.shape[2]
-    whole = pl.BlockSpec(near.shape, lambda i: (0, 0, 0))
+    half = grads[0].shape[1] // 2
     return pl.pallas_call(
         weight_gradient_body,
-        grid=(4,),
-        in_specs=[pl.BlockSpec((rows // 4, seq), lambda i: (i, 0))] * 4 + [whole] * 2,
-        out_specs=pl.BlockSpec((16, 1, 24, features), lambda i: (0, i, 0, 0)),
-        out_shape=jax.ShapeDtypeStruct((16, 4, 24, features), BF16),
+        grid_spec=pltpu.PrefetchScalarGridSpec(
+            num_scalar_prefetch=1,
+            grid=(4,),
+            in_specs=[pl.BlockSpec((rows // 4, seq), lambda i, place: (i, 0))] * 4
+            + [pl.BlockSpec((seq, half), lambda i, place: (0, place[0]))] * 4,
+            out_specs=pl.BlockSpec((16, 1, 24, half), lambda i, place: (0, i, 0, 0)),
+        ),
+        out_shape=jax.ShapeDtypeStruct((16, 4, 24, half), BF16),
         compiler_params=params(),
-        cost_estimate=cost(8 * seq * features * rows, 8 * 2**20),
+        cost_estimate=cost(8 * seq * half * rows, 12 * 2**20),
         name="weight_gradient",
-    )(*contexts, near, away)
+    )(core, *contexts, *grads)
 
 
 def sums_on_owners(terms, zh, c):
@@ -300,7 +306,7 @@
     q, k, v = (a.reshape(seq, total) for a in (queries, keys, values))
     grad = grad_output.reshape(seq, features)
     zh, zl, xl, c, y = (lax.axis_index(name) for name in ("zh", "zl", "xl", "c", "y"))
-    half = features // 2
+    core = c.astype(jnp.int32).reshape(1)
     width = 384
     own_parity = zl.astype(jnp.int32).reshape(1)
     other_parity = 1 - own_parity
@@ -315,58 +321,48 @@
     context_other = forward(late_parity, q, k, v, width)
     (pair,) = after((pair,), (context_other,))
     low, high = by_zh(pair, behind)
-    start = low
     beside_low = lax.ppermute(low, ("xl", "xh"), x_ring(1))
     beside_high = lax.ppermute(high, ("xl", "xh"), x_ring(-1))
 
+    d1 = lax.ppermute(grad, "c", SWAP)
+
     (context_other,) = after((context_other,), (behind[1], behind[2]))
     c2 = lax.ppermute(context_other, "zl", SWAP)
-    context_own = forward(own_parity, q, k, v, width)
+
+    low, high = by_xl(low, high, beside_low, beside_high)
+    low, high = after((low, high), (d1,))
+    (sent,) = after((grad,), (c2, low))
+    d2 = lax.ppermute(sent, "zl", SWAP)
+    (late_parity,) = after((own_parity,), (low,))
+    context_own = forward(late_parity, q, k, v, width)
     c1 = lax.ppermute(context_own, "c", SWAP)
-
-    part = half // 2
-    nears, grads = [], []
-    for index in range(2):
-        own, partner = (
-            lax.dynamic_slice_in_dim(grad, side * half + index * part, part, 1)
-            for side in (c, 1 - c)
-        )
-        nears.append(jnp.stack([own, lax.ppermute(partner, "c", SWAP)]))
-        (sent,) = after(nears[-1:], (grads[0][1] if index else start,))
-        grads.append((nears[-1], lax.ppermute(sent, "zl", SWAP)))
-
-    low, high = by_xl(low, high, beside_low, beside_high)
     lows, highs = ([piece.reshape(-1, width)] for piece in (low, high))
     for step in (1, -1):
         lows.append(lax.ppermute(lows[0], "y", ring(4, step)))
         highs.append(lax.ppermute(highs[0], "y", ring(4, step)))
     lows.append(lax.ppermute(lows[1], "y", ring(4, 1)))
     highs.append(lax.ppermute(highs[2], "y", ring(4, -1)))
-    (event,) = after((c2,), (lows[1], highs[2], nears[1]))
-    c3 = lax.ppermute(event, "c", SWAP)
-
-    (c1,) = after((c1,), (lows[2], highs[1]))
-    terms = []
-    for near, away in grads:
-        term = weight_gradient((context_own, c1, c2, c3), near, away)
-        (term,) = after((term,), (lows[3], highs[3]))
-        terms.append(lax.all_to_all(term, ("xl", "xh", "y"), 0, 0, tiled=True))
-
-    places = jnp.stack([y, (y + 3) % 4, (y + 1) % 4, (y + 2) % 4]).astype(jnp.int32)
-    g0, g1, g2, g3 = context_gradient(places, grads[0] + grads[1], lows, highs)
+    (sent,) = after((c2,), (lows[1], highs[2]))
+    c3 = lax.ppermute(sent, "c", SWAP)
+    (sent,) = after((d2,), (c1, c3, lows[2], highs[1]))
+    grads = (grad, d1, d2, lax.ppermute(sent, "c", SWAP))
+
+    terms = weight_gradient(core, (context_own, c1, c2, c3), grads)
+    (terms,) = after((terms,), (lows[3], highs[3]))
+    terms = lax.all_to_all(terms, ("xl", "xh", "y"), 0, 0, tiled=True)
+
+    places = jnp.stack([y, (y + 3) % 4, (y + 1) % 4, (y + 2) % 4, c]).astype(jnp.int32)
+    g0, g1, g2, g3 = context_gradient(places, grads, lows, highs)
     r3 = lax.ppermute(g3, "c", SWAP)
     r1 = lax.ppermute(g1, "c", SWAP)
     g_other = lax.ppermute((g2 + r3.astype(F32)).astype(BF16), "zl", SWAP)
     first = backward(own_parity, q, k, v, (g0, r1), width)
-
-    kept_a, got_a = sums_on_owners(terms[0], zh, c)
-    (g_other,) = after((g_other,), (kept_a, got_a))
     outs = backward(other_parity, q, k, v, (g_other,), width, first)
-    (last,) = after((terms[1],), tuple(outs))
-    kept_b, got_b = sums_on_owners(last, zh, c)
-    kept, got = (kept_a, kept_b), (got_a, got_b)
+
+    (terms,) = after((terms,), tuple(outs))
+    kept, got = sums_on_owners(terms, zh, c)
     grad_weight = jnp.where(
-        c == 0, jnp.concatenate(kept + got, 1), jnp.concatenate(got + kept, 1)
+        c == 0, jnp.concatenate([kept, got], 1), jnp.concatenate([got, kept], 1)
     )
     return tuple(out.reshape(1, seq, total) for out in outs) + (grad_weight,)
 

time: 213 us -> 199 us (0.934)
  starting transfers between devices: 78.4 us -> 52 us
  waiting for transfers between devices: 56 us -> 73.9 us
  Pallas kernels: 63.2 us -> 59.3 us
    all_to_all x2 -> x1, waiting for transfers between devices: 0.01 us -> 19.7 us  [per_device(): terms = lax.all_to_all(terms, ('xl', 'xh', 'y'), 0, 0, tiled=True)]
    ppermute x6 -> x3, waiting for transfers between devices: 21.1 us -> 5.37 us  [sums_on_owners(): mine = mine + lax.ppermute(away, 'zh', ring(4, step)).astype(F32)]
    ppermute x5 -> x4, waiting for transfers between devices: 16.4 us -> 2.74 us  [the longest x1 1.78 us: per_device(): grads = (grad, d1, d2, lax.ppermute(sent, 'c', SWAP))]
    ppermute x2, waiting for transfers between devices: 6.92 us -> 16.8 us  [per_device(): lows.append(lax.ppermute(lows[0], 'y', ring(4, step)))]
    all_to_all x2 -> x1, starting transfers between devices: 16.2 us -> 8.08 us  [per_device(): terms = lax.all_to_all(terms, ('xl', 'xh', 'y'), 0, 0, tiled=True)]
    ppermute x1, waiting for transfers between devices: 0.01 us -> 7.26 us  [per_device(): g_other = lax.ppermute((g2 + r3.astype(F32)).astype(BF16), 'zl', SWAP)]
    ppermute x6 -> x3, starting transfers between devices: 12.7 us -> 6.03 us  [sums_on_owners(): mine = mine + lax.ppermute(away, 'zh', ring(4, step)).astype(F32)]
    ppermute x5 -> x4, starting transfers between devices: 14.3 us -> 7.93 us  [the longest x1 3.45 us: per_device(): c3 = lax.ppermute(sent, 'c', SWAP)]
  transfers between devices with their start and end apart: 32 -> 26, of which waited for: 13 -> 20; matrix products, arithmetic and copies ran while one was open for 2% -> 2% of each run, Pallas kernels for 28% -> 30%
where the time goes in v6:
time: 199 us; the launch traced here: 197 us
  waiting for transfers between devices  73.9 us (37%)
  Pallas kernels  59.3 us (30%)
  starting transfers between devices  52 us (26%)
  other arithmetic  6.41 us (3%)
  local copies, waits for them, and re-layouts  5.13 us (3%)
    pallas_call x2, Pallas kernels, backward(): pl.pallas_call(functools.partial(backward_body, before is None), grid_spe...  20.6 us
    all_to_all x1, waiting for transfers between devices, per_device(): terms = lax.all_to_all(terms, ('xl', 'xh', 'y'), 0, 0, tiled=True)  19.7 us
    ppermute x2, waiting for transfers between devices, per_device(): lows.append(lax.ppermute(lows[0], 'y', ring(4, step)))  16.8 us
    pallas_call x1, Pallas kernels, context_gradient(): pl.pallas_call(context_gradient_body, grid_spec=pltpu.PrefetchScalarGridS...  12.3 us
    pallas_call x2, Pallas kernels, forward(): pl.pallas_call(forward_body, grid_spec=pltpu.PrefetchScalarGridSpec(num_s...  10.6 us
    ppermute x3, starting transfers between devices, per_device(): behind = [lax.ppermute(pair, 'zh', ring(4, step)) for step in (1, 2, 3)]  10.6 us
    pallas_call x1, Pallas kernels, weight_gradient(): pl.pallas_call(weight_gradient_body, grid_spec=pltpu.PrefetchScalarGridSp...  9.17 us
    all_to_all x1, starting transfers between devices, per_device(): terms = lax.all_to_all(terms, ('xl', 'xh', 'y'), 0, 0, tiled=True)  8.08 us
  transfers between devices with their start and end apart: 26, of which 20 were waited for; matrix products, arithmetic and copies ran while one was open for 2% of the time, Pallas kernels for 30%

profile of v6, /device:TPU:19, one launch (start us, length us, event | category | flops | bytes accessed | tf_op | source)
XLA Modules:
  0.0 197.4 jit_solution(1655333889734645902)
XLA Ops:
  1.4 2.1 %weight_pieces.1 = (bf16[96,384]{1,0:T(8,128)(2,1)}, bf16[96,384]{1,0:T(8,128)(2,1)}) custom-call(bf16[96,3072]{1,0:T(8,128)(2,1)} %codes_ref.1, f32[12,96]{1,0:T(8,128)} %bitcast.40), custom_call_target="tpu_custom_call" | custom-call | flops 73728 | bytes 294912 | tf_op jit(solution)/shard_map/weight_pieces/pallas_call | solution.py:162
  3.6 1.5 collective-permute-done.1
  5.0 1.0 maximum_select_fusion.1.own_ref
  6.0 3.1 %collective-permute-start.2 = (bf16[192,384]{1,0:T(8,128)(2,1)S(1)}, bf16[192,384]{1,0:T(8,128)(2,1)S(1)}, u32[]{:S(2)}, u32[]{:S(2)}) collective-permute-start(bf16[192,384]{1,0:T(8,128)(2,1)S(1)} %maximum_select_fusion.1.own_ref), channel_id=1, source_target_pairs={{0,64},{64,128},{128,192},{192,0},{1,65},{65,129},{129,193},{193,1... | collective-permute-start | bytes 442376 | tf_op jit(solution)/shard_map/ppermute | solution.py:319
  9.1 3.1 %collective-permute-start.4 = (bf16[192,384]{1,0:T(8,128)(2,1)S(1)}, bf16[192,384]{1,0:T(8,128)(2,1)S(1)}, u32[]{:S(2)}, u32[]{:S(2)}) collective-permute-start(bf16[192,384]{1,0:T(8,128)(2,1)S(1)} %maximum_select_fusion.1.own_ref), channel_id=1, source_target_pairs={{0,192},{64,0},{128,64},{192,128},{1,193},{65,1},{129,65},{193,129... | collective-permute-start | bytes 442376 | tf_op jit(solution)/shard_map/ppermute | solution.py:319
  12.2 4.4 %collective-permute-start.3 = (bf16[192,384]{1,0:T(8,128)(2,1)S(1)}, bf16[192,384]{1,0:T(8,128)(2,1)S(1)}, u32[]{:S(2)}, u32[]{:S(2)}) collective-permute-start(bf16[192,384]{1,0:T(8,128)(2,1)S(1)} %maximum_select_fusion.1.own_ref), channel_id=1, source_target_pairs={{0,128},{64,192},{128,0},{192,64},{1,129},{65,193},{129,1},{193,65... | collective-permute-start | bytes 442376 | tf_op jit(solution)/shard_map/ppermute | solution.py:319
  16.8 5.3 %context_half.2 = bf16[1536,256]{1,0:T(8,128)(2,1)} custom-call(s32[1]{0:T(128)S(6)} %sub.3.pick, bf16[256,3072]{1,0:T(8,128)(2,1)} %bitcast.25, bf16[256,3072]{1,0:T(8,128)(2,1)} %bitcast.29, bf16[256,3072]{1,0:T(8,128)(2,1)} %bitcast.33), custom_call_target="tpu_custom_call" | custom-call | flops 402653184 | bytes 3145728 | tf_op jit(solution)/shard_map/context_half/pallas_call | solution.py:73
  22.1 1.5 collective-permute-done.4.b3
  23.7 2.2 %collective-permute-done.3.b2 = bf16[192,384]{1,0:T(8,128)(2,1)S(1)} collective-permute-done((bf16[192,384]{1,0:T(8,128)(2,1)S(1)}, bf16[192,384]{1,0:T(8,128)(2,1)S(1)}, u32[]{:S(2)}, u32[]{:S(2)}) %collective-permute-start.3) | collective-permute-done | bytes 147488 | tf_op jit(solution)/shard_map/ppermute | solution.py:319
  25.8 4.3 %collective-permute-start.5 = (bf16[1536,256]{1,0:T(8,128)(2,1)}, bf16[1536,256]{1,0:T(8,128)(2,1)S(1)}, u32[]{:S(2)}, u32[]{:S(2)}) collective-permute-start(bf16[1536,256]{1,0:T(8,128)(2,1)} %context_half.2), channel_id=1, source_target_pairs={{0,32},{32,0},{1,33},{33,1},{2,34},{34,2},{3,35},{35,3},{4,36},{36... | collective-permute-start | bytes 2359304 | tf_op jit(solution)/shard_map/ppermute | solution.py:330
  30.1 2.0 %weight_by_zh.1 = (bf16[2,192,384]{2,1,0:T(8,128)(2,1)}, bf16[2,192,384]{2,1,0:T(8,128)(2,1)}) custom-call(bf16[192,384]{1,0:T(8,128)(2,1)} %copy-done.2, bf16[192,384]{1,0:T(8,128)(2,1)} %copy-done.5, bf16[192,384]{1,0:T(8,128)(2,1)} %copy-done.7, bf16[192,384]{1,0:T(8,128)(2,1)} %copy-done.6), custom_call_target="tpu_custom_call" | custom-call | flops 73728 | bytes 1179648 | tf_op jit(solution)/shard_map/weight_by_zh/pallas_call | solution.py:186
  32.1 1.2 collective-permute-start.6
  33.6 5.9 %collective-permute-done.6.beside_low = bf16[2,192,384]{2,1,0:T(8,128)(2,1)S(1)} collective-permute-done((bf16[2,192,384]{2,1,0:T(8,128)(2,1)}, bf16[2,192,384]{2,1,0:T(8,128)(2,1)S(1)}, u32[]{:S(2)}, u32[]{:S(2)}) %collective-permute-start.6) | collective-permute-done | bytes 294944 | tf_op jit(solution)/shard_map/ppermute | solution.py:324
  39.5 0.9 collective-permute-done.7.beside_high
  41.2 2.3 %weight_by_xl.1 = (bf16[2,2,192,384]{3,2,1,0:T(8,128)(2,1)}, bf16[2,2,192,384]{3,2,1,0:T(8,128)(2,1)}) custom-call(bf16[2,192,384]{2,1,0:T(8,128)(2,1)} %get-tuple-element.36.low, bf16[2,192,384]{2,1,0:T(8,128)(2,1)} %get-tuple-element.37.high, bf16[2,192,384]{2,1,0:T(8,128)(2,1)} %copy-done.3, bf16[2,192,384]{2,1,0:T(8,128)(2,1)} %copy-done.4), custom_call_target="tpu_custom_call" | custom-call | flops 147456 | bytes 2359296 | tf_op jit(solution)/shard_map/weight_by_xl/pallas_call | solution.py:205
  43.5 3.7 %collective-permute-done.5.c2 = bf16[1536,256]{1,0:T(8,128)(2,1)S(1)} collective-permute-done((bf16[1536,256]{1,0:T(8,128)(2,1)}, bf16[1536,256]{1,0:T(8,128)(2,1)S(1)}, u32[]{:S(2)}, u32[]{:S(2)}) %collective-permute-start.5) | collective-permute-done | bytes 786464 | tf_op jit(solution)/shard_map/ppermute | solution.py:330
  47.2 1.1 collective-permute-start.8
  48.3 1.0 collective-permute-start.10
  49.8 5.3 %context_half.3.c0 = bf16[1536,256]{1,0:T(8,128)(2,1)} custom-call(s32[1]{0:T(128)} %bitcast.pick, bf16[256,3072]{1,0:T(8,128)(2,1)} %bitcast.26, bf16[256,3072]{1,0:T(8,128)(2,1)} %bitcast.30, bf16[256,3072]{1,0:T(8,128)(2,1)} %bitcast.34), custom_call_target="tpu_custom_call" | custom-call | flops 402653184 | bytes 3145728 | tf_op jit(solution)/shard_map/context_half/pallas_call | solution.py:73
  55.1 2.8 %collective-permute-start.9 = (bf16[1536,256]{1,0:T(8,128)(2,1)}, bf16[1536,256]{1,0:T(8,128)(2,1)S(1)}, u32[]{:S(2)}, u32[]{:S(2)}) collective-permute-start(bf16[1536,256]{1,0:T(8,128)(2,1)} %context_half.3.c0), channel_id=1, source_target_pairs={{0,8},{8,0},{1,9},{9,1},{2,10},{10,2},{3,11},{11,3},{4,12},{12,4},... | collective-permute-start | bytes 2359304 | tf_op jit(solution)/shard_map/ppermute | solution.py:338
  57.9 3.3 %collective-permute-done.10.refs_5_ = bf16[768,384]{1,0:T(8,128)(2,1)S(1)} collective-permute-done((bf16[768,384]{1,0:T(8,128)(2,1)}, bf16[768,384]{1,0:T(8,128)(2,1)S(1)}, u32[]{:S(2)}, u32[]{:S(2)}) %collective-permute-start.10) | collective-permute-done | bytes 589856 | tf_op jit(solution)/shard_map/ppermute | solution.py:341
  61.9 3.5 %collective-permute-start.12 = (bf16[1536,256]{1,0:T(8,128)(2,1)S(1)}, bf16[1536,256]{1,0:T(8,128)(2,1)S(1)}, u32[]{:S(2)}, u32[]{:S(2)}) collective-permute-start(bf16[1536,256]{1,0:T(8,128)(2,1)S(1)} %collective-permute-done.5.c2), channel_id=1, source_target_pairs={{0,8},{8,0},{1,9},{9,1},{2,10},{10,2},{3,11},{11,3},{4,12},{12,4},... | collective-permute-start | bytes 2359304 | tf_op jit(solution)/shard_map/ppermute | solution.py:346
  65.9 1.0 collective-permute-start.14
  66.9 13.5 %collective-permute-done.13.refs_6_ = bf16[768,384]{1,0:T(8,128)(2,1)S(1)} collective-permute-done((bf16[768,384]{1,0:T(8,128)(2,1)S(1)}, bf16[768,384]{1,0:T(8,128)(2,1)S(1)}, u32[]{:S(2)}, u32[]{:S(2)}) %collective-permute-start.13) | collective-permute-done | bytes 589856 | tf_op jit(solution)/shard_map/ppermute | solution.py:341
  80.6 0.9 collective-permute-done.8.refs_2_.d2
  81.5 2.6 %collective-permute-start.15 = (bf16[256,3072]{1,0:T(8,128)(2,1)}, bf16[256,3072]{1,0:T(8,128)(2,1)S(1)}, u32[]{:S(2)}, u32[]{:S(2)}) collective-permute-start(bf16[256,3072]{1,0:T(8,128)(2,1)} %collective-permute-done.8.refs_2_.d2), channel_id=1, source_target_pairs={{0,8},{8,0},{1,9},{9,1},{2,10},{10,2},{3,11},{11,3},{4,12},{12,4},... | collective-permute-start | bytes 4718600 | tf_op jit(solution)/shard_map/ppermute | solution.py:348
  84.1 1.0 collective-permute-start.16
  85.5 1.8 collective-permute-done.15.refs_3_.d3
  87.4 1.1 copy-done.9
  88.5 9.2 %weight_gradient.1 = bf16[16,4,24,1536]{3,2,1,0:T(8,128)(2,1)} custom-call(s32[1]{0:T(128)} %bitcast.8.place, bf16[1536,256]{1,0:T(8,128)(2,1)} %context_half.3.c0, bf16[1536,256]{1,0:T(8,128)(2,1)} %copy-done.11, bf16[1536,256]{1,0:T(8,128)(2,1)} %copy-done.10, bf16[1536,256]{1,0:T(8,128)(2,1)} %copy-done.12, bf16[256,3072]{1,0:T(8,128)(2,1)} %bitcast.42, ...), custom_call_target="tpu_custom_call" | custom-call | flops 4831838208 | bytes 12582912 | tf_op jit(solution)/shard_map/weight_gradient/pallas_call | solution.py:275
  97.7 1.4 collective-permute-done.16.refs_7_
  99.0 0.9 collective-permute-done.17.refs_11_
  100.8 8.1 %all-to-all-start = ((bf16[16,4,24,1536]{3,2,1,0:T(8,128)(2,1)}), bf16[16,4,24,1536]{3,2,1,0:T(8,128)(2,1)}, u32[]{:S(2)}, u32[]{:S(2)}) async-start(bf16[16,4,24,1536]{3,2,1,0:T(8,128)(2,1)} %weight_gradient.1), calls=%async_computation | async-start | bytes 9437184 | tf_op jit(solution)/shard_map/all_to_all | solution.py:352
  109.5 12.3 %context_gradient.1 = (f32[256,1536]{1,0:T(8,128)}, bf16[256,1536]{1,0:T(8,128)(2,1)}, f32[256,1536]{1,0:T(8,128)}, bf16[256,1536]{1,0:T(8,128)(2,1)}) custom-call(s32[5]{0:T(128)} %stack.23.place, bf16[256,3072]{1,0:T(8,128)(2,1)} %bitcast.43, bf16[256,3072]{1,0:T(8,128)(2,1)} %collective-permute-done.refs_1_.d1, ...), custom_call_target="tpu_custom_call" | custom-call | flops 4831838208 | bytes 20971520 | tf_op jit(solution)/shard_map/context_gradient/pallas_call | solution.py:243
  121.8 1.8 collective-permute-start.18
  123.7 2.0 %collective-permute-done.18 = bf16[256,1536]{1,0:T(8,128)(2,1)S(1)} collective-permute-done((bf16[256,1536]{1,0:T(8,128)(2,1)}, bf16[256,1536]{1,0:T(8,128)(2,1)S(1)}, u32[]{:S(2)}, u32[]{:S(2)}) %collective-permute-start.18) | collective-permute-done | bytes 786464 | tf_op jit(solution)/shard_map/ppermute | solution.py:356
  125.7 1.6 add_convert_fusion
  127.8 0.9 copy-done
  128.7 10.4 %attention_gradients.2 = (bf16[256,3072]{1,0:T(8,128)(2,1)}, bf16[256,3072]{1,0:T(8,128)(2,1)}, bf16[256,3072]{1,0:T(8,128)(2,1)}) custom-call(s32[1]{0:T(128)} %bitcast.pick, bf16[256,3072]{1,0:T(8,128)(2,1)} %bitcast.27, bf16[256,3072]{1,0:T(8,128)(2,1)} %bitcast.31, bf16[256,3072]{1,0:T(8,128)(2,1)} %bitcast.35, f32[256,1536]{1,0:T(8,128)} %get-tuple-element.48.refs_0_, ...), custom_call_target="tpu_custom_call" | custom-call | flops 1006632960 | bytes 5505024 | tf_op jit(solution)/shard_map/attention_gradients/pallas_call | solution.py:117
  139.0 7.3 %collective-permute-done.19.refs_0_ = bf16[256,1536]{1,0:T(8,128)(2,1)S(1)} collective-permute-done((bf16[256,1536]{1,0:T(8,128)(2,1)S(1)}, bf16[256,1536]{1,0:T(8,128)(2,1)S(1)}, u32[]{:S(2)}, u32[]{:S(2)}) %collective-permute-start.19) | collective-permute-done | bytes 786464 | tf_op jit(solution)/shard_map/ppermute | solution.py:358
  147.2 10.3 %attention_gradients.3 = (bf16[256,3072]{1,0:T(8,128)(2,1)}, bf16[256,3072]{1,0:T(8,128)(2,1)}, bf16[256,3072]{1,0:T(8,128)(2,1)}) custom-call(s32[1]{0:T(128)S(6)} %sub.3.pick, bf16[256,3072]{1,0:T(8,128)(2,1)} %bitcast.28, bf16[256,3072]{1,0:T(8,128)(2,1)} %bitcast.32, ...), custom_call_target="tpu_custom_call", output_to_operand_aliasing={{0}: (5, {}), {1}: (6, {}), {2}: (7, {})} | custom-call | flops 1006632960 | bytes 5505024 | tf_op jit(solution)/shard_map/attention_gradients/pallas_call | solution.py:117
  157.5 19.7 %all-to-all-done = bf16[16,4,24,1536]{3,2,1,0:T(8,128)(2,1)} async-done(((bf16[16,4,24,1536]{3,2,1,0:T(8,128)(2,1)}), bf16[16,4,24,1536]{3,2,1,0:T(8,128)(2,1)}, u32[]{:S(2)}, u32[]{:S(2)}) %all-to-all-start) | async-done | bytes 4718624 | tf_op jit(solution)/shard_map/all_to_all | solution.py:352
  177.2 3.0 %reduce_sum.12 = bf16[4,24,1536]{2,1,0:T(8,128)(2,1)S(1)} reduce(bf16[16,4,24,1536]{3,2,1,0:T(8,128)(2,1)} %all-to-all-done, bf16[]{:T(256)} %constant.69.clone.1), dimensions={0}, to_apply=%region_0.1 | reduce | flops 2211840 | bytes 5013506 | tf_op jit(solution)/shard_map/reduce_sum | solution.py:292
  180.3 3.6 %collective-permute-start.23 = (bf16[24,1536]{1,0:T(8,128)(2,1)S(1)}, bf16[24,1536]{1,0:T(8,128)(2,1)S(1)}, u32[]{:S(2)}, u32[]{:S(2)}) collective-permute-start(bf16[24,1536]{1,0:T(8,128)(2,1)S(1)} %get-tuple-element.59), channel_id=1, source_target_pairs={{0,192},{64,0},{128,64},{192,128},{1,193},{65,1},{129,65},{193,129... | collective-permute-start | bytes 221192 | tf_op jit(solution)/shard_map/ppermute | solution.py:296
  183.9 2.4 %collective-permute-start.22 = (bf16[24,1536]{1,0:T(8,128)(2,1)S(1)}, bf16[24,1536]{1,0:T(8,128)(2,1)S(1)}, u32[]{:S(2)}, u32[]{:S(2)}) collective-permute-start(bf16[24,1536]{1,0:T(8,128)(2,1)S(1)} %get-tuple-element.60), channel_id=1, source_target_pairs={{0,128},{64,192},{128,0},{192,64},{1,129},{65,193},{129,1},{193,65... | collective-permute-start | bytes 221192 | tf_op jit(solution)/shard_map/ppermute | solution.py:296
  186.3 5.4 %collective-permute-done.22 = bf16[24,1536]{1,0:T(8,128)(2,1)S(1)} collective-permute-done((bf16[24,1536]{1,0:T(8,128)(2,1)S(1)}, bf16[24,1536]{1,0:T(8,128)(2,1)S(1)}, u32[]{:S(2)}, u32[]{:S(2)}) %collective-permute-start.22) | collective-permute-done | bytes 73760 | tf_op jit(solution)/shard_map/ppermute | solution.py:296
  191.7 4.0 %collective-permute-start.24 = (f32[12,1536]{1,0:T(8,128)S(1)}, f32[12,1536]{1,0:T(8,128)S(1)}, u32[]{:S(2)}, u32[]{:S(2)}) collective-permute-start(f32[12,1536]{1,0:T(8,128)S(1)} %get-tuple-element.62), channel_id=1, source_target_pairs={{0,8},{8,0},{1,9},{9,1},{2,10},{10,2},{3,11},{11,3},{4,12},{12,4},... | collective-permute-start | bytes 221192 | tf_op jit(solution)/shard_map/ppermute | solution.py:300
  195.8 0.9 collective-permute-done.24
  (61 shorter events, 8.0 us)
Async XLA Ops:
  0.6 42.9 %collective-permute-start = (bf16[256,3072]{1,0:T(8,128)(2,1)}, bf16[256,3072]{1,0:T(8,128)(2,1)}, u32[]{:S(2)}, u32[]{:S(2)}) collective-permute-start(bf16[256,3072]{1,0:T(8,128)(2,1)} %bitcast.41), channel_id=1, source_target_pairs={{0,8},{8,0},{1,9},{9,1},{2,10},{10,2},{3,11},{11,3},{4,12},{12,4},... | collective-permute-start | bytes 4718600 | tf_op jit(solution)/shard_map/ppermute | solution.py:327
  3.5 1.5 collective-permute-start.1
  6.0 16.1 %copy-start.2 = (bf16[192,384]{1,0:T(8,128)(2,1)}, bf16[192,384]{1,0:T(8,128)(2,1)S(1)}, u32[]{:S(2)}) copy-start(bf16[192,384]{1,0:T(8,128)(2,1)S(1)} %maximum_select_fusion.1.own_ref) | copy-start | bytes 442372
  6.0 10.8 %collective-permute-start.2 = (bf16[192,384]{1,0:T(8,128)(2,1)S(1)}, bf16[192,384]{1,0:T(8,128)(2,1)S(1)}, u32[]{:S(2)}, u32[]{:S(2)}) collective-permute-start(bf16[192,384]{1,0:T(8,128)(2,1)S(1)} %maximum_select_fusion.1.own_ref), channel_id=1, source_target_pairs={{0,64},{64,128},{128,192},{192,0},{1,65},{65,129},{129,193},{193,1... | collective-permute-start | bytes 442376 | tf_op jit(solution)/shard_map/ppermute | solution.py:319
  9.1 14.6 %collective-permute-start.4 = (bf16[192,384]{1,0:T(8,128)(2,1)S(1)}, bf16[192,384]{1,0:T(8,128)(2,1)S(1)}, u32[]{:S(2)}, u32[]{:S(2)}) collective-permute-start(bf16[192,384]{1,0:T(8,128)(2,1)S(1)} %maximum_select_fusion.1.own_ref), channel_id=1, source_target_pairs={{0,192},{64,0},{128,64},{192,128},{1,193},{65,1},{129,65},{193,129... | collective-permute-start | bytes 442376 | tf_op jit(solution)/shard_map/ppermute | solution.py:319
  12.2 13.6 %collective-permute-start.3 = (bf16[192,384]{1,0:T(8,128)(2,1)S(1)}, bf16[192,384]{1,0:T(8,128)(2,1)S(1)}, u32[]{:S(2)}, u32[]{:S(2)}) collective-permute-start(bf16[192,384]{1,0:T(8,128)(2,1)S(1)} %maximum_select_fusion.1.own_ref), channel_id=1, source_target_pairs={{0,128},{64,192},{128,0},{192,64},{1,129},{65,193},{129,1},{193,65... | collective-permute-start | bytes 442376 | tf_op jit(solution)/shard_map/ppermute | solution.py:319
  16.8 5.4 %copy-start.5 = (bf16[192,384]{1,0:T(8,128)(2,1)}, bf16[192,384]{1,0:T(8,128)(2,1)S(1)}, u32[]{:S(2)}) copy-start(bf16[192,384]{1,0:T(8,128)(2,1)S(1)} %collective-permute-done.2.b1) | copy-start | bytes 442372
  22.1 25.0 %copy-start.8 = (bf16[1,256,3072]{2,1,0:T(8,128)(2,1)S(1)}, bf16[1,256,3072]{2,1,0:T(8,128)(2,1)}, u32[]{:S(2)}) copy-start(bf16[1,256,3072]{2,1,0:T(8,128)(2,1)} %param.9) | copy-start | bytes 4718596
  23.7 6.4 %copy-start.6 = (bf16[192,384]{1,0:T(8,128)(2,1)}, bf16[192,384]{1,0:T(8,128)(2,1)S(1)}, u32[]{:S(2)}) copy-start(bf16[192,384]{1,0:T(8,128)(2,1)S(1)} %collective-permute-done.4.b3) | copy-start | bytes 442372
  25.8 4.3 %copy-start.7 = (bf16[192,384]{1,0:T(8,128)(2,1)}, bf16[192,384]{1,0:T(8,128)(2,1)S(1)}, u32[]{:S(2)}) copy-start(bf16[192,384]{1,0:T(8,128)(2,1)S(1)} %collective-permute-done.3.b2) | copy-start | bytes 442372
  25.8 21.3 %collective-permute-start.5 = (bf16[1536,256]{1,0:T(8,128)(2,1)}, bf16[1536,256]{1,0:T(8,128)(2,1)S(1)}, u32[]{:S(2)}, u32[]{:S(2)}) collective-permute-start(bf16[1536,256]{1,0:T(8,128)(2,1)} %context_half.2), channel_id=1, source_target_pairs={{0,32},{32,0},{1,33},{33,1},{2,34},{34,2},{3,35},{35,3},{4,36},{36... | collective-permute-start | bytes 2359304 | tf_op jit(solution)/shard_map/ppermute | solution.py:330
  32.1 7.4 %collective-permute-start.6 = (bf16[2,192,384]{2,1,0:T(8,128)(2,1)}, bf16[2,192,384]{2,1,0:T(8,128)(2,1)S(1)}, u32[]{:S(2)}, u32[]{:S(2)}) collective-permute-start(bf16[2,192,384]{2,1,0:T(8,128)(2,1)} %get-tuple-element.36.low), channel_id=1, source_target_pairs={{0,16},{16,4},{4,20},{20,0},{1,17},{17,5},{5,21},{21,1},{2,18},{18... | collective-permute-start | bytes 884744 | tf_op jit(solution)/shard_map/ppermute | solution.py:324
  33.3 7.1 %collective-permute-start.7 = (bf16[2,192,384]{2,1,0:T(8,128)(2,1)}, bf16[2,192,384]{2,1,0:T(8,128)(2,1)S(1)}, u32[]{:S(2)}, u32[]{:S(2)}) collective-permute-start(bf16[2,192,384]{2,1,0:T(8,128)(2,1)} %get-tuple-element.37.high), channel_id=1, source_target_pairs={{0,20},{16,0},{4,16},{20,4},{1,21},{17,1},{5,17},{21,5},{2,22},{18... | collective-permute-start | bytes 884744 | tf_op jit(solution)/shard_map/ppermute | solution.py:325
  39.5 0.9 copy-start.3
  40.4 0.7 copy-start.4
  47.2 14.8 %copy-start.10 = (bf16[1536,256]{1,0:T(8,128)(2,1)}, bf16[1536,256]{1,0:T(8,128)(2,1)S(1)}, u32[]{:S(2)}) copy-start(bf16[1536,256]{1,0:T(8,128)(2,1)S(1)} %collective-permute-done.5.c2) | copy-start | bytes 2359300
  47.2 34.3 %collective-permute-start.8 = (bf16[256,3072]{1,0:T(8,128)(2,1)S(1)}, bf16[256,3072]{1,0:T(8,128)(2,1)}, u32[]{:S(2)}, u32[]{:S(2)}) collective-permute-start(bf16[256,3072]{1,0:T(8,128)(2,1)S(1)} %bitcast.44), channel_id=1, source_target_pairs={{0,32},{32,0},{1,33},{33,1},{2,34},{34,2},{3,35},{35,3},{4,36},{36... | collective-permute-start | bytes 4718600 | tf_op jit(solution)/shard_map/ppermute | solution.py:335
  48.3 12.9 %collective-permute-start.10 = (bf16[768,384]{1,0:T(8,128)(2,1)}, bf16[768,384]{1,0:T(8,128)(2,1)S(1)}, u32[]{:S(2)}, u32[]{:S(2)}) collective-permute-start(bf16[768,384]{1,0:T(8,128)(2,1)} %bitcast.45), channel_id=1, source_target_pairs={{0,1},{1,2},{2,3},{3,0},{4,5},{5,6},{6,7},{7,4},{8,9},{9,10},{10,1... | collective-permute-start | bytes 1769480 | tf_op jit(solution)/shard_map/ppermute | solution.py:341
  49.3 16.1 %copy-start.13 = (bf16[2,2,192,384]{3,2,1,0:T(8,128)(2,1)S(1)}, bf16[2,2,192,384]{3,2,1,0:T(8,128)(2,1)}, u32[]{:S(2)}) copy-start(bf16[2,2,192,384]{3,2,1,0:T(8,128)(2,1)} %get-tuple-element.40) | copy-start | bytes 1769476
  49.3 16.5 %copy-start.14 = (bf16[2,2,192,384]{3,2,1,0:T(8,128)(2,1)S(1)}, bf16[2,2,192,384]{3,2,1,0:T(8,128)(2,1)}, u32[]{:S(2)}) copy-start(bf16[2,2,192,384]{3,2,1,0:T(8,128)(2,1)} %get-tuple-element.43) | copy-start | bytes 1769476
  49.3 12.6 %collective-permute-start.11 = (bf16[768,384]{1,0:T(8,128)(2,1)}, bf16[768,384]{1,0:T(8,128)(2,1)}, u32[]{:S(2)}, u32[]{:S(2)}) collective-permute-start(bf16[768,384]{1,0:T(8,128)(2,1)} %bitcast.48), channel_id=1, source_target_pairs={{0,3},{1,0},{2,1},{3,2},{4,7},{5,4},{6,5},{7,6},{8,11},{9,8},{10,9... | collective-permute-start | bytes 1769480 | tf_op jit(solution)/shard_map/ppermute | solution.py:342
  55.1 25.5 %collective-permute-start.9 = (bf16[1536,256]{1,0:T(8,128)(2,1)}, bf16[1536,256]{1,0:T(8,128)(2,1)S(1)}, u32[]{:S(2)}, u32[]{:S(2)}) collective-permute-start(bf16[1536,256]{1,0:T(8,128)(2,1)} %context_half.3.c0), channel_id=1, source_target_pairs={{0,8},{8,0},{1,9},{9,1},{2,10},{10,2},{3,11},{11,3},{4,12},{12,4},... | collective-permute-start | bytes 2359304 | tf_op jit(solution)/shard_map/ppermute | solution.py:338
  61.2 36.5 %copy-start.15 = (bf16[768,384]{1,0:T(8,128)(2,1)}, bf16[768,384]{1,0:T(8,128)(2,1)S(1)}, u32[]{:S(2)}) copy-start(bf16[768,384]{1,0:T(8,128)(2,1)S(1)} %collective-permute-done.10.refs_5_) | copy-start | bytes 1769476
  61.9 18.6 %collective-permute-start.12 = (bf16[1536,256]{1,0:T(8,128)(2,1)S(1)}, bf16[1536,256]{1,0:T(8,128)(2,1)S(1)}, u32[]{:S(2)}, u32[]{:S(2)}) collective-permute-start(bf16[1536,256]{1,0:T(8,128)(2,1)S(1)} %collective-permute-done.5.c2), channel_id=1, source_target_pairs={{0,8},{8,0},{1,9},{9,1},{2,10},{10,2},{3,11},{11,3},{4,12},{12,4},... | collective-permute-start | bytes 2359304 | tf_op jit(solution)/shard_map/ppermute | solution.py:346
  65.4 15.0 %collective-permute-start.13 = (bf16[768,384]{1,0:T(8,128)(2,1)S(1)}, bf16[768,384]{1,0:T(8,128)(2,1)S(1)}, u32[]{:S(2)}, u32[]{:S(2)}) collective-permute-start(bf16[768,384]{1,0:T(8,128)(2,1)S(1)} %bitcast.47), channel_id=1, source_target_pairs={{0,3},{1,0},{2,1},{3,2},{4,7},{5,4},{6,5},{7,6},{8,11},{9,8},{10,9... | collective-permute-start | bytes 1769480 | tf_op jit(solution)/shard_map/ppermute | solution.py:341
  65.9 14.7 %collective-permute-start.14 = (bf16[768,384]{1,0:T(8,128)(2,1)S(1)}, bf16[768,384]{1,0:T(8,128)(2,1)S(1)}, u32[]{:S(2)}, u32[]{:S(2)}) collective-permute-start(bf16[768,384]{1,0:T(8,128)(2,1)S(1)} %bitcast.50), channel_id=1, source_target_pairs={{0,1},{1,2},{2,3},{3,0},{4,5},{5,6},{6,7},{7,4},{8,9},{9,10},{10,1... | collective-permute-start | bytes 1769480 | tf_op jit(solution)/shard_map/ppermute | solution.py:342
  80.4 6.9 %copy-start.16 = (bf16[768,384]{1,0:T(8,128)(2,1)}, bf16[768,384]{1,0:T(8,128)(2,1)S(1)}, u32[]{:S(2)}) copy-start(bf16[768,384]{1,0:T(8,128)(2,1)S(1)} %collective-permute-done.13.refs_6_) | copy-start | bytes 1769476
  80.5 6.8 %copy-start.17 = (bf16[768,384]{1,0:T(8,128)(2,1)}, bf16[768,384]{1,0:T(8,128)(2,1)S(1)}, u32[]{:S(2)}) copy-start(bf16[768,384]{1,0:T(8,128)(2,1)S(1)} %collective-permute-done.14.refs_9_) | copy-start | bytes 1769476
  80.5 6.8 %copy-start.11 = (bf16[1536,256]{1,0:T(8,128)(2,1)}, bf16[1536,256]{1,0:T(8,128)(2,1)S(1)}, u32[]{:S(2)}) copy-start(bf16[1536,256]{1,0:T(8,128)(2,1)S(1)} %collective-permute-done.9.c1) | copy-start | bytes 2359300
  80.5 6.8 %copy-start.12 = (bf16[1536,256]{1,0:T(8,128)(2,1)}, bf16[1536,256]{1,0:T(8,128)(2,1)S(1)}, u32[]{:S(2)}) copy-start(bf16[1536,256]{1,0:T(8,128)(2,1)S(1)} %collective-permute-done.12.c3) | copy-start | bytes 2359300
  81.5 5.8 %collective-permute-start.15 = (bf16[256,3072]{1,0:T(8,128)(2,1)}, bf16[256,3072]{1,0:T(8,128)(2,1)S(1)}, u32[]{:S(2)}, u32[]{:S(2)}) collective-permute-start(bf16[256,3072]{1,0:T(8,128)(2,1)} %collective-permute-done.8.refs_2_.d2), channel_id=1, source_target_pairs={{0,8},{8,0},{1,9},{9,1},{2,10},{10,2},{3,11},{11,3},{4,12},{12,4},... | collective-permute-start | bytes 4718600 | tf_op jit(solution)/shard_map/ppermute | solution.py:348
  84.1 15.0 %collective-permute-start.16 = (bf16[768,384]{1,0:T(8,128)(2,1)S(1)}, bf16[768,384]{1,0:T(8,128)(2,1)S(1)}, u32[]{:S(2)}, u32[]{:S(2)}) collective-permute-start(bf16[768,384]{1,0:T(8,128)(2,1)S(1)} %collective-permute-done.10.refs_5_), channel_id=1, source_target_pairs={{0,1},{1,2},{2,3},{3,0},{4,5},{5,6},{6,7},{7,4},{8,9},{9,10},{10,1... | collective-permute-start | bytes 1769480 | tf_op jit(solution)/shard_map/ppermute | solution.py:343
  85.1 14.9 %collective-permute-start.17 = (bf16[768,384]{1,0:T(8,128)(2,1)}, bf16[768,384]{1,0:T(8,128)(2,1)S(1)}, u32[]{:S(2)}, u32[]{:S(2)}) collective-permute-start(bf16[768,384]{1,0:T(8,128)(2,1)} %collective-permute-done.11.refs_10_), channel_id=1, source_target_pairs={{0,3},{1,0},{2,1},{3,2},{4,7},{5,4},{6,5},{7,6},{8,11},{9,8},{10,9... | collective-permute-start | bytes 1769480 | tf_op jit(solution)/shard_map/ppermute | solution.py:344
  87.3 1.1 copy-start.9
  99.0 0.9 copy-start.18
  100.0 0.8 copy-start.19
  100.8 76.4 %all-to-all-start = ((bf16[16,4,24,1536]{3,2,1,0:T(8,128)(2,1)}), bf16[16,4,24,1536]{3,2,1,0:T(8,128)(2,1)}, u32[]{:S(2)}, u32[]{:S(2)}) async-start(bf16[16,4,24,1536]{3,2,1,0:T(8,128)(2,1)} %weight_gradient.1), calls=%async_computation | async-start | bytes 9437184 | tf_op jit(solution)/shard_map/all_to_all | solution.py:352
  121.8 4.0 %collective-permute-start.18 = (bf16[256,1536]{1,0:T(8,128)(2,1)}, bf16[256,1536]{1,0:T(8,128)(2,1)S(1)}, u32[]{:S(2)}, u32[]{:S(2)}) collective-permute-start(bf16[256,1536]{1,0:T(8,128)(2,1)} %get-tuple-element.47), channel_id=1, source_target_pairs={{0,8},{8,0},{1,9},{9,1},{2,10},{10,2},{3,11},{11,3},{4,12},{12,4},... | collective-permute-start | bytes 2359304 | tf_op jit(solution)/shard_map/ppermute | solution.py:356
  123.6 4.2 %collective-permute-start.20 = (bf16[256,1536]{1,0:T(8,128)(2,1)}, bf16[256,1536]{1,0:T(8,128)(2,1)S(1)}, u32[]{:S(2)}, u32[]{:S(2)}) collective-permute-start(bf16[256,1536]{1,0:T(8,128)(2,1)} %get-tuple-element.49), channel_id=1, source_target_pairs={{0,8},{8,0},{1,9},{9,1},{2,10},{10,2},{3,11},{11,3},{4,12},{12,4},... | collective-permute-start | bytes 2359304 | tf_op jit(solution)/shard_map/ppermute | solution.py:357
  127.3 18.9 %collective-permute-start.19 = (bf16[256,1536]{1,0:T(8,128)(2,1)S(1)}, bf16[256,1536]{1,0:T(8,128)(2,1)S(1)}, u32[]{:S(2)}, u32[]{:S(2)}) collective-permute-start(bf16[256,1536]{1,0:T(8,128)(2,1)S(1)} %add_convert_fusion), channel_id=1, source_target_pairs={{0,32},{32,0},{1,33},{33,1},{2,34},{34,2},{3,35},{35,3},{4,36},{36... | collective-permute-start | bytes 2359304 | tf_op jit(solution)/shard_map/ppermute | solution.py:358
  127.8 0.9 copy-start
  146.3 0.9 copy-start.1
  180.3 6.0 %collective-permute-start.21 = (bf16[24,1536]{1,0:T(8,128)(2,1)S(1)}, bf16[24,1536]{1,0:T(8,128)(2,1)S(1)}, u32[]{:S(2)}, u32[]{:S(2)}) collective-permute-start(bf16[24,1536]{1,0:T(8,128)(2,1)S(1)} %get-tuple-element.58), channel_id=1, source_target_pairs={{0,64},{64,128},{128,192},{192,0},{1,65},{65,129},{129,193},{193,1... | collective-permute-start | bytes 221192 | tf_op jit(solution)/shard_map/ppermute | solution.py:296
  180.3 6.0 %collective-permute-start.23 = (bf16[24,1536]{1,0:T(8,128)(2,1)S(1)}, bf16[24,1536]{1,0:T(8,128)(2,1)S(1)}, u32[]{:S(2)}, u32[]{:S(2)}) collective-permute-start(bf16[24,1536]{1,0:T(8,128)(2,1)S(1)} %get-tuple-element.59), channel_id=1, source_target_pairs={{0,192},{64,0},{128,64},{192,128},{1,193},{65,1},{129,65},{193,129... | collective-permute-start | bytes 221192 | tf_op jit(solution)/shard_map/ppermute | solution.py:296
  183.9 7.8 %collective-permute-start.22 = (bf16[24,1536]{1,0:T(8,128)(2,1)S(1)}, bf16[24,1536]{1,0:T(8,128)(2,1)S(1)}, u32[]{:S(2)}, u32[]{:S(2)}) collective-permute-start(bf16[24,1536]{1,0:T(8,128)(2,1)S(1)} %get-tuple-element.60), channel_id=1, source_target_pairs={{0,128},{64,192},{128,0},{192,64},{1,129},{65,193},{129,1},{193,65... | collective-permute-start | bytes 221192 | tf_op jit(solution)/shard_map/ppermute | solution.py:296
  191.7 5.0 %collective-permute-start.24 = (f32[12,1536]{1,0:T(8,128)S(1)}, f32[12,1536]{1,0:T(8,128)S(1)}, u32[]{:S(2)}, u32[]{:S(2)}) collective-permute-start(f32[12,1536]{1,0:T(8,128)S(1)} %get-tuple-element.62), channel_id=1, source_target_pairs={{0,8},{8,0},{1,9},{9,1},{2,10},{10,2},{3,11},{11,3},{4,12},{12,4},... | collective-permute-start | bytes 221192 | tf_op jit(solution)/shard_map/ppermute | solution.py:300

commit v7 on v6

--- a/solution.py
+++ b/solution.py
@@ -162,7 +162,7 @@
     return pl.pallas_call(
         restore_body,
         out_shape=[jax.ShapeDtypeStruct((rows, 384), BF16)] * 2,
-        compiler_params=pltpu.CompilerParams(vmem_limit_bytes=VMEM_LIMIT),
+        compiler_params=pltpu.CompilerParams(vmem_limit_bytes=8 * 2**20),
         cost_estimate=cost(rows * 768, rows * 3072),
         name="weight_pieces",
     )(codes, scales)
@@ -185,8 +185,10 @@
 def by_zh(own, pieces):
     return pl.pallas_call(
         by_zh_body,
+        in_specs=[pl.BlockSpec(memory_space=pltpu.VMEM)] * 4,
+        out_specs=[pl.BlockSpec(memory_space=pltpu.VMEM)] * 2,
         out_shape=[jax.ShapeDtypeStruct((2, *own.shape), BF16)] * 2,
-        compiler_params=pltpu.CompilerParams(vmem_limit_bytes=VMEM_LIMIT),
+        compiler_params=pltpu.CompilerParams(vmem_limit_bytes=8 * 2**20),
         cost_estimate=cost(own.size, own.size * 16),
         name="weight_by_zh",
     )(own, *pieces)
@@ -204,8 +206,10 @@
     shape = (2, 2, *low.shape[1:])
     return pl.pallas_call(
         by_xl_body,
+        in_specs=[pl.BlockSpec(memory_space=pltpu.VMEM)] * 4,
+        out_specs=[pl.BlockSpec(memory_space=pltpu.VMEM)] * 2,
         out_shape=[jax.ShapeDtypeStruct(shape, BF16)] * 2,
-        compiler_params=pltpu.CompilerParams(vmem_limit_bytes=VMEM_LIMIT),
+        compiler_params=pltpu.CompilerParams(vmem_limit_bytes=8 * 2**20),
         cost_estimate=cost(low.size, low.size * 16),
         name="weight_by_xl",
     )(low, high, beside_low, beside_high)
@@ -233,10 +237,10 @@
 
 
 def context_gradient(places, grads, lows, highs):
-    seq, half = grads[0].shape[0], grads[0].shape[1] // 2
+    seq, half = grads[0].shape
     block, width = lows[0].shape[0] // 2, lows[0].shape[1]
     rows = 4 * block
-    image = pl.BlockSpec((seq, half), lambda i, place: (0, place[4]))
+    image = pl.BlockSpec((seq, half), lambda i, place: (0, 0))
     low = pl.BlockSpec((block, width), lambda i, place: (jnp.minimum(i, 1), 0))
     high = pl.BlockSpec((block, width), lambda i, place: (jnp.maximum(i - 2, 0), 0))
     out = pl.BlockSpec((seq, block), lambda i, place: (0, i))
@@ -258,7 +262,7 @@
     )(places, *grads, *lows, *highs)
 
 
-def weight_gradient_body(place, c0, c1, c2, c3, d0, d1, d2, d3, out_ref):
+def weight_gradient_body(c0, c1, c2, c3, d0, d1, d2, d3, out_ref):
     context_t = jnp.concatenate([c[...] for c in (c0, c1, c2, c3)], axis=1)
     part = d0.shape[1] // 2
     for half in range(2):
@@ -269,23 +273,20 @@
             out_ref[chip, 0, :, cols] = total[chip * 24 : (chip + 1) * 24].astype(BF16)
 
 
-def weight_gradient(core, contexts, grads):
+def weight_gradient(contexts, grads):
     rows, seq = contexts[0].shape
-    half = grads[0].shape[1] // 2
+    half = grads[0].shape[1]
     return pl.pallas_call(
         weight_gradient_body,
-        grid_spec=pltpu.PrefetchScalarGridSpec(
-            num_scalar_prefetch=1,
-            grid=(4,),
-            in_specs=[pl.BlockSpec((rows // 4, seq), lambda i, place: (i, 0))] * 4
-            + [pl.BlockSpec((seq, half), lambda i, place: (0, place[0]))] * 4,
-            out_specs=pl.BlockSpec((16, 1, 24, half), lambda i, place: (0, i, 0, 0)),
-        ),
+        grid=(4,),
+        in_specs=[pl.BlockSpec((rows // 4, seq), lambda i: (i, 0))] * 4
+        + [pl.BlockSpec((seq, half), lambda i: (0, 0))] * 4,
+        out_specs=pl.BlockSpec((16, 1, 24, half), lambda i: (0, i, 0, 0)),
         out_shape=jax.ShapeDtypeStruct((16, 4, 24, half), BF16),
         compiler_params=params(),
         cost_estimate=cost(8 * seq * half * rows, 12 * 2**20),
         name="weight_gradient",
-    )(core, *contexts, *grads)
+    )(*contexts, *grads)
 
 
 def sums_on_owners(terms, zh, c):
@@ -306,7 +307,6 @@
     q, k, v = (a.reshape(seq, total) for a in (queries, keys, values))
     grad = grad_output.reshape(seq, features)
     zh, zl, xl, c, y = (lax.axis_index(name) for name in ("zh", "zl", "xl", "c", "y"))
-    core = c.astype(jnp.int32).reshape(1)
     width = 384
     own_parity = zl.astype(jnp.int32).reshape(1)
     other_parity = 1 - own_parity
@@ -324,34 +324,38 @@
     beside_low = lax.ppermute(low, ("xl", "xh"), x_ring(1))
     beside_high = lax.ppermute(high, ("xl", "xh"), x_ring(-1))
 
-    d1 = lax.ppermute(grad, "c", SWAP)
+    half = features // 2
+    (late_grad,) = after((grad,), (context_other,))
+    mine, other = (
+        lax.dynamic_slice_in_dim(late_grad, side * half, half, 1) for side in (c, 1 - c)
+    )
+    d1 = lax.ppermute(other, "c", SWAP)
 
     (context_other,) = after((context_other,), (behind[1], behind[2]))
     c2 = lax.ppermute(context_other, "zl", SWAP)
 
     low, high = by_xl(low, high, beside_low, beside_high)
-    low, high = after((low, high), (d1,))
-    (sent,) = after((grad,), (c2, low))
-    d2 = lax.ppermute(sent, "zl", SWAP)
+    near, diagonal = after((mine, other), (c2, low, d1))
+    d2 = lax.ppermute(near, "zl", SWAP)
+    d3 = lax.ppermute(diagonal, ("zl", "c"), [(i, 3 - i) for i in range(4)])
+    grads = (mine, d1, d2, d3)
     (late_parity,) = after((own_parity,), (low,))
     context_own = forward(late_parity, q, k, v, width)
-    c1 = lax.ppermute(context_own, "c", SWAP)
     lows, highs = ([piece.reshape(-1, width)] for piece in (low, high))
     for step in (1, -1):
         lows.append(lax.ppermute(lows[0], "y", ring(4, step)))
         highs.append(lax.ppermute(highs[0], "y", ring(4, step)))
     lows.append(lax.ppermute(lows[1], "y", ring(4, 1)))
     highs.append(lax.ppermute(highs[2], "y", ring(4, -1)))
-    (sent,) = after((c2,), (lows[1], highs[2]))
-    c3 = lax.ppermute(sent, "c", SWAP)
-    (sent,) = after((d2,), (c1, c3, lows[2], highs[1]))
-    grads = (grad, d1, d2, lax.ppermute(sent, "c", SWAP))
-
-    terms = weight_gradient(core, (context_own, c1, c2, c3), grads)
-    (terms,) = after((terms,), (lows[3], highs[3]))
+    sent_own, sent_away = after((context_own, c2), (*lows[1:3], *highs[1:3]))
+    c1 = lax.ppermute(sent_own, "c", SWAP)
+    c3 = lax.ppermute(sent_away, "c", SWAP)
+
+    terms = weight_gradient((context_own, c1, c2, c3), grads)
+    (terms,) = after((terms,), (*lows[2:], *highs[1:]))
     terms = lax.all_to_all(terms, ("xl", "xh", "y"), 0, 0, tiled=True)
 
-    places = jnp.stack([y, (y + 3) % 4, (y + 1) % 4, (y + 2) % 4, c]).astype(jnp.int32)
+    places = jnp.stack([y, (y + 3) % 4, (y + 1) % 4, (y + 2) % 4]).astype(jnp.int32)
     g0, g1, g2, g3 = context_gradient(places, grads, lows, highs)
     r3 = lax.ppermute(g3, "c", SWAP)
     r1 = lax.ppermute(g1, "c", SWAP)

time: 199 us -> 193 us (0.970)
  waiting for transfers between devices: 73.9 us -> 82.3 us
  starting transfers between devices: 52 us -> 44.9 us
  Pallas kernels: 59.3 us -> 53.5 us
    ppermute x2, waiting for transfers between devices: 16.8 us -> 0.75 us  [per_device(): lows.append(lax.ppermute(lows[0], 'y', ring(4, step)))]
    ppermute x5, waiting for transfers between devices: 2.74 us -> 12.5 us  [the longest x1 12.5 us: per_device(): d3 = lax.ppermute(diagonal, ('zl', 'c'), [(i, 3 - i) for i in range(4)])]
    ppermute x2, waiting for transfers between devices: 0.87 us -> 9.63 us  [per_device(): highs.append(lax.ppermute(highs[0], 'y', ring(4, step)))]
    all_to_all x1, waiting for transfers between devices: 19.7 us -> 26 us  [per_device(): terms = lax.all_to_all(terms, ('xl', 'xh', 'y'), 0, 0, tiled=True)]
    pallas_call x3, Pallas kernels: 13.5 us -> 9.35 us  [the longest x1 9.15 us: weight_gradient(): pl.pallas_call(weight_gradient_body, grid=(4,), in_specs=[pl.BlockSpec((r...]
    ppermute x1, starting transfers between devices: 4.04 us -> 0.9 us  [sums_on_owners(): return (kept, lax.ppermute(sent, 'c', SWAP))]
    ppermute x5, starting transfers between devices: 10.7 us -> 7.81 us  [the longest x1 3.01 us: per_device(): d3 = lax.ppermute(diagonal, ('zl', 'c'), [(i, 3 - i) for i in range(4)])]
    unnamed x40 -> x28, local copies, waits for them, and re-layouts: 4.5 us -> 4.72 us
  transfers between devices with their start and end apart: 26 -> 26, of which waited for: 20 -> 17; matrix products, arithmetic and copies ran while one was open for 2% -> 1% of each run, Pallas kernels for 30% -> 28%
where the time goes in v7:
time: 193 us; the launch traced here: 192 us
  waiting for transfers between devices  82.3 us (43%)
  Pallas kernels  53.5 us (28%)
  starting transfers between devices  44.9 us (23%)
  other arithmetic  6.03 us (3%)
  local copies, waits for them, and re-layouts  4.86 us (3%)
    all_to_all x1, waiting for transfers between devices, per_device(): terms = lax.all_to_all(terms, ('xl', 'xh', 'y'), 0, 0, tiled=True)  26 us
    pallas_call x2, Pallas kernels, backward(): pl.pallas_call(functools.partial(backward_body, before is None), grid_spe...  20.6 us
    ppermute x1, waiting for transfers between devices, per_device(): d3 = lax.ppermute(diagonal, ('zl', 'c'), [(i, 3 - i) for i in range(4)])  12.5 us
    pallas_call x1, Pallas kernels, context_gradient(): pl.pallas_call(context_gradient_body, grid_spec=pltpu.PrefetchScalarGridS...  12.3 us
    pallas_call x2, Pallas kernels, forward(): pl.pallas_call(forward_body, grid_spec=pltpu.PrefetchScalarGridSpec(num_s...  10.7 us
    ppermute x3, starting transfers between devices, per_device(): behind = [lax.ppermute(pair, 'zh', ring(4, step)) for step in (1, 2, 3)]  10.6 us
    ppermute x2, waiting for transfers between devices, per_device(): highs.append(lax.ppermute(highs[0], 'y', ring(4, step)))  9.63 us
    pallas_call x1, Pallas kernels, weight_gradient(): pl.pallas_call(weight_gradient_body, grid=(4,), in_specs=[pl.BlockSpec((r...  9.15 us
  transfers between devices with their start and end apart: 26, of which 17 were waited for; matrix products, arithmetic and copies ran while one was open for 1% of the time, Pallas kernels for 28%

profile of v7, /device:TPU:19, one launch (start us, length us, event | category | flops | bytes accessed | tf_op | source)
XLA Modules:
  0.0 192.3 jit_solution(8797022465222788342)
XLA Ops:
  0.6 1.1 copy-done
  1.7 0.7 copy-done.1
  2.8 0.8 collective-permute-start
  3.6 0.9 collective-permute-done
  4.5 3.1 %collective-permute-start.1 = (bf16[192,384]{1,0:T(8,128)(2,1)S(1)}, bf16[192,384]{1,0:T(8,128)(2,1)S(1)}, u32[]{:S(2)}, u32[]{:S(2)}) collective-permute-start(bf16[192,384]{1,0:T(8,128)(2,1)S(1)} %maximum_select_fusion.1.own_ref), channel_id=1, source_target_pairs={{0,64},{64,128},{128,192},{192,0},{1,65},{65,129},{129,193},{193,1... | collective-permute-start | bytes 442376 | tf_op jit(solution)/shard_map/ppermute | solution.py:319
  7.6 3.1 %collective-permute-start.4 = (bf16[192,384]{1,0:T(8,128)(2,1)S(1)}, bf16[192,384]{1,0:T(8,128)(2,1)S(1)}, u32[]{:S(2)}, u32[]{:S(2)}) collective-permute-start(bf16[192,384]{1,0:T(8,128)(2,1)S(1)} %maximum_select_fusion.1.own_ref), channel_id=1, source_target_pairs={{0,192},{64,0},{128,64},{192,128},{1,193},{65,1},{129,65},{193,129... | collective-permute-start | bytes 442376 | tf_op jit(solution)/shard_map/ppermute | solution.py:319
  10.7 4.4 %collective-permute-start.3 = (bf16[192,384]{1,0:T(8,128)(2,1)S(1)}, bf16[192,384]{1,0:T(8,128)(2,1)S(1)}, u32[]{:S(2)}, u32[]{:S(2)}) collective-permute-start(bf16[192,384]{1,0:T(8,128)(2,1)S(1)} %maximum_select_fusion.1.own_ref), channel_id=1, source_target_pairs={{0,128},{64,192},{128,0},{192,64},{1,129},{65,193},{129,1},{193,65... | collective-permute-start | bytes 442376 | tf_op jit(solution)/shard_map/ppermute | solution.py:319
  15.2 5.4 %context_half.2 = bf16[1536,256]{1,0:T(8,128)(2,1)} custom-call(s32[1]{0:T(128)S(6)} %sub.6.pick, bf16[256,3072]{1,0:T(8,128)(2,1)} %bitcast.31, bf16[256,3072]{1,0:T(8,128)(2,1)} %bitcast.35, bf16[256,3072]{1,0:T(8,128)(2,1)} %bitcast.39), custom_call_target="tpu_custom_call" | custom-call | flops 402653184 | bytes 3145728 | tf_op jit(solution)/shard_map/context_half/pallas_call | solution.py:73
  20.6 1.6 collective-permute-done.4.b3
  22.2 1.8 collective-permute-done.3.b2
  24.0 4.6 %collective-permute-start.5 = (bf16[1536,256]{1,0:T(8,128)(2,1)}, bf16[1536,256]{1,0:T(8,128)(2,1)}, u32[]{:S(2)}, u32[]{:S(2)}) collective-permute-start(bf16[1536,256]{1,0:T(8,128)(2,1)} %context_half.2), channel_id=1, source_target_pairs={{0,32},{32,0},{1,33},{33,1},{2,34},{34,2},{3,35},{35,3},{4,36},{36... | collective-permute-start | bytes 2359304 | tf_op jit(solution)/shard_map/ppermute | solution.py:335
  28.7 1.4 collective-permute-start.2
  30.3 1.3 collective-permute-start.6
  31.8 7.2 %collective-permute-done.6.beside_low = bf16[2,192,384]{2,1,0:T(8,128)(2,1)S(1)} collective-permute-done((bf16[2,192,384]{2,1,0:T(8,128)(2,1)S(1)}, bf16[2,192,384]{2,1,0:T(8,128)(2,1)S(1)}, u32[]{:S(2)}, u32[]{:S(2)}) %collective-permute-start.6) | collective-permute-done | bytes 294944 | tf_op jit(solution)/shard_map/ppermute | solution.py:324
  39.1 0.9 collective-permute-done.7.beside_high
  40.3 1.3 collective-permute-start.10
  41.8 3.9 %collective-permute-done.5.c2 = bf16[1536,256]{1,0:T(8,128)(2,1)} collective-permute-done((bf16[1536,256]{1,0:T(8,128)(2,1)}, bf16[1536,256]{1,0:T(8,128)(2,1)}, u32[]{:S(2)}, u32[]{:S(2)}) %collective-permute-start.5) | collective-permute-done | bytes 786464 | tf_op jit(solution)/shard_map/ppermute | solution.py:335
  45.7 1.0 collective-permute-start.13
  46.7 1.2 collective-permute-start.8
  48.0 5.3 %context_half.3.c0 = bf16[1536,256]{1,0:T(8,128)(2,1)} custom-call(s32[1]{0:T(128)} %bitcast.pick, bf16[256,3072]{1,0:T(8,128)(2,1)} %bitcast.32, bf16[256,3072]{1,0:T(8,128)(2,1)} %bitcast.36, bf16[256,3072]{1,0:T(8,128)(2,1)} %bitcast.40), custom_call_target="tpu_custom_call" | custom-call | flops 402653184 | bytes 3145728 | tf_op jit(solution)/shard_map/context_half/pallas_call | solution.py:73
  53.3 0.8 collective-permute-done.11.refs_6_
  54.1 3.0 %collective-permute-start.9 = (bf16[256,1536]{1,0:T(8,128)(2,1)S(1)}, bf16[256,1536]{1,0:T(8,128)(2,1)S(1)}, u32[]{:S(2)}, u32[]{:S(2)}) collective-permute-start(bf16[256,1536]{1,0:T(8,128)(2,1)S(1)} %copy-done.9), channel_id=1, source_target_pairs={{0,40},{8,32},{32,8},{40,0},{1,41},{9,33},{33,9},{41,1},{2,42},{10... | collective-permute-start | bytes 2359304 | tf_op jit(solution)/shard_map/ppermute | solution.py:340
  57.1 9.6 %collective-permute-done.14.refs_10_ = bf16[768,384]{1,0:T(8,128)(2,1)} collective-permute-done((bf16[768,384]{1,0:T(8,128)(2,1)S(1)}, bf16[768,384]{1,0:T(8,128)(2,1)}, u32[]{:S(2)}, u32[]{:S(2)}) %collective-permute-start.14) | collective-permute-done | bytes 589856 | tf_op jit(solution)/shard_map/ppermute | solution.py:347
  66.7 2.1 %collective-permute-start.19 = (bf16[1536,256]{1,0:T(8,128)(2,1)}, bf16[1536,256]{1,0:T(8,128)(2,1)S(1)}, u32[]{:S(2)}, u32[]{:S(2)}) collective-permute-start(bf16[1536,256]{1,0:T(8,128)(2,1)} %context_half.3.c0), channel_id=1, source_target_pairs={{0,8},{8,0},{1,9},{9,1},{2,10},{10,2},{3,11},{11,3},{4,12},{12,4},... | collective-permute-start | bytes 2359304 | tf_op jit(solution)/shard_map/ppermute | solution.py:351
  68.8 2.0 %collective-permute-start.12 = (bf16[768,384]{1,0:T(8,128)(2,1)}, bf16[768,384]{1,0:T(8,128)(2,1)}, u32[]{:S(2)}, u32[]{:S(2)}) collective-permute-start(bf16[768,384]{1,0:T(8,128)(2,1)} %collective-permute-done.10.refs_5_), channel_id=1, source_target_pairs={{0,1},{1,2},{2,3},{3,0},{4,5},{5,6},{6,7},{7,4},{8,9},{9,10},{10,1... | collective-permute-start | bytes 1769480 | tf_op jit(solution)/shard_map/ppermute | solution.py:348
  70.9 12.5 %collective-permute-done.9.refs_3_.d3 = bf16[256,1536]{1,0:T(8,128)(2,1)S(1)} collective-permute-done((bf16[256,1536]{1,0:T(8,128)(2,1)S(1)}, bf16[256,1536]{1,0:T(8,128)(2,1)S(1)}, u32[]{:S(2)}, u32[]{:S(2)}) %collective-permute-start.9) | collective-permute-done | bytes 786464 | tf_op jit(solution)/shard_map/ppermute | solution.py:340
  83.4 0.9 copy-done.11
  84.5 9.2 %weight_gradient.1 = bf16[16,4,24,1536]{3,2,1,0:T(8,128)(2,1)} custom-call(bf16[1536,256]{1,0:T(8,128)(2,1)} %context_half.3.c0, bf16[1536,256]{1,0:T(8,128)(2,1)} %copy-done.12, bf16[1536,256]{1,0:T(8,128)(2,1)} %collective-permute-done.5.c2, bf16[1536,256]{1,0:T(8,128)(2,1)} %collective-permute-done.20.c3, bf16[256,1536]{1,0:T(8,128)(2,1)} %copy-done.7, ...), custom_call_target="tpu_custom_call" | custom-call | flops 4831838208 | bytes 12582912 | tf_op jit(solution)/shard_map/weight_gradient/pallas_call | solution.py:279
  93.7 6.7 %all-to-all-start = ((bf16[16,4,24,1536]{3,2,1,0:T(8,128)(2,1)}), bf16[16,4,24,1536]{3,2,1,0:T(8,128)(2,1)}, u32[]{:S(2)}, u32[]{:S(2)}) async-start(bf16[16,4,24,1536]{3,2,1,0:T(8,128)(2,1)} %weight_gradient.1), calls=%async_computation | async-start | bytes 9437184 | tf_op jit(solution)/shard_map/all_to_all | solution.py:356
  100.4 0.6 pad_add_fusion.place
  101.0 12.3 %context_gradient.1 = (f32[256,1536]{1,0:T(8,128)}, bf16[256,1536]{1,0:T(8,128)(2,1)}, f32[256,1536]{1,0:T(8,128)}, bf16[256,1536]{1,0:T(8,128)(2,1)}) custom-call(s32[4]{0:T(128)} %pad_add_fusion.place, bf16[256,1536]{1,0:T(8,128)(2,1)} %copy-done.7, bf16[256,1536]{1,0:T(8,128)(2,1)} %copy-done.10, bf16[256,1536]{1,0:T(8,128)(2,1)} %collective-permute-done.8.refs_2_.d2, ...), custom_call_target="tpu_custom_call" | custom-call | flops 4831838208 | bytes 20971520 | tf_op jit(solution)/shard_map/context_gradient/pallas_call | solution.py:247
  113.9 2.0 %collective-permute-done.16 = bf16[256,1536]{1,0:T(8,128)(2,1)S(1)} collective-permute-done((bf16[256,1536]{1,0:T(8,128)(2,1)}, bf16[256,1536]{1,0:T(8,128)(2,1)S(1)}, u32[]{:S(2)}, u32[]{:S(2)}) %collective-permute-start.16) | collective-permute-done | bytes 786464 | tf_op jit(solution)/shard_map/ppermute | solution.py:360
  115.9 1.6 add_convert_fusion
  117.5 1.2 collective-permute-start.17
  118.7 0.9 copy-done.5
  119.6 10.4 %attention_gradients.2 = (bf16[256,3072]{1,0:T(8,128)(2,1)}, bf16[256,3072]{1,0:T(8,128)(2,1)}, bf16[256,3072]{1,0:T(8,128)(2,1)}) custom-call(s32[1]{0:T(128)} %bitcast.pick, bf16[256,3072]{1,0:T(8,128)(2,1)} %bitcast.33, bf16[256,3072]{1,0:T(8,128)(2,1)} %bitcast.37, bf16[256,3072]{1,0:T(8,128)(2,1)} %bitcast.41, f32[256,1536]{1,0:T(8,128)} %get-tuple-element.45.refs_0_, ...), custom_call_target="tpu_custom_call" | custom-call | flops 1006632960 | bytes 5505024 | tf_op jit(solution)/shard_map/attention_gradients/pallas_call | solution.py:117
  130.0 6.7 %collective-permute-done.17.refs_0_ = bf16[256,1536]{1,0:T(8,128)(2,1)S(1)} collective-permute-done((bf16[256,1536]{1,0:T(8,128)(2,1)S(1)}, bf16[256,1536]{1,0:T(8,128)(2,1)S(1)}, u32[]{:S(2)}, u32[]{:S(2)}) %collective-permute-start.17) | collective-permute-done | bytes 786464 | tf_op jit(solution)/shard_map/ppermute | solution.py:362
  136.7 0.9 copy-done.6
  137.6 10.3 %attention_gradients.3 = (bf16[256,3072]{1,0:T(8,128)(2,1)}, bf16[256,3072]{1,0:T(8,128)(2,1)}, bf16[256,3072]{1,0:T(8,128)(2,1)}) custom-call(s32[1]{0:T(128)S(6)} %sub.6.pick, bf16[256,3072]{1,0:T(8,128)(2,1)} %bitcast.34, bf16[256,3072]{1,0:T(8,128)(2,1)} %bitcast.38, ...), custom_call_target="tpu_custom_call", output_to_operand_aliasing={{0}: (5, {}), {1}: (6, {}), {2}: (7, {})} | custom-call | flops 1006632960 | bytes 5505024 | tf_op jit(solution)/shard_map/attention_gradients/pallas_call | solution.py:117
  147.9 26.0 %all-to-all-done = bf16[16,4,24,1536]{3,2,1,0:T(8,128)(2,1)} async-done(((bf16[16,4,24,1536]{3,2,1,0:T(8,128)(2,1)}), bf16[16,4,24,1536]{3,2,1,0:T(8,128)(2,1)}, u32[]{:S(2)}, u32[]{:S(2)}) %all-to-all-start) | async-done | bytes 4718624 | tf_op jit(solution)/shard_map/all_to_all | solution.py:356
  173.9 3.0 %reduce_sum.12 = bf16[4,24,1536]{2,1,0:T(8,128)(2,1)S(1)} reduce(bf16[16,4,24,1536]{3,2,1,0:T(8,128)(2,1)} %all-to-all-done, bf16[]{:T(256)} %constant.73.clone.1), dimensions={0}, to_apply=%region_0.1 | reduce | flops 2211840 | bytes 5013506 | tf_op jit(solution)/shard_map/reduce_sum | solution.py:293
  177.1 3.6 %collective-permute-start.23 = (bf16[24,1536]{1,0:T(8,128)(2,1)S(1)}, bf16[24,1536]{1,0:T(8,128)(2,1)S(1)}, u32[]{:S(2)}, u32[]{:S(2)}) collective-permute-start(bf16[24,1536]{1,0:T(8,128)(2,1)S(1)} %get-tuple-element.61), channel_id=1, source_target_pairs={{0,192},{64,0},{128,64},{192,128},{1,193},{65,1},{129,65},{193,129... | collective-permute-start | bytes 221192 | tf_op jit(solution)/shard_map/ppermute | solution.py:297
  180.6 1.7 collective-permute-start.22
  182.4 2.3 %collective-permute-done.21 = bf16[24,1536]{1,0:T(8,128)(2,1)S(1)} collective-permute-done((bf16[24,1536]{1,0:T(8,128)(2,1)S(1)}, bf16[24,1536]{1,0:T(8,128)(2,1)S(1)}, u32[]{:S(2)}, u32[]{:S(2)}) %collective-permute-start.21) | collective-permute-done | bytes 73760 | tf_op jit(solution)/shard_map/ppermute | solution.py:297
  185.2 4.5 %collective-permute-done.22 = bf16[24,1536]{1,0:T(8,128)(2,1)S(1)} collective-permute-done((bf16[24,1536]{1,0:T(8,128)(2,1)S(1)}, bf16[24,1536]{1,0:T(8,128)(2,1)S(1)}, u32[]{:S(2)}, u32[]{:S(2)}) %collective-permute-start.22) | collective-permute-done | bytes 73760 | tf_op jit(solution)/shard_map/ppermute | solution.py:297
  189.8 0.9 collective-permute-start.24
  190.7 0.9 collective-permute-done.24
  191.6 0.7 maximum_select_fusion
  (50 shorter events, 3.0 us)
Async XLA Ops:
  0.6 1.1 copy-start
  1.7 0.7 copy-start.1
  2.8 1.7 collective-permute-start
  4.5 10.6 %collective-permute-start.1 = (bf16[192,384]{1,0:T(8,128)(2,1)S(1)}, bf16[192,384]{1,0:T(8,128)(2,1)S(1)}, u32[]{:S(2)}, u32[]{:S(2)}) collective-permute-start(bf16[192,384]{1,0:T(8,128)(2,1)S(1)} %maximum_select_fusion.1.own_ref), channel_id=1, source_target_pairs={{0,64},{64,128},{128,192},{192,0},{1,65},{65,129},{129,193},{193,1... | collective-permute-start | bytes 442376 | tf_op jit(solution)/shard_map/ppermute | solution.py:319
  7.6 14.6 %collective-permute-start.4 = (bf16[192,384]{1,0:T(8,128)(2,1)S(1)}, bf16[192,384]{1,0:T(8,128)(2,1)S(1)}, u32[]{:S(2)}, u32[]{:S(2)}) collective-permute-start(bf16[192,384]{1,0:T(8,128)(2,1)S(1)} %maximum_select_fusion.1.own_ref), channel_id=1, source_target_pairs={{0,192},{64,0},{128,64},{192,128},{1,193},{65,1},{129,65},{193,129... | collective-permute-start | bytes 442376 | tf_op jit(solution)/shard_map/ppermute | solution.py:319
  10.7 13.2 %collective-permute-start.3 = (bf16[192,384]{1,0:T(8,128)(2,1)S(1)}, bf16[192,384]{1,0:T(8,128)(2,1)S(1)}, u32[]{:S(2)}, u32[]{:S(2)}) collective-permute-start(bf16[192,384]{1,0:T(8,128)(2,1)S(1)} %maximum_select_fusion.1.own_ref), channel_id=1, source_target_pairs={{0,128},{64,192},{128,0},{192,64},{1,129},{65,193},{129,1},{193,65... | collective-permute-start | bytes 442376 | tf_op jit(solution)/shard_map/ppermute | solution.py:319
  15.2 13.4 %copy-start.4 = (bf16[1,256,3072]{2,1,0:T(8,128)(2,1)S(1)}, bf16[1,256,3072]{2,1,0:T(8,128)(2,1)}, u32[]{:S(2)}) copy-start(bf16[1,256,3072]{2,1,0:T(8,128)(2,1)} %param.9) | copy-start | bytes 4718596
  24.0 21.7 %collective-permute-start.5 = (bf16[1536,256]{1,0:T(8,128)(2,1)}, bf16[1536,256]{1,0:T(8,128)(2,1)}, u32[]{:S(2)}, u32[]{:S(2)}) collective-permute-start(bf16[1536,256]{1,0:T(8,128)(2,1)} %context_half.2), channel_id=1, source_target_pairs={{0,32},{32,0},{1,33},{33,1},{2,34},{34,2},{3,35},{35,3},{4,36},{36... | collective-permute-start | bytes 2359304 | tf_op jit(solution)/shard_map/ppermute | solution.py:335
  28.7 18.0 %copy-start.8 = (bf16[256,1536]{1,0:T(8,128)(2,1)}, bf16[256,1536]{1,0:T(8,128)(2,1)S(1)}, u32[]{:S(2)}) copy-start(bf16[256,1536]{1,0:T(8,128)(2,1)S(1)} %get-tuple-element.41) | copy-start | bytes 2359300
  28.7 24.6 %copy-start.7 = (bf16[256,1536]{1,0:T(8,128)(2,1)}, bf16[256,1536]{1,0:T(8,128)(2,1)S(1)}, u32[]{:S(2)}) copy-start(bf16[256,1536]{1,0:T(8,128)(2,1)S(1)} %get-tuple-element.40.refs_0_.d0) | copy-start | bytes 2359300
  28.7 18.0 %collective-permute-start.2 = (bf16[256,1536]{1,0:T(8,128)(2,1)S(1)}, bf16[256,1536]{1,0:T(8,128)(2,1)S(1)}, u32[]{:S(2)}, u32[]{:S(2)}) collective-permute-start(bf16[256,1536]{1,0:T(8,128)(2,1)S(1)} %get-tuple-element.41), channel_id=1, source_target_pairs={{0,8},{8,0},{1,9},{9,1},{2,10},{10,2},{3,11},{11,3},{4,12},{12,4},... | collective-permute-start | bytes 2359304 | tf_op jit(solution)/shard_map/ppermute | solution.py:332
  30.3 8.8 %collective-permute-start.6 = (bf16[2,192,384]{2,1,0:T(8,128)(2,1)S(1)}, bf16[2,192,384]{2,1,0:T(8,128)(2,1)S(1)}, u32[]{:S(2)}, u32[]{:S(2)}) collective-permute-start(bf16[2,192,384]{2,1,0:T(8,128)(2,1)S(1)} %get-tuple-element.37.low), channel_id=1, source_target_pairs={{0,16},{16,4},{4,20},{20,0},{1,17},{17,5},{5,21},{21,1},{2,18},{18... | collective-permute-start | bytes 884744 | tf_op jit(solution)/shard_map/ppermute | solution.py:324
  31.6 8.4 %collective-permute-start.7 = (bf16[2,192,384]{2,1,0:T(8,128)(2,1)S(1)}, bf16[2,192,384]{2,1,0:T(8,128)(2,1)S(1)}, u32[]{:S(2)}, u32[]{:S(2)}) collective-permute-start(bf16[2,192,384]{2,1,0:T(8,128)(2,1)S(1)} %get-tuple-element.38.high), channel_id=1, source_target_pairs={{0,20},{16,0},{4,16},{20,4},{1,21},{17,1},{5,17},{21,5},{2,22},{18... | collective-permute-start | bytes 884744 | tf_op jit(solution)/shard_map/ppermute | solution.py:325
  40.1 13.2 %copy-start.2 = (bf16[2,2,192,384]{3,2,1,0:T(8,128)(2,1)}, bf16[2,2,192,384]{3,2,1,0:T(8,128)(2,1)S(1)}, u32[]{:S(2)}) copy-start(bf16[2,2,192,384]{3,2,1,0:T(8,128)(2,1)S(1)} %get-tuple-element.39) | copy-start | bytes 1769476
  40.1 13.2 %copy-start.3 = (bf16[2,2,192,384]{3,2,1,0:T(8,128)(2,1)}, bf16[2,2,192,384]{3,2,1,0:T(8,128)(2,1)S(1)}, u32[]{:S(2)}) copy-start(bf16[2,2,192,384]{3,2,1,0:T(8,128)(2,1)S(1)} %get-tuple-element.42) | copy-start | bytes 1769476
  40.1 14.0 %collective-permute-start.11 = (bf16[768,384]{1,0:T(8,128)(2,1)S(1)}, bf16[768,384]{1,0:T(8,128)(2,1)S(1)}, u32[]{:S(2)}, u32[]{:S(2)}) collective-permute-start(bf16[768,384]{1,0:T(8,128)(2,1)S(1)} %bitcast.25), channel_id=1, source_target_pairs={{0,3},{1,0},{2,1},{3,2},{4,7},{5,4},{6,5},{7,6},{8,11},{9,8},{10,9... | collective-permute-start | bytes 1769480 | tf_op jit(solution)/shard_map/ppermute | solution.py:346
  40.3 16.7 %collective-permute-start.10 = (bf16[768,384]{1,0:T(8,128)(2,1)S(1)}, bf16[768,384]{1,0:T(8,128)(2,1)}, u32[]{:S(2)}, u32[]{:S(2)}) collective-permute-start(bf16[768,384]{1,0:T(8,128)(2,1)S(1)} %bitcast.26), channel_id=1, source_target_pairs={{0,1},{1,2},{2,3},{3,0},{4,5},{5,6},{6,7},{7,4},{8,9},{9,10},{10,1... | collective-permute-start | bytes 1769480 | tf_op jit(solution)/shard_map/ppermute | solution.py:346
  41.6 25.1 %collective-permute-start.14 = (bf16[768,384]{1,0:T(8,128)(2,1)S(1)}, bf16[768,384]{1,0:T(8,128)(2,1)}, u32[]{:S(2)}, u32[]{:S(2)}) collective-permute-start(bf16[768,384]{1,0:T(8,128)(2,1)S(1)} %bitcast.28), channel_id=1, source_target_pairs={{0,3},{1,0},{2,1},{3,2},{4,7},{5,4},{6,5},{7,6},{8,11},{9,8},{10,9... | collective-permute-start | bytes 1769480 | tf_op jit(solution)/shard_map/ppermute | solution.py:347
  45.7 21.0 %collective-permute-start.13 = (bf16[768,384]{1,0:T(8,128)(2,1)S(1)}, bf16[768,384]{1,0:T(8,128)(2,1)}, u32[]{:S(2)}, u32[]{:S(2)}) collective-permute-start(bf16[768,384]{1,0:T(8,128)(2,1)S(1)} %bitcast.29), channel_id=1, source_target_pairs={{0,1},{1,2},{2,3},{3,0},{4,5},{5,6},{6,7},{7,4},{8,9},{9,10},{10,1... | collective-permute-start | bytes 1769480 | tf_op jit(solution)/shard_map/ppermute | solution.py:347
  46.7 6.6 %copy-start.10 = (bf16[256,1536]{1,0:T(8,128)(2,1)}, bf16[256,1536]{1,0:T(8,128)(2,1)S(1)}, u32[]{:S(2)}) copy-start(bf16[256,1536]{1,0:T(8,128)(2,1)S(1)} %collective-permute-done.2.refs_1_.d1) | copy-start | bytes 2359300
  46.7 7.3 %copy-start.9 = (bf16[256,1536]{1,0:T(8,128)(2,1)S(1)}, bf16[256,1536]{1,0:T(8,128)(2,1)}, u32[]{:S(2)}) copy-start(bf16[256,1536]{1,0:T(8,128)(2,1)} %copy-done.8) | copy-start | bytes 2359300
  46.7 24.1 %collective-permute-start.8 = (bf16[256,1536]{1,0:T(8,128)(2,1)S(1)}, bf16[256,1536]{1,0:T(8,128)(2,1)}, u32[]{:S(2)}, u32[]{:S(2)}) collective-permute-start(bf16[256,1536]{1,0:T(8,128)(2,1)S(1)} %get-tuple-element.40.refs_0_.d0), channel_id=1, source_target_pairs={{0,32},{32,0},{1,33},{33,1},{2,34},{34,2},{3,35},{35,3},{4,36},{36... | collective-permute-start | bytes 2359304 | tf_op jit(solution)/shard_map/ppermute | solution.py:339
  54.1 39.6 %copy-start.13 = (bf16[768,384]{1,0:T(8,128)(2,1)}, bf16[768,384]{1,0:T(8,128)(2,1)S(1)}, u32[]{:S(2)}) copy-start(bf16[768,384]{1,0:T(8,128)(2,1)S(1)} %collective-permute-done.11.refs_6_) | copy-start | bytes 1769476
  54.1 29.3 %collective-permute-start.9 = (bf16[256,1536]{1,0:T(8,128)(2,1)S(1)}, bf16[256,1536]{1,0:T(8,128)(2,1)S(1)}, u32[]{:S(2)}, u32[]{:S(2)}) collective-permute-start(bf16[256,1536]{1,0:T(8,128)(2,1)S(1)} %copy-done.9), channel_id=1, source_target_pairs={{0,40},{8,32},{32,8},{40,0},{1,41},{9,33},{33,9},{41,1},{2,42},{10... | collective-permute-start | bytes 2359304 | tf_op jit(solution)/shard_map/ppermute | solution.py:340
  66.7 16.6 %collective-permute-start.19 = (bf16[1536,256]{1,0:T(8,128)(2,1)}, bf16[1536,256]{1,0:T(8,128)(2,1)S(1)}, u32[]{:S(2)}, u32[]{:S(2)}) collective-permute-start(bf16[1536,256]{1,0:T(8,128)(2,1)} %context_half.3.c0), channel_id=1, source_target_pairs={{0,8},{8,0},{1,9},{9,1},{2,10},{10,2},{3,11},{11,3},{4,12},{12,4},... | collective-permute-start | bytes 2359304 | tf_op jit(solution)/shard_map/ppermute | solution.py:351
  68.8 14.5 %collective-permute-start.20 = (bf16[1536,256]{1,0:T(8,128)(2,1)}, bf16[1536,256]{1,0:T(8,128)(2,1)}, u32[]{:S(2)}, u32[]{:S(2)}) collective-permute-start(bf16[1536,256]{1,0:T(8,128)(2,1)} %collective-permute-done.5.c2), channel_id=1, source_target_pairs={{0,8},{8,0},{1,9},{9,1},{2,10},{10,2},{3,11},{11,3},{4,12},{12,4},... | collective-permute-start | bytes 2359304 | tf_op jit(solution)/shard_map/ppermute | solution.py:352
  68.8 24.8 %collective-permute-start.12 = (bf16[768,384]{1,0:T(8,128)(2,1)}, bf16[768,384]{1,0:T(8,128)(2,1)}, u32[]{:S(2)}, u32[]{:S(2)}) collective-permute-start(bf16[768,384]{1,0:T(8,128)(2,1)} %collective-permute-done.10.refs_5_), channel_id=1, source_target_pairs={{0,1},{1,2},{2,3},{3,0},{4,5},{5,6},{6,7},{7,4},{8,9},{9,10},{10,1... | collective-permute-start | bytes 1769480 | tf_op jit(solution)/shard_map/ppermute | solution.py:348
  70.9 22.8 %collective-permute-start.15 = (bf16[768,384]{1,0:T(8,128)(2,1)}, bf16[768,384]{1,0:T(8,128)(2,1)}, u32[]{:S(2)}, u32[]{:S(2)}) collective-permute-start(bf16[768,384]{1,0:T(8,128)(2,1)} %collective-permute-done.14.refs_10_), channel_id=1, source_target_pairs={{0,3},{1,0},{2,1},{3,2},{4,7},{5,4},{6,5},{7,6},{8,11},{9,8},{10,9... | collective-permute-start | bytes 1769480 | tf_op jit(solution)/shard_map/ppermute | solution.py:349
  83.4 0.9 copy-start.11
  83.4 1.1 copy-start.12
  93.7 80.2 %all-to-all-start = ((bf16[16,4,24,1536]{3,2,1,0:T(8,128)(2,1)}), bf16[16,4,24,1536]{3,2,1,0:T(8,128)(2,1)}, u32[]{:S(2)}, u32[]{:S(2)}) async-start(bf16[16,4,24,1536]{3,2,1,0:T(8,128)(2,1)} %weight_gradient.1), calls=%async_computation | async-start | bytes 9437184 | tf_op jit(solution)/shard_map/all_to_all | solution.py:356
  113.3 2.6 %collective-permute-start.16 = (bf16[256,1536]{1,0:T(8,128)(2,1)}, bf16[256,1536]{1,0:T(8,128)(2,1)S(1)}, u32[]{:S(2)}, u32[]{:S(2)}) collective-permute-start(bf16[256,1536]{1,0:T(8,128)(2,1)} %get-tuple-element.44), channel_id=1, source_target_pairs={{0,8},{8,0},{1,9},{9,1},{2,10},{10,2},{3,11},{11,3},{4,12},{12,4},... | collective-permute-start | bytes 2359304 | tf_op jit(solution)/shard_map/ppermute | solution.py:360
  113.4 5.3 %collective-permute-start.18 = (bf16[256,1536]{1,0:T(8,128)(2,1)}, bf16[256,1536]{1,0:T(8,128)(2,1)S(1)}, u32[]{:S(2)}, u32[]{:S(2)}) collective-permute-start(bf16[256,1536]{1,0:T(8,128)(2,1)} %get-tuple-element.46), channel_id=1, source_target_pairs={{0,8},{8,0},{1,9},{9,1},{2,10},{10,2},{3,11},{11,3},{4,12},{12,4},... | collective-permute-start | bytes 2359304 | tf_op jit(solution)/shard_map/ppermute | solution.py:361
  117.5 19.2 %collective-permute-start.17 = (bf16[256,1536]{1,0:T(8,128)(2,1)S(1)}, bf16[256,1536]{1,0:T(8,128)(2,1)S(1)}, u32[]{:S(2)}, u32[]{:S(2)}) collective-permute-start(bf16[256,1536]{1,0:T(8,128)(2,1)S(1)} %add_convert_fusion), channel_id=1, source_target_pairs={{0,32},{32,0},{1,33},{33,1},{2,34},{34,2},{3,35},{35,3},{4,36},{36... | collective-permute-start | bytes 2359304 | tf_op jit(solution)/shard_map/ppermute | solution.py:362
  118.7 0.9 copy-start.5
  136.7 0.9 copy-start.6
  177.0 7.7 %collective-permute-start.21 = (bf16[24,1536]{1,0:T(8,128)(2,1)S(1)}, bf16[24,1536]{1,0:T(8,128)(2,1)S(1)}, u32[]{:S(2)}, u32[]{:S(2)}) collective-permute-start(bf16[24,1536]{1,0:T(8,128)(2,1)S(1)} %get-tuple-element.60), channel_id=1, source_target_pairs={{0,64},{64,128},{128,192},{192,0},{1,65},{65,129},{129,193},{193,1... | collective-permute-start | bytes 221192 | tf_op jit(solution)/shard_map/ppermute | solution.py:297
  177.1 8.1 %collective-permute-start.23 = (bf16[24,1536]{1,0:T(8,128)(2,1)S(1)}, bf16[24,1536]{1,0:T(8,128)(2,1)S(1)}, u32[]{:S(2)}, u32[]{:S(2)}) collective-permute-start(bf16[24,1536]{1,0:T(8,128)(2,1)S(1)} %get-tuple-element.61), channel_id=1, source_target_pairs={{0,192},{64,0},{128,64},{192,128},{1,193},{65,1},{129,65},{193,129... | collective-permute-start | bytes 221192 | tf_op jit(solution)/shard_map/ppermute | solution.py:297
  180.6 9.1 %collective-permute-start.22 = (bf16[24,1536]{1,0:T(8,128)(2,1)S(1)}, bf16[24,1536]{1,0:T(8,128)(2,1)S(1)}, u32[]{:S(2)}, u32[]{:S(2)}) collective-permute-start(bf16[24,1536]{1,0:T(8,128)(2,1)S(1)} %get-tuple-element.62), channel_id=1, source_target_pairs={{0,128},{64,192},{128,0},{192,64},{1,129},{65,193},{129,1},{193,65... | collective-permute-start | bytes 221192 | tf_op jit(solution)/shard_map/ppermute | solution.py:297
  189.8 1.8 collective-permute-start.24

commit v8 on v7

--- a/solution.py
+++ b/solution.py
@@ -264,24 +264,24 @@
 
 def weight_gradient_body(c0, c1, c2, c3, d0, d1, d2, d3, out_ref):
     context_t = jnp.concatenate([c[...] for c in (c0, c1, c2, c3)], axis=1)
-    part = d0.shape[1] // 2
-    for half in range(2):
-        cols = slice(half * part, (half + 1) * part)
-        grads = jnp.concatenate([d[:, cols] for d in (d0, d1, d2, d3)], axis=0)
-        total = dot(context_t, grads, (((1,), (0,)), ((), ())))
+    total = dot(context_t, stacked((d0, d1, d2, d3)), (((1,), (0,)), ((), ())))
+    block = context_t.shape[0] // 4
+    for place in range(4):
         for chip in range(16):
-            out_ref[chip, 0, :, cols] = total[chip * 24 : (chip + 1) * 24].astype(BF16)
+            first = place * block + chip * 24
+            out_ref[chip, place] = total[first : first + 24].astype(BF16)
 
 
 def weight_gradient(contexts, grads):
     rows, seq = contexts[0].shape
     half = grads[0].shape[1]
+    width = half // 4
     return pl.pallas_call(
         weight_gradient_body,
         grid=(4,),
-        in_specs=[pl.BlockSpec((rows // 4, seq), lambda i: (i, 0))] * 4
-        + [pl.BlockSpec((seq, half), lambda i: (0, 0))] * 4,
-        out_specs=pl.BlockSpec((16, 1, 24, half), lambda i: (0, i, 0, 0)),
+        in_specs=[pl.BlockSpec((rows, seq), lambda i: (0, 0))] * 4
+        + [pl.BlockSpec((seq, width), lambda i: (0, i))] * 4,
+        out_specs=pl.BlockSpec((16, 4, 24, width), lambda i: (0, 0, 0, i)),
         out_shape=jax.ShapeDtypeStruct((16, 4, 24, half), BF16),
         compiler_params=params(),
         cost_estimate=cost(8 * seq * half * rows, 12 * 2**20),

time: 193 us -> 195 us (1.010)
  no operation moved by 1% of the time
where the time goes in v8:
time: 195 us; the launch traced here: 194 us
  waiting for transfers between devices  82.5 us (42%)
  Pallas kernels  55.1 us (28%)
  starting transfers between devices  44.9 us (23%)
  other arithmetic  6.03 us (3%)
  local copies, waits for them, and re-layouts  4.86 us (2%)
    all_to_all x1, waiting for transfers between devices, per_device(): terms = lax.all_to_all(terms, ('xl', 'xh', 'y'), 0, 0, tiled=True)  26.2 us
    pallas_call x2, Pallas kernels, backward(): pl.pallas_call(functools.partial(backward_body, before is None), grid_spe...  20.6 us
    ppermute x1, waiting for transfers between devices, per_device(): d3 = lax.ppermute(diagonal, ('zl', 'c'), [(i, 3 - i) for i in range(4)])  12.5 us
    pallas_call x1, Pallas kernels, context_gradient(): pl.pallas_call(context_gradient_body, grid_spec=pltpu.PrefetchScalarGridS...  12.3 us
    pallas_call x2, Pallas kernels, forward(): pl.pallas_call(forward_body, grid_spec=pltpu.PrefetchScalarGridSpec(num_s...  10.7 us
    pallas_call x1, Pallas kernels, weight_gradient(): pl.pallas_call(weight_gradient_body, grid=(4,), in_specs=[pl.BlockSpec((r...  10.7 us
    ppermute x3, starting transfers between devices, per_device(): behind = [lax.ppermute(pair, 'zh', ring(4, step)) for step in (1, 2, 3)]  10.6 us
    ppermute x2, waiting for transfers between devices, per_device(): highs.append(lax.ppermute(highs[0], 'y', ring(4, step)))  9.63 us
  transfers between devices with their start and end apart: 26, of which 17 were waited for; matrix products, arithmetic and copies ran while one was open for 1% of the time, Pallas kernels for 28%

profile of v8, /device:TPU:19, one launch (start us, length us, event | category | flops | bytes accessed | tf_op | source)
XLA Modules:
  0.0 194.1 jit_solution(8389513519357488546)
XLA Ops:
  0.6 1.1 copy-done
  1.7 0.7 copy-done.1
  2.8 0.8 collective-permute-start
  3.6 0.9 collective-permute-done
  4.5 3.1 %collective-permute-start.1 = (bf16[192,384]{1,0:T(8,128)(2,1)S(1)}, bf16[192,384]{1,0:T(8,128)(2,1)S(1)}, u32[]{:S(2)}, u32[]{:S(2)}) collective-permute-start(bf16[192,384]{1,0:T(8,128)(2,1)S(1)} %maximum_select_fusion.1.own_ref), channel_id=1, source_target_pairs={{0,64},{64,128},{128,192},{192,0},{1,65},{65,129},{129,193},{193,1... | collective-permute-start | bytes 442376 | tf_op jit(solution)/shard_map/ppermute | solution.py:319
  7.6 3.1 %collective-permute-start.4 = (bf16[192,384]{1,0:T(8,128)(2,1)S(1)}, bf16[192,384]{1,0:T(8,128)(2,1)S(1)}, u32[]{:S(2)}, u32[]{:S(2)}) collective-permute-start(bf16[192,384]{1,0:T(8,128)(2,1)S(1)} %maximum_select_fusion.1.own_ref), channel_id=1, source_target_pairs={{0,192},{64,0},{128,64},{192,128},{1,193},{65,1},{129,65},{193,129... | collective-permute-start | bytes 442376 | tf_op jit(solution)/shard_map/ppermute | solution.py:319
  10.7 4.4 %collective-permute-start.3 = (bf16[192,384]{1,0:T(8,128)(2,1)S(1)}, bf16[192,384]{1,0:T(8,128)(2,1)S(1)}, u32[]{:S(2)}, u32[]{:S(2)}) collective-permute-start(bf16[192,384]{1,0:T(8,128)(2,1)S(1)} %maximum_select_fusion.1.own_ref), channel_id=1, source_target_pairs={{0,128},{64,192},{128,0},{192,64},{1,129},{65,193},{129,1},{193,65... | collective-permute-start | bytes 442376 | tf_op jit(solution)/shard_map/ppermute | solution.py:319
  15.2 5.4 %context_half.2 = bf16[1536,256]{1,0:T(8,128)(2,1)} custom-call(s32[1]{0:T(128)S(6)} %sub.6.pick, bf16[256,3072]{1,0:T(8,128)(2,1)} %bitcast.31, bf16[256,3072]{1,0:T(8,128)(2,1)} %bitcast.35, bf16[256,3072]{1,0:T(8,128)(2,1)} %bitcast.39), custom_call_target="tpu_custom_call" | custom-call | flops 402653184 | bytes 3145728 | tf_op jit(solution)/shard_map/context_half/pallas_call | solution.py:73
  20.6 1.6 collective-permute-done.4.b3
  22.2 1.8 collective-permute-done.3.b2
  24.0 4.6 %collective-permute-start.5 = (bf16[1536,256]{1,0:T(8,128)(2,1)}, bf16[1536,256]{1,0:T(8,128)(2,1)}, u32[]{:S(2)}, u32[]{:S(2)}) collective-permute-start(bf16[1536,256]{1,0:T(8,128)(2,1)} %context_half.2), channel_id=1, source_target_pairs={{0,32},{32,0},{1,33},{33,1},{2,34},{34,2},{3,35},{35,3},{4,36},{36... | collective-permute-start | bytes 2359304 | tf_op jit(solution)/shard_map/ppermute | solution.py:335
  28.7 1.4 collective-permute-start.2
  30.3 1.3 collective-permute-start.6
  31.8 7.2 %collective-permute-done.6.beside_low = bf16[2,192,384]{2,1,0:T(8,128)(2,1)S(1)} collective-permute-done((bf16[2,192,384]{2,1,0:T(8,128)(2,1)S(1)}, bf16[2,192,384]{2,1,0:T(8,128)(2,1)S(1)}, u32[]{:S(2)}, u32[]{:S(2)}) %collective-permute-start.6) | collective-permute-done | bytes 294944 | tf_op jit(solution)/shard_map/ppermute | solution.py:324
  39.1 0.9 collective-permute-done.7.beside_high
  40.3 1.3 collective-permute-start.10
  41.8 3.9 %collective-permute-done.5.c2 = bf16[1536,256]{1,0:T(8,128)(2,1)} collective-permute-done((bf16[1536,256]{1,0:T(8,128)(2,1)}, bf16[1536,256]{1,0:T(8,128)(2,1)}, u32[]{:S(2)}, u32[]{:S(2)}) %collective-permute-start.5) | collective-permute-done | bytes 786464 | tf_op jit(solution)/shard_map/ppermute | solution.py:335
  45.7 1.0 collective-permute-start.13
  46.7 1.2 collective-permute-start.8
  48.0 5.3 %context_half.3.c0 = bf16[1536,256]{1,0:T(8,128)(2,1)} custom-call(s32[1]{0:T(128)} %bitcast.pick, bf16[256,3072]{1,0:T(8,128)(2,1)} %bitcast.32, bf16[256,3072]{1,0:T(8,128)(2,1)} %bitcast.36, bf16[256,3072]{1,0:T(8,128)(2,1)} %bitcast.40), custom_call_target="tpu_custom_call" | custom-call | flops 402653184 | bytes 3145728 | tf_op jit(solution)/shard_map/context_half/pallas_call | solution.py:73
  53.3 0.8 collective-permute-done.11.refs_6_
  54.1 3.0 %collective-permute-start.9 = (bf16[256,1536]{1,0:T(8,128)(2,1)S(1)}, bf16[256,1536]{1,0:T(8,128)(2,1)S(1)}, u32[]{:S(2)}, u32[]{:S(2)}) collective-permute-start(bf16[256,1536]{1,0:T(8,128)(2,1)S(1)} %copy-done.9), channel_id=1, source_target_pairs={{0,40},{8,32},{32,8},{40,0},{1,41},{9,33},{33,9},{41,1},{2,42},{10... | collective-permute-start | bytes 2359304 | tf_op jit(solution)/shard_map/ppermute | solution.py:340
  57.1 9.6 %collective-permute-done.14.refs_10_ = bf16[768,384]{1,0:T(8,128)(2,1)} collective-permute-done((bf16[768,384]{1,0:T(8,128)(2,1)S(1)}, bf16[768,384]{1,0:T(8,128)(2,1)}, u32[]{:S(2)}, u32[]{:S(2)}) %collective-permute-start.14) | collective-permute-done | bytes 589856 | tf_op jit(solution)/shard_map/ppermute | solution.py:347
  66.7 2.1 %collective-permute-start.19 = (bf16[1536,256]{1,0:T(8,128)(2,1)}, bf16[1536,256]{1,0:T(8,128)(2,1)S(1)}, u32[]{:S(2)}, u32[]{:S(2)}) collective-permute-start(bf16[1536,256]{1,0:T(8,128)(2,1)} %context_half.3.c0), channel_id=1, source_target_pairs={{0,8},{8,0},{1,9},{9,1},{2,10},{10,2},{3,11},{11,3},{4,12},{12,4},... | collective-permute-start | bytes 2359304 | tf_op jit(solution)/shard_map/ppermute | solution.py:351
  68.8 2.0 %collective-permute-start.12 = (bf16[768,384]{1,0:T(8,128)(2,1)}, bf16[768,384]{1,0:T(8,128)(2,1)}, u32[]{:S(2)}, u32[]{:S(2)}) collective-permute-start(bf16[768,384]{1,0:T(8,128)(2,1)} %collective-permute-done.10.refs_5_), channel_id=1, source_target_pairs={{0,1},{1,2},{2,3},{3,0},{4,5},{5,6},{6,7},{7,4},{8,9},{9,10},{10,1... | collective-permute-start | bytes 1769480 | tf_op jit(solution)/shard_map/ppermute | solution.py:348
  70.9 12.5 %collective-permute-done.9.refs_3_.d3 = bf16[256,1536]{1,0:T(8,128)(2,1)S(1)} collective-permute-done((bf16[256,1536]{1,0:T(8,128)(2,1)S(1)}, bf16[256,1536]{1,0:T(8,128)(2,1)S(1)}, u32[]{:S(2)}, u32[]{:S(2)}) %collective-permute-start.9) | collective-permute-done | bytes 786464 | tf_op jit(solution)/shard_map/ppermute | solution.py:340
  83.4 0.9 copy-done.11
  84.5 10.7 %weight_gradient.1 = bf16[16,4,24,1536]{3,2,1,0:T(8,128)(2,1)} custom-call(bf16[1536,256]{1,0:T(8,128)(2,1)} %context_half.3.c0, bf16[1536,256]{1,0:T(8,128)(2,1)} %copy-done.12, bf16[1536,256]{1,0:T(8,128)(2,1)} %collective-permute-done.5.c2, bf16[1536,256]{1,0:T(8,128)(2,1)} %collective-permute-done.20.c3, bf16[256,1536]{1,0:T(8,128)(2,1)} %copy-done.7, ...), custom_call_target="tpu_custom_call" | custom-call | flops 4831838208 | bytes 12582912 | tf_op jit(solution)/shard_map/weight_gradient/pallas_call | solution.py:279
  95.2 6.7 %all-to-all-start = ((bf16[16,4,24,1536]{3,2,1,0:T(8,128)(2,1)}), bf16[16,4,24,1536]{3,2,1,0:T(8,128)(2,1)}, u32[]{:S(2)}, u32[]{:S(2)}) async-start(bf16[16,4,24,1536]{3,2,1,0:T(8,128)(2,1)} %weight_gradient.1), calls=%async_computation | async-start | bytes 9437184 | tf_op jit(solution)/shard_map/all_to_all | solution.py:356
  101.9 0.6 pad_add_fusion.place
  102.5 12.3 %context_gradient.1 = (f32[256,1536]{1,0:T(8,128)}, bf16[256,1536]{1,0:T(8,128)(2,1)}, f32[256,1536]{1,0:T(8,128)}, bf16[256,1536]{1,0:T(8,128)(2,1)}) custom-call(s32[4]{0:T(128)} %pad_add_fusion.place, bf16[256,1536]{1,0:T(8,128)(2,1)} %copy-done.7, bf16[256,1536]{1,0:T(8,128)(2,1)} %copy-done.10, bf16[256,1536]{1,0:T(8,128)(2,1)} %collective-permute-done.8.refs_2_.d2, ...), custom_call_target="tpu_custom_call" | custom-call | flops 4831838208 | bytes 20971520 | tf_op jit(solution)/shard_map/context_gradient/pallas_call | solution.py:247
  115.4 2.0 %collective-permute-done.16 = bf16[256,1536]{1,0:T(8,128)(2,1)S(1)} collective-permute-done((bf16[256,1536]{1,0:T(8,128)(2,1)}, bf16[256,1536]{1,0:T(8,128)(2,1)S(1)}, u32[]{:S(2)}, u32[]{:S(2)}) %collective-permute-start.16) | collective-permute-done | bytes 786464 | tf_op jit(solution)/shard_map/ppermute | solution.py:360
  117.4 1.6 add_convert_fusion
  119.0 1.2 collective-permute-start.17
  120.3 0.9 copy-done.5
  121.2 10.4 %attention_gradients.2 = (bf16[256,3072]{1,0:T(8,128)(2,1)}, bf16[256,3072]{1,0:T(8,128)(2,1)}, bf16[256,3072]{1,0:T(8,128)(2,1)}) custom-call(s32[1]{0:T(128)} %bitcast.pick, bf16[256,3072]{1,0:T(8,128)(2,1)} %bitcast.33, bf16[256,3072]{1,0:T(8,128)(2,1)} %bitcast.37, bf16[256,3072]{1,0:T(8,128)(2,1)} %bitcast.41, f32[256,1536]{1,0:T(8,128)} %get-tuple-element.45.refs_0_, ...), custom_call_target="tpu_custom_call" | custom-call | flops 1006632960 | bytes 5505024 | tf_op jit(solution)/shard_map/attention_gradients/pallas_call | solution.py:117
  131.6 6.7 %collective-permute-done.17.refs_0_ = bf16[256,1536]{1,0:T(8,128)(2,1)S(1)} collective-permute-done((bf16[256,1536]{1,0:T(8,128)(2,1)S(1)}, bf16[256,1536]{1,0:T(8,128)(2,1)S(1)}, u32[]{:S(2)}, u32[]{:S(2)}) %collective-permute-start.17) | collective-permute-done | bytes 786464 | tf_op jit(solution)/shard_map/ppermute | solution.py:362
  138.2 0.9 copy-done.6
  139.2 10.3 %attention_gradients.3 = (bf16[256,3072]{1,0:T(8,128)(2,1)}, bf16[256,3072]{1,0:T(8,128)(2,1)}, bf16[256,3072]{1,0:T(8,128)(2,1)}) custom-call(s32[1]{0:T(128)S(6)} %sub.6.pick, bf16[256,3072]{1,0:T(8,128)(2,1)} %bitcast.34, bf16[256,3072]{1,0:T(8,128)(2,1)} %bitcast.38, ...), custom_call_target="tpu_custom_call", output_to_operand_aliasing={{0}: (5, {}), {1}: (6, {}), {2}: (7, {})} | custom-call | flops 1006632960 | bytes 5505024 | tf_op jit(solution)/shard_map/attention_gradients/pallas_call | solution.py:117
  149.4 26.2 %all-to-all-done = bf16[16,4,24,1536]{3,2,1,0:T(8,128)(2,1)} async-done(((bf16[16,4,24,1536]{3,2,1,0:T(8,128)(2,1)}), bf16[16,4,24,1536]{3,2,1,0:T(8,128)(2,1)}, u32[]{:S(2)}, u32[]{:S(2)}) %all-to-all-start) | async-done | bytes 4718624 | tf_op jit(solution)/shard_map/all_to_all | solution.py:356
  175.6 3.0 %reduce_sum.12 = bf16[4,24,1536]{2,1,0:T(8,128)(2,1)S(1)} reduce(bf16[16,4,24,1536]{3,2,1,0:T(8,128)(2,1)} %all-to-all-done, bf16[]{:T(256)} %constant.73.clone.1), dimensions={0}, to_apply=%region_0.1 | reduce | flops 2211840 | bytes 5013506 | tf_op jit(solution)/shard_map/reduce_sum | solution.py:293
  178.8 3.6 %collective-permute-start.23 = (bf16[24,1536]{1,0:T(8,128)(2,1)S(1)}, bf16[24,1536]{1,0:T(8,128)(2,1)S(1)}, u32[]{:S(2)}, u32[]{:S(2)}) collective-permute-start(bf16[24,1536]{1,0:T(8,128)(2,1)S(1)} %get-tuple-element.61), channel_id=1, source_target_pairs={{0,192},{64,0},{128,64},{192,128},{1,193},{65,1},{129,65},{193,129... | collective-permute-start | bytes 221192 | tf_op jit(solution)/shard_map/ppermute | solution.py:297
  182.4 1.7 collective-permute-start.22
  184.1 2.3 %collective-permute-done.21 = bf16[24,1536]{1,0:T(8,128)(2,1)S(1)} collective-permute-done((bf16[24,1536]{1,0:T(8,128)(2,1)S(1)}, bf16[24,1536]{1,0:T(8,128)(2,1)S(1)}, u32[]{:S(2)}, u32[]{:S(2)}) %collective-permute-start.21) | collective-permute-done | bytes 73760 | tf_op jit(solution)/shard_map/ppermute | solution.py:297
  186.7 4.8 %collective-permute-done.22 = bf16[24,1536]{1,0:T(8,128)(2,1)S(1)} collective-permute-done((bf16[24,1536]{1,0:T(8,128)(2,1)S(1)}, bf16[24,1536]{1,0:T(8,128)(2,1)S(1)}, u32[]{:S(2)}, u32[]{:S(2)}) %collective-permute-start.22) | collective-permute-done | bytes 73760 | tf_op jit(solution)/shard_map/ppermute | solution.py:297
  191.5 0.9 collective-permute-start.24
  192.4 0.9 collective-permute-done.24
  193.4 0.7 maximum_select_fusion
  (50 shorter events, 2.8 us)
Async XLA Ops:
  0.6 1.1 copy-start
  1.7 0.7 copy-start.1
  2.8 1.7 collective-permute-start
  4.5 10.6 %collective-permute-start.1 = (bf16[192,384]{1,0:T(8,128)(2,1)S(1)}, bf16[192,384]{1,0:T(8,128)(2,1)S(1)}, u32[]{:S(2)}, u32[]{:S(2)}) collective-permute-start(bf16[192,384]{1,0:T(8,128)(2,1)S(1)} %maximum_select_fusion.1.own_ref), channel_id=1, source_target_pairs={{0,64},{64,128},{128,192},{192,0},{1,65},{65,129},{129,193},{193,1... | collective-permute-start | bytes 442376 | tf_op jit(solution)/shard_map/ppermute | solution.py:319
  7.6 14.6 %collective-permute-start.4 = (bf16[192,384]{1,0:T(8,128)(2,1)S(1)}, bf16[192,384]{1,0:T(8,128)(2,1)S(1)}, u32[]{:S(2)}, u32[]{:S(2)}) collective-permute-start(bf16[192,384]{1,0:T(8,128)(2,1)S(1)} %maximum_select_fusion.1.own_ref), channel_id=1, source_target_pairs={{0,192},{64,0},{128,64},{192,128},{1,193},{65,1},{129,65},{193,129... | collective-permute-start | bytes 442376 | tf_op jit(solution)/shard_map/ppermute | solution.py:319
  10.7 13.2 %collective-permute-start.3 = (bf16[192,384]{1,0:T(8,128)(2,1)S(1)}, bf16[192,384]{1,0:T(8,128)(2,1)S(1)}, u32[]{:S(2)}, u32[]{:S(2)}) collective-permute-start(bf16[192,384]{1,0:T(8,128)(2,1)S(1)} %maximum_select_fusion.1.own_ref), channel_id=1, source_target_pairs={{0,128},{64,192},{128,0},{192,64},{1,129},{65,193},{129,1},{193,65... | collective-permute-start | bytes 442376 | tf_op jit(solution)/shard_map/ppermute | solution.py:319
  15.2 13.4 %copy-start.4 = (bf16[1,256,3072]{2,1,0:T(8,128)(2,1)S(1)}, bf16[1,256,3072]{2,1,0:T(8,128)(2,1)}, u32[]{:S(2)}) copy-start(bf16[1,256,3072]{2,1,0:T(8,128)(2,1)} %param.9) | copy-start | bytes 4718596
  24.0 21.7 %collective-permute-start.5 = (bf16[1536,256]{1,0:T(8,128)(2,1)}, bf16[1536,256]{1,0:T(8,128)(2,1)}, u32[]{:S(2)}, u32[]{:S(2)}) collective-permute-start(bf16[1536,256]{1,0:T(8,128)(2,1)} %context_half.2), channel_id=1, source_target_pairs={{0,32},{32,0},{1,33},{33,1},{2,34},{34,2},{3,35},{35,3},{4,36},{36... | collective-permute-start | bytes 2359304 | tf_op jit(solution)/shard_map/ppermute | solution.py:335
  28.7 18.0 %copy-start.8 = (bf16[256,1536]{1,0:T(8,128)(2,1)}, bf16[256,1536]{1,0:T(8,128)(2,1)S(1)}, u32[]{:S(2)}) copy-start(bf16[256,1536]{1,0:T(8,128)(2,1)S(1)} %get-tuple-element.41) | copy-start | bytes 2359300
  28.7 24.6 %copy-start.7 = (bf16[256,1536]{1,0:T(8,128)(2,1)}, bf16[256,1536]{1,0:T(8,128)(2,1)S(1)}, u32[]{:S(2)}) copy-start(bf16[256,1536]{1,0:T(8,128)(2,1)S(1)} %get-tuple-element.40.refs_0_.d0) | copy-start | bytes 2359300
  28.7 18.0 %collective-permute-start.2 = (bf16[256,1536]{1,0:T(8,128)(2,1)S(1)}, bf16[256,1536]{1,0:T(8,128)(2,1)S(1)}, u32[]{:S(2)}, u32[]{:S(2)}) collective-permute-start(bf16[256,1536]{1,0:T(8,128)(2,1)S(1)} %get-tuple-element.41), channel_id=1, source_target_pairs={{0,8},{8,0},{1,9},{9,1},{2,10},{10,2},{3,11},{11,3},{4,12},{12,4},... | collective-permute-start | bytes 2359304 | tf_op jit(solution)/shard_map/ppermute | solution.py:332
  30.3 8.8 %collective-permute-start.6 = (bf16[2,192,384]{2,1,0:T(8,128)(2,1)S(1)}, bf16[2,192,384]{2,1,0:T(8,128)(2,1)S(1)}, u32[]{:S(2)}, u32[]{:S(2)}) collective-permute-start(bf16[2,192,384]{2,1,0:T(8,128)(2,1)S(1)} %get-tuple-element.37.low), channel_id=1, source_target_pairs={{0,16},{16,4},{4,20},{20,0},{1,17},{17,5},{5,21},{21,1},{2,18},{18... | collective-permute-start | bytes 884744 | tf_op jit(solution)/shard_map/ppermute | solution.py:324
  31.6 8.4 %collective-permute-start.7 = (bf16[2,192,384]{2,1,0:T(8,128)(2,1)S(1)}, bf16[2,192,384]{2,1,0:T(8,128)(2,1)S(1)}, u32[]{:S(2)}, u32[]{:S(2)}) collective-permute-start(bf16[2,192,384]{2,1,0:T(8,128)(2,1)S(1)} %get-tuple-element.38.high), channel_id=1, source_target_pairs={{0,20},{16,0},{4,16},{20,4},{1,21},{17,1},{5,17},{21,5},{2,22},{18... | collective-permute-start | bytes 884744 | tf_op jit(solution)/shard_map/ppermute | solution.py:325
  40.1 13.2 %copy-start.2 = (bf16[2,2,192,384]{3,2,1,0:T(8,128)(2,1)}, bf16[2,2,192,384]{3,2,1,0:T(8,128)(2,1)S(1)}, u32[]{:S(2)}) copy-start(bf16[2,2,192,384]{3,2,1,0:T(8,128)(2,1)S(1)} %get-tuple-element.39) | copy-start | bytes 1769476
  40.1 13.2 %copy-start.3 = (bf16[2,2,192,384]{3,2,1,0:T(8,128)(2,1)}, bf16[2,2,192,384]{3,2,1,0:T(8,128)(2,1)S(1)}, u32[]{:S(2)}) copy-start(bf16[2,2,192,384]{3,2,1,0:T(8,128)(2,1)S(1)} %get-tuple-element.42) | copy-start | bytes 1769476
  40.1 14.0 %collective-permute-start.11 = (bf16[768,384]{1,0:T(8,128)(2,1)S(1)}, bf16[768,384]{1,0:T(8,128)(2,1)S(1)}, u32[]{:S(2)}, u32[]{:S(2)}) collective-permute-start(bf16[768,384]{1,0:T(8,128)(2,1)S(1)} %bitcast.25), channel_id=1, source_target_pairs={{0,3},{1,0},{2,1},{3,2},{4,7},{5,4},{6,5},{7,6},{8,11},{9,8},{10,9... | collective-permute-start | bytes 1769480 | tf_op jit(solution)/shard_map/ppermute | solution.py:346
  40.3 16.7 %collective-permute-start.10 = (bf16[768,384]{1,0:T(8,128)(2,1)S(1)}, bf16[768,384]{1,0:T(8,128)(2,1)}, u32[]{:S(2)}, u32[]{:S(2)}) collective-permute-start(bf16[768,384]{1,0:T(8,128)(2,1)S(1)} %bitcast.26), channel_id=1, source_target_pairs={{0,1},{1,2},{2,3},{3,0},{4,5},{5,6},{6,7},{7,4},{8,9},{9,10},{10,1... | collective-permute-start | bytes 1769480 | tf_op jit(solution)/shard_map/ppermute | solution.py:346
  41.6 25.1 %collective-permute-start.14 = (bf16[768,384]{1,0:T(8,128)(2,1)S(1)}, bf16[768,384]{1,0:T(8,128)(2,1)}, u32[]{:S(2)}, u32[]{:S(2)}) collective-permute-start(bf16[768,384]{1,0:T(8,128)(2,1)S(1)} %bitcast.28), channel_id=1, source_target_pairs={{0,3},{1,0},{2,1},{3,2},{4,7},{5,4},{6,5},{7,6},{8,11},{9,8},{10,9... | collective-permute-start | bytes 1769480 | tf_op jit(solution)/shard_map/ppermute | solution.py:347
  45.7 21.0 %collective-permute-start.13 = (bf16[768,384]{1,0:T(8,128)(2,1)S(1)}, bf16[768,384]{1,0:T(8,128)(2,1)}, u32[]{:S(2)}, u32[]{:S(2)}) collective-permute-start(bf16[768,384]{1,0:T(8,128)(2,1)S(1)} %bitcast.29), channel_id=1, source_target_pairs={{0,1},{1,2},{2,3},{3,0},{4,5},{5,6},{6,7},{7,4},{8,9},{9,10},{10,1... | collective-permute-start | bytes 1769480 | tf_op jit(solution)/shard_map/ppermute | solution.py:347
  46.7 6.6 %copy-start.10 = (bf16[256,1536]{1,0:T(8,128)(2,1)}, bf16[256,1536]{1,0:T(8,128)(2,1)S(1)}, u32[]{:S(2)}) copy-start(bf16[256,1536]{1,0:T(8,128)(2,1)S(1)} %collective-permute-done.2.refs_1_.d1) | copy-start | bytes 2359300
  46.7 7.3 %copy-start.9 = (bf16[256,1536]{1,0:T(8,128)(2,1)S(1)}, bf16[256,1536]{1,0:T(8,128)(2,1)}, u32[]{:S(2)}) copy-start(bf16[256,1536]{1,0:T(8,128)(2,1)} %copy-done.8) | copy-start | bytes 2359300
  46.7 24.1 %collective-permute-start.8 = (bf16[256,1536]{1,0:T(8,128)(2,1)S(1)}, bf16[256,1536]{1,0:T(8,128)(2,1)}, u32[]{:S(2)}, u32[]{:S(2)}) collective-permute-start(bf16[256,1536]{1,0:T(8,128)(2,1)S(1)} %get-tuple-element.40.refs_0_.d0), channel_id=1, source_target_pairs={{0,32},{32,0},{1,33},{33,1},{2,34},{34,2},{3,35},{35,3},{4,36},{36... | collective-permute-start | bytes 2359304 | tf_op jit(solution)/shard_map/ppermute | solution.py:339
  54.1 41.1 %copy-start.13 = (bf16[768,384]{1,0:T(8,128)(2,1)}, bf16[768,384]{1,0:T(8,128)(2,1)S(1)}, u32[]{:S(2)}) copy-start(bf16[768,384]{1,0:T(8,128)(2,1)S(1)} %collective-permute-done.11.refs_6_) | copy-start | bytes 1769476
  54.1 29.3 %collective-permute-start.9 = (bf16[256,1536]{1,0:T(8,128)(2,1)S(1)}, bf16[256,1536]{1,0:T(8,128)(2,1)S(1)}, u32[]{:S(2)}, u32[]{:S(2)}) collective-permute-start(bf16[256,1536]{1,0:T(8,128)(2,1)S(1)} %copy-done.9), channel_id=1, source_target_pairs={{0,40},{8,32},{32,8},{40,0},{1,41},{9,33},{33,9},{41,1},{2,42},{10... | collective-permute-start | bytes 2359304 | tf_op jit(solution)/shard_map/ppermute | solution.py:340
  66.7 16.6 %collective-permute-start.19 = (bf16[1536,256]{1,0:T(8,128)(2,1)}, bf16[1536,256]{1,0:T(8,128)(2,1)S(1)}, u32[]{:S(2)}, u32[]{:S(2)}) collective-permute-start(bf16[1536,256]{1,0:T(8,128)(2,1)} %context_half.3.c0), channel_id=1, source_target_pairs={{0,8},{8,0},{1,9},{9,1},{2,10},{10,2},{3,11},{11,3},{4,12},{12,4},... | collective-permute-start | bytes 2359304 | tf_op jit(solution)/shard_map/ppermute | solution.py:351
  68.8 14.5 %collective-permute-start.20 = (bf16[1536,256]{1,0:T(8,128)(2,1)}, bf16[1536,256]{1,0:T(8,128)(2,1)}, u32[]{:S(2)}, u32[]{:S(2)}) collective-permute-start(bf16[1536,256]{1,0:T(8,128)(2,1)} %collective-permute-done.5.c2), channel_id=1, source_target_pairs={{0,8},{8,0},{1,9},{9,1},{2,10},{10,2},{3,11},{11,3},{4,12},{12,4},... | collective-permute-start | bytes 2359304 | tf_op jit(solution)/shard_map/ppermute | solution.py:352
  68.8 26.4 %collective-permute-start.12 = (bf16[768,384]{1,0:T(8,128)(2,1)}, bf16[768,384]{1,0:T(8,128)(2,1)}, u32[]{:S(2)}, u32[]{:S(2)}) collective-permute-start(bf16[768,384]{1,0:T(8,128)(2,1)} %collective-permute-done.10.refs_5_), channel_id=1, source_target_pairs={{0,1},{1,2},{2,3},{3,0},{4,5},{5,6},{6,7},{7,4},{8,9},{9,10},{10,1... | collective-permute-start | bytes 1769480 | tf_op jit(solution)/shard_map/ppermute | solution.py:348
  70.9 24.3 %collective-permute-start.15 = (bf16[768,384]{1,0:T(8,128)(2,1)}, bf16[768,384]{1,0:T(8,128)(2,1)}, u32[]{:S(2)}, u32[]{:S(2)}) collective-permute-start(bf16[768,384]{1,0:T(8,128)(2,1)} %collective-permute-done.14.refs_10_), channel_id=1, source_target_pairs={{0,3},{1,0},{2,1},{3,2},{4,7},{5,4},{6,5},{7,6},{8,11},{9,8},{10,9... | collective-permute-start | bytes 1769480 | tf_op jit(solution)/shard_map/ppermute | solution.py:349
  83.4 0.9 copy-start.11
  83.4 1.1 copy-start.12
  95.2 80.4 %all-to-all-start = ((bf16[16,4,24,1536]{3,2,1,0:T(8,128)(2,1)}), bf16[16,4,24,1536]{3,2,1,0:T(8,128)(2,1)}, u32[]{:S(2)}, u32[]{:S(2)}) async-start(bf16[16,4,24,1536]{3,2,1,0:T(8,128)(2,1)} %weight_gradient.1), calls=%async_computation | async-start | bytes 9437184 | tf_op jit(solution)/shard_map/all_to_all | solution.py:356
  114.8 2.6 %collective-permute-start.16 = (bf16[256,1536]{1,0:T(8,128)(2,1)}, bf16[256,1536]{1,0:T(8,128)(2,1)S(1)}, u32[]{:S(2)}, u32[]{:S(2)}) collective-permute-start(bf16[256,1536]{1,0:T(8,128)(2,1)} %get-tuple-element.44), channel_id=1, source_target_pairs={{0,8},{8,0},{1,9},{9,1},{2,10},{10,2},{3,11},{11,3},{4,12},{12,4},... | collective-permute-start | bytes 2359304 | tf_op jit(solution)/shard_map/ppermute | solution.py:360
  114.9 5.4 %collective-permute-start.18 = (bf16[256,1536]{1,0:T(8,128)(2,1)}, bf16[256,1536]{1,0:T(8,128)(2,1)S(1)}, u32[]{:S(2)}, u32[]{:S(2)}) collective-permute-start(bf16[256,1536]{1,0:T(8,128)(2,1)} %get-tuple-element.46), channel_id=1, source_target_pairs={{0,8},{8,0},{1,9},{9,1},{2,10},{10,2},{3,11},{11,3},{4,12},{12,4},... | collective-permute-start | bytes 2359304 | tf_op jit(solution)/shard_map/ppermute | solution.py:361
  119.0 19.2 %collective-permute-start.17 = (bf16[256,1536]{1,0:T(8,128)(2,1)S(1)}, bf16[256,1536]{1,0:T(8,128)(2,1)S(1)}, u32[]{:S(2)}, u32[]{:S(2)}) collective-permute-start(bf16[256,1536]{1,0:T(8,128)(2,1)S(1)} %add_convert_fusion), channel_id=1, source_target_pairs={{0,32},{32,0},{1,33},{33,1},{2,34},{34,2},{3,35},{35,3},{4,36},{36... | collective-permute-start | bytes 2359304 | tf_op jit(solution)/shard_map/ppermute | solution.py:362
  120.3 0.9 copy-start.5
  138.2 0.9 copy-start.6
  178.7 7.7 %collective-permute-start.21 = (bf16[24,1536]{1,0:T(8,128)(2,1)S(1)}, bf16[24,1536]{1,0:T(8,128)(2,1)S(1)}, u32[]{:S(2)}, u32[]{:S(2)}) collective-permute-start(bf16[24,1536]{1,0:T(8,128)(2,1)S(1)} %get-tuple-element.60), channel_id=1, source_target_pairs={{0,64},{64,128},{128,192},{192,0},{1,65},{65,129},{129,193},{193,1... | collective-permute-start | bytes 221192 | tf_op jit(solution)/shard_map/ppermute | solution.py:297
  178.8 7.9 %collective-permute-start.23 = (bf16[24,1536]{1,0:T(8,128)(2,1)S(1)}, bf16[24,1536]{1,0:T(8,128)(2,1)S(1)}, u32[]{:S(2)}, u32[]{:S(2)}) collective-permute-start(bf16[24,1536]{1,0:T(8,128)(2,1)S(1)} %get-tuple-element.61), channel_id=1, source_target_pairs={{0,192},{64,0},{128,64},{192,128},{1,193},{65,1},{129,65},{193,129... | collective-permute-start | bytes 221192 | tf_op jit(solution)/shard_map/ppermute | solution.py:297
  182.4 9.1 %collective-permute-start.22 = (bf16[24,1536]{1,0:T(8,128)(2,1)S(1)}, bf16[24,1536]{1,0:T(8,128)(2,1)S(1)}, u32[]{:S(2)}, u32[]{:S(2)}) collective-permute-start(bf16[24,1536]{1,0:T(8,128)(2,1)S(1)} %get-tuple-element.62), channel_id=1, source_target_pairs={{0,128},{64,192},{128,0},{192,64},{1,129},{65,193},{129,1},{193,65... | collective-permute-start | bytes 221192 | tf_op jit(solution)/shard_map/ppermute | solution.py:297
  191.5 1.8 collective-permute-start.24

commit v9 on v7

--- a/solution.py
+++ b/solution.py
@@ -168,24 +168,27 @@
     )(codes, scales)
 
 
-def by_zh_body(own_ref, b1, b2, b3, low_ref, high_ref):
+def by_zh_body(own_ref, lower_ref, upper_ref, far_a, far_b, low_ref, high_ref):
     zh = lax.axis_index("zh")
-    for step, piece in enumerate((own_ref, b1, b2, b3)):
-        place = lax.rem(zh - step + 4, 4)
-
-        @pl.when(place < 2)
-        def _():
-            low_ref[place] = piece[...]
-
-        @pl.when(place >= 2)
-        def _():
-            high_ref[place - 2] = piece[...]
+    half = far_a.shape[0]
+    for step, piece in ((0, own_ref), (3, lower_ref), (1, upper_ref), (2, None)):
+        place = lax.rem(zh + step, 4)
+
+        def put(out, index):
+            if piece is None:
+                out[index, :half] = far_a[...]
+                out[index, half:] = far_b[...]
+            else:
+                out[index] = piece[...]
+
+        pl.when(place < 2)(lambda: put(low_ref, place))
+        pl.when(place >= 2)(lambda: put(high_ref, place - 2))
 
 
 def by_zh(own, pieces):
     return pl.pallas_call(
         by_zh_body,
-        in_specs=[pl.BlockSpec(memory_space=pltpu.VMEM)] * 4,
+        in_specs=[pl.BlockSpec(memory_space=pltpu.VMEM)] * 5,
         out_specs=[pl.BlockSpec(memory_space=pltpu.VMEM)] * 2,
         out_shape=[jax.ShapeDtypeStruct((2, *own.shape), BF16)] * 2,
         compiler_params=pltpu.CompilerParams(vmem_limit_bytes=8 * 2**20),
@@ -316,11 +319,16 @@
     pair = jnp.where(
         c == 0, jnp.concatenate([piece, arrived], 0), jnp.concatenate([arrived, piece], 0)
     )
-    behind = [lax.ppermute(pair, "zh", ring(4, step)) for step in (1, 2, 3)]
+    behind = [lax.ppermute(pair, "zh", ring(4, step)) for step in (1, -1)]
+    edge = pair.shape[0] // 2
+    relayed = [
+        lax.ppermute(behind[0][:edge], "zh", ring(4, 1)),
+        lax.ppermute(behind[1][edge:], "zh", ring(4, -1)),
+    ]
     (late_parity,) = after((other_parity,), (behind[0],))
     context_other = forward(late_parity, q, k, v, width)
     (pair,) = after((pair,), (context_other,))
-    low, high = by_zh(pair, behind)
+    low, high = by_zh(pair, behind + relayed)
     beside_low = lax.ppermute(low, ("xl", "xh"), x_ring(1))
     beside_high = lax.ppermute(high, ("xl", "xh"), x_ring(-1))
 
@@ -331,7 +339,7 @@
     )
     d1 = lax.ppermute(other, "c", SWAP)
 
-    (context_other,) = after((context_other,), (behind[1], behind[2]))
+    (context_other,) = after((context_other,), tuple(behind))
     c2 = lax.ppermute(context_other, "zl", SWAP)
 
     low, high = by_xl(low, high, beside_low, beside_high)

time: 193 us -> 202 us (1.047)
  starting transfers between devices: 44.9 us -> 52.4 us
    ppermute x3 -> x4, waiting for transfers between devices: 3.46 us -> 21.7 us  [the longest x1 17.3 us: per_device(): lax.ppermute(behind[0][:edge], 'zh', ring(4, 1))]
    all_to_all x1, waiting for transfers between devices: 26 us -> 20.8 us  [per_device(): terms = lax.all_to_all(terms, ('xl', 'xh', 'y'), 0, 0, tiled=True)]
    ppermute x1, starting transfers between devices: 3.01 us -> 7.09 us  [per_device(): d3 = lax.ppermute(diagonal, ('zl', 'c'), [(i, 3 - i) for i in range(4)])]
    ppermute x2, waiting for transfers between devices: 9.63 us -> 5.55 us  [per_device(): highs.append(lax.ppermute(highs[0], 'y', ring(4, step)))]
    ppermute x1, waiting for transfers between devices: 3.92 us -> 0.01 us  [per_device(): c2 = lax.ppermute(context_other, 'zl', SWAP)]
    ppermute x3, starting transfers between devices: 5.39 us -> 8.82 us  [sums_on_owners(): mine = mine + lax.ppermute(away, 'zh', ring(4, step)).astype(F32)]
    ppermute x1, waiting for transfers between devices: 12.5 us -> 9.59 us  [per_device(): d3 = lax.ppermute(diagonal, ('zl', 'c'), [(i, 3 - i) for i in range(4)])]
    ppermute x1, waiting for transfers between devices: 7.24 us -> 4.92 us  [per_device(): beside_low = lax.ppermute(low, ('xl', 'xh'), x_ring(1))]
  transfers between devices with their start and end apart: 26 -> 27, of which waited for: 17 -> 14; matrix products, arithmetic and copies ran while one was open for 1% -> 1% of each run, Pallas kernels for 28% -> 27%
where the time goes in v9:
time: 202 us; the launch traced here: 201 us
  waiting for transfers between devices  82.9 us (41%)
  Pallas kernels  53.9 us (27%)
  starting transfers between devices  52.4 us (26%)
  other arithmetic  6.09 us (3%)
  local copies, waits for them, and re-layouts  4.87 us (2%)
    all_to_all x1, waiting for transfers between devices, per_device(): terms = lax.all_to_all(terms, ('xl', 'xh', 'y'), 0, 0, tiled=True)  20.8 us
    pallas_call x2, Pallas kernels, backward(): pl.pallas_call(functools.partial(backward_body, before is None), grid_spe...  20.6 us
    ppermute x1, waiting for transfers between devices, per_device(): lax.ppermute(behind[0][:edge], 'zh', ring(4, 1))  17.3 us
    pallas_call x1, Pallas kernels, context_gradient(): pl.pallas_call(context_gradient_body, grid_spec=pltpu.PrefetchScalarGridS...  12.3 us
    pallas_call x2, Pallas kernels, forward(): pl.pallas_call(forward_body, grid_spec=pltpu.PrefetchScalarGridSpec(num_s...  11.1 us
    ppermute x1, waiting for transfers between devices, per_device(): d3 = lax.ppermute(diagonal, ('zl', 'c'), [(i, 3 - i) for i in range(4)])  9.59 us
    pallas_call x1, Pallas kernels, weight_gradient(): pl.pallas_call(weight_gradient_body, grid=(4,), in_specs=[pl.BlockSpec((r...  9.22 us
    ppermute x3, starting transfers between devices, sums_on_owners(): mine = mine + lax.ppermute(away, 'zh', ring(4, step)).astype(F32)  8.82 us
  transfers between devices with their start and end apart: 27, of which 14 were waited for; matrix products, arithmetic and copies ran while one was open for 1% of the time, Pallas kernels for 27%

profile of v9, /device:TPU:19, one launch (start us, length us, event | category | flops | bytes accessed | tf_op | source)
XLA Modules:
  0.0 201.1 jit_solution(3648724625168124127)
XLA Ops:
  0.6 1.1 copy-done
  1.7 0.7 copy-done.1
  2.4 0.4 weight_pieces.1
  2.8 0.8 collective-permute-start
  3.6 0.9 collective-permute-done
  4.5 3.1 %collective-permute-start.1 = (bf16[192,384]{1,0:T(8,128)(2,1)S(1)}, bf16[192,384]{1,0:T(8,128)(2,1)S(1)}, u32[]{:S(2)}, u32[]{:S(2)}) collective-permute-start(bf16[192,384]{1,0:T(8,128)(2,1)S(1)} %maximum_select_fusion.1.own_ref), channel_id=1, source_target_pairs={{0,64},{64,128},{128,192},{192,0},{1,65},{65,129},{129,193},{193,1... | collective-permute-start | bytes 442376 | tf_op jit(solution)/shard_map/ppermute | solution.py:322
  7.6 3.1 %collective-permute-start.3 = (bf16[192,384]{1,0:T(8,128)(2,1)S(1)}, bf16[192,384]{1,0:T(8,128)(2,1)S(1)}, u32[]{:S(2)}, u32[]{:S(2)}) collective-permute-start(bf16[192,384]{1,0:T(8,128)(2,1)S(1)} %maximum_select_fusion.1.own_ref), channel_id=1, source_target_pairs={{0,192},{64,0},{128,64},{192,128},{1,193},{65,1},{129,65},{193,129... | collective-permute-start | bytes 442376 | tf_op jit(solution)/shard_map/ppermute | solution.py:322
  10.7 4.4 %collective-permute-done.1.lower_ref = bf16[192,384]{1,0:T(8,128)(2,1)S(1)} collective-permute-done((bf16[192,384]{1,0:T(8,128)(2,1)S(1)}, bf16[192,384]{1,0:T(8,128)(2,1)S(1)}, u32[]{:S(2)}, u32[]{:S(2)}) %collective-permute-start.1) | collective-permute-done | bytes 147488 | tf_op jit(solution)/shard_map/ppermute | solution.py:322
  15.2 5.4 %context_half.2 = bf16[1536,256]{1,0:T(8,128)(2,1)} custom-call(s32[1]{0:T(128)S(6)} %sub.6.pick, bf16[256,3072]{1,0:T(8,128)(2,1)} %bitcast.31, bf16[256,3072]{1,0:T(8,128)(2,1)} %bitcast.35, bf16[256,3072]{1,0:T(8,128)(2,1)} %bitcast.39), custom_call_target="tpu_custom_call" | custom-call | flops 402653184 | bytes 3145728 | tf_op jit(solution)/shard_map/context_half/pallas_call | solution.py:73
  20.6 3.3 %collective-permute-start.4 = (bf16[1536,256]{1,0:T(8,128)(2,1)}, bf16[1536,256]{1,0:T(8,128)(2,1)}, u32[]{:S(2)}, u32[]{:S(2)}) collective-permute-start(bf16[1536,256]{1,0:T(8,128)(2,1)} %context_half.2), channel_id=1, source_target_pairs={{0,32},{32,0},{1,33},{33,1},{2,34},{34,2},{3,35},{35,3},{4,36},{36... | collective-permute-start | bytes 2359304 | tf_op jit(solution)/shard_map/ppermute | solution.py:343
  23.9 2.1 %collective-permute-start.6 = (bf16[96,384]{1,0:T(8,128)(2,1)S(1)}, bf16[96,384]{1,0:T(8,128)(2,1)S(1)}, u32[]{:S(2)}, u32[]{:S(2)}) collective-permute-start(bf16[96,384]{1,0:T(8,128)(2,1)S(1)} %slice.21), channel_id=1, source_target_pairs={{0,192},{64,0},{128,64},{192,128},{1,193},{65,1},{129,65},{193,129... | collective-permute-start | bytes 221192 | tf_op jit(solution)/shard_map/ppermute | solution.py:326
  26.0 0.5 collective-permute-start.5
  26.6 1.8 collective-permute-start.2
  28.4 17.3 %collective-permute-done.5.far_a = bf16[96,384]{1,0:T(8,128)(2,1)S(1)} collective-permute-done((bf16[96,384]{1,0:T(8,128)(2,1)S(1)}, bf16[96,384]{1,0:T(8,128)(2,1)S(1)}, u32[]{:S(2)}, u32[]{:S(2)}) %collective-permute-start.5) | collective-permute-done | bytes 73760 | tf_op jit(solution)/shard_map/ppermute | solution.py:325
  45.7 1.3 collective-permute-start.7
  47.3 4.9 %collective-permute-done.7.beside_low = bf16[2,192,384]{2,1,0:T(8,128)(2,1)S(1)} collective-permute-done((bf16[2,192,384]{2,1,0:T(8,128)(2,1)S(1)}, bf16[2,192,384]{2,1,0:T(8,128)(2,1)S(1)}, u32[]{:S(2)}, u32[]{:S(2)}) %collective-permute-start.7) | collective-permute-done | bytes 294944 | tf_op jit(solution)/shard_map/ppermute | solution.py:332
  52.2 0.9 collective-permute-done.8.beside_high
  53.5 1.3 collective-permute-start.11
  55.0 2.0 %collective-permute-start.14 = (bf16[768,384]{1,0:T(8,128)(2,1)S(1)}, bf16[768,384]{1,0:T(8,128)(2,1)}, u32[]{:S(2)}, u32[]{:S(2)}) collective-permute-start(bf16[768,384]{1,0:T(8,128)(2,1)S(1)} %bitcast.29), channel_id=1, source_target_pairs={{0,1},{1,2},{2,3},{3,0},{4,5},{5,6},{6,7},{7,4},{8,9},{9,10},{10,1... | collective-permute-start | bytes 1769480 | tf_op jit(solution)/shard_map/ppermute | solution.py:355
  57.2 5.7 %context_half.3.c0 = bf16[1536,256]{1,0:T(8,128)(2,1)} custom-call(s32[1]{0:T(128)} %bitcast.pick, bf16[256,3072]{1,0:T(8,128)(2,1)} %bitcast.32, bf16[256,3072]{1,0:T(8,128)(2,1)} %bitcast.36, bf16[256,3072]{1,0:T(8,128)(2,1)} %bitcast.40), custom_call_target="tpu_custom_call" | custom-call | flops 402653184 | bytes 3145728 | tf_op jit(solution)/shard_map/context_half/pallas_call | solution.py:73
  62.9 2.1 %collective-permute-done.12.refs_6_ = bf16[768,384]{1,0:T(8,128)(2,1)S(1)} collective-permute-done((bf16[768,384]{1,0:T(8,128)(2,1)S(1)}, bf16[768,384]{1,0:T(8,128)(2,1)S(1)}, u32[]{:S(2)}, u32[]{:S(2)}) %collective-permute-start.12) | collective-permute-done | bytes 589856 | tf_op jit(solution)/shard_map/ppermute | solution.py:354
  65.0 7.1 %collective-permute-start.10 = (bf16[256,1536]{1,0:T(8,128)(2,1)S(1)}, bf16[256,1536]{1,0:T(8,128)(2,1)S(1)}, u32[]{:S(2)}, u32[]{:S(2)}) collective-permute-start(bf16[256,1536]{1,0:T(8,128)(2,1)S(1)} %copy-done.9), channel_id=1, source_target_pairs={{0,40},{8,32},{32,8},{40,0},{1,41},{9,33},{33,9},{41,1},{2,42},{10... | collective-permute-start | bytes 2359304 | tf_op jit(solution)/shard_map/ppermute | solution.py:348
  72.1 5.5 %collective-permute-done.15.refs_10_ = bf16[768,384]{1,0:T(8,128)(2,1)} collective-permute-done((bf16[768,384]{1,0:T(8,128)(2,1)S(1)}, bf16[768,384]{1,0:T(8,128)(2,1)}, u32[]{:S(2)}, u32[]{:S(2)}) %collective-permute-start.15) | collective-permute-done | bytes 589856 | tf_op jit(solution)/shard_map/ppermute | solution.py:355
  77.6 4.4 %collective-permute-start.20 = (bf16[1536,256]{1,0:T(8,128)(2,1)}, bf16[1536,256]{1,0:T(8,128)(2,1)S(1)}, u32[]{:S(2)}, u32[]{:S(2)}) collective-permute-start(bf16[1536,256]{1,0:T(8,128)(2,1)} %context_half.3.c0), channel_id=1, source_target_pairs={{0,8},{8,0},{1,9},{9,1},{2,10},{10,2},{3,11},{11,3},{4,12},{12,4},... | collective-permute-start | bytes 2359304 | tf_op jit(solution)/shard_map/ppermute | solution.py:359
  82.0 2.0 %collective-permute-start.13 = (bf16[768,384]{1,0:T(8,128)(2,1)}, bf16[768,384]{1,0:T(8,128)(2,1)}, u32[]{:S(2)}, u32[]{:S(2)}) collective-permute-start(bf16[768,384]{1,0:T(8,128)(2,1)} %collective-permute-done.11.refs_5_), channel_id=1, source_target_pairs={{0,1},{1,2},{2,3},{3,0},{4,5},{5,6},{6,7},{7,4},{8,9},{9,10},{10,1... | collective-permute-start | bytes 1769480 | tf_op jit(solution)/shard_map/ppermute | solution.py:356
  84.1 9.6 %collective-permute-done.10.refs_3_.d3 = bf16[256,1536]{1,0:T(8,128)(2,1)S(1)} collective-permute-done((bf16[256,1536]{1,0:T(8,128)(2,1)S(1)}, bf16[256,1536]{1,0:T(8,128)(2,1)S(1)}, u32[]{:S(2)}, u32[]{:S(2)}) %collective-permute-start.10) | collective-permute-done | bytes 786464 | tf_op jit(solution)/shard_map/ppermute | solution.py:348
  93.7 0.9 copy-done.11
  94.8 9.2 %weight_gradient.1 = bf16[16,4,24,1536]{3,2,1,0:T(8,128)(2,1)} custom-call(bf16[1536,256]{1,0:T(8,128)(2,1)} %context_half.3.c0, bf16[1536,256]{1,0:T(8,128)(2,1)} %copy-done.12, bf16[1536,256]{1,0:T(8,128)(2,1)} %collective-permute-done.4.c2, bf16[1536,256]{1,0:T(8,128)(2,1)} %collective-permute-done.21.c3, bf16[256,1536]{1,0:T(8,128)(2,1)} %copy-done.7, ...), custom_call_target="tpu_custom_call" | custom-call | flops 4831838208 | bytes 12582912 | tf_op jit(solution)/shard_map/weight_gradient/pallas_call | solution.py:282
  104.0 8.1 %all-to-all-start = ((bf16[16,4,24,1536]{3,2,1,0:T(8,128)(2,1)}), bf16[16,4,24,1536]{3,2,1,0:T(8,128)(2,1)}, u32[]{:S(2)}, u32[]{:S(2)}) async-start(bf16[16,4,24,1536]{3,2,1,0:T(8,128)(2,1)} %weight_gradient.1), calls=%async_computation | async-start | bytes 9437184 | tf_op jit(solution)/shard_map/all_to_all | solution.py:364
  112.1 0.6 pad_add_fusion.place
  112.8 12.3 %context_gradient.1 = (f32[256,1536]{1,0:T(8,128)}, bf16[256,1536]{1,0:T(8,128)(2,1)}, f32[256,1536]{1,0:T(8,128)}, bf16[256,1536]{1,0:T(8,128)(2,1)}) custom-call(s32[4]{0:T(128)} %pad_add_fusion.place, bf16[256,1536]{1,0:T(8,128)(2,1)} %copy-done.7, bf16[256,1536]{1,0:T(8,128)(2,1)} %copy-done.10, bf16[256,1536]{1,0:T(8,128)(2,1)} %collective-permute-done.9.refs_2_.d2, ...), custom_call_target="tpu_custom_call" | custom-call | flops 4831838208 | bytes 20971520 | tf_op jit(solution)/shard_map/context_gradient/pallas_call | solution.py:250
  125.2 0.5 collective-permute-start.19
  125.7 2.0 collective-permute-done.17
  127.7 1.6 add_convert_fusion
  129.5 0.9 copy-done.5
  130.3 10.4 %attention_gradients.2 = (bf16[256,3072]{1,0:T(8,128)(2,1)}, bf16[256,3072]{1,0:T(8,128)(2,1)}, bf16[256,3072]{1,0:T(8,128)(2,1)}) custom-call(s32[1]{0:T(128)} %bitcast.pick, bf16[256,3072]{1,0:T(8,128)(2,1)} %bitcast.33, bf16[256,3072]{1,0:T(8,128)(2,1)} %bitcast.37, bf16[256,3072]{1,0:T(8,128)(2,1)} %bitcast.41, f32[256,1536]{1,0:T(8,128)} %get-tuple-element.45.refs_0_, ...), custom_call_target="tpu_custom_call" | custom-call | flops 1006632960 | bytes 5505024 | tf_op jit(solution)/shard_map/attention_gradients/pallas_call | solution.py:117
  140.7 7.8 %collective-permute-done.18.refs_0_ = bf16[256,1536]{1,0:T(8,128)(2,1)S(1)} collective-permute-done((bf16[256,1536]{1,0:T(8,128)(2,1)S(1)}, bf16[256,1536]{1,0:T(8,128)(2,1)S(1)}, u32[]{:S(2)}, u32[]{:S(2)}) %collective-permute-start.18) | collective-permute-done | bytes 786464 | tf_op jit(solution)/shard_map/ppermute | solution.py:370
  148.5 0.9 copy-done.6
  149.4 10.3 %attention_gradients.3 = (bf16[256,3072]{1,0:T(8,128)(2,1)}, bf16[256,3072]{1,0:T(8,128)(2,1)}, bf16[256,3072]{1,0:T(8,128)(2,1)}) custom-call(s32[1]{0:T(128)S(6)} %sub.6.pick, bf16[256,3072]{1,0:T(8,128)(2,1)} %bitcast.34, bf16[256,3072]{1,0:T(8,128)(2,1)} %bitcast.38, ...), custom_call_target="tpu_custom_call", output_to_operand_aliasing={{0}: (5, {}), {1}: (6, {}), {2}: (7, {})} | custom-call | flops 1006632960 | bytes 5505024 | tf_op jit(solution)/shard_map/attention_gradients/pallas_call | solution.py:117
  159.7 20.8 %all-to-all-done = bf16[16,4,24,1536]{3,2,1,0:T(8,128)(2,1)} async-done(((bf16[16,4,24,1536]{3,2,1,0:T(8,128)(2,1)}), bf16[16,4,24,1536]{3,2,1,0:T(8,128)(2,1)}, u32[]{:S(2)}, u32[]{:S(2)}) %all-to-all-start) | async-done | bytes 4718624 | tf_op jit(solution)/shard_map/all_to_all | solution.py:364
  180.5 3.0 %reduce_sum.12 = bf16[4,24,1536]{2,1,0:T(8,128)(2,1)S(1)} reduce(bf16[16,4,24,1536]{3,2,1,0:T(8,128)(2,1)} %all-to-all-done, bf16[]{:T(256)} %constant.73.clone.1), dimensions={0}, to_apply=%region_0.1 | reduce | flops 2211840 | bytes 5013506 | tf_op jit(solution)/shard_map/reduce_sum | solution.py:296
  183.5 5.4 %collective-permute-start.22 = (bf16[24,1536]{1,0:T(8,128)(2,1)S(1)}, bf16[24,1536]{1,0:T(8,128)(2,1)S(1)}, u32[]{:S(2)}, u32[]{:S(2)}) collective-permute-start(bf16[24,1536]{1,0:T(8,128)(2,1)S(1)} %get-tuple-element.60), channel_id=1, source_target_pairs={{0,64},{64,128},{128,192},{192,0},{1,65},{65,129},{129,193},{193,1... | collective-permute-start | bytes 221192 | tf_op jit(solution)/shard_map/ppermute | solution.py:300
  189.0 3.4 %collective-permute-start.23 = (bf16[24,1536]{1,0:T(8,128)(2,1)S(1)}, bf16[24,1536]{1,0:T(8,128)(2,1)S(1)}, u32[]{:S(2)}, u32[]{:S(2)}) collective-permute-start(bf16[24,1536]{1,0:T(8,128)(2,1)S(1)} %get-tuple-element.62), channel_id=1, source_target_pairs={{0,128},{64,192},{128,0},{192,64},{1,129},{65,193},{129,1},{193,65... | collective-permute-start | bytes 221192 | tf_op jit(solution)/shard_map/ppermute | solution.py:300
  192.4 0.8 collective-permute-done.24
  193.2 4.9 %collective-permute-done.23 = bf16[24,1536]{1,0:T(8,128)(2,1)S(1)} collective-permute-done((bf16[24,1536]{1,0:T(8,128)(2,1)S(1)}, bf16[24,1536]{1,0:T(8,128)(2,1)S(1)}, u32[]{:S(2)}, u32[]{:S(2)}) %collective-permute-start.23) | collective-permute-done | bytes 73760 | tf_op jit(solution)/shard_map/ppermute | solution.py:300
  198.1 1.3 collective-permute-start.25
  199.4 0.9 collective-permute-done.25
  200.4 0.7 maximum_select_fusion
  (54 shorter events, 1.7 us)
Async XLA Ops:
  0.6 1.1 copy-start
  1.7 0.7 copy-start.1
  2.8 1.7 collective-permute-start
  4.5 10.6 %collective-permute-start.1 = (bf16[192,384]{1,0:T(8,128)(2,1)S(1)}, bf16[192,384]{1,0:T(8,128)(2,1)S(1)}, u32[]{:S(2)}, u32[]{:S(2)}) collective-permute-start(bf16[192,384]{1,0:T(8,128)(2,1)S(1)} %maximum_select_fusion.1.own_ref), channel_id=1, source_target_pairs={{0,64},{64,128},{128,192},{192,0},{1,65},{65,129},{129,193},{193,1... | collective-permute-start | bytes 442376 | tf_op jit(solution)/shard_map/ppermute | solution.py:322
  7.6 13.0 %collective-permute-start.3 = (bf16[192,384]{1,0:T(8,128)(2,1)S(1)}, bf16[192,384]{1,0:T(8,128)(2,1)S(1)}, u32[]{:S(2)}, u32[]{:S(2)}) collective-permute-start(bf16[192,384]{1,0:T(8,128)(2,1)S(1)} %maximum_select_fusion.1.own_ref), channel_id=1, source_target_pairs={{0,192},{64,0},{128,64},{192,128},{1,193},{65,1},{129,65},{193,129... | collective-permute-start | bytes 442376 | tf_op jit(solution)/shard_map/ppermute | solution.py:322
  15.2 11.3 %copy-start.4 = (bf16[1,256,3072]{2,1,0:T(8,128)(2,1)S(1)}, bf16[1,256,3072]{2,1,0:T(8,128)(2,1)}, u32[]{:S(2)}) copy-start(bf16[1,256,3072]{2,1,0:T(8,128)(2,1)} %param.9) | copy-start | bytes 4718596
  20.6 34.4 %collective-permute-start.4 = (bf16[1536,256]{1,0:T(8,128)(2,1)}, bf16[1536,256]{1,0:T(8,128)(2,1)}, u32[]{:S(2)}, u32[]{:S(2)}) collective-permute-start(bf16[1536,256]{1,0:T(8,128)(2,1)} %context_half.2), channel_id=1, source_target_pairs={{0,32},{32,0},{1,33},{33,1},{2,34},{34,2},{3,35},{35,3},{4,36},{36... | collective-permute-start | bytes 2359304 | tf_op jit(solution)/shard_map/ppermute | solution.py:343
  23.9 4.5 %collective-permute-start.6 = (bf16[96,384]{1,0:T(8,128)(2,1)S(1)}, bf16[96,384]{1,0:T(8,128)(2,1)S(1)}, u32[]{:S(2)}, u32[]{:S(2)}) collective-permute-start(bf16[96,384]{1,0:T(8,128)(2,1)S(1)} %slice.21), channel_id=1, source_target_pairs={{0,192},{64,0},{128,64},{192,128},{1,193},{65,1},{129,65},{193,129... | collective-permute-start | bytes 221192 | tf_op jit(solution)/shard_map/ppermute | solution.py:326
  26.0 19.6 %collective-permute-start.5 = (bf16[96,384]{1,0:T(8,128)(2,1)S(1)}, bf16[96,384]{1,0:T(8,128)(2,1)S(1)}, u32[]{:S(2)}, u32[]{:S(2)}) collective-permute-start(bf16[96,384]{1,0:T(8,128)(2,1)S(1)} %slice.20), channel_id=1, source_target_pairs={{0,64},{64,128},{128,192},{192,0},{1,65},{65,129},{129,193},{193,1... | collective-permute-start | bytes 221192 | tf_op jit(solution)/shard_map/ppermute | solution.py:325
  26.6 30.5 %copy-start.8 = (bf16[256,1536]{1,0:T(8,128)(2,1)}, bf16[256,1536]{1,0:T(8,128)(2,1)S(1)}, u32[]{:S(2)}) copy-start(bf16[256,1536]{1,0:T(8,128)(2,1)S(1)} %get-tuple-element.41) | copy-start | bytes 2359300
  26.6 36.3 %copy-start.7 = (bf16[256,1536]{1,0:T(8,128)(2,1)}, bf16[256,1536]{1,0:T(8,128)(2,1)S(1)}, u32[]{:S(2)}) copy-start(bf16[256,1536]{1,0:T(8,128)(2,1)S(1)} %get-tuple-element.40.refs_0_.d0) | copy-start | bytes 2359300
  26.6 30.5 %collective-permute-start.2 = (bf16[256,1536]{1,0:T(8,128)(2,1)S(1)}, bf16[256,1536]{1,0:T(8,128)(2,1)S(1)}, u32[]{:S(2)}, u32[]{:S(2)}) collective-permute-start(bf16[256,1536]{1,0:T(8,128)(2,1)S(1)} %get-tuple-element.41), channel_id=1, source_target_pairs={{0,8},{8,0},{1,9},{9,1},{2,10},{10,2},{3,11},{11,3},{4,12},{12,4},... | collective-permute-start | bytes 2359304 | tf_op jit(solution)/shard_map/ppermute | solution.py:340
  45.7 6.5 %collective-permute-start.7 = (bf16[2,192,384]{2,1,0:T(8,128)(2,1)S(1)}, bf16[2,192,384]{2,1,0:T(8,128)(2,1)S(1)}, u32[]{:S(2)}, u32[]{:S(2)}) collective-permute-start(bf16[2,192,384]{2,1,0:T(8,128)(2,1)S(1)} %get-tuple-element.37.low), channel_id=1, source_target_pairs={{0,16},{16,4},{4,20},{20,0},{1,17},{17,5},{5,21},{21,1},{2,18},{18... | collective-permute-start | bytes 884744 | tf_op jit(solution)/shard_map/ppermute | solution.py:332
  47.0 6.1 %collective-permute-start.8 = (bf16[2,192,384]{2,1,0:T(8,128)(2,1)S(1)}, bf16[2,192,384]{2,1,0:T(8,128)(2,1)S(1)}, u32[]{:S(2)}, u32[]{:S(2)}) collective-permute-start(bf16[2,192,384]{2,1,0:T(8,128)(2,1)S(1)} %get-tuple-element.38.high), channel_id=1, source_target_pairs={{0,20},{16,0},{4,16},{20,4},{1,21},{17,1},{5,17},{21,5},{2,22},{18... | collective-permute-start | bytes 884744 | tf_op jit(solution)/shard_map/ppermute | solution.py:333
  53.3 9.6 %copy-start.2 = (bf16[2,2,192,384]{3,2,1,0:T(8,128)(2,1)}, bf16[2,2,192,384]{3,2,1,0:T(8,128)(2,1)S(1)}, u32[]{:S(2)}) copy-start(bf16[2,2,192,384]{3,2,1,0:T(8,128)(2,1)S(1)} %get-tuple-element.39) | copy-start | bytes 1769476
  53.3 9.6 %copy-start.3 = (bf16[2,2,192,384]{3,2,1,0:T(8,128)(2,1)}, bf16[2,2,192,384]{3,2,1,0:T(8,128)(2,1)S(1)}, u32[]{:S(2)}) copy-start(bf16[2,2,192,384]{3,2,1,0:T(8,128)(2,1)S(1)} %get-tuple-element.42) | copy-start | bytes 1769476
  53.3 11.7 %collective-permute-start.12 = (bf16[768,384]{1,0:T(8,128)(2,1)S(1)}, bf16[768,384]{1,0:T(8,128)(2,1)S(1)}, u32[]{:S(2)}, u32[]{:S(2)}) collective-permute-start(bf16[768,384]{1,0:T(8,128)(2,1)S(1)} %bitcast.25), channel_id=1, source_target_pairs={{0,3},{1,0},{2,1},{3,2},{4,7},{5,4},{6,5},{7,6},{8,11},{9,8},{10,9... | collective-permute-start | bytes 1769480 | tf_op jit(solution)/shard_map/ppermute | solution.py:354
  53.5 18.5 %collective-permute-start.11 = (bf16[768,384]{1,0:T(8,128)(2,1)S(1)}, bf16[768,384]{1,0:T(8,128)(2,1)}, u32[]{:S(2)}, u32[]{:S(2)}) collective-permute-start(bf16[768,384]{1,0:T(8,128)(2,1)S(1)} %bitcast.26), channel_id=1, source_target_pairs={{0,1},{1,2},{2,3},{3,0},{4,5},{5,6},{6,7},{7,4},{8,9},{9,10},{10,1... | collective-permute-start | bytes 1769480 | tf_op jit(solution)/shard_map/ppermute | solution.py:354
  54.8 22.8 %collective-permute-start.15 = (bf16[768,384]{1,0:T(8,128)(2,1)S(1)}, bf16[768,384]{1,0:T(8,128)(2,1)}, u32[]{:S(2)}, u32[]{:S(2)}) collective-permute-start(bf16[768,384]{1,0:T(8,128)(2,1)S(1)} %bitcast.28), channel_id=1, source_target_pairs={{0,3},{1,0},{2,1},{3,2},{4,7},{5,4},{6,5},{7,6},{8,11},{9,8},{10,9... | collective-permute-start | bytes 1769480 | tf_op jit(solution)/shard_map/ppermute | solution.py:355
  55.0 22.6 %collective-permute-start.14 = (bf16[768,384]{1,0:T(8,128)(2,1)S(1)}, bf16[768,384]{1,0:T(8,128)(2,1)}, u32[]{:S(2)}, u32[]{:S(2)}) collective-permute-start(bf16[768,384]{1,0:T(8,128)(2,1)S(1)} %bitcast.29), channel_id=1, source_target_pairs={{0,1},{1,2},{2,3},{3,0},{4,5},{5,6},{6,7},{7,4},{8,9},{9,10},{10,1... | collective-permute-start | bytes 1769480 | tf_op jit(solution)/shard_map/ppermute | solution.py:355
  57.0 5.8 %copy-start.10 = (bf16[256,1536]{1,0:T(8,128)(2,1)}, bf16[256,1536]{1,0:T(8,128)(2,1)S(1)}, u32[]{:S(2)}) copy-start(bf16[256,1536]{1,0:T(8,128)(2,1)S(1)} %collective-permute-done.2.refs_1_.d1) | copy-start | bytes 2359300
  57.0 7.9 %copy-start.9 = (bf16[256,1536]{1,0:T(8,128)(2,1)S(1)}, bf16[256,1536]{1,0:T(8,128)(2,1)}, u32[]{:S(2)}) copy-start(bf16[256,1536]{1,0:T(8,128)(2,1)} %copy-done.8) | copy-start | bytes 2359300
  57.1 27.0 %collective-permute-start.9 = (bf16[256,1536]{1,0:T(8,128)(2,1)S(1)}, bf16[256,1536]{1,0:T(8,128)(2,1)}, u32[]{:S(2)}, u32[]{:S(2)}) collective-permute-start(bf16[256,1536]{1,0:T(8,128)(2,1)S(1)} %get-tuple-element.40.refs_0_.d0), channel_id=1, source_target_pairs={{0,32},{32,0},{1,33},{33,1},{2,34},{34,2},{3,35},{35,3},{4,36},{36... | collective-permute-start | bytes 2359304 | tf_op jit(solution)/shard_map/ppermute | solution.py:347
  65.0 39.1 %copy-start.13 = (bf16[768,384]{1,0:T(8,128)(2,1)}, bf16[768,384]{1,0:T(8,128)(2,1)S(1)}, u32[]{:S(2)}) copy-start(bf16[768,384]{1,0:T(8,128)(2,1)S(1)} %collective-permute-done.12.refs_6_) | copy-start | bytes 1769476
  65.0 28.7 %collective-permute-start.10 = (bf16[256,1536]{1,0:T(8,128)(2,1)S(1)}, bf16[256,1536]{1,0:T(8,128)(2,1)S(1)}, u32[]{:S(2)}, u32[]{:S(2)}) collective-permute-start(bf16[256,1536]{1,0:T(8,128)(2,1)S(1)} %copy-done.9), channel_id=1, source_target_pairs={{0,40},{8,32},{32,8},{40,0},{1,41},{9,33},{33,9},{41,1},{2,42},{10... | collective-permute-start | bytes 2359304 | tf_op jit(solution)/shard_map/ppermute | solution.py:348
  77.6 16.1 %collective-permute-start.20 = (bf16[1536,256]{1,0:T(8,128)(2,1)}, bf16[1536,256]{1,0:T(8,128)(2,1)S(1)}, u32[]{:S(2)}, u32[]{:S(2)}) collective-permute-start(bf16[1536,256]{1,0:T(8,128)(2,1)} %context_half.3.c0), channel_id=1, source_target_pairs={{0,8},{8,0},{1,9},{9,1},{2,10},{10,2},{3,11},{11,3},{4,12},{12,4},... | collective-permute-start | bytes 2359304 | tf_op jit(solution)/shard_map/ppermute | solution.py:359
  82.0 11.6 %collective-permute-start.21 = (bf16[1536,256]{1,0:T(8,128)(2,1)}, bf16[1536,256]{1,0:T(8,128)(2,1)}, u32[]{:S(2)}, u32[]{:S(2)}) collective-permute-start(bf16[1536,256]{1,0:T(8,128)(2,1)} %collective-permute-done.4.c2), channel_id=1, source_target_pairs={{0,8},{8,0},{1,9},{9,1},{2,10},{10,2},{3,11},{11,3},{4,12},{12,4},... | collective-permute-start | bytes 2359304 | tf_op jit(solution)/shard_map/ppermute | solution.py:360
  82.0 22.0 %collective-permute-start.13 = (bf16[768,384]{1,0:T(8,128)(2,1)}, bf16[768,384]{1,0:T(8,128)(2,1)}, u32[]{:S(2)}, u32[]{:S(2)}) collective-permute-start(bf16[768,384]{1,0:T(8,128)(2,1)} %collective-permute-done.11.refs_5_), channel_id=1, source_target_pairs={{0,1},{1,2},{2,3},{3,0},{4,5},{5,6},{6,7},{7,4},{8,9},{9,10},{10,1... | collective-permute-start | bytes 1769480 | tf_op jit(solution)/shard_map/ppermute | solution.py:356
  84.1 20.0 %collective-permute-start.16 = (bf16[768,384]{1,0:T(8,128)(2,1)}, bf16[768,384]{1,0:T(8,128)(2,1)}, u32[]{:S(2)}, u32[]{:S(2)}) collective-permute-start(bf16[768,384]{1,0:T(8,128)(2,1)} %collective-permute-done.15.refs_10_), channel_id=1, source_target_pairs={{0,3},{1,0},{2,1},{3,2},{4,7},{5,4},{6,5},{7,6},{8,11},{9,8},{10,9... | collective-permute-start | bytes 1769480 | tf_op jit(solution)/shard_map/ppermute | solution.py:357
  93.7 0.9 copy-start.11
  93.7 1.1 copy-start.12
  104.0 76.4 %all-to-all-start = ((bf16[16,4,24,1536]{3,2,1,0:T(8,128)(2,1)}), bf16[16,4,24,1536]{3,2,1,0:T(8,128)(2,1)}, u32[]{:S(2)}, u32[]{:S(2)}) async-start(bf16[16,4,24,1536]{3,2,1,0:T(8,128)(2,1)} %weight_gradient.1), calls=%async_computation | async-start | bytes 9437184 | tf_op jit(solution)/shard_map/all_to_all | solution.py:364
  125.1 2.6 %collective-permute-start.17 = (bf16[256,1536]{1,0:T(8,128)(2,1)}, bf16[256,1536]{1,0:T(8,128)(2,1)S(1)}, u32[]{:S(2)}, u32[]{:S(2)}) collective-permute-start(bf16[256,1536]{1,0:T(8,128)(2,1)} %get-tuple-element.44), channel_id=1, source_target_pairs={{0,8},{8,0},{1,9},{9,1},{2,10},{10,2},{3,11},{11,3},{4,12},{12,4},... | collective-permute-start | bytes 2359304 | tf_op jit(solution)/shard_map/ppermute | solution.py:368
  125.2 4.3 %collective-permute-start.19 = (bf16[256,1536]{1,0:T(8,128)(2,1)}, bf16[256,1536]{1,0:T(8,128)(2,1)S(1)}, u32[]{:S(2)}, u32[]{:S(2)}) collective-permute-start(bf16[256,1536]{1,0:T(8,128)(2,1)} %get-tuple-element.46), channel_id=1, source_target_pairs={{0,8},{8,0},{1,9},{9,1},{2,10},{10,2},{3,11},{11,3},{4,12},{12,4},... | collective-permute-start | bytes 2359304 | tf_op jit(solution)/shard_map/ppermute | solution.py:369
  129.3 19.2 %collective-permute-start.18 = (bf16[256,1536]{1,0:T(8,128)(2,1)S(1)}, bf16[256,1536]{1,0:T(8,128)(2,1)S(1)}, u32[]{:S(2)}, u32[]{:S(2)}) collective-permute-start(bf16[256,1536]{1,0:T(8,128)(2,1)S(1)} %add_convert_fusion), channel_id=1, source_target_pairs={{0,32},{32,0},{1,33},{33,1},{2,34},{34,2},{3,35},{35,3},{4,36},{36... | collective-permute-start | bytes 2359304 | tf_op jit(solution)/shard_map/ppermute | solution.py:370
  129.4 0.9 copy-start.5
  148.5 0.9 copy-start.6
  183.5 8.8 %collective-permute-start.22 = (bf16[24,1536]{1,0:T(8,128)(2,1)S(1)}, bf16[24,1536]{1,0:T(8,128)(2,1)S(1)}, u32[]{:S(2)}, u32[]{:S(2)}) collective-permute-start(bf16[24,1536]{1,0:T(8,128)(2,1)S(1)} %get-tuple-element.60), channel_id=1, source_target_pairs={{0,64},{64,128},{128,192},{192,0},{1,65},{65,129},{129,193},{193,1... | collective-permute-start | bytes 221192 | tf_op jit(solution)/shard_map/ppermute | solution.py:300
  189.0 4.2 %collective-permute-start.24 = (bf16[24,1536]{1,0:T(8,128)(2,1)S(1)}, bf16[24,1536]{1,0:T(8,128)(2,1)S(1)}, u32[]{:S(2)}, u32[]{:S(2)}) collective-permute-start(bf16[24,1536]{1,0:T(8,128)(2,1)S(1)} %get-tuple-element.61), channel_id=1, source_target_pairs={{0,192},{64,0},{128,64},{192,128},{1,193},{65,1},{129,65},{193,129... | collective-permute-start | bytes 221192 | tf_op jit(solution)/shard_map/ppermute | solution.py:300
  189.0 9.1 %collective-permute-start.23 = (bf16[24,1536]{1,0:T(8,128)(2,1)S(1)}, bf16[24,1536]{1,0:T(8,128)(2,1)S(1)}, u32[]{:S(2)}, u32[]{:S(2)}) collective-permute-start(bf16[24,1536]{1,0:T(8,128)(2,1)S(1)} %get-tuple-element.62), channel_id=1, source_target_pairs={{0,128},{64,192},{128,0},{192,64},{1,129},{65,193},{129,1},{193,65... | collective-permute-start | bytes 221192 | tf_op jit(solution)/shard_map/ppermute | solution.py:300
  198.1 2.2 %collective-permute-start.25 = (f32[12,1536]{1,0:T(8,128)S(1)}, f32[12,1536]{1,0:T(8,128)S(1)}, u32[]{:S(2)}, u32[]{:S(2)}) collective-permute-start(f32[12,1536]{1,0:T(8,128)S(1)} %get-tuple-element.64), channel_id=1, source_target_pairs={{0,8},{8,0},{1,9},{9,1},{2,10},{10,2},{3,11},{11,3},{4,12},{12,4},... | collective-permute-start | bytes 221192 | tf_op jit(solution)/shard_map/ppermute | solution.py:304
